TPU v7x, 32 devices: a whole 2x2x4 slice. The times are simulated.
32 devices in a mesh: dp: 4 (over x, core), tensor: 8 (over z, y).
Axes of the slice: x: 2, y: 2, z: 4, core: 2. Of those that a mesh axis runs over, the one named last changes fastest.
Arguments:
- activations: bfloat16 [512, 7168], P('dp', 'tensor'), may hold values from -6 to 6
- cotangent: bfloat16 [512, 7168], P('dp', 'tensor'), may hold values from -6 to 6
- up_weight_blocks: bfloat16 [1792, 128, 128], P('tensor'), may hold values from -0.125 to 0.125
- down_weight_blocks: bfloat16 [1792, 128, 128], P('tensor'), may hold values from -0.09375 to 0.09375
- up_first_moment: float32 [1792, 128, 128], P('tensor', 'dp'), may hold values from -60 to 60
- up_second_moment: float32 [1792, 128, 128], P('tensor', 'dp'), may hold values from 16 to 400
- down_first_moment: float32 [1792, 128, 128], P('tensor', 'dp'), may hold values from -60 to 60
- down_second_moment: float32 [1792, 128, 128], P('tensor', 'dp'), may hold values from 16 to 400
- source: int32 [1792], replicated, may hold values from -1 to 1791, as said below
- new_row: int32 [1792], P('tensor'), may hold values from 0 to 55, as said below
- new_col: int32 [1792], P('tensor'), may hold values from 0 to 127, as said below
- col_owner: int32 [128], replicated, may hold values from 0 to 7, as said below
Outputs:
- output: bfloat16 [512, 7168], P('dp', 'tensor')
- input_grad: bfloat16 [512, 7168], P('dp', 'tensor')
- up_step: float32 [1792, 128, 128], P('tensor', 'dp')
- down_step: float32 [1792, 128, 128], P('tensor', 'dp')
Inputs may be any that keep to these rules, and one draw needn't show every extreme that they name: source names each old slot (device of tensor * 224 + slot) at most once; the blocks that move from one device of tensor to another device number at most 28, and exactly 28 for some pairs in every draw; the share of regrown blocks differs from device to device. `new_row`: the blocks of one column block lie in distinct row blocks. `new_col`: every slot of a device of tensor holds a column block that col_owner gives to that device; a column block holds 1 to 27 blocks. `col_owner`: each device of tensor owns exactly 16 column blocks.
All inputs are finite; a program needn't handle non-finite values.
Results may differ from a plain program's by a relative error of at most 0.012.
Values may be sent and summed in bfloat16 or wider, within the bound.
No kernel may reach another device: no remote copies, remote signals or barrier semaphores. Data moves between devices by JAX's collectives and lax.ppermute only.
A program may use at most 256 MiB of HBM per device.

v0:
```python
import functools
import math

import jax
import jax.numpy as jnp
from jax import lax
from jax.experimental import pallas as pl
from jax.experimental.pallas import tpu as pltpu
from jax.sharding import PartitionSpec as P


gelu_scale = math.sqrt(2.0 / math.pi)
VMEM_LIMIT = 60 * 1024 * 1024

F32 = jnp.float32
BF16 = jnp.bfloat16
ANY = pl.BlockSpec(memory_space=pl.ANY)


def gelu_pair(pre_act):
    inner = gelu_scale * (pre_act + 0.044715 * pre_act * pre_act * pre_act)
    tangent = jnp.tanh(inner)
    gelu_value = 0.5 * pre_act * (1.0 + tangent)
    gelu_slope = 0.5 * (1.0 + tangent) + 0.5 * pre_act * (1.0 - tangent * tangent) * gelu_scale * (
        1.0 + 3.0 * 0.044715 * pre_act * pre_act
    )
    return (gelu_value, gelu_slope)


def local_columns(col_owner):
    count_all = col_owner.shape[0]
    order = jnp.arange(count_all, dtype=jnp.int32)
    same = (col_owner[None, :] == col_owner[:, None]) & (order[None, :] < order[:, None])
    return jnp.sum(same.astype(jnp.int32), axis=1)


def pack_weight(tiles, send_slots, dp_index, rows):
    slots, _, width = tiles.shape
    count = send_slots.shape[0]

    def kernel(send_ref, dp_ref, in_ref, out_ref):
        def step(i, carry):
            out_ref[i] = in_ref[send_ref[i]]
            return carry

        lax.fori_loop(0, count, step, 0, unroll=8)

    return pl.pallas_call(
        kernel,
        out_shape=jax.ShapeDtypeStruct((count, rows, width), tiles.dtype),
        grid_spec=pltpu.PrefetchScalarGridSpec(
            num_scalar_prefetch=2,
            grid=(1,),
            in_specs=[pl.BlockSpec((slots, rows, width), lambda i, s, d: (0, d[0], 0))],
            out_specs=pl.BlockSpec((count, rows, width), lambda i, s, d: (0, 0, 0)),
        ),
        compiler_params=pltpu.CompilerParams(vmem_limit_bytes=VMEM_LIMIT),
        cost_estimate=pl.CostEstimate(flops=0, transcendentals=0, bytes_accessed=4 * count * rows * width),
        name="pack_weight",
    )(send_slots, dp_index, tiles)


def pack_moments(arrays, send_slots):
    slots, rows, width = arrays[0].shape
    count = send_slots.shape[0]
    kinds = len(arrays)

    def kernel(send_ref, *refs):
        out_ref = refs[-1]

        def step(i, carry):
            s = send_ref[i]
            for k in range(kinds):
                out_ref[i, k] = refs[k][s].astype(BF16)
            return carry

        lax.fori_loop(0, count, step, 0, unroll=4)

    whole = pl.BlockSpec((slots, rows, width), lambda i, s: (0, 0, 0))
    return pl.pallas_call(
        kernel,
        out_shape=jax.ShapeDtypeStruct((count, kinds, rows, width), BF16),
        grid_spec=pltpu.PrefetchScalarGridSpec(
            num_scalar_prefetch=1,
            grid=(1,),
            in_specs=[whole] * kinds,
            out_specs=pl.BlockSpec((count, kinds, rows, width), lambda i, s: (0, 0, 0, 0)),
        ),
        compiler_params=pltpu.CompilerParams(vmem_limit_bytes=VMEM_LIMIT),
        cost_estimate=pl.CostEstimate(
            flops=0, transcendentals=0, bytes_accessed=6 * kinds * count * rows * width
        ),
        name="pack_moments",
    )(send_slots, *arrays)


def columns(ref, r, block):
    per = ref.shape[2] // block
    a = lax.div(r, per)
    off = pl.multiple_of((r - a * per) * block, block)
    return ref[a, :, pl.ds(off, block)]


def weight(own, came, home_ref, came_ref, kind_ref, g):
    kind = kind_ref[g]
    mine = own[home_ref[g]]
    at = came_ref[g]
    theirs = jnp.concatenate([came[q, at] for q in range(came.shape[0])], axis=0)
    picked = lax.select(kind == 1, mine, theirs)
    return lax.select(kind == 0, jnp.zeros_like(picked), picked)


def feature_copies(parts, which, place_ref, buf, sem):
    copies = []
    for m, part in enumerate(parts):
        at = (place_ref[2] ^ m) if len(parts) > 1 else 0
        copies.append(pltpu.make_async_copy(part.at[which], buf.at[at], sem.at[m]))
    return copies


def weight_copies(own, own_v, parts, parts_v, place_ref, sem):
    n_dp = len(parts)
    nx = n_dp // 2
    copies = [pltpu.make_async_copy(own, own_v, sem.at[0])]
    for j in range(nx):
        for other in range(2):
            k = 2 * j + other
            owner = lax.rem(place_ref[0] + nx - j, nx) * 2 + (place_ref[1] + other) % 2
            copies.append(pltpu.make_async_copy(parts[k], parts_v.at[owner], sem.at[1 + k]))
    return copies


def forward_kernel(n_feat, n_dp, row_blocks, *refs):
    row_ref, col_ref, home_ref, came_ref, kind_ref, place_ref = refs[:6]
    feats = refs[6 : 6 + n_feat]
    up_hbm = refs[6 + n_feat]
    parts = refs[7 + n_feat : 7 + n_feat + n_dp]
    pre, x_t, wu_hbm, x_v, up_v, up_a, wu, feat_sem, in_sem, out_sem = refs[7 + n_feat + n_dp :]
    slots, block, _ = up_v.shape
    copies = feature_copies(feats, 0, place_ref, x_v, feat_sem)
    copies += weight_copies(up_hbm, up_v, parts, up_a, place_ref, in_sem)
    for copy in copies:
        copy.start()
    pre[...] = jnp.zeros(pre.shape, F32)
    for copy in copies:
        copy.wait()
    unroll = 4

    def step(i, carry):
        got = []
        for u in range(unroll):
            g = i * unroll + u
            w = weight(up_v, up_a, home_ref, came_ref, kind_ref, g)
            wu[g] = w
            got.append(jnp.dot(columns(x_v, row_ref[g], block), w, preferred_element_type=F32))
        for u in range(unroll):
            c = col_ref[i * unroll + u]
            pre[c] = pre[c] + got[u]
        return carry

    lax.fori_loop(0, slots // unroll, step, 0)
    keep = pltpu.make_async_copy(wu, wu_hbm, out_sem)
    keep.start()

    def turn(r, carry):
        x_t[r] = columns(x_v, r, block).T
        return carry

    lax.fori_loop(0, row_blocks, turn, 0)
    keep.wait()


def gradient_kernel(n_feat, n_dp, *refs):
    row_ref, col_ref, home_ref, came_ref, kind_ref, place_ref = refs[:6]
    feats = refs[6 : 6 + n_feat]
    down_hbm = refs[6 + n_feat]
    parts = refs[7 + n_feat : 7 + n_feat + n_dp]
    pre, x_t = refs[7 + n_feat + n_dp : 9 + n_feat + n_dp]
    outs = refs[9 + n_feat + n_dp :]
    act, bpre, wd_hbm = outs[:3]
    grad_refs = outs[3 : 3 + n_dp]
    back_v, down_v, down_a, wd, back, act_t, stage, feat_sem, in_sem, keep_sem, out_sem = outs[3 + n_dp :]
    slots, block, _ = down_v.shape
    rows = block // n_dp
    nx = n_dp // 2
    chunk = stage.shape[2]
    copies = feature_copies(feats, 1, place_ref, back_v, feat_sem)
    copies += weight_copies(down_hbm, down_v, parts, down_a, place_ref, in_sem)
    for copy in copies:
        copy.start()
    back[...] = jnp.zeros(back.shape, F32)
    for copy in copies:
        copy.wait()
    unroll = 4

    def backward(i, carry):
        got = []
        for u in range(unroll):
            g = i * unroll + u
            w = weight(down_v, down_a, home_ref, came_ref, kind_ref, g)
            wd[g] = w
            got.append(
                lax.dot_general(
                    columns(back_v, row_ref[g], block), w, (((1,), (1,)), ((), ())), preferred_element_type=F32
                )
            )
        for u in range(unroll):
            c = col_ref[i * unroll + u]
            back[c] = back[c] + got[u]
        return carry

    lax.fori_loop(0, slots // unroll, backward, 0)
    keep = pltpu.make_async_copy(wd, wd_hbm, keep_sem)
    keep.start()

    def bend(c, carry):
        value, slope = gelu_pair(pre[c])
        narrow = value.astype(BF16)
        act[c] = narrow
        act_t[c] = narrow.T
        bpre[c] = (back[c] * slope).astype(BF16)
        return carry

    lax.fori_loop(0, pre.shape[0], bend, 0)

    def ship(i, slot):
        out = []
        for j in range(nx):
            for other in range(2):
                owner = lax.rem(place_ref[0] + j, nx) * 2 + (place_ref[1] + other) % 2
                start = pl.multiple_of(owner * rows, rows)
                for p in range(2):
                    out.append(
                        pltpu.make_async_copy(
                            stage.at[slot, p, :, pl.ds(start, rows), :],
                            grad_refs[2 * j + other].at[p, pl.ds(i * chunk, chunk)],
                            out_sem.at[slot, 2 * (2 * j + other) + p],
                        )
                    )
        return out

    def last(i, carry):
        slot = lax.rem(i, 2)

        @pl.when(i >= 2)
        def _():
            for copy in ship(i - 2, slot):
                copy.wait()

        for u in range(chunk):
            g = i * chunk + u
            r = row_ref[g]
            c = col_ref[g]
            stage[slot, 0, u] = jnp.dot(x_t[r], bpre[c], preferred_element_type=F32).astype(BF16)
            stage[slot, 1, u] = jnp.dot(
                act_t[c], columns(back_v, r, block), preferred_element_type=F32
            ).astype(BF16)
        for copy in ship(i, slot):
            copy.start()
        return carry

    chunks = slots // chunk
    lax.fori_loop(0, chunks, last, 0)
    for i in range(max(chunks - 2, 0), chunks):
        for copy in ship(i, i % 2):
            copy.wait()
    keep.wait()


def output_kernel(pieces, *refs):
    row_ref, col_ref, place_ref = refs[:3]
    wu_hbm, wd_hbm, act, bpre = refs[3:7]
    outs = refs[7 : 7 + len(pieces)]
    wu, wd, out_acc, in_acc, staged, in_sem, out_sem = refs[7 + len(pieces) :]
    slots, block, _ = wu.shape
    parts = 4
    some = slots // parts
    loads = []
    for k in range(parts):
        for hbm, buf, s in ((wd_hbm, wd, 0), (wu_hbm, wu, 1)):
            at = pl.ds(k * some, some)
            loads.append(pltpu.make_async_copy(hbm.at[at], buf.at[at], in_sem.at[2 * k + s]))
    for copy in loads:
        copy.start()
    out_acc[...] = jnp.zeros(out_acc.shape, F32)
    in_acc[...] = jnp.zeros(in_acc.shape, F32)
    unroll = 2

    def step(i, carry):
        got = []
        for u in range(unroll):
            g = i * unroll + u
            r = row_ref[g]
            c = col_ref[g]
            got.append(
                (
                    r,
                    jnp.dot(act[c], wd[g], preferred_element_type=F32),
                    lax.dot_general(bpre[c], wu[g], (((1,), (1,)), ((), ())), preferred_element_type=F32),
                )
            )
        for r, o, n in got:
            out_acc[r] = out_acc[r] + o
            in_acc[r] = in_acc[r] + n
        return carry

    for k in range(parts):
        loads[2 * k].wait()
        loads[2 * k + 1].wait()
        lax.fori_loop(k * some // unroll, (k + 1) * some // unroll, step, 0)

    count = staged.shape[0]
    per = staged.shape[3] // block
    bits = count.bit_length() - 1
    for a in range(count):
        if count == 1:
            at = 0
        else:
            far = place_ref[2] ^ a
            at = 0
            for b in range(bits):
                at = at + ((far >> b) & 1) * (count >> (b + 1))
        for q in range(per):
            staged[at, 0, :, q * block : (q + 1) * block] = out_acc[a * per + q].astype(BF16)
            staged[at, 1, :, q * block : (q + 1) * block] = in_acc[a * per + q].astype(BF16)
    copies = [
        pltpu.make_async_copy(staged.at[pl.ds(start, size)], out, out_sem.at[k])
        for k, ((start, size), out) in enumerate(zip(pieces, outs))
    ]
    for copy in copies:
        copy.start()
    for copy in copies:
        copy.wait()


VMEM = pl.BlockSpec(memory_space=pltpu.VMEM)
SMEM = pl.BlockSpec(memory_space=pltpu.SMEM)


def cost(flops, size):
    return pl.CostEstimate(flops=flops, transcendentals=0, bytes_accessed=size)


def forward_products(tables, place, feats, up, parts, col_count, row_blocks, feat_shape):
    slots, block, _ = up.shape
    n_dp, n_feat = len(parts), len(feats)
    tokens = feat_shape[1]
    return pl.pallas_call(
        functools.partial(forward_kernel, n_feat, n_dp, row_blocks),
        out_shape=[
            jax.ShapeDtypeStruct((col_count, tokens, block), F32),
            jax.ShapeDtypeStruct((row_blocks, block, tokens), BF16),
            jax.ShapeDtypeStruct(up.shape, BF16),
        ],
        in_specs=[SMEM] * 6 + [ANY] * (n_feat + 1 + n_dp),
        out_specs=[VMEM, VMEM, ANY],
        scratch_shapes=[
            pltpu.VMEM(feat_shape, BF16),
            pltpu.VMEM(up.shape, BF16),
            pltpu.VMEM((n_dp,) + parts[0].shape, BF16),
            pltpu.VMEM(up.shape, BF16),
            pltpu.SemaphoreType.DMA((n_feat,)),
            pltpu.SemaphoreType.DMA((1 + n_dp,)),
            pltpu.SemaphoreType.DMA,
        ],
        compiler_params=pltpu.CompilerParams(vmem_limit_bytes=VMEM_LIMIT),
        cost_estimate=cost(2 * slots * tokens * block * block, 12 * slots * block * block),
        name="forward_products",
    )(*tables, place, *feats, up, *parts)


def gradient_products(tables, place, feats, down, parts, pre, x_t, feat_shape):
    slots, block, _ = down.shape
    n_dp, n_feat = len(parts), len(feats)
    rows = block // n_dp
    chunk = 8
    col_count, tokens, _ = pre.shape
    grad = jax.ShapeDtypeStruct((2, slots, rows, block), BF16)
    return pl.pallas_call(
        functools.partial(gradient_kernel, n_feat, n_dp),
        out_shape=[jax.ShapeDtypeStruct(pre.shape, BF16)] * 2
        + [jax.ShapeDtypeStruct(down.shape, BF16)]
        + [grad] * n_dp,
        in_specs=[SMEM] * 6 + [ANY] * (n_feat + 1 + n_dp) + [VMEM] * 2,
        out_specs=[VMEM, VMEM] + [ANY] * (1 + n_dp),
        scratch_shapes=[
            pltpu.VMEM(feat_shape, BF16),
            pltpu.VMEM(down.shape, BF16),
            pltpu.VMEM((n_dp,) + parts[0].shape, BF16),
            pltpu.VMEM(down.shape, BF16),
            pltpu.VMEM(pre.shape, F32),
            pltpu.VMEM((col_count, block, tokens), BF16),
            pltpu.VMEM((2, 2, chunk, block, block), BF16),
            pltpu.SemaphoreType.DMA((n_feat,)),
            pltpu.SemaphoreType.DMA((1 + n_dp,)),
            pltpu.SemaphoreType.DMA,
            pltpu.SemaphoreType.DMA((2, 2 * n_dp)),
        ],
        compiler_params=pltpu.CompilerParams(vmem_limit_bytes=VMEM_LIMIT),
        cost_estimate=cost(6 * slots * tokens * block * block, 20 * slots * block * block),
        name="gradient_products",
    )(*tables, place, *feats, down, *parts, pre, x_t)


def output_products(row, col, place, wu, wd, act, bpre, pieces, feat_shape, row_blocks):
    slots, block, _ = wu.shape
    count, tokens, shard = feat_shape
    return pl.pallas_call(
        functools.partial(output_kernel, pieces),
        out_shape=[jax.ShapeDtypeStruct((size, 2, tokens, shard), BF16) for _, size in pieces],
        in_specs=[SMEM] * 3 + [ANY] * 2 + [VMEM] * 2,
        out_specs=[ANY] * len(pieces),
        scratch_shapes=[
            pltpu.VMEM(wu.shape, BF16),
            pltpu.VMEM(wd.shape, BF16),
            pltpu.VMEM((row_blocks, tokens, block), F32),
            pltpu.VMEM((row_blocks, tokens, block), F32),
            pltpu.VMEM((count, 2, tokens, shard), BF16),
            pltpu.SemaphoreType.DMA((8,)),
            pltpu.SemaphoreType.DMA((len(pieces),)),
        ],
        compiler_params=pltpu.CompilerParams(vmem_limit_bytes=VMEM_LIMIT),
        cost_estimate=cost(4 * slots * tokens * block * block, 8 * slots * block * block),
        name="output_products",
    )(row, col, place, wu, wd, act, bpre)


def adam_step(tables, grads, which, moments, arrived):
    slots, rows, block = moments[0].shape
    n_grads = len(grads)

    def kernel(home_ref, came_ref, kind_ref, *refs):
        grad_refs = refs[:n_grads]
        moment_refs = refs[n_grads : n_grads + 2]
        arrived_ref = refs[n_grads + 2]
        out = refs[n_grads + 3]

        def step(g, carry):
            at = came_ref[g]
            own = home_ref[g]
            kind = kind_ref[g]

            def moved(k):
                picked = lax.select(kind == 1, moment_refs[k][own], arrived_ref[at, k].astype(F32))
                return lax.select(kind == 0, jnp.zeros_like(picked), picked)

            total = grad_refs[0][0, g].astype(F32)
            for ref in grad_refs[1:]:
                total = total + ref[0, g].astype(F32)
            first = 0.9 * moved(0) + 0.1 * total
            second = 0.95 * moved(1) + 0.05 * total * total
            out[g] = first / (jnp.sqrt(second) + 1.0)
            return carry

        lax.fori_loop(0, slots, step, 0, unroll=4)

    half = pl.BlockSpec((1, slots, rows, block), lambda i: (which, 0, 0, 0))

    def whole(array):
        return pl.BlockSpec(array.shape, lambda i: (0,) * array.ndim)

    return pl.pallas_call(
        kernel,
        out_shape=jax.ShapeDtypeStruct(moments[0].shape, F32),
        grid=(1,),
        in_specs=[SMEM] * 3 + [half] * n_grads + [whole(m) for m in moments] + [whole(arrived)],
        out_specs=whole(moments[0]),
        compiler_params=pltpu.CompilerParams(vmem_limit_bytes=VMEM_LIMIT),
        cost_estimate=cost(15 * slots * rows * block, 17 * slots * rows * block),
        name="adam_step",
    )(*tables, *grads, *moments, arrived)


def layer(
    activations,
    cotangent,
    up_weight_blocks,
    down_weight_blocks,
    up_first_moment,
    up_second_moment,
    down_first_moment,
    down_second_moment,
    source,
    new_row,
    new_col,
    col_owner,
):
    tensor_size = lax.axis_size("tensor")
    n_dp = lax.axis_size("dp")
    nx = n_dp // 2
    my_index = lax.axis_index("tensor")
    my_dp = lax.axis_index("dp")
    slot_count, block, _ = up_weight_blocks.shape
    rows = block // n_dp
    bucket = (slot_count + tensor_size - 2) // tensor_size

    sources = source.reshape(tensor_size, slot_count)
    is_live = sources >= 0
    sender_dev = jnp.where(is_live, sources // slot_count, -1)
    sender_slot = jnp.where(is_live, sources % slot_count, 0)
    targets = jnp.arange(tensor_size, dtype=jnp.int32)[:, None]
    outgoing = is_live & (sender_dev == my_index) & (targets != my_index)
    out_flags = outgoing.astype(jnp.int32)
    out_rank = jnp.cumsum(out_flags, axis=1) - out_flags
    chosen = outgoing[:, :, None] & (
        out_rank[:, :, None] == jnp.arange(bucket, dtype=jnp.int32)[None, None, :]
    )
    send_slots = jnp.sum(jnp.where(chosen, sender_slot[:, :, None], 0), axis=1).reshape(-1)
    mine_dev = lax.dynamic_index_in_dim(sender_dev, my_index, 0, keepdims=False)
    mine_slot = lax.dynamic_index_in_dim(sender_slot, my_index, 0, keepdims=False)
    mine_live = mine_dev >= 0
    stays = mine_live & (mine_dev == my_index)
    positions = jnp.arange(slot_count, dtype=jnp.int32)
    earlier = (
        (mine_dev[:, None] == mine_dev[None, :])
        & mine_live[None, :]
        & (positions[None, :] < positions[:, None])
    )
    recv_rank = jnp.minimum(jnp.sum(earlier.astype(jnp.int32), axis=1), bucket - 1)
    home = jnp.where(stays, mine_slot, 0)
    came = jnp.where(mine_live & ~stays, mine_dev * bucket + recv_rank, 0)
    kind = jnp.where(stays, 1, jnp.where(mine_live, 2, 0)).astype(jnp.int32)
    col_count = col_owner.shape[0] // tensor_size
    col_slot = jnp.take(local_columns(col_owner), new_col)
    place = jnp.stack([my_dp // 2, my_dp % 2, my_index]).astype(jnp.int32)
    dp_index = my_dp.reshape(1).astype(jnp.int32)
    tables = (new_row, col_slot, home, came, kind)

    def exchange(packed):
        shaped = packed.reshape((tensor_size, bucket) + packed.shape[1:])
        got = lax.all_to_all(shaped, "tensor", split_axis=0, concat_axis=0, tiled=True)
        return got.reshape((tensor_size * bucket,) + packed.shape[1:])

    core_pairs = [(d, d ^ 1) for d in range(n_dp)]

    def x_pairs(j):
        return [(d, ((d // 2 + j) % nx) * 2 + d % 2) for d in range(n_dp)]

    def far_pairs(bit):
        return [(t, t ^ bit) for t in range(tensor_size)]

    def spread(own):
        parts = []
        for j in range(nx):
            mine = own
            if j:
                mine = lax.ppermute(own, "dp", x_pairs(j))
            parts += [mine, lax.ppermute(mine, "dp", core_pairs)]
        return parts

    up_pack = pack_weight(up_weight_blocks, send_slots, dp_index, rows)
    down_pack = pack_weight(down_weight_blocks, send_slots, dp_index, rows)
    up_in = exchange(up_pack)
    down_in = exchange(down_pack)
    up_parts = spread(up_in)
    down_parts = spread(down_in)

    shard = activations.shape[1]
    stacked = shard % block == 0 and tensor_size & (tensor_size - 1) == 0
    if stacked:
        bits = [1 << k for k in reversed(range(tensor_size.bit_length() - 1))]
        held = {0: jnp.stack([activations, cotangent])}
        for bit in bits:
            for m in list(held):
                held[m ^ bit] = lax.ppermute(held[m], "tensor", far_pairs(bit))
        feats = [held[m] for m in range(tensor_size)]
        feat_shape = (tensor_size,) + activations.shape
    else:
        x = lax.all_gather(activations, "tensor", axis=1, tiled=True)
        back = lax.all_gather(cotangent, "tensor", axis=1, tiled=True)
        feats = [jnp.stack([x, back])[:, None].reshape((2,) + x.shape)]
        feat_shape = (1,) + x.shape
    row_blocks = feat_shape[0] * feat_shape[2] // block

    ups = (up_first_moment, up_second_moment)
    downs = (down_first_moment, down_second_moment)
    ups_pack = pack_moments(ups, send_slots)
    downs_pack = pack_moments(downs, send_slots)
    ups_in = exchange(ups_pack)
    downs_in = exchange(downs_pack)

    pre, x_t, wu = forward_products(
        tables, place, feats, up_weight_blocks, up_parts, col_count, row_blocks, feat_shape
    )
    act, bpre, wd, *grads = gradient_products(
        tables, place, feats, down_weight_blocks, down_parts, pre, x_t, feat_shape
    )
    terms = []
    for j in range(nx):
        there = lax.ppermute(grads[2 * j + 1], "dp", core_pairs)
        if j == 0:
            terms += [grads[0], there]
        else:
            both = (grads[2 * j].astype(F32) + there.astype(F32)).astype(BF16)
            terms.append(lax.ppermute(both, "dp", x_pairs(j)))

    if stacked:
        half = tensor_size // 2
        keep, send = output_products(
            new_row, col_slot, place, wu, wd, act, bpre, ((0, half), (half, half)), feat_shape, row_blocks
        )
        sums = [keep]
        bit = 1
        while True:
            sums.append(lax.ppermute(send, "tensor", far_pairs(bit)))
            bit *= 2
            if bit >= tensor_size:
                break
            half = sums[-1].shape[0] // 2
            total = sum(s[half : 2 * half].astype(F32) for s in sums)
            send = total.astype(BF16)
            sums = [s[:half] for s in sums]
        total = sum(s[0].astype(F32) for s in sums).astype(BF16)
        out_sum, in_sum = total[0], total[1]
    else:
        (whole,) = output_products(
            new_row, col_slot, place, wu, wd, act, bpre, ((0, 1),), feat_shape, row_blocks
        )
        out_sum = lax.psum_scatter(whole[0, 0], "tensor", scatter_dimension=1, tiled=True)
        in_sum = lax.psum_scatter(whole[0, 1], "tensor", scatter_dimension=1, tiled=True)

    up_step = adam_step((home, came, kind), terms, 0, ups, ups_in)
    down_step = adam_step((home, came, kind), terms, 1, downs, downs_in)
    return (out_sum, in_sum, up_step, down_step)


def solution(mesh):
    placed = (
        P("dp", "tensor"),
        P("dp", "tensor"),
        P("tensor", None, None),
        P("tensor", None, None),
        P("tensor", "dp", None),
        P("tensor", "dp", None),
        P("tensor", "dp", None),
        P("tensor", "dp", None),
        P(),
        P("tensor"),
        P("tensor"),
        P(),
    )
    return jax.shard_map(
        layer,
        mesh=mesh,
        in_specs=placed,
        out_specs=(
            P("dp", "tensor"),
            P("dp", "tensor"),
            P("tensor", "dp", None),
            P("tensor", "dp", None),
        ),
        check_vma=False,
    )
```

profile of v0, /device:TPU:0, one launch (start us, length us, event | category | flops | bytes accessed | tf_op | source)
XLA Modules:
  0.0 483.8 jit_solution(14000386256109057387)
XLA Ops:
  0.6 0.7 sign_compare_fusion
  1.3 0.7 broadcast_divide_fusion
  2.5 0.6 reduce-window.6
  3.4 0.6 select_reduce_fusion
  4.0 0.6 reshape.137.send_ref
  4.7 3.8 pack_weight.2
  8.5 7.3 %all-to-all-start = ((bf16[8,28,32,128]{3,2,1,0:T(8,128)(2,1)}), bf16[8,28,32,128]{3,2,1,0:T(8,128)(2,1)S(1)}, u32[]{:S(2)}, u32[]{:S(2)}) async-start(bf16[8,28,32,128]{3,2,1,0:T(8,128)(2,1)} %bitcast.30), calls=%async_computation | async-start | bytes 3670016 | tf_op jit(solution)/shard_map/all_to_all | solution.py:531
  15.8 3.8 pack_weight.3
  19.6 38.8 %all-to-all-done = bf16[8,28,32,128]{3,2,1,0:T(8,128)(2,1)S(1)} async-done(((bf16[8,28,32,128]{3,2,1,0:T(8,128)(2,1)}), bf16[8,28,32,128]{3,2,1,0:T(8,128)(2,1)S(1)}, u32[]{:S(2)}, u32[]{:S(2)}) %all-to-all-start) | async-done | bytes 1835040 | tf_op jit(solution)/shard_map/all_to_all | solution.py:531
  58.4 4.3 all-to-all-start.1
  62.7 6.4 %pack_moments.2 = bf16[224,2,32,128]{3,2,1,0:T(8,128)(2,1)} custom-call(s32[224]{0:T(256)} %reshape.137.send_ref, f32[224,32,128]{2,1,0:T(8,128)} %refs_3_.2, f32[224,32,128]{2,1,0:T(8,128)} %refs_4_.2), custom_call_target="tpu_custom_call" | custom-call | bytes 11010048 | tf_op jit(solution)/shard_map/pack_moments/pallas_call | solution.py:80
  69.1 35.9 %all-to-all-done.1 = bf16[8,28,32,128]{3,2,1,0:T(8,128)(2,1)} async-done(((bf16[8,28,32,128]{3,2,1,0:T(8,128)(2,1)}), bf16[8,28,32,128]{3,2,1,0:T(8,128)(2,1)}, u32[]{:S(2)}, u32[]{:S(2)}) %all-to-all-start.1) | async-done | bytes 1835040 | tf_op jit(solution)/shard_map/all_to_all | solution.py:531
  105.0 4.7 all-to-all-start.2
  109.6 1.6 collective-permute-start.8
  111.2 0.5 collective-permute-start.11
  111.8 1.9 collective-permute-start.1
  113.7 1.5 collective-permute-start
  115.2 2.4 collective-permute-start.3
  117.6 62.9 %collective-permute-done.1.refs_8_ = bf16[2,128,896]{2,1,0:T(8,128)(2,1)S(1)} collective-permute-done((bf16[2,128,896]{2,1,0:T(8,128)(2,1)S(1)}, bf16[2,128,896]{2,1,0:T(8,128)(2,1)S(1)}, u32[]{:S(2)}, u32[]{:S(2)}) %collective-permute-start.1) | collective-permute-done | bytes 458784 | tf_op jit(solution)/shard_map/ppermute | solution.py:565
  180.5 1.7 collective-permute-start.2
  182.8 27.8 %collective-permute-done.3.refs_10_ = bf16[2,128,896]{2,1,0:T(8,128)(2,1)} collective-permute-done((bf16[2,128,896]{2,1,0:T(8,128)(2,1)S(1)}, bf16[2,128,896]{2,1,0:T(8,128)(2,1)}, u32[]{:S(2)}, u32[]{:S(2)}) %collective-permute-start.3) | collective-permute-done | bytes 458784 | tf_op jit(solution)/shard_map/ppermute | solution.py:565
  211.2 0.8 copy-done.6
  211.9 1.5 collective-permute-start.4
  213.4 11.3 %collective-permute-done.4.refs_11_ = bf16[2,128,896]{2,1,0:T(8,128)(2,1)} collective-permute-done((bf16[2,128,896]{2,1,0:T(8,128)(2,1)}, bf16[2,128,896]{2,1,0:T(8,128)(2,1)}, u32[]{:S(2)}, u32[]{:S(2)}) %collective-permute-start.4) | collective-permute-done | bytes 458784 | tf_op jit(solution)/shard_map/ppermute | solution.py:565
  225.1 11.5 %collective-permute-done.5.refs_12_ = bf16[2,128,896]{2,1,0:T(8,128)(2,1)} collective-permute-done((bf16[2,128,896]{2,1,0:T(8,128)(2,1)}, bf16[2,128,896]{2,1,0:T(8,128)(2,1)}, u32[]{:S(2)}, u32[]{:S(2)}) %collective-permute-start.5) | collective-permute-done | bytes 458784 | tf_op jit(solution)/shard_map/ppermute | solution.py:565
  236.6 1.5 collective-permute-start.6
  238.0 0.6 pad_add_fusion.refs_5_.refs_2_
  238.6 1.9 gather_fusion
  240.5 0.6 and_select_fusion.1.refs_1_
  241.0 0.6 select_select_fusion
  241.6 6.0 %collective-permute-done.6.refs_13_ = bf16[2,128,896]{2,1,0:T(8,128)(2,1)} collective-permute-done((bf16[2,128,896]{2,1,0:T(8,128)(2,1)}, bf16[2,128,896]{2,1,0:T(8,128)(2,1)}, u32[]{:S(2)}, u32[]{:S(2)}) %collective-permute-start.6) | collective-permute-done | bytes 458784 | tf_op jit(solution)/shard_map/ppermute | solution.py:565
  247.6 23.3 %forward_products.1 = (f32[16,128,128]{2,1,0:T(8,128)}, bf16[56,128,128]{2,1,0:T(8,128)(2,1)}, bf16[224,128,128]{2,1,0:T(8,128)(2,1)}) custom-call(s32[224]{0:T(256)} %refs_0_.7, s32[224]{0:T(256)} %and_select_fusion.1.refs_1_, s32[224]{0:T(256)} %get-tuple-element.41.refs_2_.home_ref, s32[224]{0:T(256)} %get-tuple-element.40.refs_3_.came_ref, ...), custom_call_target="tpu_custom_call" | custom-call | flops 939524096 | bytes 44040192 | tf_op jit(solution)/shard_map/forward_products/pallas_call | solution.py:348
  271.0 38.5 %gradient_products.1 = (bf16[16,128,128]{2,1,0:T(8,128)(2,1)}, bf16[16,128,128]{2,1,0:T(8,128)(2,1)}, bf16[224,128,128]{2,1,0:T(8,128)(2,1)}, bf16[2,224,32,128]...) custom-call(s32[224]{0:T(256)} %refs_0_.7, ...), custom_call_target="tpu_custom_call" | custom-call | flops 2818572288 | bytes 73400320 | tf_op jit(solution)/shard_map/gradient_products/pallas_call | solution.py:379
  309.5 6.4 %pack_moments.3 = bf16[224,2,32,128]{3,2,1,0:T(8,128)(2,1)} custom-call(s32[224]{0:T(256)} %reshape.137.send_ref, f32[224,32,128]{2,1,0:T(8,128)} %refs_3_.3, f32[224,32,128]{2,1,0:T(8,128)} %refs_4_.3), custom_call_target="tpu_custom_call" | custom-call | bytes 11010048 | tf_op jit(solution)/shard_map/pack_moments/pallas_call | solution.py:80
  315.9 4.5 all-to-all-start.3
  320.4 28.1 %output_products.1 = (bf16[4,2,128,896]{3,2,1,0:T(8,128)(2,1)}, bf16[4,2,128,896]{3,2,1,0:T(8,128)(2,1)}) custom-call(s32[224]{0:T(256)} %refs_0_.7, s32[224]{0:T(256)} %and_select_fusion.1.refs_1_, s32[3]{0:T(128)} %pad_add_fusion.refs_5_.refs_2_, bf16[224,128,128]{2,1,0:T(8,128)(2,1)} %get-tuple-element.16.refs_3_, ...), custom_call_target="tpu_custom_call" | custom-call | flops 1879048192 | bytes 29360128 | tf_op jit(solution)/shard_map/output_products/pallas_call | solution.py:408
  348.6 2.0 collective-permute-start.13
  350.5 4.2 add_convert_fusion
  354.7 1.6 collective-permute-start.18
  356.3 52.6 %collective-permute-done.13 = bf16[4,2,128,896]{3,2,1,0:T(8,128)(2,1)S(1)} collective-permute-done((bf16[4,2,128,896]{3,2,1,0:T(8,128)(2,1)}, bf16[4,2,128,896]{3,2,1,0:T(8,128)(2,1)S(1)}, u32[]{:S(2)}, u32[]{:S(2)}) %collective-permute-start.13) | collective-permute-done | bytes 1835040 | tf_op jit(solution)/shard_map/ppermute | solution.py:605
  409.2 3.7 collective-permute-start.14
  412.8 20.0 %collective-permute-done.14 = bf16[2,2,128,896]{3,2,1,0:T(8,128)(2,1)S(1)} collective-permute-done((bf16[2,2,128,896]{3,2,1,0:T(8,128)(2,1)S(1)}, bf16[2,2,128,896]{3,2,1,0:T(8,128)(2,1)S(1)}, u32[]{:S(2)}, u32[]{:S(2)}) %collective-permute-start.14) | collective-permute-done | bytes 917536 | tf_op jit(solution)/shard_map/ppermute | solution.py:605
  433.0 4.0 collective-permute-start.15
  436.9 20.2 %collective-permute-done.15 = bf16[1,2,128,896]{3,2,1,0:T(8,128)(2,1)S(1)} collective-permute-done((bf16[1,2,128,896]{3,2,1,0:T(8,128)(2,1)S(1)}, bf16[1,2,128,896]{3,2,1,0:T(8,128)(2,1)S(1)}, u32[]{:S(2)}, u32[]{:S(2)}) %collective-permute-start.15) | collective-permute-done | bytes 458784 | tf_op jit(solution)/shard_map/ppermute | solution.py:605
  457.4 0.8 slice_bitcast_fusion
  458.2 1.8 copy-done
  460.0 11.9 %adam_step.2 = f32[224,32,128]{2,1,0:T(8,128)} custom-call(s32[224]{0:T(256)} %get-tuple-element.41.refs_2_.home_ref, s32[224]{0:T(256)} %get-tuple-element.40.refs_3_.came_ref, s32[224]{0:T(256)} %get-tuple-element.39.refs_4_.kind_ref, bf16[2,224,32,128]{3,2,1,0:T(8,128)(2,1)} %get-tuple-element.24.refs_0_, bf16[2,224,32,128]{3,2,1,0:T(8,128)(2,1)} %copy-done, ...), custom_call_target="tpu_custom_call" | custom-call | flops 13762560 | bytes 15597568 | tf_op jit(solution)/shard_map/adam_step/pallas_call | solution.py:462
  471.9 11.9 %adam_step.3 = f32[224,32,128]{2,1,0:T(8,128)} custom-call(s32[224]{0:T(256)} %get-tuple-element.41.refs_2_.home_ref, s32[224]{0:T(256)} %get-tuple-element.40.refs_3_.came_ref, s32[224]{0:T(256)} %get-tuple-element.39.refs_4_.kind_ref, bf16[2,224,32,128]{3,2,1,0:T(8,128)(2,1)} %get-tuple-element.24.refs_0_, bf16[2,224,32,128]{3,2,1,0:T(8,128)(2,1)} %copy-done, ...), custom_call_target="tpu_custom_call" | custom-call | flops 13762560 | bytes 15597568 | tf_op jit(solution)/shard_map/adam_step/pallas_call | solution.py:462
  (63 shorter events, 3.1 us)
Async XLA Ops:
  8.5 49.9 %all-to-all-start = ((bf16[8,28,32,128]{3,2,1,0:T(8,128)(2,1)}), bf16[8,28,32,128]{3,2,1,0:T(8,128)(2,1)S(1)}, u32[]{:S(2)}, u32[]{:S(2)}) async-start(bf16[8,28,32,128]{3,2,1,0:T(8,128)(2,1)} %bitcast.30), calls=%async_computation | async-start | bytes 3670016 | tf_op jit(solution)/shard_map/all_to_all | solution.py:531
  58.4 123.8 %copy-start.1 = (bf16[8,28,32,128]{3,2,1,0:T(8,128)(2,1)}, bf16[8,28,32,128]{3,2,1,0:T(8,128)(2,1)S(1)}, u32[]{:S(2)}) copy-start(bf16[8,28,32,128]{3,2,1,0:T(8,128)(2,1)S(1)} %all-to-all-done) | copy-start | bytes 5505028
  58.4 46.6 %all-to-all-start.1 = ((bf16[8,28,32,128]{3,2,1,0:T(8,128)(2,1)}), bf16[8,28,32,128]{3,2,1,0:T(8,128)(2,1)}, u32[]{:S(2)}, u32[]{:S(2)}) async-start(bf16[8,28,32,128]{3,2,1,0:T(8,128)(2,1)} %bitcast.29), calls=%async_computation.1 | async-start | bytes 3670016 | tf_op jit(solution)/shard_map/all_to_all | solution.py:531
  105.0 6.8 %copy-start.7 = (bf16[128,896]{1,0:T(8,128)(2,1)S(1)}, bf16[128,896]{1,0:T(8,128)(2,1)}, u32[]{:S(2)}) copy-start(bf16[128,896]{1,0:T(8,128)(2,1)} %param.13) | copy-start | bytes 688132
  105.0 6.8 %copy-start.8 = (bf16[128,896]{1,0:T(8,128)(2,1)S(1)}, bf16[128,896]{1,0:T(8,128)(2,1)}, u32[]{:S(2)}) copy-start(bf16[128,896]{1,0:T(8,128)(2,1)} %param.12) | copy-start | bytes 688132
  105.0 108.4 %copy-start.9 = (s32[224]{0:T(256)S(1)}, s32[224]{0:T(256)}, u32[]{:S(2)}) copy-start(s32[224]{0:T(256)} %param.22) | copy-start | bytes 2692
  105.0 119.7 %copy-start.10 = (s32[128]{0:T(128)S(1)}, s32[128]{0:T(128)}, u32[]{:S(2)}) copy-start(s32[128]{0:T(128)} %param.23) | copy-start | bytes 1540
  105.0 210.9 %all-to-all-start.2 = ((bf16[8,28,2,32,128]{4,3,2,1,0:T(8,128)(2,1)}), bf16[8,28,2,32,128]{4,3,2,1,0:T(8,128)(2,1)}, u32[]{:S(2)}, u32[]{:S(2)}) async-start(bf16[8,28,2,32,128]{4,3,2,1,0:T(8,128)(2,1)} %bitcast.24), calls=%async_computation.2 | async-start | bytes 7340032 | tf_op jit(solution)/shard_map/all_to_all | solution.py:531
  109.6 72.7 %collective-permute-start.8 = (bf16[224,32,128]{2,1,0:T(8,128)(2,1)S(1)}, bf16[224,32,128]{2,1,0:T(8,128)(2,1)}, u32[]{:S(2)}, u32[]{:S(2)}) collective-permute-start(bf16[224,32,128]{2,1,0:T(8,128)(2,1)S(1)} %bitcast.26), channel_id=1, source_target_pairs={{0,16},{8,24},{16,0},{24,8},{1,17},{9,25},{17,1},{25,9},{2,18},{10... | collective-permute-start | bytes 5505032 | tf_op jit(solution)/shard_map/ppermute | solution.py:547
  111.2 99.5 %collective-permute-start.11 = (bf16[224,32,128]{2,1,0:T(8,128)(2,1)}, bf16[224,32,128]{2,1,0:T(8,128)(2,1)}, u32[]{:S(2)}, u32[]{:S(2)}) collective-permute-start(bf16[224,32,128]{2,1,0:T(8,128)(2,1)} %bitcast.13.refs_15_), channel_id=1, source_target_pairs={{0,16},{8,24},{16,0},{24,8},{1,17},{9,25},{17,1},{25,9},{2,18},{10... | collective-permute-start | bytes 5505032 | tf_op jit(solution)/shard_map/ppermute | solution.py:547
  111.8 135.8 %copy-start.2 = (bf16[2,128,896]{2,1,0:T(8,128)(2,1)}, bf16[2,128,896]{2,1,0:T(8,128)(2,1)S(1)}, u32[]{:S(2)}) copy-start(bf16[2,128,896]{2,1,0:T(8,128)(2,1)S(1)} %pad_maximum_fusion.refs_6_) | copy-start | bytes 1376260
  111.8 68.7 %collective-permute-start.1 = (bf16[2,128,896]{2,1,0:T(8,128)(2,1)S(1)}, bf16[2,128,896]{2,1,0:T(8,128)(2,1)S(1)}, u32[]{:S(2)}, u32[]{:S(2)}) collective-permute-start(bf16[2,128,896]{2,1,0:T(8,128)(2,1)S(1)} %pad_maximum_fusion.refs_6_), channel_id=1, source_target_pairs={{0,2},{1,3},{2,0},{3,1},{4,6},{5,7},{6,4},{7,5},{8,10},{9,11},{10,... | collective-permute-start | bytes 1376264 | tf_op jit(solution)/shard_map/ppermute | solution.py:565
  113.7 68.5 %collective-permute-start = (bf16[2,128,896]{2,1,0:T(8,128)(2,1)S(1)}, bf16[2,128,896]{2,1,0:T(8,128)(2,1)S(1)}, u32[]{:S(2)}, u32[]{:S(2)}) collective-permute-start(bf16[2,128,896]{2,1,0:T(8,128)(2,1)S(1)} %pad_maximum_fusion.refs_6_), channel_id=1, source_target_pairs={{0,1},{1,0},{2,3},{3,2},{4,5},{5,4},{6,7},{7,6},{8,9},{9,8},{10,11... | collective-permute-start | bytes 1376264 | tf_op jit(solution)/shard_map/ppermute | solution.py:565
  115.2 95.5 %collective-permute-start.3 = (bf16[2,128,896]{2,1,0:T(8,128)(2,1)S(1)}, bf16[2,128,896]{2,1,0:T(8,128)(2,1)}, u32[]{:S(2)}, u32[]{:S(2)}) collective-permute-start(bf16[2,128,896]{2,1,0:T(8,128)(2,1)S(1)} %pad_maximum_fusion.refs_6_), channel_id=1, source_target_pairs={{0,4},{1,5},{2,6},{3,7},{4,0},{5,1},{6,2},{7,3},{8,12},{9,13},{10,... | collective-permute-start | bytes 1376264 | tf_op jit(solution)/shard_map/ppermute | solution.py:565
  180.5 67.1 %copy-start.4 = (bf16[2,128,896]{2,1,0:T(8,128)(2,1)}, bf16[2,128,896]{2,1,0:T(8,128)(2,1)S(1)}, u32[]{:S(2)}) copy-start(bf16[2,128,896]{2,1,0:T(8,128)(2,1)S(1)} %collective-permute-done.1.refs_8_) | copy-start | bytes 1376260
  180.5 30.7 %collective-permute-start.2 = (bf16[2,128,896]{2,1,0:T(8,128)(2,1)S(1)}, bf16[2,128,896]{2,1,0:T(8,128)(2,1)S(1)}, u32[]{:S(2)}, u32[]{:S(2)}) collective-permute-start(bf16[2,128,896]{2,1,0:T(8,128)(2,1)S(1)} %collective-permute-done.1.refs_8_), channel_id=1, source_target_pairs={{0,1},{1,0},{2,3},{3,2},{4,5},{5,4},{6,7},{7,6},{8,9},{9,8},{10,11... | collective-permute-start | bytes 1376264 | tf_op jit(solution)/shard_map/ppermute | solution.py:565
  182.3 65.4 %copy-start.5 = (bf16[2,128,896]{2,1,0:T(8,128)(2,1)}, bf16[2,128,896]{2,1,0:T(8,128)(2,1)S(1)}, u32[]{:S(2)}) copy-start(bf16[2,128,896]{2,1,0:T(8,128)(2,1)S(1)} %collective-permute-done.refs_7_) | copy-start | bytes 1376260
  182.3 65.4 %collective-permute-start.7 = (bf16[224,32,128]{2,1,0:T(8,128)(2,1)S(1)}, bf16[224,32,128]{2,1,0:T(8,128)(2,1)}, u32[]{:S(2)}, u32[]{:S(2)}) collective-permute-start(bf16[224,32,128]{2,1,0:T(8,128)(2,1)S(1)} %bitcast.27), channel_id=1, source_target_pairs={{0,8},{8,0},{16,24},{24,16},{1,9},{9,1},{17,25},{25,17},{2,10},{10... | collective-permute-start | bytes 5505032 | tf_op jit(solution)/shard_map/ppermute | solution.py:548
  182.3 65.3 %collective-permute-start.9 = (bf16[224,32,128]{2,1,0:T(8,128)(2,1)}, bf16[224,32,128]{2,1,0:T(8,128)(2,1)}, u32[]{:S(2)}, u32[]{:S(2)}) collective-permute-start(bf16[224,32,128]{2,1,0:T(8,128)(2,1)} %collective-permute-done.8.refs_17_), channel_id=1, source_target_pairs={{0,8},{8,0},{16,24},{24,16},{1,9},{9,1},{17,25},{25,17},{2,10},{10... | collective-permute-start | bytes 5505032 | tf_op jit(solution)/shard_map/ppermute | solution.py:548
  210.7 60.3 %collective-permute-start.10 = (bf16[224,32,128]{2,1,0:T(8,128)(2,1)}, bf16[224,32,128]{2,1,0:T(8,128)(2,1)}, u32[]{:S(2)}, u32[]{:S(2)}) collective-permute-start(bf16[224,32,128]{2,1,0:T(8,128)(2,1)} %bitcast.13.refs_15_), channel_id=1, source_target_pairs={{0,8},{8,0},{16,24},{24,16},{1,9},{9,1},{17,25},{25,17},{2,10},{10... | collective-permute-start | bytes 5505032 | tf_op jit(solution)/shard_map/ppermute | solution.py:548
  210.7 60.3 %collective-permute-start.12 = (bf16[224,32,128]{2,1,0:T(8,128)(2,1)}, bf16[224,32,128]{2,1,0:T(8,128)(2,1)}, u32[]{:S(2)}, u32[]{:S(2)}) collective-permute-start(bf16[224,32,128]{2,1,0:T(8,128)(2,1)} %collective-permute-done.11.refs_17_), channel_id=1, source_target_pairs={{0,8},{8,0},{16,24},{24,16},{1,9},{9,1},{17,25},{25,17},{2,10},{10... | collective-permute-start | bytes 5505032 | tf_op jit(solution)/shard_map/ppermute | solution.py:548
  211.2 0.8 copy-start.6
  211.9 12.7 %collective-permute-start.4 = (bf16[2,128,896]{2,1,0:T(8,128)(2,1)}, bf16[2,128,896]{2,1,0:T(8,128)(2,1)}, u32[]{:S(2)}, u32[]{:S(2)}) collective-permute-start(bf16[2,128,896]{2,1,0:T(8,128)(2,1)} %collective-permute-done.3.refs_10_), channel_id=1, source_target_pairs={{0,1},{1,0},{2,3},{3,2},{4,5},{5,4},{6,7},{7,6},{8,9},{9,8},{10,11... | collective-permute-start | bytes 1376264 | tf_op jit(solution)/shard_map/ppermute | solution.py:565
  224.7 11.9 %collective-permute-start.5 = (bf16[2,128,896]{2,1,0:T(8,128)(2,1)}, bf16[2,128,896]{2,1,0:T(8,128)(2,1)}, u32[]{:S(2)}, u32[]{:S(2)}) collective-permute-start(bf16[2,128,896]{2,1,0:T(8,128)(2,1)} %collective-permute-done.3.refs_10_), channel_id=1, source_target_pairs={{0,2},{1,3},{2,0},{3,1},{4,6},{5,7},{6,4},{7,5},{8,10},{9,11},{10,... | collective-permute-start | bytes 1376264 | tf_op jit(solution)/shard_map/ppermute | solution.py:565
  236.6 11.0 %collective-permute-start.6 = (bf16[2,128,896]{2,1,0:T(8,128)(2,1)}, bf16[2,128,896]{2,1,0:T(8,128)(2,1)}, u32[]{:S(2)}, u32[]{:S(2)}) collective-permute-start(bf16[2,128,896]{2,1,0:T(8,128)(2,1)} %collective-permute-done.5.refs_12_), channel_id=1, source_target_pairs={{0,1},{1,0},{2,3},{3,2},{4,5},{5,4},{6,7},{7,6},{8,9},{9,8},{10,11... | collective-permute-start | bytes 1376264 | tf_op jit(solution)/shard_map/ppermute | solution.py:565
  309.5 41.1 %collective-permute-start.17 = (bf16[2,224,32,128]{3,2,1,0:T(8,128)(2,1)}, bf16[2,224,32,128]{3,2,1,0:T(8,128)(2,1)}, u32[]{:S(2)}, u32[]{:S(2)}) collective-permute-start(bf16[2,224,32,128]{3,2,1,0:T(8,128)(2,1)} %get-tuple-element.27), channel_id=1, source_target_pairs={{0,8},{8,0},{16,24},{24,16},{1,9},{9,1},{17,25},{25,17},{2,10},{10... | collective-permute-start | bytes 11010056 | tf_op jit(solution)/shard_map/ppermute | solution.py:590
  315.9 156.0 %all-to-all-start.3 = ((bf16[8,28,2,32,128]{4,3,2,1,0:T(8,128)(2,1)}), bf16[8,28,2,32,128]{4,3,2,1,0:T(8,128)(2,1)}, u32[]{:S(2)}, u32[]{:S(2)}) async-start(bf16[8,28,2,32,128]{4,3,2,1,0:T(8,128)(2,1)} %bitcast.25), calls=%async_computation.3 | async-start | bytes 7340032 | tf_op jit(solution)/shard_map/all_to_all | solution.py:531
  348.6 60.4 %collective-permute-start.13 = (bf16[4,2,128,896]{3,2,1,0:T(8,128)(2,1)}, bf16[4,2,128,896]{3,2,1,0:T(8,128)(2,1)S(1)}, u32[]{:S(2)}, u32[]{:S(2)}) collective-permute-start(bf16[4,2,128,896]{3,2,1,0:T(8,128)(2,1)} %get-tuple-element.23), channel_id=1, source_target_pairs={{0,1},{1,0},{2,3},{3,2},{4,5},{5,4},{6,7},{7,6},{8,9},{9,8},{10,11... | collective-permute-start | bytes 5505032 | tf_op jit(solution)/shard_map/ppermute | solution.py:605
  350.5 107.7 %collective-permute-start.16 = (bf16[2,224,32,128]{3,2,1,0:T(8,128)(2,1)}, bf16[2,224,32,128]{3,2,1,0:T(8,128)(2,1)S(1)}, u32[]{:S(2)}, u32[]{:S(2)}) collective-permute-start(bf16[2,224,32,128]{3,2,1,0:T(8,128)(2,1)} %get-tuple-element.25), channel_id=1, source_target_pairs={{0,8},{8,0},{16,24},{24,16},{1,9},{9,1},{17,25},{25,17},{2,10},{10... | collective-permute-start | bytes 11010056 | tf_op jit(solution)/shard_map/ppermute | solution.py:590
  350.5 58.4 %copy-start.3 = (bf16[4,2,128,896]{3,2,1,0:T(8,128)(2,1)S(1)}, bf16[4,2,128,896]{3,2,1,0:T(8,128)(2,1)}, u32[]{:S(2)}) copy-start(bf16[4,2,128,896]{3,2,1,0:T(8,128)(2,1)} %get-tuple-element.22) | copy-start | bytes 5505028
  354.7 103.4 %collective-permute-start.18 = (bf16[2,224,32,128]{3,2,1,0:T(8,128)(2,1)S(1)}, bf16[2,224,32,128]{3,2,1,0:T(8,128)(2,1)}, u32[]{:S(2)}, u32[]{:S(2)}) collective-permute-start(bf16[2,224,32,128]{3,2,1,0:T(8,128)(2,1)S(1)} %add_convert_fusion), channel_id=1, source_target_pairs={{0,16},{8,24},{16,0},{24,8},{1,17},{9,25},{17,1},{25,9},{2,18},{10... | collective-permute-start | bytes 11010056 | tf_op jit(solution)/shard_map/ppermute | solution.py:595
  409.2 23.6 %collective-permute-start.14 = (bf16[2,2,128,896]{3,2,1,0:T(8,128)(2,1)S(1)}, bf16[2,2,128,896]{3,2,1,0:T(8,128)(2,1)S(1)}, u32[]{:S(2)}, u32[]{:S(2)}) collective-permute-start(bf16[2,2,128,896]{3,2,1,0:T(8,128)(2,1)S(1)} %add_convert_fusion.1), channel_id=1, source_target_pairs={{0,2},{1,3},{2,0},{3,1},{4,6},{5,7},{6,4},{7,5},{8,10},{9,11},{10,... | collective-permute-start | bytes 2752520 | tf_op jit(solution)/shard_map/ppermute | solution.py:605
  433.0 24.2 %collective-permute-start.15 = (bf16[1,2,128,896]{3,2,1,0:T(8,128)(2,1)S(1)}, bf16[1,2,128,896]{3,2,1,0:T(8,128)(2,1)S(1)}, u32[]{:S(2)}, u32[]{:S(2)}) collective-permute-start(bf16[1,2,128,896]{3,2,1,0:T(8,128)(2,1)S(1)} %add_convert_fusion.3), channel_id=1, source_target_pairs={{0,4},{1,5},{2,6},{3,7},{4,0},{5,1},{6,2},{7,3},{8,12},{9,13},{10,... | collective-permute-start | bytes 1376264 | tf_op jit(solution)/shard_map/ppermute | solution.py:605
  458.2 1.8 copy-start
where the time goes:
time: 484 us
  waiting for transfers between devices  287 us (59%)
  Pallas kernels  134 us (28%)
  starting transfers between devices  45.6 us (9%)
  other arithmetic  9.78 us (2%)
  local copies, waits for them, and re-layouts  6.56 us (1%)
    ppermute x7, waiting for transfers between devices, layer(): held[m ^ bit] = lax.ppermute(held[m], 'tensor', far_pairs(bit))  119 us
    ppermute x3, waiting for transfers between devices, layer(): sums.append(lax.ppermute(send, 'tensor', far_pairs(bit)))  92.8 us
    all_to_all x4, waiting for transfers between devices, exchange(): lax.all_to_all(shaped, 'tensor', split_axis=0, concat_axis=0, tiled=True)  74.7 us
    pallas_call x1, Pallas kernels, gradient_products(): pl.pallas_call(functools.partial(gradient_kernel, n_feat, n_dp), out_shap...  38.5 us
    pallas_call x1, Pallas kernels, output_products(): pl.pallas_call(functools.partial(output_kernel, pieces), out_shape=[jax.S...  28.1 us
    pallas_call x2, Pallas kernels, adam_step(): pl.pallas_call(kernel, out_shape=jax.ShapeDtypeStruct(moments[0].shape, F...  23.8 us
    pallas_call x1, Pallas kernels, forward_products(): pl.pallas_call(functools.partial(forward_kernel, n_feat, n_dp, row_blocks...  23.3 us
    all_to_all x4, starting transfers between devices, exchange(): lax.all_to_all(shaped, 'tensor', split_axis=0, concat_axis=0, tiled=True)  20.8 us
  transfers between devices with their start and end apart: 23, of which 10 were waited for; matrix products, arithmetic and copies ran while one was open for 2% of the time, Pallas kernels for 24%

commit v1 on v0

--- a/solution.py
+++ b/solution.py
@@ -267,50 +267,40 @@
     keep.wait()
 
 
-def output_kernel(pieces, *refs):
+def output_kernel(pieces, turned, *refs):
     row_ref, col_ref, place_ref = refs[:3]
-    wu_hbm, wd_hbm, act, bpre = refs[3:7]
-    outs = refs[7 : 7 + len(pieces)]
-    wu, wd, out_acc, in_acc, staged, in_sem, out_sem = refs[7 + len(pieces) :]
-    slots, block, _ = wu.shape
+    w_hbm, left = refs[3:5]
+    outs = refs[5 : 5 + len(pieces)]
+    w_v, acc, staged, in_sem, out_sem = refs[5 + len(pieces) :]
+    slots, block, _ = w_v.shape
     parts = 4
     some = slots // parts
     loads = []
     for k in range(parts):
-        for hbm, buf, s in ((wd_hbm, wd, 0), (wu_hbm, wu, 1)):
-            at = pl.ds(k * some, some)
-            loads.append(pltpu.make_async_copy(hbm.at[at], buf.at[at], in_sem.at[2 * k + s]))
+        at = pl.ds(k * some, some)
+        loads.append(pltpu.make_async_copy(w_hbm.at[at], w_v.at[at], in_sem.at[k]))
     for copy in loads:
         copy.start()
-    out_acc[...] = jnp.zeros(out_acc.shape, F32)
-    in_acc[...] = jnp.zeros(in_acc.shape, F32)
+    acc[...] = jnp.zeros(acc.shape, F32)
     unroll = 2
+    dims = (((1,), (1 if turned else 0,)), ((), ()))
 
     def step(i, carry):
         got = []
         for u in range(unroll):
             g = i * unroll + u
-            r = row_ref[g]
-            c = col_ref[g]
-            got.append(
-                (
-                    r,
-                    jnp.dot(act[c], wd[g], preferred_element_type=F32),
-                    lax.dot_general(bpre[c], wu[g], (((1,), (1,)), ((), ())), preferred_element_type=F32),
-                )
-            )
-        for r, o, n in got:
-            out_acc[r] = out_acc[r] + o
-            in_acc[r] = in_acc[r] + n
+            got.append(lax.dot_general(left[col_ref[g]], w_v[g], dims, preferred_element_type=F32))
+        for u in range(unroll):
+            r = row_ref[i * unroll + u]
+            acc[r] = acc[r] + got[u]
         return carry
 
     for k in range(parts):
-        loads[2 * k].wait()
-        loads[2 * k + 1].wait()
+        loads[k].wait()
         lax.fori_loop(k * some // unroll, (k + 1) * some // unroll, step, 0)
 
     count = staged.shape[0]
-    per = staged.shape[3] // block
+    per = staged.shape[2] // block
     bits = count.bit_length() - 1
     for a in range(count):
         if count == 1:
@@ -321,8 +311,7 @@
             for b in range(bits):
                 at = at + ((far >> b) & 1) * (count >> (b + 1))
         for q in range(per):
-            staged[at, 0, :, q * block : (q + 1) * block] = out_acc[a * per + q].astype(BF16)
-            staged[at, 1, :, q * block : (q + 1) * block] = in_acc[a * per + q].astype(BF16)
+            staged[at, :, q * block : (q + 1) * block] = acc[a * per + q].astype(BF16)
     copies = [
         pltpu.make_async_copy(staged.at[pl.ds(start, size)], out, out_sem.at[k])
         for k, ((start, size), out) in enumerate(zip(pieces, outs))
@@ -402,27 +391,25 @@
     )(*tables, place, *feats, down, *parts, pre, x_t)
 
 
-def output_products(row, col, place, wu, wd, act, bpre, pieces, feat_shape, row_blocks):
-    slots, block, _ = wu.shape
+def output_products(row, col, place, w, left, turned, pieces, feat_shape, row_blocks):
+    slots, block, _ = w.shape
     count, tokens, shard = feat_shape
     return pl.pallas_call(
-        functools.partial(output_kernel, pieces),
-        out_shape=[jax.ShapeDtypeStruct((size, 2, tokens, shard), BF16) for _, size in pieces],
-        in_specs=[SMEM] * 3 + [ANY] * 2 + [VMEM] * 2,
+        functools.partial(output_kernel, pieces, turned),
+        out_shape=[jax.ShapeDtypeStruct((size, tokens, shard), BF16) for _, size in pieces],
+        in_specs=[SMEM] * 3 + [ANY, VMEM],
         out_specs=[ANY] * len(pieces),
         scratch_shapes=[
-            pltpu.VMEM(wu.shape, BF16),
-            pltpu.VMEM(wd.shape, BF16),
+            pltpu.VMEM(w.shape, BF16),
             pltpu.VMEM((row_blocks, tokens, block), F32),
-            pltpu.VMEM((row_blocks, tokens, block), F32),
-            pltpu.VMEM((count, 2, tokens, shard), BF16),
-            pltpu.SemaphoreType.DMA((8,)),
+            pltpu.VMEM((count, tokens, shard), BF16),
+            pltpu.SemaphoreType.DMA((4,)),
             pltpu.SemaphoreType.DMA((len(pieces),)),
         ],
         compiler_params=pltpu.CompilerParams(vmem_limit_bytes=VMEM_LIMIT),
-        cost_estimate=cost(4 * slots * tokens * block * block, 8 * slots * block * block),
+        cost_estimate=cost(2 * slots * tokens * block * block, 4 * slots * block * block),
         name="output_products",
-    )(row, col, place, wu, wd, act, bpre)
+    )(row, col, place, w, left)
 
 
 def adam_step(tables, grads, which, moments, arrived):
@@ -594,30 +581,29 @@
             both = (grads[2 * j].astype(F32) + there.astype(F32)).astype(BF16)
             terms.append(lax.ppermute(both, "dp", x_pairs(j)))
 
-    if stacked:
+    sums = []
+    for w, left, turned in ((wd, act, False), (wu, bpre, True)):
         half = tensor_size // 2
-        keep, send = output_products(
-            new_row, col_slot, place, wu, wd, act, bpre, ((0, half), (half, half)), feat_shape, row_blocks
+        pieces = ((0, half), (half, half)) if stacked else ((0, 1),)
+        got = output_products(
+            new_row, col_slot, place, w, left, turned, pieces, feat_shape, row_blocks
         )
-        sums = [keep]
+        if not stacked:
+            sums.append(lax.psum_scatter(got[0][0], "tensor", scatter_dimension=1, tiled=True))
+            continue
+        held, send = got
+        held = [held]
         bit = 1
         while True:
-            sums.append(lax.ppermute(send, "tensor", far_pairs(bit)))
+            held.append(lax.ppermute(send, "tensor", far_pairs(bit)))
             bit *= 2
             if bit >= tensor_size:
                 break
-            half = sums[-1].shape[0] // 2
-            total = sum(s[half : 2 * half].astype(F32) for s in sums)
-            send = total.astype(BF16)
-            sums = [s[:half] for s in sums]
-        total = sum(s[0].astype(F32) for s in sums).astype(BF16)
-        out_sum, in_sum = total[0], total[1]
-    else:
-        (whole,) = output_products(
-            new_row, col_slot, place, wu, wd, act, bpre, ((0, 1),), feat_shape, row_blocks
-        )
-        out_sum = lax.psum_scatter(whole[0, 0], "tensor", scatter_dimension=1, tiled=True)
-        in_sum = lax.psum_scatter(whole[0, 1], "tensor", scatter_dimension=1, tiled=True)
+            half = held[-1].shape[0] // 2
+            send = sum(s[half : 2 * half].astype(F32) for s in held).astype(BF16)
+            held = [s[:half] for s in held]
+        sums.append(sum(s[0].astype(F32) for s in held).astype(BF16))
+    out_sum, in_sum = sums
 
     up_step = adam_step((home, came, kind), terms, 0, ups, ups_in)
     down_step = adam_step((home, came, kind), terms, 1, downs, downs_in)

time: 484 us -> 479 us (0.990)
  waiting for transfers between devices: 287 us -> 251 us
  Pallas kernels: 134 us -> 152 us
  other arithmetic: 9.78 us -> 17.2 us
    ppermute x3 -> x6, waiting for transfers between devices: 92.8 us -> 52.8 us  [layer(): held.append(lax.ppermute(send, 'tensor', far_pairs(bit)))]
    pallas_call x1 -> x2, Pallas kernels: 28.1 us -> 46.5 us  [output_products(): pl.pallas_call(functools.partial(output_kernel, pieces, turned), out_shap...]
    ppermute x3 -> x6, starting transfers between devices: 9.59 us -> 10.6 us  [layer(): held.append(lax.ppermute(send, 'tensor', far_pairs(bit)))]
  transfers between devices with their start and end apart: 23 -> 26, of which waited for: 10 -> 11; matrix products, arithmetic and copies ran while one was open for 2% -> 3% of each run, Pallas kernels for 24% -> 29%
where the time goes in v1:
time: 479 us; the launch traced here: 478 us
  waiting for transfers between devices  251 us (52%)
  Pallas kernels  152 us (32%)
  starting transfers between devices  50.3 us (11%)
  other arithmetic  17.2 us (4%)
  local copies, waits for them, and re-layouts  5.73 us (1%)
    ppermute x7, waiting for transfers between devices, layer(): held[m ^ bit] = lax.ppermute(held[m], 'tensor', far_pairs(bit))  124 us
    all_to_all x4, waiting for transfers between devices, exchange(): lax.all_to_all(shaped, 'tensor', split_axis=0, concat_axis=0, tiled=True)  74.6 us
    ppermute x6, waiting for transfers between devices, layer(): held.append(lax.ppermute(send, 'tensor', far_pairs(bit)))  52.8 us
    pallas_call x2, Pallas kernels, output_products(): pl.pallas_call(functools.partial(output_kernel, pieces, turned), out_shap...  46.5 us
    pallas_call x1, Pallas kernels, gradient_products(): pl.pallas_call(functools.partial(gradient_kernel, n_feat, n_dp), out_shap...  38.6 us
    pallas_call x2, Pallas kernels, adam_step(): pl.pallas_call(kernel, out_shape=jax.ShapeDtypeStruct(moments[0].shape, F...  23.8 us
    pallas_call x1, Pallas kernels, forward_products(): pl.pallas_call(functools.partial(forward_kernel, n_feat, n_dp, row_blocks...  23.2 us
    all_to_all x4, starting transfers between devices, exchange(): lax.all_to_all(shaped, 'tensor', split_axis=0, concat_axis=0, tiled=True)  23 us
  transfers between devices with their start and end apart: 26, of which 11 were waited for; matrix products, arithmetic and copies ran while one was open for 3% of the time, Pallas kernels for 29%

profile of v1, /device:TPU:0, one launch (start us, length us, event | category | flops | bytes accessed | tf_op | source)
XLA Modules:
  0.0 478.0 jit_solution(4925616968010058165)
XLA Ops:
  0.6 0.7 broadcast_divide_fusion
  1.3 0.7 sign_compare_fusion
  4.7 3.8 pack_weight.3
  8.5 7.3 %all-to-all-start.1 = ((bf16[8,28,32,128]{3,2,1,0:T(8,128)(2,1)}), bf16[8,28,32,128]{3,2,1,0:T(8,128)(2,1)S(1)}, u32[]{:S(2)}, u32[]{:S(2)}) async-start(bf16[8,28,32,128]{3,2,1,0:T(8,128)(2,1)} %bitcast.30), calls=%async_computation.1 | async-start | bytes 3670016 | tf_op jit(solution)/shard_map/all_to_all | solution.py:518
  15.8 3.8 pack_weight.2
  19.6 38.8 %all-to-all-done.1 = bf16[8,28,32,128]{3,2,1,0:T(8,128)(2,1)S(1)} async-done(((bf16[8,28,32,128]{3,2,1,0:T(8,128)(2,1)}), bf16[8,28,32,128]{3,2,1,0:T(8,128)(2,1)S(1)}, u32[]{:S(2)}, u32[]{:S(2)}) %all-to-all-start.1) | async-done | bytes 1835040 | tf_op jit(solution)/shard_map/all_to_all | solution.py:518
  58.4 4.3 all-to-all-start
  62.8 6.4 %pack_moments.3 = bf16[224,2,32,128]{3,2,1,0:T(8,128)(2,1)} custom-call(s32[224]{0:T(256)} %reshape.141.send_ref, f32[224,32,128]{2,1,0:T(8,128)} %refs_3_.3, f32[224,32,128]{2,1,0:T(8,128)} %refs_4_.3), custom_call_target="tpu_custom_call" | custom-call | bytes 11010048 | tf_op jit(solution)/shard_map/pack_moments/pallas_call | solution.py:80
  69.2 35.8 %all-to-all-done = bf16[8,28,32,128]{3,2,1,0:T(8,128)(2,1)} async-done(((bf16[8,28,32,128]{3,2,1,0:T(8,128)(2,1)}), bf16[8,28,32,128]{3,2,1,0:T(8,128)(2,1)}, u32[]{:S(2)}, u32[]{:S(2)}) %all-to-all-start) | async-done | bytes 1835040 | tf_op jit(solution)/shard_map/all_to_all | solution.py:518
  105.0 4.6 all-to-all-start.3
  109.6 1.6 collective-permute-start.11
  111.8 2.8 collective-permute-start.3
  114.6 1.5 collective-permute-start.1
  116.1 1.5 collective-permute-start
  117.6 93.0 %collective-permute-done.3.refs_10_ = bf16[2,128,896]{2,1,0:T(8,128)(2,1)S(1)} collective-permute-done((bf16[2,128,896]{2,1,0:T(8,128)(2,1)S(1)}, bf16[2,128,896]{2,1,0:T(8,128)(2,1)S(1)}, u32[]{:S(2)}, u32[]{:S(2)}) %collective-permute-start.3) | collective-permute-done | bytes 458784 | tf_op jit(solution)/shard_map/ppermute | solution.py:552
  211.7 9.4 %collective-permute-done.5.refs_12_ = bf16[2,128,896]{2,1,0:T(8,128)(2,1)S(1)} collective-permute-done((bf16[2,128,896]{2,1,0:T(8,128)(2,1)S(1)}, bf16[2,128,896]{2,1,0:T(8,128)(2,1)S(1)}, u32[]{:S(2)}, u32[]{:S(2)}) %collective-permute-start.5) | collective-permute-done | bytes 458784 | tf_op jit(solution)/shard_map/ppermute | solution.py:552
  221.1 0.8 copy-done.6
  221.9 2.4 collective-permute-start.4
  224.3 9.0 %collective-permute-done.4.refs_11_ = bf16[2,128,896]{2,1,0:T(8,128)(2,1)} collective-permute-done((bf16[2,128,896]{2,1,0:T(8,128)(2,1)S(1)}, bf16[2,128,896]{2,1,0:T(8,128)(2,1)}, u32[]{:S(2)}, u32[]{:S(2)}) %collective-permute-start.4) | collective-permute-done | bytes 458784 | tf_op jit(solution)/shard_map/ppermute | solution.py:552
  233.4 1.7 collective-permute-start.2
  235.5 8.3 %collective-permute-done.2.refs_9_ = bf16[2,128,896]{2,1,0:T(8,128)(2,1)} collective-permute-done((bf16[2,128,896]{2,1,0:T(8,128)(2,1)S(1)}, bf16[2,128,896]{2,1,0:T(8,128)(2,1)}, u32[]{:S(2)}, u32[]{:S(2)}) %collective-permute-start.2) | collective-permute-done | bytes 458784 | tf_op jit(solution)/shard_map/ppermute | solution.py:552
  243.8 1.7 collective-permute-start.6
  245.6 0.7 pad_add_fusion.refs_5_.refs_2_
  246.2 1.9 gather_fusion
  249.3 4.1 collective-permute-done.6.refs_13_
  253.4 23.2 %forward_products.1 = (f32[16,128,128]{2,1,0:T(8,128)}, bf16[56,128,128]{2,1,0:T(8,128)(2,1)}, bf16[224,128,128]{2,1,0:T(8,128)(2,1)}) custom-call(s32[224]{0:T(256)} %refs_0_.9, s32[224]{0:T(256)} %and_select_fusion.1.refs_1_, s32[224]{0:T(256)} %get-tuple-element.43.refs_2_.home_ref, s32[224]{0:T(256)} %get-tuple-element.42.refs_3_.came_ref, ...), custom_call_target="tpu_custom_call" | custom-call | flops 939524096 | bytes 44040192 | tf_op jit(solution)/shard_map/forward_products/pallas_call | solution.py:337
  276.7 38.6 %gradient_products.1 = (bf16[16,128,128]{2,1,0:T(8,128)(2,1)}, bf16[16,128,128]{2,1,0:T(8,128)(2,1)}, bf16[224,128,128]{2,1,0:T(8,128)(2,1)}, bf16[2,224,32,128]...) custom-call(s32[224]{0:T(256)} %refs_0_.9, ...), custom_call_target="tpu_custom_call" | custom-call | flops 2818572288 | bytes 73400320 | tf_op jit(solution)/shard_map/gradient_products/pallas_call | solution.py:368
  315.4 6.3 %pack_moments.2 = bf16[224,2,32,128]{3,2,1,0:T(8,128)(2,1)} custom-call(s32[224]{0:T(256)} %reshape.141.send_ref, f32[224,32,128]{2,1,0:T(8,128)} %refs_3_.2, f32[224,32,128]{2,1,0:T(8,128)} %refs_4_.2), custom_call_target="tpu_custom_call" | custom-call | bytes 11010048 | tf_op jit(solution)/shard_map/pack_moments/pallas_call | solution.py:80
  321.7 6.7 %all-to-all-start.2 = ((bf16[8,28,2,32,128]{4,3,2,1,0:T(8,128)(2,1)}), bf16[8,28,2,32,128]{4,3,2,1,0:T(8,128)(2,1)}, u32[]{:S(2)}, u32[]{:S(2)}) async-start(bf16[8,28,2,32,128]{4,3,2,1,0:T(8,128)(2,1)} %bitcast.25), calls=%async_computation.2 | async-start | bytes 7340032 | tf_op jit(solution)/shard_map/all_to_all | solution.py:518
  328.6 5.9 %add_convert_fusion = bf16[2,224,32,128]{3,2,1,0:T(8,128)(2,1)} fusion(bf16[2,224,32,128]{3,2,1,0:T(8,128)(2,1)} %collective-permute-done.20, bf16[2,224,32,128]{3,2,1,0:T(8,128)(2,1)} %get-tuple-element.30), kind=kLoop, calls=%fused_computation.1 | loop fusion | flops 7340032 | bytes 11010048 | tf_op jit(solution)/shard_map/convert_element_type | solution.py:581
  334.6 1.5 collective-permute-start.21
  336.1 24.2 %output_products.3 = (bf16[4,128,896]{2,1,0:T(8,128)(2,1)}, bf16[4,128,896]{2,1,0:T(8,128)(2,1)}) custom-call(s32[224]{0:T(256)} %refs_0_.9, s32[224]{0:T(256)} %and_select_fusion.1.refs_1_, s32[3]{0:T(128)} %pad_add_fusion.refs_5_.refs_2_, bf16[224,128,128]{2,1,0:T(8,128)(2,1)} %get-tuple-element.24.refs_3_, bf16[16,128,128]{2,1,0:T(8,128)(2,1)} %get-tuple-element.25.refs_4_), custom_call_target="tpu_custom_call" | custom-call | flops 939524096 | bytes 14680064 | tf_op jit(solution)/shard_map/output_products/pallas_call | solution.py:397
  360.3 1.9 collective-permute-start.16
  362.2 22.3 %output_products.2 = (bf16[4,128,896]{2,1,0:T(8,128)(2,1)}, bf16[4,128,896]{2,1,0:T(8,128)(2,1)}) custom-call(s32[224]{0:T(256)} %refs_0_.9, s32[224]{0:T(256)} %and_select_fusion.1.refs_1_, s32[3]{0:T(128)} %pad_add_fusion.refs_5_.refs_2_, bf16[224,128,128]{2,1,0:T(8,128)(2,1)} %get-tuple-element.20.refs_3_, bf16[16,128,128]{2,1,0:T(8,128)(2,1)} %get-tuple-element.21.refs_4_), custom_call_target="tpu_custom_call" | custom-call | flops 939524096 | bytes 14680064 | tf_op jit(solution)/shard_map/output_products/pallas_call | solution.py:397
  384.8 16.3 %collective-permute-done.16 = bf16[4,128,896]{2,1,0:T(8,128)(2,1)} collective-permute-done((bf16[4,128,896]{2,1,0:T(8,128)(2,1)}, bf16[4,128,896]{2,1,0:T(8,128)(2,1)}, u32[]{:S(2)}, u32[]{:S(2)}) %collective-permute-start.16) | collective-permute-done | bytes 917536 | tf_op jit(solution)/shard_map/ppermute | solution.py:598
  401.1 1.3 add_convert_fusion.1
  402.3 4.4 collective-permute-start.17
  406.7 13.6 %collective-permute-done.13 = bf16[4,128,896]{2,1,0:T(8,128)(2,1)S(1)} collective-permute-done((bf16[4,128,896]{2,1,0:T(8,128)(2,1)}, bf16[4,128,896]{2,1,0:T(8,128)(2,1)S(1)}, u32[]{:S(2)}, u32[]{:S(2)}) %collective-permute-start.13) | collective-permute-done | bytes 917536 | tf_op jit(solution)/shard_map/ppermute | solution.py:598
  420.3 1.1 add_convert_fusion.2
  421.4 4.0 collective-permute-start.14
  425.4 1.1 add_convert_fusion.4
  426.6 13.7 %collective-permute-done.14 = bf16[2,128,896]{2,1,0:T(8,128)(2,1)S(1)} collective-permute-done((bf16[2,128,896]{2,1,0:T(8,128)(2,1)S(1)}, bf16[2,128,896]{2,1,0:T(8,128)(2,1)S(1)}, u32[]{:S(2)}, u32[]{:S(2)}) %collective-permute-start.14) | collective-permute-done | bytes 458784 | tf_op jit(solution)/shard_map/ppermute | solution.py:598
  440.5 1.9 fusion.1
  442.4 9.2 %collective-permute-done.15 = bf16[1,128,896]{2,1,0:T(8,128)(2,1)S(1)} collective-permute-done((bf16[1,128,896]{2,1,0:T(8,128)(2,1)S(1)}, bf16[1,128,896]{2,1,0:T(8,128)(2,1)S(1)}, u32[]{:S(2)}, u32[]{:S(2)}) %collective-permute-start.15) | collective-permute-done | bytes 229408 | tf_op jit(solution)/shard_map/ppermute | solution.py:598
  451.6 0.8 fusion
  452.4 1.8 copy-done
  454.2 11.9 %adam_step.3 = f32[224,32,128]{2,1,0:T(8,128)} custom-call(s32[224]{0:T(256)} %get-tuple-element.43.refs_2_.home_ref, s32[224]{0:T(256)} %get-tuple-element.42.refs_3_.came_ref, s32[224]{0:T(256)} %get-tuple-element.41.refs_4_.kind_ref, bf16[2,224,32,128]{3,2,1,0:T(8,128)(2,1)} %get-tuple-element.28.refs_0_, bf16[2,224,32,128]{3,2,1,0:T(8,128)(2,1)} %copy-done, ...), custom_call_target="tpu_custom_call" | custom-call | flops 13762560 | bytes 15597568 | tf_op jit(solution)/shard_map/adam_step/pallas_call | solution.py:449
  466.1 11.9 %adam_step.2 = f32[224,32,128]{2,1,0:T(8,128)} custom-call(s32[224]{0:T(256)} %get-tuple-element.43.refs_2_.home_ref, s32[224]{0:T(256)} %get-tuple-element.42.refs_3_.came_ref, s32[224]{0:T(256)} %get-tuple-element.41.refs_4_.kind_ref, bf16[2,224,32,128]{3,2,1,0:T(8,128)(2,1)} %get-tuple-element.28.refs_0_, bf16[2,224,32,128]{3,2,1,0:T(8,128)(2,1)} %copy-done, ...), custom_call_target="tpu_custom_call" | custom-call | flops 13762560 | bytes 15597568 | tf_op jit(solution)/shard_map/adam_step/pallas_call | solution.py:449
  (74 shorter events, 6.7 us)
Async XLA Ops:
  8.5 49.9 %all-to-all-start.1 = ((bf16[8,28,32,128]{3,2,1,0:T(8,128)(2,1)}), bf16[8,28,32,128]{3,2,1,0:T(8,128)(2,1)S(1)}, u32[]{:S(2)}, u32[]{:S(2)}) async-start(bf16[8,28,32,128]{3,2,1,0:T(8,128)(2,1)} %bitcast.30), calls=%async_computation.1 | async-start | bytes 3670016 | tf_op jit(solution)/shard_map/all_to_all | solution.py:518
  58.4 152.2 %copy-start.1 = (bf16[8,28,32,128]{3,2,1,0:T(8,128)(2,1)}, bf16[8,28,32,128]{3,2,1,0:T(8,128)(2,1)S(1)}, u32[]{:S(2)}) copy-start(bf16[8,28,32,128]{3,2,1,0:T(8,128)(2,1)S(1)} %all-to-all-done.1) | copy-start | bytes 5505028
  58.4 46.6 %all-to-all-start = ((bf16[8,28,32,128]{3,2,1,0:T(8,128)(2,1)}), bf16[8,28,32,128]{3,2,1,0:T(8,128)(2,1)}, u32[]{:S(2)}, u32[]{:S(2)}) async-start(bf16[8,28,32,128]{3,2,1,0:T(8,128)(2,1)} %bitcast.29), calls=%async_computation | async-start | bytes 3670016 | tf_op jit(solution)/shard_map/all_to_all | solution.py:518
  105.0 6.8 %copy-start.8 = (bf16[128,896]{1,0:T(8,128)(2,1)S(1)}, bf16[128,896]{1,0:T(8,128)(2,1)}, u32[]{:S(2)}) copy-start(bf16[128,896]{1,0:T(8,128)(2,1)} %param.13) | copy-start | bytes 688132
  105.0 6.8 %copy-start.9 = (bf16[128,896]{1,0:T(8,128)(2,1)S(1)}, bf16[128,896]{1,0:T(8,128)(2,1)}, u32[]{:S(2)}) copy-start(bf16[128,896]{1,0:T(8,128)(2,1)} %param.12) | copy-start | bytes 688132
  105.0 119.4 %copy-start.10 = (s32[224]{0:T(256)S(1)}, s32[224]{0:T(256)}, u32[]{:S(2)}) copy-start(s32[224]{0:T(256)} %param.22) | copy-start | bytes 2692
  105.0 130.2 %copy-start.11 = (s32[128]{0:T(128)S(1)}, s32[128]{0:T(128)}, u32[]{:S(2)}) copy-start(s32[128]{0:T(128)} %param.23) | copy-start | bytes 1540
  105.0 216.7 %all-to-all-start.3 = ((bf16[8,28,2,32,128]{4,3,2,1,0:T(8,128)(2,1)}), bf16[8,28,2,32,128]{4,3,2,1,0:T(8,128)(2,1)}, u32[]{:S(2)}, u32[]{:S(2)}) async-start(bf16[8,28,2,32,128]{4,3,2,1,0:T(8,128)(2,1)} %bitcast.24), calls=%async_computation.3 | async-start | bytes 7340032 | tf_op jit(solution)/shard_map/all_to_all | solution.py:518
  109.6 101.0 %collective-permute-start.11 = (bf16[224,32,128]{2,1,0:T(8,128)(2,1)S(1)}, bf16[224,32,128]{2,1,0:T(8,128)(2,1)}, u32[]{:S(2)}, u32[]{:S(2)}) collective-permute-start(bf16[224,32,128]{2,1,0:T(8,128)(2,1)S(1)} %bitcast.26), channel_id=1, source_target_pairs={{0,16},{8,24},{16,0},{24,8},{1,17},{9,25},{17,1},{25,9},{2,18},{10... | collective-permute-start | bytes 5505032 | tf_op jit(solution)/shard_map/ppermute | solution.py:534
  111.2 100.1 %collective-permute-start.8 = (bf16[224,32,128]{2,1,0:T(8,128)(2,1)}, bf16[224,32,128]{2,1,0:T(8,128)(2,1)}, u32[]{:S(2)}, u32[]{:S(2)}) collective-permute-start(bf16[224,32,128]{2,1,0:T(8,128)(2,1)} %bitcast.11.refs_15_), channel_id=1, source_target_pairs={{0,16},{8,24},{16,0},{24,8},{1,17},{9,25},{17,1},{25,9},{2,18},{10... | collective-permute-start | bytes 5505032 | tf_op jit(solution)/shard_map/ppermute | solution.py:534
  111.8 141.6 %copy-start.2 = (bf16[2,128,896]{2,1,0:T(8,128)(2,1)}, bf16[2,128,896]{2,1,0:T(8,128)(2,1)S(1)}, u32[]{:S(2)}) copy-start(bf16[2,128,896]{2,1,0:T(8,128)(2,1)S(1)} %pad_maximum_fusion.refs_6_) | copy-start | bytes 1376260
  111.8 98.8 %collective-permute-start.3 = (bf16[2,128,896]{2,1,0:T(8,128)(2,1)S(1)}, bf16[2,128,896]{2,1,0:T(8,128)(2,1)S(1)}, u32[]{:S(2)}, u32[]{:S(2)}) collective-permute-start(bf16[2,128,896]{2,1,0:T(8,128)(2,1)S(1)} %pad_maximum_fusion.refs_6_), channel_id=1, source_target_pairs={{0,4},{1,5},{2,6},{3,7},{4,0},{5,1},{6,2},{7,3},{8,12},{9,13},{10,... | collective-permute-start | bytes 1376264 | tf_op jit(solution)/shard_map/ppermute | solution.py:552
  114.6 95.9 %collective-permute-start.1 = (bf16[2,128,896]{2,1,0:T(8,128)(2,1)S(1)}, bf16[2,128,896]{2,1,0:T(8,128)(2,1)S(1)}, u32[]{:S(2)}, u32[]{:S(2)}) collective-permute-start(bf16[2,128,896]{2,1,0:T(8,128)(2,1)S(1)} %pad_maximum_fusion.refs_6_), channel_id=1, source_target_pairs={{0,2},{1,3},{2,0},{3,1},{4,6},{5,7},{6,4},{7,5},{8,10},{9,11},{10,... | collective-permute-start | bytes 1376264 | tf_op jit(solution)/shard_map/ppermute | solution.py:552
  116.1 95.1 %collective-permute-start = (bf16[2,128,896]{2,1,0:T(8,128)(2,1)S(1)}, bf16[2,128,896]{2,1,0:T(8,128)(2,1)S(1)}, u32[]{:S(2)}, u32[]{:S(2)}) collective-permute-start(bf16[2,128,896]{2,1,0:T(8,128)(2,1)S(1)} %pad_maximum_fusion.refs_6_), channel_id=1, source_target_pairs={{0,1},{1,0},{2,3},{3,2},{4,5},{5,4},{6,7},{7,6},{8,9},{9,8},{10,11... | collective-permute-start | bytes 1376264 | tf_op jit(solution)/shard_map/ppermute | solution.py:552
  210.6 42.9 %copy-start.3 = (bf16[2,128,896]{2,1,0:T(8,128)(2,1)}, bf16[2,128,896]{2,1,0:T(8,128)(2,1)S(1)}, u32[]{:S(2)}) copy-start(bf16[2,128,896]{2,1,0:T(8,128)(2,1)S(1)} %collective-permute-done.3.refs_10_) | copy-start | bytes 1376260
  210.6 10.6 %collective-permute-start.5 = (bf16[2,128,896]{2,1,0:T(8,128)(2,1)S(1)}, bf16[2,128,896]{2,1,0:T(8,128)(2,1)S(1)}, u32[]{:S(2)}, u32[]{:S(2)}) collective-permute-start(bf16[2,128,896]{2,1,0:T(8,128)(2,1)S(1)} %collective-permute-done.3.refs_10_), channel_id=1, source_target_pairs={{0,2},{1,3},{2,0},{3,1},{4,6},{5,7},{6,4},{7,5},{8,10},{9,11},{10,... | collective-permute-start | bytes 1376264 | tf_op jit(solution)/shard_map/ppermute | solution.py:552
  210.6 42.9 %copy-start.4 = (bf16[2,128,896]{2,1,0:T(8,128)(2,1)}, bf16[2,128,896]{2,1,0:T(8,128)(2,1)S(1)}, u32[]{:S(2)}) copy-start(bf16[2,128,896]{2,1,0:T(8,128)(2,1)S(1)} %collective-permute-done.1.refs_8_) | copy-start | bytes 1376260
  210.6 42.8 %collective-permute-start.10 = (bf16[224,32,128]{2,1,0:T(8,128)(2,1)S(1)}, bf16[224,32,128]{2,1,0:T(8,128)(2,1)}, u32[]{:S(2)}, u32[]{:S(2)}) collective-permute-start(bf16[224,32,128]{2,1,0:T(8,128)(2,1)S(1)} %bitcast.27), channel_id=1, source_target_pairs={{0,8},{8,0},{16,24},{24,16},{1,9},{9,1},{17,25},{25,17},{2,10},{10... | collective-permute-start | bytes 5505032 | tf_op jit(solution)/shard_map/ppermute | solution.py:535
  210.7 42.7 %collective-permute-start.12 = (bf16[224,32,128]{2,1,0:T(8,128)(2,1)}, bf16[224,32,128]{2,1,0:T(8,128)(2,1)}, u32[]{:S(2)}, u32[]{:S(2)}) collective-permute-start(bf16[224,32,128]{2,1,0:T(8,128)(2,1)} %collective-permute-done.11.refs_17_), channel_id=1, source_target_pairs={{0,8},{8,0},{16,24},{24,16},{1,9},{9,1},{17,25},{25,17},{2,10},{10... | collective-permute-start | bytes 5505032 | tf_op jit(solution)/shard_map/ppermute | solution.py:535
  211.2 10.0 %copy-start.5 = (bf16[2,128,896]{2,1,0:T(8,128)(2,1)}, bf16[2,128,896]{2,1,0:T(8,128)(2,1)S(1)}, u32[]{:S(2)}) copy-start(bf16[2,128,896]{2,1,0:T(8,128)(2,1)S(1)} %collective-permute-done.refs_7_) | copy-start | bytes 1376260
  211.2 65.5 %collective-permute-start.7 = (bf16[224,32,128]{2,1,0:T(8,128)(2,1)}, bf16[224,32,128]{2,1,0:T(8,128)(2,1)}, u32[]{:S(2)}, u32[]{:S(2)}) collective-permute-start(bf16[224,32,128]{2,1,0:T(8,128)(2,1)} %bitcast.11.refs_15_), channel_id=1, source_target_pairs={{0,8},{8,0},{16,24},{24,16},{1,9},{9,1},{17,25},{25,17},{2,10},{10... | collective-permute-start | bytes 5505032 | tf_op jit(solution)/shard_map/ppermute | solution.py:535
  211.3 65.4 %collective-permute-start.9 = (bf16[224,32,128]{2,1,0:T(8,128)(2,1)}, bf16[224,32,128]{2,1,0:T(8,128)(2,1)}, u32[]{:S(2)}, u32[]{:S(2)}) collective-permute-start(bf16[224,32,128]{2,1,0:T(8,128)(2,1)} %collective-permute-done.8.refs_17_), channel_id=1, source_target_pairs={{0,8},{8,0},{16,24},{24,16},{1,9},{9,1},{17,25},{25,17},{2,10},{10... | collective-permute-start | bytes 5505032 | tf_op jit(solution)/shard_map/ppermute | solution.py:535
  221.1 0.8 copy-start.6
  221.9 11.5 %collective-permute-start.4 = (bf16[2,128,896]{2,1,0:T(8,128)(2,1)S(1)}, bf16[2,128,896]{2,1,0:T(8,128)(2,1)}, u32[]{:S(2)}, u32[]{:S(2)}) collective-permute-start(bf16[2,128,896]{2,1,0:T(8,128)(2,1)S(1)} %collective-permute-done.3.refs_10_), channel_id=1, source_target_pairs={{0,1},{1,0},{2,3},{3,2},{4,5},{5,4},{6,7},{7,6},{8,9},{9,8},{10,11... | collective-permute-start | bytes 1376264 | tf_op jit(solution)/shard_map/ppermute | solution.py:552
  233.4 10.5 %collective-permute-start.2 = (bf16[2,128,896]{2,1,0:T(8,128)(2,1)S(1)}, bf16[2,128,896]{2,1,0:T(8,128)(2,1)}, u32[]{:S(2)}, u32[]{:S(2)}) collective-permute-start(bf16[2,128,896]{2,1,0:T(8,128)(2,1)S(1)} %collective-permute-done.1.refs_8_), channel_id=1, source_target_pairs={{0,1},{1,0},{2,3},{3,2},{4,5},{5,4},{6,7},{7,6},{8,9},{9,8},{10,11... | collective-permute-start | bytes 1376264 | tf_op jit(solution)/shard_map/ppermute | solution.py:552
  243.8 9.6 %collective-permute-start.6 = (bf16[2,128,896]{2,1,0:T(8,128)(2,1)}, bf16[2,128,896]{2,1,0:T(8,128)(2,1)}, u32[]{:S(2)}, u32[]{:S(2)}) collective-permute-start(bf16[2,128,896]{2,1,0:T(8,128)(2,1)} %copy-done.6), channel_id=1, source_target_pairs={{0,1},{1,0},{2,3},{3,2},{4,5},{5,4},{6,7},{7,6},{8,9},{9,8},{10,11... | collective-permute-start | bytes 1376264 | tf_op jit(solution)/shard_map/ppermute | solution.py:552
  315.3 13.4 %collective-permute-start.20 = (bf16[2,224,32,128]{3,2,1,0:T(8,128)(2,1)}, bf16[2,224,32,128]{3,2,1,0:T(8,128)(2,1)}, u32[]{:S(2)}, u32[]{:S(2)}) collective-permute-start(bf16[2,224,32,128]{3,2,1,0:T(8,128)(2,1)} %get-tuple-element.31), channel_id=1, source_target_pairs={{0,8},{8,0},{16,24},{24,16},{1,9},{9,1},{17,25},{25,17},{2,10},{10... | collective-permute-start | bytes 11010056 | tf_op jit(solution)/shard_map/ppermute | solution.py:577
  321.7 144.4 %all-to-all-start.2 = ((bf16[8,28,2,32,128]{4,3,2,1,0:T(8,128)(2,1)}), bf16[8,28,2,32,128]{4,3,2,1,0:T(8,128)(2,1)}, u32[]{:S(2)}, u32[]{:S(2)}) async-start(bf16[8,28,2,32,128]{4,3,2,1,0:T(8,128)(2,1)} %bitcast.25), calls=%async_computation.2 | async-start | bytes 7340032 | tf_op jit(solution)/shard_map/all_to_all | solution.py:518
  328.4 124.0 %collective-permute-start.19 = (bf16[2,224,32,128]{3,2,1,0:T(8,128)(2,1)}, bf16[2,224,32,128]{3,2,1,0:T(8,128)(2,1)S(1)}, u32[]{:S(2)}, u32[]{:S(2)}) collective-permute-start(bf16[2,224,32,128]{3,2,1,0:T(8,128)(2,1)} %get-tuple-element.29), channel_id=1, source_target_pairs={{0,8},{8,0},{16,24},{24,16},{1,9},{9,1},{17,25},{25,17},{2,10},{10... | collective-permute-start | bytes 11010056 | tf_op jit(solution)/shard_map/ppermute | solution.py:577
  334.6 117.8 %collective-permute-start.21 = (bf16[2,224,32,128]{3,2,1,0:T(8,128)(2,1)}, bf16[2,224,32,128]{3,2,1,0:T(8,128)(2,1)}, u32[]{:S(2)}, u32[]{:S(2)}) collective-permute-start(bf16[2,224,32,128]{3,2,1,0:T(8,128)(2,1)} %add_convert_fusion), channel_id=1, source_target_pairs={{0,16},{8,24},{16,0},{24,8},{1,17},{9,25},{17,1},{25,9},{2,18},{10... | collective-permute-start | bytes 11010056 | tf_op jit(solution)/shard_map/ppermute | solution.py:582
  360.3 40.8 %collective-permute-start.16 = (bf16[4,128,896]{2,1,0:T(8,128)(2,1)}, bf16[4,128,896]{2,1,0:T(8,128)(2,1)}, u32[]{:S(2)}, u32[]{:S(2)}) collective-permute-start(bf16[4,128,896]{2,1,0:T(8,128)(2,1)} %get-tuple-element.27), channel_id=1, source_target_pairs={{0,1},{1,0},{2,3},{3,2},{4,5},{5,4},{6,7},{7,6},{8,9},{9,8},{10,11... | collective-permute-start | bytes 2752520 | tf_op jit(solution)/shard_map/ppermute | solution.py:598
  384.5 55.8 %copy-start.7 = (bf16[4,128,896]{2,1,0:T(8,128)(2,1)S(1)}, bf16[4,128,896]{2,1,0:T(8,128)(2,1)}, u32[]{:S(2)}) copy-start(bf16[4,128,896]{2,1,0:T(8,128)(2,1)} %get-tuple-element.22) | copy-start | bytes 2752516
  384.5 35.8 %collective-permute-start.13 = (bf16[4,128,896]{2,1,0:T(8,128)(2,1)}, bf16[4,128,896]{2,1,0:T(8,128)(2,1)S(1)}, u32[]{:S(2)}, u32[]{:S(2)}) collective-permute-start(bf16[4,128,896]{2,1,0:T(8,128)(2,1)} %get-tuple-element.23), channel_id=1, source_target_pairs={{0,1},{1,0},{2,3},{3,2},{4,5},{5,4},{6,7},{7,6},{8,9},{9,8},{10,11... | collective-permute-start | bytes 2752520 | tf_op jit(solution)/shard_map/ppermute | solution.py:598
  402.3 23.0 %collective-permute-start.17 = (bf16[2,128,896]{2,1,0:T(8,128)(2,1)S(1)}, bf16[2,128,896]{2,1,0:T(8,128)(2,1)S(1)}, u32[]{:S(2)}, u32[]{:S(2)}) collective-permute-start(bf16[2,128,896]{2,1,0:T(8,128)(2,1)S(1)} %add_convert_fusion.1), channel_id=1, source_target_pairs={{0,2},{1,3},{2,0},{3,1},{4,6},{5,7},{6,4},{7,5},{8,10},{9,11},{10,... | collective-permute-start | bytes 1376264 | tf_op jit(solution)/shard_map/ppermute | solution.py:598
  421.4 18.9 %collective-permute-start.14 = (bf16[2,128,896]{2,1,0:T(8,128)(2,1)S(1)}, bf16[2,128,896]{2,1,0:T(8,128)(2,1)S(1)}, u32[]{:S(2)}, u32[]{:S(2)}) collective-permute-start(bf16[2,128,896]{2,1,0:T(8,128)(2,1)S(1)} %add_convert_fusion.2), channel_id=1, source_target_pairs={{0,2},{1,3},{2,0},{3,1},{4,6},{5,7},{6,4},{7,5},{8,10},{9,11},{10,... | collective-permute-start | bytes 1376264 | tf_op jit(solution)/shard_map/ppermute | solution.py:598
  426.5 14.0 %collective-permute-start.18 = (bf16[1,128,896]{2,1,0:T(8,128)(2,1)S(1)}, bf16[1,128,896]{2,1,0:T(8,128)(2,1)S(1)}, u32[]{:S(2)}, u32[]{:S(2)}) collective-permute-start(bf16[1,128,896]{2,1,0:T(8,128)(2,1)S(1)} %add_convert_fusion.4), channel_id=1, source_target_pairs={{0,4},{1,5},{2,6},{3,7},{4,0},{5,1},{6,2},{7,3},{8,12},{9,13},{10,... | collective-permute-start | bytes 688136 | tf_op jit(solution)/shard_map/ppermute | solution.py:598
  440.4 11.2 %collective-permute-start.15 = (bf16[1,128,896]{2,1,0:T(8,128)(2,1)S(1)}, bf16[1,128,896]{2,1,0:T(8,128)(2,1)S(1)}, u32[]{:S(2)}, u32[]{:S(2)}) collective-permute-start(bf16[1,128,896]{2,1,0:T(8,128)(2,1)S(1)} %add_convert_fusion.6), channel_id=1, source_target_pairs={{0,4},{1,5},{2,6},{3,7},{4,0},{5,1},{6,2},{7,3},{8,12},{9,13},{10,... | collective-permute-start | bytes 688136 | tf_op jit(solution)/shard_map/ppermute | solution.py:598
  452.4 1.8 copy-start

commit v2 on v1

--- a/solution.py
+++ b/solution.py
@@ -11,6 +11,11 @@
 
 gelu_scale = math.sqrt(2.0 / math.pi)
 VMEM_LIMIT = 60 * 1024 * 1024
+IN_UNROLL = 32
+OUT_UNROLL = 56
+CHUNK = 28
+ADAM_UNROLL = 8
+ADAM_PARTS = 4
 
 F32 = jnp.float32
 BF16 = jnp.bfloat16
@@ -60,35 +65,33 @@
     )(send_slots, dp_index, tiles)
 
 
-def pack_moments(arrays, send_slots):
-    slots, rows, width = arrays[0].shape
-    count = send_slots.shape[0]
+def pack_moments(arrays, send_slots, bucket):
+    _, rows, width = arrays[0].shape
+    targets = send_slots.shape[0] // bucket
     kinds = len(arrays)
 
     def kernel(send_ref, *refs):
-        out_ref = refs[-1]
-
-        def step(i, carry):
-            s = send_ref[i]
-            for k in range(kinds):
-                out_ref[i, k] = refs[k][s].astype(BF16)
-            return carry
-
-        lax.fori_loop(0, count, step, 0, unroll=4)
-
-    whole = pl.BlockSpec((slots, rows, width), lambda i, s: (0, 0, 0))
+        outs = refs[kinds:]
+        unroll = math.gcd(bucket, 4)
+        for m in range(targets):
+
+            def step(i, carry, m=m):
+                for u in range(unroll):
+                    s = send_ref[m * bucket + i * unroll + u]
+                    for k in range(kinds):
+                        outs[m][i * unroll + u, k] = refs[k][s].astype(BF16)
+                return carry
+
+            lax.fori_loop(0, bucket // unroll, step, 0)
+
     return pl.pallas_call(
         kernel,
-        out_shape=jax.ShapeDtypeStruct((count, kinds, rows, width), BF16),
-        grid_spec=pltpu.PrefetchScalarGridSpec(
-            num_scalar_prefetch=1,
-            grid=(1,),
-            in_specs=[whole] * kinds,
-            out_specs=pl.BlockSpec((count, kinds, rows, width), lambda i, s: (0, 0, 0, 0)),
-        ),
+        out_shape=[jax.ShapeDtypeStruct((bucket, kinds, rows, width), BF16)] * targets,
+        in_specs=[SMEM] + [pl.BlockSpec(memory_space=pltpu.VMEM)] * kinds,
+        out_specs=[pl.BlockSpec(memory_space=pltpu.VMEM)] * targets,
         compiler_params=pltpu.CompilerParams(vmem_limit_bytes=VMEM_LIMIT),
         cost_estimate=pl.CostEstimate(
-            flops=0, transcendentals=0, bytes_accessed=6 * kinds * count * rows * width
+            flops=0, transcendentals=0, bytes_accessed=6 * kinds * targets * bucket * rows * width
         ),
         name="pack_moments",
     )(send_slots, *arrays)
@@ -135,7 +138,7 @@
     feats = refs[6 : 6 + n_feat]
     up_hbm = refs[6 + n_feat]
     parts = refs[7 + n_feat : 7 + n_feat + n_dp]
-    pre, x_t, wu_hbm, x_v, up_v, up_a, wu, feat_sem, in_sem, out_sem = refs[7 + n_feat + n_dp :]
+    act, act_t, slopes, x_t, wu_hbm, x_v, up_v, up_a, wu, pre, feat_sem, in_sem, out_sem = refs[7 + n_feat + n_dp :]
     slots, block, _ = up_v.shape
     copies = feature_copies(feats, 0, place_ref, x_v, feat_sem)
     copies += weight_copies(up_hbm, up_v, parts, up_a, place_ref, in_sem)
@@ -144,7 +147,7 @@
     pre[...] = jnp.zeros(pre.shape, F32)
     for copy in copies:
         copy.wait()
-    unroll = 4
+    unroll = math.gcd(slots, IN_UNROLL)
 
     def step(i, carry):
         got = []
@@ -167,6 +170,16 @@
         return carry
 
     lax.fori_loop(0, row_blocks, turn, 0)
+
+    def bend(c, carry):
+        value, slope = gelu_pair(pre[c])
+        narrow = value.astype(BF16)
+        act[c] = narrow
+        act_t[c] = narrow.T
+        slopes[c] = slope
+        return carry
+
+    lax.fori_loop(0, pre.shape[0], bend, 0)
     keep.wait()
 
 
@@ -175,11 +188,11 @@
     feats = refs[6 : 6 + n_feat]
     down_hbm = refs[6 + n_feat]
     parts = refs[7 + n_feat : 7 + n_feat + n_dp]
-    pre, x_t = refs[7 + n_feat + n_dp : 9 + n_feat + n_dp]
-    outs = refs[9 + n_feat + n_dp :]
-    act, bpre, wd_hbm = outs[:3]
-    grad_refs = outs[3 : 3 + n_dp]
-    back_v, down_v, down_a, wd, back, act_t, stage, feat_sem, in_sem, keep_sem, out_sem = outs[3 + n_dp :]
+    act_t, slopes, x_t = refs[7 + n_feat + n_dp : 10 + n_feat + n_dp]
+    outs = refs[10 + n_feat + n_dp :]
+    bpre, wd_hbm = outs[:2]
+    grad_refs = outs[2 : 2 + n_dp]
+    back_v, down_v, down_a, wd, back, stage, feat_sem, in_sem, keep_sem, out_sem = outs[2 + n_dp :]
     slots, block, _ = down_v.shape
     rows = block // n_dp
     nx = n_dp // 2
@@ -191,7 +204,7 @@
     back[...] = jnp.zeros(back.shape, F32)
     for copy in copies:
         copy.wait()
-    unroll = 4
+    unroll = math.gcd(slots, IN_UNROLL)
 
     def backward(i, carry):
         got = []
@@ -214,14 +227,10 @@
     keep.start()
 
     def bend(c, carry):
-        value, slope = gelu_pair(pre[c])
-        narrow = value.astype(BF16)
-        act[c] = narrow
-        act_t[c] = narrow.T
-        bpre[c] = (back[c] * slope).astype(BF16)
+        bpre[c] = (back[c] * slopes[c]).astype(BF16)
         return carry
 
-    lax.fori_loop(0, pre.shape[0], bend, 0)
+    lax.fori_loop(0, slopes.shape[0], bend, 0)
 
     def ship(i, slot):
         out = []
@@ -282,7 +291,7 @@
     for copy in loads:
         copy.start()
     acc[...] = jnp.zeros(acc.shape, F32)
-    unroll = 2
+    unroll = math.gcd(some, OUT_UNROLL)
     dims = (((1,), (1 if turned else 0,)), ((), ()))
 
     def step(i, carry):
@@ -337,17 +346,20 @@
     return pl.pallas_call(
         functools.partial(forward_kernel, n_feat, n_dp, row_blocks),
         out_shape=[
+            jax.ShapeDtypeStruct((col_count, tokens, block), BF16),
+            jax.ShapeDtypeStruct((col_count, block, tokens), BF16),
             jax.ShapeDtypeStruct((col_count, tokens, block), F32),
             jax.ShapeDtypeStruct((row_blocks, block, tokens), BF16),
             jax.ShapeDtypeStruct(up.shape, BF16),
         ],
         in_specs=[SMEM] * 6 + [ANY] * (n_feat + 1 + n_dp),
-        out_specs=[VMEM, VMEM, ANY],
+        out_specs=[VMEM] * 4 + [ANY],
         scratch_shapes=[
             pltpu.VMEM(feat_shape, BF16),
             pltpu.VMEM(up.shape, BF16),
             pltpu.VMEM((n_dp,) + parts[0].shape, BF16),
             pltpu.VMEM(up.shape, BF16),
+            pltpu.VMEM((col_count, tokens, block), F32),
             pltpu.SemaphoreType.DMA((n_feat,)),
             pltpu.SemaphoreType.DMA((1 + n_dp,)),
             pltpu.SemaphoreType.DMA,
@@ -358,27 +370,26 @@
     )(*tables, place, *feats, up, *parts)
 
 
-def gradient_products(tables, place, feats, down, parts, pre, x_t, feat_shape):
+def gradient_products(tables, place, feats, down, parts, act_t, slopes, x_t, feat_shape):
     slots, block, _ = down.shape
     n_dp, n_feat = len(parts), len(feats)
     rows = block // n_dp
-    chunk = 8
-    col_count, tokens, _ = pre.shape
+    chunk = math.gcd(slots, CHUNK)
+    tokens = slopes.shape[1]
     grad = jax.ShapeDtypeStruct((2, slots, rows, block), BF16)
     return pl.pallas_call(
         functools.partial(gradient_kernel, n_feat, n_dp),
-        out_shape=[jax.ShapeDtypeStruct(pre.shape, BF16)] * 2
+        out_shape=[jax.ShapeDtypeStruct(slopes.shape, BF16)]
         + [jax.ShapeDtypeStruct(down.shape, BF16)]
         + [grad] * n_dp,
-        in_specs=[SMEM] * 6 + [ANY] * (n_feat + 1 + n_dp) + [VMEM] * 2,
-        out_specs=[VMEM, VMEM] + [ANY] * (1 + n_dp),
+        in_specs=[SMEM] * 6 + [ANY] * (n_feat + 1 + n_dp) + [VMEM] * 3,
+        out_specs=[VMEM] + [ANY] * (1 + n_dp),
         scratch_shapes=[
             pltpu.VMEM(feat_shape, BF16),
             pltpu.VMEM(down.shape, BF16),
             pltpu.VMEM((n_dp,) + parts[0].shape, BF16),
             pltpu.VMEM(down.shape, BF16),
-            pltpu.VMEM(pre.shape, F32),
-            pltpu.VMEM((col_count, block, tokens), BF16),
+            pltpu.VMEM(slopes.shape, F32),
             pltpu.VMEM((2, 2, chunk, block, block), BF16),
             pltpu.SemaphoreType.DMA((n_feat,)),
             pltpu.SemaphoreType.DMA((1 + n_dp,)),
@@ -388,7 +399,7 @@
         compiler_params=pltpu.CompilerParams(vmem_limit_bytes=VMEM_LIMIT),
         cost_estimate=cost(6 * slots * tokens * block * block, 20 * slots * block * block),
         name="gradient_products",
-    )(*tables, place, *feats, down, *parts, pre, x_t)
+    )(*tables, place, *feats, down, *parts, act_t, slopes, x_t)
 
 
 def output_products(row, col, place, w, left, turned, pieces, feat_shape, row_blocks):
@@ -415,12 +426,43 @@
 def adam_step(tables, grads, which, moments, arrived):
     slots, rows, block = moments[0].shape
     n_grads = len(grads)
+    n_from = len(arrived)
+    bucket = arrived[0].shape[0]
+    parts = math.gcd(slots, ADAM_PARTS)
+    some = slots // parts
 
     def kernel(home_ref, came_ref, kind_ref, *refs):
         grad_refs = refs[:n_grads]
         moment_refs = refs[n_grads : n_grads + 2]
-        arrived_ref = refs[n_grads + 2]
-        out = refs[n_grads + 3]
+        arrived_refs = refs[n_grads + 2 : n_grads + 2 + n_from]
+        out_hbm, grad_v, moment_v, arrived_v, out_v, grad_sem, moment_sem, arrived_sem, out_sem = refs[
+            n_grads + 2 + n_from :
+        ]
+        first = [
+            pltpu.make_async_copy(moment_refs[k], moment_v.at[k], moment_sem.at[k]) for k in range(2)
+        ] + [
+            pltpu.make_async_copy(arrived_refs[m], arrived_v.at[pl.ds(m * bucket, bucket)], arrived_sem.at[m])
+            for m in range(n_from)
+        ]
+        later = [
+            [
+                pltpu.make_async_copy(
+                    grad_refs[k].at[which, pl.ds(q * some, some)],
+                    grad_v.at[k, pl.ds(q * some, some)],
+                    grad_sem.at[q, k],
+                )
+                for k in range(n_grads)
+            ]
+            for q in range(parts)
+        ]
+        outs = [
+            pltpu.make_async_copy(
+                out_v.at[pl.ds(q * some, some)], out_hbm.at[pl.ds(q * some, some)], out_sem.at[q]
+            )
+            for q in range(parts)
+        ]
+        for copy in first + sum(later, []):
+            copy.start()
 
         def step(g, carry):
             at = came_ref[g]
@@ -428,34 +470,53 @@
             kind = kind_ref[g]
 
             def moved(k):
-                picked = lax.select(kind == 1, moment_refs[k][own], arrived_ref[at, k].astype(F32))
+                picked = lax.select(kind == 1, moment_v[k, own], arrived_v[at, k].astype(F32))
                 return lax.select(kind == 0, jnp.zeros_like(picked), picked)
 
-            total = grad_refs[0][0, g].astype(F32)
-            for ref in grad_refs[1:]:
-                total = total + ref[0, g].astype(F32)
-            first = 0.9 * moved(0) + 0.1 * total
-            second = 0.95 * moved(1) + 0.05 * total * total
-            out[g] = first / (jnp.sqrt(second) + 1.0)
+            total = grad_v[0, g].astype(F32)
+            for k in range(1, n_grads):
+                total = total + grad_v[k, g].astype(F32)
+            first_moment = 0.9 * moved(0) + 0.1 * total
+            second_moment = 0.95 * moved(1) + 0.05 * total * total
+            out_v[g] = first_moment / (jnp.sqrt(second_moment) + 1.0)
             return carry
 
-        lax.fori_loop(0, slots, step, 0, unroll=4)
-
-    half = pl.BlockSpec((1, slots, rows, block), lambda i: (which, 0, 0, 0))
-
-    def whole(array):
-        return pl.BlockSpec(array.shape, lambda i: (0,) * array.ndim)
+        for copy in first:
+            copy.wait()
+        unroll = math.gcd(some, ADAM_UNROLL)
+        for q in range(parts):
+            for copy in later[q]:
+                copy.wait()
+
+            def trip(i, carry, q=q):
+                for u in range(unroll):
+                    step(q * some + i * unroll + u, carry)
+                return carry
+
+            lax.fori_loop(0, some // unroll, trip, 0)
+            outs[q].start()
+        for copy in outs:
+            copy.wait()
 
     return pl.pallas_call(
         kernel,
         out_shape=jax.ShapeDtypeStruct(moments[0].shape, F32),
-        grid=(1,),
-        in_specs=[SMEM] * 3 + [half] * n_grads + [whole(m) for m in moments] + [whole(arrived)],
-        out_specs=whole(moments[0]),
+        in_specs=[SMEM] * 3 + [ANY] * (n_grads + 2 + n_from),
+        out_specs=ANY,
+        scratch_shapes=[
+            pltpu.VMEM((n_grads, slots, rows, block), BF16),
+            pltpu.VMEM((2, slots, rows, block), F32),
+            pltpu.VMEM((n_from * bucket, 2, rows, block), BF16),
+            pltpu.VMEM((slots, rows, block), F32),
+            pltpu.SemaphoreType.DMA((parts, n_grads)),
+            pltpu.SemaphoreType.DMA((2,)),
+            pltpu.SemaphoreType.DMA((n_from,)),
+            pltpu.SemaphoreType.DMA((parts,)),
+        ],
         compiler_params=pltpu.CompilerParams(vmem_limit_bytes=VMEM_LIMIT),
         cost_estimate=cost(15 * slots * rows * block, 17 * slots * rows * block),
         name="adam_step",
-    )(*tables, *grads, *moments, arrived)
+    )(*tables, *grads, *moments, *arrived)
 
 
 def layer(
@@ -507,6 +568,12 @@
     home = jnp.where(stays, mine_slot, 0)
     came = jnp.where(mine_live & ~stays, mine_dev * bucket + recv_rank, 0)
     kind = jnp.where(stays, 1, jnp.where(mine_live, 2, 0)).astype(jnp.int32)
+    distance = lax.rem(my_index - mine_dev + tensor_size, tensor_size)
+    came_moment = jnp.where(mine_live & ~stays, (distance - 1) * bucket + recv_rank, 0)
+    by_target = send_slots.reshape(tensor_size, bucket)
+    by_distance = lax.dynamic_slice_in_dim(
+        jnp.concatenate([by_target, by_target], axis=0), my_index + 1, tensor_size - 1, axis=0
+    ).reshape(-1)
     col_count = col_owner.shape[0] // tensor_size
     col_slot = jnp.take(local_columns(col_owner), new_col)
     place = jnp.stack([my_dp // 2, my_dp % 2, my_index]).astype(jnp.int32)
@@ -561,16 +628,24 @@
 
     ups = (up_first_moment, up_second_moment)
     downs = (down_first_moment, down_second_moment)
-    ups_pack = pack_moments(ups, send_slots)
-    downs_pack = pack_moments(downs, send_slots)
-    ups_in = exchange(ups_pack)
-    downs_in = exchange(downs_pack)
-
-    pre, x_t, wu = forward_products(
+
+    def exchange_parts(parts):
+        got = []
+        for m, part in enumerate(parts, 1):
+            pairs = [(t, (t + m) % tensor_size) for t in range(tensor_size)]
+            got.append(lax.ppermute(part, "tensor", pairs))
+        return got
+
+    ups_pack = pack_moments(ups, by_distance, bucket)
+    downs_pack = pack_moments(downs, by_distance, bucket)
+    ups_in = exchange_parts(ups_pack)
+    downs_in = exchange_parts(downs_pack)
+
+    act, act_t, slopes, x_t, wu = forward_products(
         tables, place, feats, up_weight_blocks, up_parts, col_count, row_blocks, feat_shape
     )
-    act, bpre, wd, *grads = gradient_products(
-        tables, place, feats, down_weight_blocks, down_parts, pre, x_t, feat_shape
+    bpre, wd, *grads = gradient_products(
+        tables, place, feats, down_weight_blocks, down_parts, act_t, slopes, x_t, feat_shape
     )
     terms = []
     for j in range(nx):
@@ -605,8 +680,8 @@
         sums.append(sum(s[0].astype(F32) for s in held).astype(BF16))
     out_sum, in_sum = sums
 
-    up_step = adam_step((home, came, kind), terms, 0, ups, ups_in)
-    down_step = adam_step((home, came, kind), terms, 1, downs, downs_in)
+    up_step = adam_step((home, came_moment, kind), terms, 0, ups, ups_in)
+    down_step = adam_step((home, came_moment, kind), terms, 1, downs, downs_in)
     return (out_sum, in_sum, up_step, down_step)
 
 

time: 479 us -> 477 us (level); the launches traced: 478 us -> 469 us
  Pallas kernels: 152 us -> 101 us
  starting transfers between devices: 50.3 us -> 90.2 us
    ppermute x7, waiting for transfers between devices: 124 us -> 46.2 us  [layer(): held[m ^ bit] = lax.ppermute(held[m], 'tensor', far_pairs(bit))]
    ppermute x0 -> x14, waiting for transfers between devices: none -> 61 us  [exchange_parts(): got.append(lax.ppermute(part, 'tensor', pairs))]
    ppermute x0 -> x14, starting transfers between devices: none -> 60.4 us  [exchange_parts(): got.append(lax.ppermute(part, 'tensor', pairs))]
    pallas_call x2, Pallas kernels: 46.5 us -> 16.9 us  [output_products(): pl.pallas_call(functools.partial(output_kernel, pieces, turned), out_shap...]
    ppermute x2, waiting for transfers between devices: 0.01 us -> 16.9 us  [spread(): mine = lax.ppermute(own, 'dp', x_pairs(j))]
    pallas_call x1, Pallas kernels: 38.6 us -> 24.3 us  [gradient_products(): pl.pallas_call(functools.partial(gradient_kernel, n_feat, n_dp), out_shap...]
    all_to_all x4 -> x2, starting transfers between devices: 23 us -> 11.6 us  [exchange(): lax.all_to_all(shaped, 'tensor', split_axis=0, concat_axis=0, tiled=True)]
    ppermute x6, waiting for transfers between devices: 52.8 us -> 43.9 us  [layer(): held.append(lax.ppermute(send, 'tensor', far_pairs(bit)))]
  transfers between devices with their start and end apart: 26 -> 38, of which waited for: 11 -> 22; matrix products, arithmetic and copies ran while one was open for 3% -> 3% of each run, Pallas kernels for 29% -> 13%
where the time goes in v2:
time: 477 us; the launch traced here: 469 us
  waiting for transfers between devices  254 us (53%)
  Pallas kernels  101 us (21%)
  starting transfers between devices  90.2 us (19%)
  other arithmetic  16.3 us (3%)
  local copies, waits for them, and re-layouts  6.28 us (1%)
    all_to_all x2, waiting for transfers between devices, exchange(): lax.all_to_all(shaped, 'tensor', split_axis=0, concat_axis=0, tiled=True)  79.5 us
    ppermute x14, waiting for transfers between devices, exchange_parts(): got.append(lax.ppermute(part, 'tensor', pairs))  61 us
    ppermute x14, starting transfers between devices, exchange_parts(): got.append(lax.ppermute(part, 'tensor', pairs))  60.4 us
    ppermute x7, waiting for transfers between devices, layer(): held[m ^ bit] = lax.ppermute(held[m], 'tensor', far_pairs(bit))  46.2 us
    ppermute x6, waiting for transfers between devices, layer(): held.append(lax.ppermute(send, 'tensor', far_pairs(bit)))  43.9 us
    pallas_call x1, Pallas kernels, gradient_products(): pl.pallas_call(functools.partial(gradient_kernel, n_feat, n_dp), out_shap...  24.3 us
    pallas_call x2, Pallas kernels, adam_step(): pl.pallas_call(kernel, out_shape=jax.ShapeDtypeStruct(moments[0].shape, F...  22.1 us
    pallas_call x1, Pallas kernels, forward_products(): pl.pallas_call(functools.partial(forward_kernel, n_feat, n_dp, row_blocks...  19 us
  transfers between devices with their start and end apart: 38, of which 22 were waited for; matrix products, arithmetic and copies ran while one was open for 3% of the time, Pallas kernels for 13%

profile of v2, /device:TPU:0, one launch (start us, length us, event | category | flops | bytes accessed | tf_op | source)
XLA Modules:
  0.0 468.7 jit_solution(3200241638379381020)
XLA Ops:
  4.7 3.8 pack_weight.3
  8.5 7.3 %all-to-all-start.1 = ((bf16[8,28,32,128]{3,2,1,0:T(8,128)(2,1)}), bf16[8,28,32,128]{3,2,1,0:T(8,128)(2,1)S(1)}, u32[]{:S(2)}, u32[]{:S(2)}) async-start(bf16[8,28,32,128]{3,2,1,0:T(8,128)(2,1)} %bitcast.24), calls=%async_computation.1 | async-start | bytes 3670016 | tf_op jit(solution)/shard_map/all_to_all | solution.py:585
  15.8 3.8 pack_weight.2
  19.6 38.8 %all-to-all-done.1 = bf16[8,28,32,128]{3,2,1,0:T(8,128)(2,1)S(1)} async-done(((bf16[8,28,32,128]{3,2,1,0:T(8,128)(2,1)}), bf16[8,28,32,128]{3,2,1,0:T(8,128)(2,1)S(1)}, u32[]{:S(2)}, u32[]{:S(2)}) %all-to-all-start.1) | async-done | bytes 1835040 | tf_op jit(solution)/shard_map/all_to_all | solution.py:585
  58.4 4.3 all-to-all-start
  62.7 1.6 collective-permute-start.11
  64.3 40.7 %all-to-all-done = bf16[8,28,32,128]{3,2,1,0:T(8,128)(2,1)} async-done(((bf16[8,28,32,128]{3,2,1,0:T(8,128)(2,1)}), bf16[8,28,32,128]{3,2,1,0:T(8,128)(2,1)}, u32[]{:S(2)}, u32[]{:S(2)}) %all-to-all-start) | async-done | bytes 1835040 | tf_op jit(solution)/shard_map/all_to_all | solution.py:585
  105.0 1.5 collective-permute-start.8
  106.6 2.4 collective-permute-start.1
  110.1 17.9 %collective-permute-done.3.refs_10_ = bf16[2,128,896]{2,1,0:T(8,128)(2,1)S(1)} collective-permute-done((bf16[2,128,896]{2,1,0:T(8,128)(2,1)S(1)}, bf16[2,128,896]{2,1,0:T(8,128)(2,1)S(1)}, u32[]{:S(2)}, u32[]{:S(2)}) %collective-permute-start.3) | collective-permute-done | bytes 458784 | tf_op jit(solution)/shard_map/ppermute | solution.py:619
  128.6 16.9 %collective-permute-done.8.refs_17_ = bf16[224,32,128]{2,1,0:T(8,128)(2,1)} collective-permute-done((bf16[224,32,128]{2,1,0:T(8,128)(2,1)}, bf16[224,32,128]{2,1,0:T(8,128)(2,1)}, u32[]{:S(2)}, u32[]{:S(2)}) %collective-permute-start.8) | collective-permute-done | bytes 1835040 | tf_op jit(solution)/shard_map/ppermute | solution.py:601
  146.4 2.2 collective-permute-start.4
  148.6 11.3 %collective-permute-done.4.refs_11_ = bf16[2,128,896]{2,1,0:T(8,128)(2,1)} collective-permute-done((bf16[2,128,896]{2,1,0:T(8,128)(2,1)S(1)}, bf16[2,128,896]{2,1,0:T(8,128)(2,1)}, u32[]{:S(2)}, u32[]{:S(2)}) %collective-permute-start.4) | collective-permute-done | bytes 458784 | tf_op jit(solution)/shard_map/ppermute | solution.py:619
  159.9 1.7 collective-permute-start.2
  162.0 10.3 %collective-permute-done.2.refs_9_ = bf16[2,128,896]{2,1,0:T(8,128)(2,1)} collective-permute-done((bf16[2,128,896]{2,1,0:T(8,128)(2,1)S(1)}, bf16[2,128,896]{2,1,0:T(8,128)(2,1)}, u32[]{:S(2)}, u32[]{:S(2)}) %collective-permute-start.2) | collective-permute-done | bytes 458784 | tf_op jit(solution)/shard_map/ppermute | solution.py:619
  174.4 1.9 gather_fusion
  177.4 6.7 %collective-permute-done.6.refs_13_ = bf16[2,128,896]{2,1,0:T(8,128)(2,1)} collective-permute-done((bf16[2,128,896]{2,1,0:T(8,128)(2,1)}, bf16[2,128,896]{2,1,0:T(8,128)(2,1)}, u32[]{:S(2)}, u32[]{:S(2)}) %collective-permute-start.6) | collective-permute-done | bytes 458784 | tf_op jit(solution)/shard_map/ppermute | solution.py:619
  184.2 19.0 %forward_products.1 = (bf16[16,128,128]{2,1,0:T(8,128)(2,1)}, bf16[16,128,128]{2,1,0:T(8,128)(2,1)}, f32[16,128,128]{2,1,0:T(8,128)}, bf16[56,128,128]{2,1,0:T(8,128)(2,1)}, bf16[224,128,128]{2,1,0:T(8,128)(2,1)}) custom-call(s32[224]{0:T(256)} %refs_0_.9, s32[224]{0:T(256)} %and_select_fusion.refs_1_, s32[224]{0:T(256)} %get-tuple-element.73.refs_2_.home_ref, ...), custom_call_target="tpu_custom_call" | custom-call | flops 939524096 | bytes 44040192 | tf_op jit(solution)/shard_map/forward_products/pallas_call | solution.py:346
  203.2 24.3 %gradient_products.1 = (bf16[16,128,128]{2,1,0:T(8,128)(2,1)}, bf16[224,128,128]{2,1,0:T(8,128)(2,1)}, bf16[2,224,32,128]{3,2,1,0:T(8,128)(2,1)}, bf16[2,224,32,...) custom-call(s32[224]{0:T(256)} %refs_0_.9, s32[224]{0:T(256)} %and_select_fusion.refs_1_, ...), custom_call_target="tpu_custom_call" | custom-call | flops 2818572288 | bytes 73400320 | tf_op jit(solution)/shard_map/gradient_products/pallas_call | solution.py:380
  228.1 6.1 %collective-permute-done.20 = bf16[2,224,32,128]{3,2,1,0:T(8,128)(2,1)S(1)} collective-permute-done((bf16[2,224,32,128]{3,2,1,0:T(8,128)(2,1)}, bf16[2,224,32,128]{3,2,1,0:T(8,128)(2,1)S(1)}, u32[]{:S(2)}, u32[]{:S(2)}) %collective-permute-start.20) | collective-permute-done | bytes 3670048 | tf_op jit(solution)/shard_map/ppermute | solution.py:652
  234.3 4.8 %add_convert_fusion = bf16[2,224,32,128]{3,2,1,0:T(8,128)(2,1)} fusion(bf16[2,224,32,128]{3,2,1,0:T(8,128)(2,1)S(1)} %collective-permute-done.20, bf16[2,224,32,128]{3,2,1,0:T(8,128)(2,1)} %get-tuple-element.46), kind=kLoop, calls=%fused_computation.1 | loop fusion | flops 7340032 | bytes 11010048 | tf_op jit(solution)/shard_map/convert_element_type | solution.py:656
  239.1 1.5 collective-permute-start.21
  241.4 5.6 %pack_moments.3 = (bf16[28,2,32,128]{3,2,1,0:T(8,128)(2,1)}, bf16[28,2,32,128]{3,2,1,0:T(8,128)(2,1)}, bf16[28,2,32,128]{3,2,1,0:T(8,128)(2,1)}, bf16[28,2,32,12...) custom-call(s32[196]{0:T(256)} %reshape.138.send_ref, ...), custom_call_target="tpu_custom_call" | custom-call | bytes 9633792 | tf_op jit(solution)/shard_map/pack_moments/pallas_call | solution.py:87
  248.2 3.4 collective-permute-start.31
  251.5 9.7 %output_products.3 = (bf16[4,128,896]{2,1,0:T(8,128)(2,1)}, bf16[4,128,896]{2,1,0:T(8,128)(2,1)}) custom-call(s32[224]{0:T(256)} %refs_0_.9, s32[224]{0:T(256)} %and_select_fusion.refs_1_, s32[3]{0:T(128)} %pad_add_fusion.refs_5_.refs_2_, bf16[224,128,128]{2,1,0:T(8,128)(2,1)} %get-tuple-element.40.refs_3_, bf16[16,128,128]{2,1,0:T(8,128)(2,1)} %get-tuple-element.41.refs_4_), custom_call_target="tpu_custom_call" | custom-call | flops 939524096 | bytes 14680064 | tf_op jit(solution)/shard_map/output_products/pallas_call | solution.py:408
  261.2 2.2 collective-permute-done.29.refs_5_
  264.3 7.2 %output_products.2 = (bf16[4,128,896]{2,1,0:T(8,128)(2,1)}, bf16[4,128,896]{2,1,0:T(8,128)(2,1)}) custom-call(s32[224]{0:T(256)} %refs_0_.9, s32[224]{0:T(256)} %and_select_fusion.refs_1_, s32[3]{0:T(128)} %pad_add_fusion.refs_5_.refs_2_, bf16[224,128,128]{2,1,0:T(8,128)(2,1)} %get-tuple-element.36.refs_3_, bf16[16,128,128]{2,1,0:T(8,128)(2,1)} %get-tuple-element.37.refs_4_), custom_call_target="tpu_custom_call" | custom-call | flops 939524096 | bytes 14680064 | tf_op jit(solution)/shard_map/output_products/pallas_call | solution.py:408
  271.5 30.0 %collective-permute-done.31.refs_7_ = bf16[28,2,32,128]{3,2,1,0:T(8,128)(2,1)S(1)} collective-permute-done((bf16[28,2,32,128]{3,2,1,0:T(8,128)(2,1)}, bf16[28,2,32,128]{3,2,1,0:T(8,128)(2,1)S(1)}, u32[]{:S(2)}, u32[]{:S(2)}) %collective-permute-start.31) | collective-permute-done | bytes 458784 | tf_op jit(solution)/shard_map/ppermute | solution.py:636
  301.6 9.4 %collective-permute-start.33 = (bf16[28,2,32,128]{3,2,1,0:T(8,128)(2,1)S(1)}, bf16[28,2,32,128]{3,2,1,0:T(8,128)(2,1)S(1)}, u32[]{:S(2)}, u32[]{:S(2)}) collective-permute-start(bf16[28,2,32,128]{3,2,1,0:T(8,128)(2,1)S(1)} %copy-done.19), channel_id=1, source_target_pairs={{0,5},{1,6},{2,7},{3,0},{4,1},{5,2},{6,3},{7,4},{8,13},{9,14},{10,... | collective-permute-start | bytes 1376264 | tf_op jit(solution)/shard_map/ppermute | solution.py:636
  311.9 10.1 %collective-permute-done.33.refs_9_ = bf16[28,2,32,128]{3,2,1,0:T(8,128)(2,1)S(1)} collective-permute-done((bf16[28,2,32,128]{3,2,1,0:T(8,128)(2,1)S(1)}, bf16[28,2,32,128]{3,2,1,0:T(8,128)(2,1)S(1)}, u32[]{:S(2)}, u32[]{:S(2)}) %collective-permute-start.33) | collective-permute-done | bytes 458784 | tf_op jit(solution)/shard_map/ppermute | solution.py:636
  322.0 20.5 %collective-permute-start.35 = (bf16[28,2,32,128]{3,2,1,0:T(8,128)(2,1)}, bf16[28,2,32,128]{3,2,1,0:T(8,128)(2,1)}, u32[]{:S(2)}, u32[]{:S(2)}) collective-permute-start(bf16[28,2,32,128]{3,2,1,0:T(8,128)(2,1)} %get-tuple-element.61), channel_id=1, source_target_pairs={{0,7},{1,0},{2,1},{3,2},{4,3},{5,4},{6,5},{7,6},{8,15},{9,8},{10,9... | collective-permute-start | bytes 1376264 | tf_op jit(solution)/shard_map/ppermute | solution.py:636
  342.5 1.9 add_convert_fusion.2
  345.2 2.0 collective-permute-start.14
  347.2 5.6 %pack_moments.2 = (bf16[28,2,32,128]{3,2,1,0:T(8,128)(2,1)}, bf16[28,2,32,128]{3,2,1,0:T(8,128)(2,1)}, bf16[28,2,32,128]{3,2,1,0:T(8,128)(2,1)}, bf16[28,2,32,12...) custom-call(s32[196]{0:T(256)} %reshape.138.send_ref, ...), custom_call_target="tpu_custom_call" | custom-call | bytes 9633792 | tf_op jit(solution)/shard_map/pack_moments/pallas_call | solution.py:87
  352.8 10.8 %collective-permute-done.17 = bf16[2,128,896]{2,1,0:T(8,128)(2,1)S(1)} collective-permute-done((bf16[2,128,896]{2,1,0:T(8,128)(2,1)}, bf16[2,128,896]{2,1,0:T(8,128)(2,1)S(1)}, u32[]{:S(2)}, u32[]{:S(2)}) %collective-permute-start.17) | collective-permute-done | bytes 458784 | tf_op jit(solution)/shard_map/ppermute | solution.py:673
  363.6 2.4 collective-permute-start.23
  366.1 11.3 %collective-permute-done.14 = bf16[2,128,896]{2,1,0:T(8,128)(2,1)} collective-permute-done((bf16[2,128,896]{2,1,0:T(8,128)(2,1)}, bf16[2,128,896]{2,1,0:T(8,128)(2,1)}, u32[]{:S(2)}, u32[]{:S(2)}) %collective-permute-start.14) | collective-permute-done | bytes 458784 | tf_op jit(solution)/shard_map/ppermute | solution.py:673
  379.9 1.5 collective-permute-start.15
  381.4 1.8 collective-permute-done.23.refs_6_
  383.2 21.5 %collective-permute-start.24 = (bf16[28,2,32,128]{3,2,1,0:T(8,128)(2,1)}, bf16[28,2,32,128]{3,2,1,0:T(8,128)(2,1)}, u32[]{:S(2)}, u32[]{:S(2)}) collective-permute-start(bf16[28,2,32,128]{3,2,1,0:T(8,128)(2,1)} %get-tuple-element.50), channel_id=1, source_target_pairs={{0,3},{1,4},{2,5},{3,6},{4,7},{5,0},{6,1},{7,2},{8,11},{9,12},{10,... | collective-permute-start | bytes 1376264 | tf_op jit(solution)/shard_map/ppermute | solution.py:636
  404.7 2.2 collective-permute-done.18
  406.9 19.7 %collective-permute-done.15 = bf16[1,128,896]{2,1,0:T(8,128)(2,1)S(1)} collective-permute-done((bf16[1,128,896]{2,1,0:T(8,128)(2,1)S(1)}, bf16[1,128,896]{2,1,0:T(8,128)(2,1)S(1)}, u32[]{:S(2)}, u32[]{:S(2)}) %collective-permute-start.15) | collective-permute-done | bytes 229408 | tf_op jit(solution)/shard_map/ppermute | solution.py:673
  426.6 1.9 collective-permute-start.28
  429.3 1.7 fusion
  431.1 11.1 %adam_step.3 = f32[224,32,128]{2,1,0:T(8,128)} custom-call(s32[224]{0:T(256)} %get-tuple-element.73.refs_2_.home_ref, s32[224]{0:T(256)} %get-tuple-element.71.came_ref, s32[224]{0:T(256)} %get-tuple-element.74.refs_4_.kind_ref, bf16[2,224,32,128]{3,2,1,0:T(8,128)(2,1)} %get-tuple-element.44.refs_0_, ...), custom_call_target="tpu_custom_call" | custom-call | flops 13762560 | bytes 15597568 | tf_op jit(solution)/shard_map/adam_step/pallas_call | solution.py:501
  442.2 10.6 %collective-permute-done.26.refs_9_ = bf16[28,2,32,128]{3,2,1,0:T(8,128)(2,1)} collective-permute-done((bf16[28,2,32,128]{3,2,1,0:T(8,128)(2,1)}, bf16[28,2,32,128]{3,2,1,0:T(8,128)(2,1)}, u32[]{:S(2)}, u32[]{:S(2)}) %collective-permute-start.26) | collective-permute-done | bytes 458784 | tf_op jit(solution)/shard_map/ppermute | solution.py:636
  452.8 3.3 collective-permute-done.27.refs_10_
  457.5 11.1 %adam_step.2 = f32[224,32,128]{2,1,0:T(8,128)} custom-call(s32[224]{0:T(256)} %get-tuple-element.73.refs_2_.home_ref, s32[224]{0:T(256)} %get-tuple-element.71.came_ref, s32[224]{0:T(256)} %get-tuple-element.74.refs_4_.kind_ref, bf16[2,224,32,128]{3,2,1,0:T(8,128)(2,1)} %get-tuple-element.44.refs_0_, ...), custom_call_target="tpu_custom_call" | custom-call | flops 13762560 | bytes 15597568 | tf_op jit(solution)/shard_map/adam_step/pallas_call | solution.py:501
  (119 shorter events, 20.4 us)
Async XLA Ops:
  8.5 49.9 %all-to-all-start.1 = ((bf16[8,28,32,128]{3,2,1,0:T(8,128)(2,1)}), bf16[8,28,32,128]{3,2,1,0:T(8,128)(2,1)S(1)}, u32[]{:S(2)}, u32[]{:S(2)}) async-start(bf16[8,28,32,128]{3,2,1,0:T(8,128)(2,1)} %bitcast.24), calls=%async_computation.1 | async-start | bytes 3670016 | tf_op jit(solution)/shard_map/all_to_all | solution.py:585
  19.6 86.9 %copy-start.16 = (bf16[128,896]{1,0:T(8,128)(2,1)S(1)}, bf16[128,896]{1,0:T(8,128)(2,1)}, u32[]{:S(2)}) copy-start(bf16[128,896]{1,0:T(8,128)(2,1)} %param.13) | copy-start | bytes 688132
  19.6 86.9 %copy-start.17 = (bf16[128,896]{1,0:T(8,128)(2,1)S(1)}, bf16[128,896]{1,0:T(8,128)(2,1)}, u32[]{:S(2)}) copy-start(bf16[128,896]{1,0:T(8,128)(2,1)} %param.12) | copy-start | bytes 688132
  19.6 129.0 %copy-start.18 = (s32[224]{0:T(256)S(1)}, s32[224]{0:T(256)}, u32[]{:S(2)}) copy-start(s32[224]{0:T(256)} %param.22) | copy-start | bytes 2692
  19.6 142.0 %copy-start.20 = (s32[128]{0:T(128)S(1)}, s32[128]{0:T(128)}, u32[]{:S(2)}) copy-start(s32[128]{0:T(128)} %param.23) | copy-start | bytes 1540
  58.4 125.7 %copy-start = (bf16[8,28,32,128]{3,2,1,0:T(8,128)(2,1)}, bf16[8,28,32,128]{3,2,1,0:T(8,128)(2,1)S(1)}, u32[]{:S(2)}) copy-start(bf16[8,28,32,128]{3,2,1,0:T(8,128)(2,1)S(1)} %all-to-all-done.1) | copy-start | bytes 5505028
  58.4 46.6 %all-to-all-start = ((bf16[8,28,32,128]{3,2,1,0:T(8,128)(2,1)}), bf16[8,28,32,128]{3,2,1,0:T(8,128)(2,1)}, u32[]{:S(2)}, u32[]{:S(2)}) async-start(bf16[8,28,32,128]{3,2,1,0:T(8,128)(2,1)} %bitcast.23), calls=%async_computation | async-start | bytes 3670016 | tf_op jit(solution)/shard_map/all_to_all | solution.py:585
  62.7 65.3 %collective-permute-start.11 = (bf16[224,32,128]{2,1,0:T(8,128)(2,1)S(1)}, bf16[224,32,128]{2,1,0:T(8,128)(2,1)}, u32[]{:S(2)}, u32[]{:S(2)}) collective-permute-start(bf16[224,32,128]{2,1,0:T(8,128)(2,1)S(1)} %bitcast.20), channel_id=1, source_target_pairs={{0,16},{8,24},{16,0},{24,8},{1,17},{9,25},{17,1},{25,9},{2,18},{10... | collective-permute-start | bytes 5505032 | tf_op jit(solution)/shard_map/ppermute | solution.py:601
  105.0 40.6 %collective-permute-start.8 = (bf16[224,32,128]{2,1,0:T(8,128)(2,1)}, bf16[224,32,128]{2,1,0:T(8,128)(2,1)}, u32[]{:S(2)}, u32[]{:S(2)}) collective-permute-start(bf16[224,32,128]{2,1,0:T(8,128)(2,1)} %bitcast.11.refs_15_), channel_id=1, source_target_pairs={{0,16},{8,24},{16,0},{24,8},{1,17},{9,25},{17,1},{25,9},{2,18},{10... | collective-permute-start | bytes 5505032 | tf_op jit(solution)/shard_map/ppermute | solution.py:601
  106.5 77.6 %copy-start.1 = (bf16[2,128,896]{2,1,0:T(8,128)(2,1)}, bf16[2,128,896]{2,1,0:T(8,128)(2,1)S(1)}, u32[]{:S(2)}) copy-start(bf16[2,128,896]{2,1,0:T(8,128)(2,1)S(1)} %pad_maximum_fusion.refs_6_) | copy-start | bytes 1376260
  106.5 21.4 %collective-permute-start.3 = (bf16[2,128,896]{2,1,0:T(8,128)(2,1)S(1)}, bf16[2,128,896]{2,1,0:T(8,128)(2,1)S(1)}, u32[]{:S(2)}, u32[]{:S(2)}) collective-permute-start(bf16[2,128,896]{2,1,0:T(8,128)(2,1)S(1)} %pad_maximum_fusion.refs_6_), channel_id=1, source_target_pairs={{0,4},{1,5},{2,6},{3,7},{4,0},{5,1},{6,2},{7,3},{8,12},{9,13},{10,... | collective-permute-start | bytes 1376264 | tf_op jit(solution)/shard_map/ppermute | solution.py:619
  106.6 21.4 %collective-permute-start.1 = (bf16[2,128,896]{2,1,0:T(8,128)(2,1)S(1)}, bf16[2,128,896]{2,1,0:T(8,128)(2,1)S(1)}, u32[]{:S(2)}, u32[]{:S(2)}) collective-permute-start(bf16[2,128,896]{2,1,0:T(8,128)(2,1)S(1)} %pad_maximum_fusion.refs_6_), channel_id=1, source_target_pairs={{0,2},{1,3},{2,0},{3,1},{4,6},{5,7},{6,4},{7,5},{8,10},{9,11},{10,... | collective-permute-start | bytes 1376264 | tf_op jit(solution)/shard_map/ppermute | solution.py:619
  109.0 19.5 %collective-permute-start = (bf16[2,128,896]{2,1,0:T(8,128)(2,1)S(1)}, bf16[2,128,896]{2,1,0:T(8,128)(2,1)S(1)}, u32[]{:S(2)}, u32[]{:S(2)}) collective-permute-start(bf16[2,128,896]{2,1,0:T(8,128)(2,1)S(1)} %pad_maximum_fusion.refs_6_), channel_id=1, source_target_pairs={{0,1},{1,0},{2,3},{3,2},{4,5},{5,4},{6,7},{7,6},{8,9},{9,8},{10,11... | collective-permute-start | bytes 1376264 | tf_op jit(solution)/shard_map/ppermute | solution.py:619
  127.9 56.2 %copy-start.2 = (bf16[2,128,896]{2,1,0:T(8,128)(2,1)}, bf16[2,128,896]{2,1,0:T(8,128)(2,1)S(1)}, u32[]{:S(2)}) copy-start(bf16[2,128,896]{2,1,0:T(8,128)(2,1)S(1)} %collective-permute-done.3.refs_10_) | copy-start | bytes 1376260
  127.9 17.6 %collective-permute-start.5 = (bf16[2,128,896]{2,1,0:T(8,128)(2,1)S(1)}, bf16[2,128,896]{2,1,0:T(8,128)(2,1)S(1)}, u32[]{:S(2)}, u32[]{:S(2)}) collective-permute-start(bf16[2,128,896]{2,1,0:T(8,128)(2,1)S(1)} %collective-permute-done.3.refs_10_), channel_id=1, source_target_pairs={{0,2},{1,3},{2,0},{3,1},{4,6},{5,7},{6,4},{7,5},{8,10},{9,11},{10,... | collective-permute-start | bytes 1376264 | tf_op jit(solution)/shard_map/ppermute | solution.py:619
  128.0 56.2 %copy-start.3 = (bf16[2,128,896]{2,1,0:T(8,128)(2,1)}, bf16[2,128,896]{2,1,0:T(8,128)(2,1)S(1)}, u32[]{:S(2)}) copy-start(bf16[2,128,896]{2,1,0:T(8,128)(2,1)S(1)} %collective-permute-done.1.refs_8_) | copy-start | bytes 1376260
  128.0 56.1 %collective-permute-start.10 = (bf16[224,32,128]{2,1,0:T(8,128)(2,1)S(1)}, bf16[224,32,128]{2,1,0:T(8,128)(2,1)}, u32[]{:S(2)}, u32[]{:S(2)}) collective-permute-start(bf16[224,32,128]{2,1,0:T(8,128)(2,1)S(1)} %bitcast.21), channel_id=1, source_target_pairs={{0,8},{8,0},{16,24},{24,16},{1,9},{9,1},{17,25},{25,17},{2,10},{10... | collective-permute-start | bytes 5505032 | tf_op jit(solution)/shard_map/ppermute | solution.py:602
  128.0 56.1 %collective-permute-start.12 = (bf16[224,32,128]{2,1,0:T(8,128)(2,1)}, bf16[224,32,128]{2,1,0:T(8,128)(2,1)}, u32[]{:S(2)}, u32[]{:S(2)}) collective-permute-start(bf16[224,32,128]{2,1,0:T(8,128)(2,1)} %collective-permute-done.11.refs_17_), channel_id=1, source_target_pairs={{0,8},{8,0},{16,24},{24,16},{1,9},{9,1},{17,25},{25,17},{2,10},{10... | collective-permute-start | bytes 5505032 | tf_op jit(solution)/shard_map/ppermute | solution.py:602
  128.5 74.7 %collective-permute-start.7 = (bf16[224,32,128]{2,1,0:T(8,128)(2,1)}, bf16[224,32,128]{2,1,0:T(8,128)(2,1)}, u32[]{:S(2)}, u32[]{:S(2)}) collective-permute-start(bf16[224,32,128]{2,1,0:T(8,128)(2,1)} %bitcast.11.refs_15_), channel_id=1, source_target_pairs={{0,8},{8,0},{16,24},{24,16},{1,9},{9,1},{17,25},{25,17},{2,10},{10... | collective-permute-start | bytes 5505032 | tf_op jit(solution)/shard_map/ppermute | solution.py:602
  145.6 57.7 %collective-permute-start.9 = (bf16[224,32,128]{2,1,0:T(8,128)(2,1)}, bf16[224,32,128]{2,1,0:T(8,128)(2,1)}, u32[]{:S(2)}, u32[]{:S(2)}) collective-permute-start(bf16[224,32,128]{2,1,0:T(8,128)(2,1)} %collective-permute-done.8.refs_17_), channel_id=1, source_target_pairs={{0,8},{8,0},{16,24},{24,16},{1,9},{9,1},{17,25},{25,17},{2,10},{10... | collective-permute-start | bytes 5505032 | tf_op jit(solution)/shard_map/ppermute | solution.py:602
  146.4 13.5 %collective-permute-start.4 = (bf16[2,128,896]{2,1,0:T(8,128)(2,1)S(1)}, bf16[2,128,896]{2,1,0:T(8,128)(2,1)}, u32[]{:S(2)}, u32[]{:S(2)}) collective-permute-start(bf16[2,128,896]{2,1,0:T(8,128)(2,1)S(1)} %collective-permute-done.3.refs_10_), channel_id=1, source_target_pairs={{0,1},{1,0},{2,3},{3,2},{4,5},{5,4},{6,7},{7,6},{8,9},{9,8},{10,11... | collective-permute-start | bytes 1376264 | tf_op jit(solution)/shard_map/ppermute | solution.py:619
  159.9 12.5 %collective-permute-start.2 = (bf16[2,128,896]{2,1,0:T(8,128)(2,1)S(1)}, bf16[2,128,896]{2,1,0:T(8,128)(2,1)}, u32[]{:S(2)}, u32[]{:S(2)}) collective-permute-start(bf16[2,128,896]{2,1,0:T(8,128)(2,1)S(1)} %collective-permute-done.1.refs_8_), channel_id=1, source_target_pairs={{0,1},{1,0},{2,3},{3,2},{4,5},{5,4},{6,7},{7,6},{8,9},{9,8},{10,11... | collective-permute-start | bytes 1376264 | tf_op jit(solution)/shard_map/ppermute | solution.py:619
  172.3 11.8 %collective-permute-start.6 = (bf16[2,128,896]{2,1,0:T(8,128)(2,1)}, bf16[2,128,896]{2,1,0:T(8,128)(2,1)}, u32[]{:S(2)}, u32[]{:S(2)}) collective-permute-start(bf16[2,128,896]{2,1,0:T(8,128)(2,1)} %copy-done.5), channel_id=1, source_target_pairs={{0,1},{1,0},{2,3},{3,2},{4,5},{5,4},{6,7},{7,6},{8,9},{9,8},{10,11... | collective-permute-start | bytes 1376264 | tf_op jit(solution)/shard_map/ppermute | solution.py:619
  227.6 6.7 %collective-permute-start.20 = (bf16[2,224,32,128]{3,2,1,0:T(8,128)(2,1)}, bf16[2,224,32,128]{3,2,1,0:T(8,128)(2,1)S(1)}, u32[]{:S(2)}, u32[]{:S(2)}) collective-permute-start(bf16[2,224,32,128]{3,2,1,0:T(8,128)(2,1)} %get-tuple-element.47), channel_id=1, source_target_pairs={{0,8},{8,0},{16,24},{24,16},{1,9},{9,1},{17,25},{25,17},{2,10},{10... | collective-permute-start | bytes 11010056 | tf_op jit(solution)/shard_map/ppermute | solution.py:652
  227.6 198.9 %collective-permute-start.19 = (bf16[2,224,32,128]{3,2,1,0:T(8,128)(2,1)}, bf16[2,224,32,128]{3,2,1,0:T(8,128)(2,1)}, u32[]{:S(2)}, u32[]{:S(2)}) collective-permute-start(bf16[2,224,32,128]{3,2,1,0:T(8,128)(2,1)} %get-tuple-element.45), channel_id=1, source_target_pairs={{0,8},{8,0},{16,24},{24,16},{1,9},{9,1},{17,25},{25,17},{2,10},{10... | collective-permute-start | bytes 11010056 | tf_op jit(solution)/shard_map/ppermute | solution.py:652
  239.1 187.5 %collective-permute-start.21 = (bf16[2,224,32,128]{3,2,1,0:T(8,128)(2,1)}, bf16[2,224,32,128]{3,2,1,0:T(8,128)(2,1)}, u32[]{:S(2)}, u32[]{:S(2)}) collective-permute-start(bf16[2,224,32,128]{3,2,1,0:T(8,128)(2,1)} %add_convert_fusion), channel_id=1, source_target_pairs={{0,16},{8,24},{16,0},{24,8},{1,17},{9,25},{17,1},{25,9},{2,18},{10... | collective-permute-start | bytes 11010056 | tf_op jit(solution)/shard_map/ppermute | solution.py:657
  247.0 16.4 %collective-permute-start.29 = (bf16[28,2,32,128]{3,2,1,0:T(8,128)(2,1)}, bf16[28,2,32,128]{3,2,1,0:T(8,128)(2,1)S(1)}, u32[]{:S(2)}, u32[]{:S(2)}) collective-permute-start(bf16[28,2,32,128]{3,2,1,0:T(8,128)(2,1)} %get-tuple-element.55), channel_id=1, source_target_pairs={{0,1},{1,2},{2,3},{3,4},{4,5},{5,6},{6,7},{7,0},{8,9},{9,10},{10,1... | collective-permute-start | bytes 1376264 | tf_op jit(solution)/shard_map/ppermute | solution.py:636
  248.2 15.4 %collective-permute-start.30 = (bf16[28,2,32,128]{3,2,1,0:T(8,128)(2,1)}, bf16[28,2,32,128]{3,2,1,0:T(8,128)(2,1)S(1)}, u32[]{:S(2)}, u32[]{:S(2)}) collective-permute-start(bf16[28,2,32,128]{3,2,1,0:T(8,128)(2,1)} %get-tuple-element.56), channel_id=1, source_target_pairs={{0,2},{1,3},{2,4},{3,5},{4,6},{5,7},{6,0},{7,1},{8,10},{9,11},{10,... | collective-permute-start | bytes 1376264 | tf_op jit(solution)/shard_map/ppermute | solution.py:636
  248.2 53.4 %collective-permute-start.31 = (bf16[28,2,32,128]{3,2,1,0:T(8,128)(2,1)}, bf16[28,2,32,128]{3,2,1,0:T(8,128)(2,1)S(1)}, u32[]{:S(2)}, u32[]{:S(2)}) collective-permute-start(bf16[28,2,32,128]{3,2,1,0:T(8,128)(2,1)} %get-tuple-element.57), channel_id=1, source_target_pairs={{0,3},{1,4},{2,5},{3,6},{4,7},{5,0},{6,1},{7,2},{8,11},{9,12},{10,... | collective-permute-start | bytes 1376264 | tf_op jit(solution)/shard_map/ppermute | solution.py:636
  263.4 47.6 %collective-permute-start.16 = (bf16[4,128,896]{2,1,0:T(8,128)(2,1)}, bf16[4,128,896]{2,1,0:T(8,128)(2,1)S(1)}, u32[]{:S(2)}, u32[]{:S(2)}) collective-permute-start(bf16[4,128,896]{2,1,0:T(8,128)(2,1)} %get-tuple-element.43), channel_id=1, source_target_pairs={{0,1},{1,0},{2,3},{3,2},{4,5},{5,4},{6,7},{7,6},{8,9},{9,8},{10,11... | collective-permute-start | bytes 2752520 | tf_op jit(solution)/shard_map/ppermute | solution.py:673
  263.6 38.0 %collective-permute-start.32 = (bf16[28,2,32,128]{3,2,1,0:T(8,128)(2,1)}, bf16[28,2,32,128]{3,2,1,0:T(8,128)(2,1)S(1)}, u32[]{:S(2)}, u32[]{:S(2)}) collective-permute-start(bf16[28,2,32,128]{3,2,1,0:T(8,128)(2,1)} %get-tuple-element.58), channel_id=1, source_target_pairs={{0,4},{1,5},{2,6},{3,7},{4,0},{5,1},{6,2},{7,3},{8,12},{9,13},{10,... | collective-permute-start | bytes 1376264 | tf_op jit(solution)/shard_map/ppermute | solution.py:636
  301.6 40.9 %collective-permute-start.13 = (bf16[4,128,896]{2,1,0:T(8,128)(2,1)}, bf16[4,128,896]{2,1,0:T(8,128)(2,1)S(1)}, u32[]{:S(2)}, u32[]{:S(2)}) collective-permute-start(bf16[4,128,896]{2,1,0:T(8,128)(2,1)} %get-tuple-element.39), channel_id=1, source_target_pairs={{0,1},{1,0},{2,3},{3,2},{4,5},{5,4},{6,7},{7,6},{8,9},{9,8},{10,11... | collective-permute-start | bytes 2752520 | tf_op jit(solution)/shard_map/ppermute | solution.py:673
  301.6 20.4 %collective-permute-start.33 = (bf16[28,2,32,128]{3,2,1,0:T(8,128)(2,1)S(1)}, bf16[28,2,32,128]{3,2,1,0:T(8,128)(2,1)S(1)}, u32[]{:S(2)}, u32[]{:S(2)}) collective-permute-start(bf16[28,2,32,128]{3,2,1,0:T(8,128)(2,1)S(1)} %copy-done.19), channel_id=1, source_target_pairs={{0,5},{1,6},{2,7},{3,0},{4,1},{5,2},{6,3},{7,4},{8,13},{9,14},{10,... | collective-permute-start | bytes 1376264 | tf_op jit(solution)/shard_map/ppermute | solution.py:636
  311.0 33.4 %collective-permute-start.34 = (bf16[28,2,32,128]{3,2,1,0:T(8,128)(2,1)}, bf16[28,2,32,128]{3,2,1,0:T(8,128)(2,1)S(1)}, u32[]{:S(2)}, u32[]{:S(2)}) collective-permute-start(bf16[28,2,32,128]{3,2,1,0:T(8,128)(2,1)} %get-tuple-element.60), channel_id=1, source_target_pairs={{0,6},{1,7},{2,0},{3,1},{4,2},{5,3},{6,4},{7,5},{8,14},{9,15},{10,... | collective-permute-start | bytes 1376264 | tf_op jit(solution)/shard_map/ppermute | solution.py:636
  322.0 41.7 %collective-permute-start.35 = (bf16[28,2,32,128]{3,2,1,0:T(8,128)(2,1)}, bf16[28,2,32,128]{3,2,1,0:T(8,128)(2,1)}, u32[]{:S(2)}, u32[]{:S(2)}) collective-permute-start(bf16[28,2,32,128]{3,2,1,0:T(8,128)(2,1)} %get-tuple-element.61), channel_id=1, source_target_pairs={{0,7},{1,0},{2,1},{3,2},{4,3},{5,4},{6,5},{7,6},{8,15},{9,8},{10,9... | collective-permute-start | bytes 1376264 | tf_op jit(solution)/shard_map/ppermute | solution.py:636
  342.5 21.1 %collective-permute-start.17 = (bf16[2,128,896]{2,1,0:T(8,128)(2,1)}, bf16[2,128,896]{2,1,0:T(8,128)(2,1)S(1)}, u32[]{:S(2)}, u32[]{:S(2)}) collective-permute-start(bf16[2,128,896]{2,1,0:T(8,128)(2,1)} %add_convert_fusion.1), channel_id=1, source_target_pairs={{0,2},{1,3},{2,0},{3,1},{4,6},{5,7},{6,4},{7,5},{8,10},{9,11},{10,... | collective-permute-start | bytes 1376264 | tf_op jit(solution)/shard_map/ppermute | solution.py:673
  345.2 32.2 %collective-permute-start.14 = (bf16[2,128,896]{2,1,0:T(8,128)(2,1)}, bf16[2,128,896]{2,1,0:T(8,128)(2,1)}, u32[]{:S(2)}, u32[]{:S(2)}) collective-permute-start(bf16[2,128,896]{2,1,0:T(8,128)(2,1)} %add_convert_fusion.2), channel_id=1, source_target_pairs={{0,2},{1,3},{2,0},{3,1},{4,6},{5,7},{6,4},{7,5},{8,10},{9,11},{10,... | collective-permute-start | bytes 1376264 | tf_op jit(solution)/shard_map/ppermute | solution.py:673
  363.5 16.4 %collective-permute-start.22 = (bf16[28,2,32,128]{3,2,1,0:T(8,128)(2,1)}, bf16[28,2,32,128]{3,2,1,0:T(8,128)(2,1)S(1)}, u32[]{:S(2)}, u32[]{:S(2)}) collective-permute-start(bf16[28,2,32,128]{3,2,1,0:T(8,128)(2,1)} %get-tuple-element.48), channel_id=1, source_target_pairs={{0,1},{1,2},{2,3},{3,4},{4,5},{5,6},{6,7},{7,0},{8,9},{9,10},{10,1... | collective-permute-start | bytes 1376264 | tf_op jit(solution)/shard_map/ppermute | solution.py:636
  363.6 19.6 %collective-permute-start.23 = (bf16[28,2,32,128]{3,2,1,0:T(8,128)(2,1)}, bf16[28,2,32,128]{3,2,1,0:T(8,128)(2,1)S(1)}, u32[]{:S(2)}, u32[]{:S(2)}) collective-permute-start(bf16[28,2,32,128]{3,2,1,0:T(8,128)(2,1)} %get-tuple-element.49), channel_id=1, source_target_pairs={{0,2},{1,3},{2,4},{3,5},{4,6},{5,7},{6,0},{7,1},{8,10},{9,11},{10,... | collective-permute-start | bytes 1376264 | tf_op jit(solution)/shard_map/ppermute | solution.py:636
  377.4 29.5 %collective-permute-start.18 = (bf16[1,128,896]{2,1,0:T(8,128)(2,1)S(1)}, bf16[1,128,896]{2,1,0:T(8,128)(2,1)S(1)}, u32[]{:S(2)}, u32[]{:S(2)}) collective-permute-start(bf16[1,128,896]{2,1,0:T(8,128)(2,1)S(1)} %add_convert_fusion.4), channel_id=1, source_target_pairs={{0,4},{1,5},{2,6},{3,7},{4,0},{5,1},{6,2},{7,3},{8,12},{9,13},{10,... | collective-permute-start | bytes 688136 | tf_op jit(solution)/shard_map/ppermute | solution.py:673
  379.9 51.2 %copy-start.14 = (bf16[28,2,32,128]{3,2,1,0:T(8,128)(2,1)}, bf16[28,2,32,128]{3,2,1,0:T(8,128)(2,1)S(1)}, u32[]{:S(2)}) copy-start(bf16[28,2,32,128]{3,2,1,0:T(8,128)(2,1)S(1)} %collective-permute-done.22.refs_5_) | copy-start | bytes 1376260
  379.9 46.6 %collective-permute-start.15 = (bf16[1,128,896]{2,1,0:T(8,128)(2,1)S(1)}, bf16[1,128,896]{2,1,0:T(8,128)(2,1)S(1)}, u32[]{:S(2)}, u32[]{:S(2)}) collective-permute-start(bf16[1,128,896]{2,1,0:T(8,128)(2,1)S(1)} %add_convert_fusion.6), channel_id=1, source_target_pairs={{0,4},{1,5},{2,6},{3,7},{4,0},{5,1},{6,2},{7,3},{8,12},{9,13},{10,... | collective-permute-start | bytes 688136 | tf_op jit(solution)/shard_map/ppermute | solution.py:673
  383.2 47.9 %copy-start.15 = (bf16[28,2,32,128]{3,2,1,0:T(8,128)(2,1)}, bf16[28,2,32,128]{3,2,1,0:T(8,128)(2,1)S(1)}, u32[]{:S(2)}) copy-start(bf16[28,2,32,128]{3,2,1,0:T(8,128)(2,1)S(1)} %collective-permute-done.23.refs_6_) | copy-start | bytes 1376260
  383.2 59.0 %collective-permute-start.24 = (bf16[28,2,32,128]{3,2,1,0:T(8,128)(2,1)}, bf16[28,2,32,128]{3,2,1,0:T(8,128)(2,1)}, u32[]{:S(2)}, u32[]{:S(2)}) collective-permute-start(bf16[28,2,32,128]{3,2,1,0:T(8,128)(2,1)} %get-tuple-element.50), channel_id=1, source_target_pairs={{0,3},{1,4},{2,5},{3,6},{4,7},{5,0},{6,1},{7,2},{8,11},{9,12},{10,... | collective-permute-start | bytes 1376264 | tf_op jit(solution)/shard_map/ppermute | solution.py:636
  406.9 35.3 %collective-permute-start.25 = (bf16[28,2,32,128]{3,2,1,0:T(8,128)(2,1)}, bf16[28,2,32,128]{3,2,1,0:T(8,128)(2,1)}, u32[]{:S(2)}, u32[]{:S(2)}) collective-permute-start(bf16[28,2,32,128]{3,2,1,0:T(8,128)(2,1)} %get-tuple-element.51), channel_id=1, source_target_pairs={{0,4},{1,5},{2,6},{3,7},{4,0},{5,1},{6,2},{7,3},{8,12},{9,13},{10,... | collective-permute-start | bytes 1376264 | tf_op jit(solution)/shard_map/ppermute | solution.py:636
  426.5 26.3 %collective-permute-start.26 = (bf16[28,2,32,128]{3,2,1,0:T(8,128)(2,1)}, bf16[28,2,32,128]{3,2,1,0:T(8,128)(2,1)}, u32[]{:S(2)}, u32[]{:S(2)}) collective-permute-start(bf16[28,2,32,128]{3,2,1,0:T(8,128)(2,1)} %get-tuple-element.52), channel_id=1, source_target_pairs={{0,5},{1,6},{2,7},{3,0},{4,1},{5,2},{6,3},{7,4},{8,13},{9,14},{10,... | collective-permute-start | bytes 1376264 | tf_op jit(solution)/shard_map/ppermute | solution.py:636
  426.5 29.6 %collective-permute-start.27 = (bf16[28,2,32,128]{3,2,1,0:T(8,128)(2,1)}, bf16[28,2,32,128]{3,2,1,0:T(8,128)(2,1)}, u32[]{:S(2)}, u32[]{:S(2)}) collective-permute-start(bf16[28,2,32,128]{3,2,1,0:T(8,128)(2,1)} %get-tuple-element.53), channel_id=1, source_target_pairs={{0,6},{1,7},{2,0},{3,1},{4,2},{5,3},{6,4},{7,5},{8,14},{9,15},{10,... | collective-permute-start | bytes 1376264 | tf_op jit(solution)/shard_map/ppermute | solution.py:636
  426.6 30.9 %collective-permute-start.28 = (bf16[28,2,32,128]{3,2,1,0:T(8,128)(2,1)}, bf16[28,2,32,128]{3,2,1,0:T(8,128)(2,1)}, u32[]{:S(2)}, u32[]{:S(2)}) collective-permute-start(bf16[28,2,32,128]{3,2,1,0:T(8,128)(2,1)} %get-tuple-element.54), channel_id=1, source_target_pairs={{0,7},{1,0},{2,1},{3,2},{4,3},{5,4},{6,5},{7,6},{8,15},{9,8},{10,9... | collective-permute-start | bytes 1376264 | tf_op jit(solution)/shard_map/ppermute | solution.py:636
  (11 other events, 241.3 us)

commit v3 on v2

--- a/solution.py
+++ b/solution.py
@@ -65,33 +65,35 @@
     )(send_slots, dp_index, tiles)
 
 
-def pack_moments(arrays, send_slots, bucket):
-    _, rows, width = arrays[0].shape
-    targets = send_slots.shape[0] // bucket
+def pack_moments(arrays, send_slots):
+    slots, rows, width = arrays[0].shape
+    count = send_slots.shape[0]
     kinds = len(arrays)
 
     def kernel(send_ref, *refs):
-        outs = refs[kinds:]
-        unroll = math.gcd(bucket, 4)
-        for m in range(targets):
-
-            def step(i, carry, m=m):
-                for u in range(unroll):
-                    s = send_ref[m * bucket + i * unroll + u]
-                    for k in range(kinds):
-                        outs[m][i * unroll + u, k] = refs[k][s].astype(BF16)
-                return carry
-
-            lax.fori_loop(0, bucket // unroll, step, 0)
-
+        out_ref = refs[-1]
+
+        def step(i, carry):
+            s = send_ref[i]
+            for k in range(kinds):
+                out_ref[i, k] = refs[k][s].astype(BF16)
+            return carry
+
+        lax.fori_loop(0, count, step, 0, unroll=4)
+
+    whole = pl.BlockSpec((slots, rows, width), lambda i, s: (0, 0, 0))
     return pl.pallas_call(
         kernel,
-        out_shape=[jax.ShapeDtypeStruct((bucket, kinds, rows, width), BF16)] * targets,
-        in_specs=[SMEM] + [pl.BlockSpec(memory_space=pltpu.VMEM)] * kinds,
-        out_specs=[pl.BlockSpec(memory_space=pltpu.VMEM)] * targets,
+        out_shape=jax.ShapeDtypeStruct((count, kinds, rows, width), BF16),
+        grid_spec=pltpu.PrefetchScalarGridSpec(
+            num_scalar_prefetch=1,
+            grid=(1,),
+            in_specs=[whole] * kinds,
+            out_specs=pl.BlockSpec((count, kinds, rows, width), lambda i, s: (0, 0, 0, 0)),
+        ),
         compiler_params=pltpu.CompilerParams(vmem_limit_bytes=VMEM_LIMIT),
         cost_estimate=pl.CostEstimate(
-            flops=0, transcendentals=0, bytes_accessed=6 * kinds * targets * bucket * rows * width
+            flops=0, transcendentals=0, bytes_accessed=6 * kinds * count * rows * width
         ),
         name="pack_moments",
     )(send_slots, *arrays)
@@ -568,12 +570,6 @@
     home = jnp.where(stays, mine_slot, 0)
     came = jnp.where(mine_live & ~stays, mine_dev * bucket + recv_rank, 0)
     kind = jnp.where(stays, 1, jnp.where(mine_live, 2, 0)).astype(jnp.int32)
-    distance = lax.rem(my_index - mine_dev + tensor_size, tensor_size)
-    came_moment = jnp.where(mine_live & ~stays, (distance - 1) * bucket + recv_rank, 0)
-    by_target = send_slots.reshape(tensor_size, bucket)
-    by_distance = lax.dynamic_slice_in_dim(
-        jnp.concatenate([by_target, by_target], axis=0), my_index + 1, tensor_size - 1, axis=0
-    ).reshape(-1)
     col_count = col_owner.shape[0] // tensor_size
     col_slot = jnp.take(local_columns(col_owner), new_col)
     place = jnp.stack([my_dp // 2, my_dp % 2, my_index]).astype(jnp.int32)
@@ -628,18 +624,10 @@
 
     ups = (up_first_moment, up_second_moment)
     downs = (down_first_moment, down_second_moment)
-
-    def exchange_parts(parts):
-        got = []
-        for m, part in enumerate(parts, 1):
-            pairs = [(t, (t + m) % tensor_size) for t in range(tensor_size)]
-            got.append(lax.ppermute(part, "tensor", pairs))
-        return got
-
-    ups_pack = pack_moments(ups, by_distance, bucket)
-    downs_pack = pack_moments(downs, by_distance, bucket)
-    ups_in = exchange_parts(ups_pack)
-    downs_in = exchange_parts(downs_pack)
+    ups_pack = pack_moments(ups, send_slots)
+    downs_pack = pack_moments(downs, send_slots)
+    ups_in = [exchange(ups_pack)]
+    downs_in = [exchange(downs_pack)]
 
     act, act_t, slopes, x_t, wu = forward_products(
         tables, place, feats, up_weight_blocks, up_parts, col_count, row_blocks, feat_shape
@@ -680,8 +668,8 @@
         sums.append(sum(s[0].astype(F32) for s in held).astype(BF16))
     out_sum, in_sum = sums
 
-    up_step = adam_step((home, came_moment, kind), terms, 0, ups, ups_in)
-    down_step = adam_step((home, came_moment, kind), terms, 1, downs, downs_in)
+    up_step = adam_step((home, came, kind), terms, 0, ups, ups_in)
+    down_step = adam_step((home, came, kind), terms, 1, downs, downs_in)
     return (out_sum, in_sum, up_step, down_step)
 
 

time: 477 us -> 456 us (0.956); the launches traced: 469 us -> 456 us
  starting transfers between devices: 90.2 us -> 44 us
  waiting for transfers between devices: 254 us -> 285 us
    ppermute x7, waiting for transfers between devices: 46.2 us -> 124 us  [layer(): held[m ^ bit] = lax.ppermute(held[m], 'tensor', far_pairs(bit))]
    ppermute x14 -> x0, waiting for transfers between devices: 61 us -> none  [exchange_parts(): got.append(lax.ppermute(part, 'tensor', pairs))]
    ppermute x14 -> x0, starting transfers between devices: 60.4 us -> none  [exchange_parts(): got.append(lax.ppermute(part, 'tensor', pairs))]
    ppermute x6, waiting for transfers between devices: 43.9 us -> 86.3 us  [layer(): held.append(lax.ppermute(send, 'tensor', far_pairs(bit)))]
    ppermute x2, waiting for transfers between devices: 16.9 us -> 0.01 us  [spread(): mine = lax.ppermute(own, 'dp', x_pairs(j))]
    all_to_all x2 -> x4, starting transfers between devices: 11.6 us -> 23.1 us  [exchange(): lax.all_to_all(shaped, 'tensor', split_axis=0, concat_axis=0, tiled=True)]
    ppermute x2, waiting for transfers between devices: 6.11 us -> 0.01 us  [layer(): there = lax.ppermute(grads[2 * j + 1], 'dp', core_pairs)]
    all_to_all x2 -> x4, waiting for transfers between devices: 79.5 us -> 74.6 us  [exchange(): lax.all_to_all(shaped, 'tensor', split_axis=0, concat_axis=0, tiled=True)]
  transfers between devices with their start and end apart: 38 -> 26, of which waited for: 22 -> 12; matrix products, arithmetic and copies ran while one was open for 3% -> 4% of each run, Pallas kernels for 13% -> 19%
where the time goes in v3:
time: 456 us
  waiting for transfers between devices  285 us (62%)
  Pallas kernels  103 us (23%)
  starting transfers between devices  44 us (10%)
  other arithmetic  17.2 us (4%)
  local copies, waits for them, and re-layouts  5.72 us (1%)
    ppermute x7, waiting for transfers between devices, layer(): held[m ^ bit] = lax.ppermute(held[m], 'tensor', far_pairs(bit))  124 us
    ppermute x6, waiting for transfers between devices, layer(): held.append(lax.ppermute(send, 'tensor', far_pairs(bit)))  86.3 us
    all_to_all x4, waiting for transfers between devices, exchange(): lax.all_to_all(shaped, 'tensor', split_axis=0, concat_axis=0, tiled=True)  74.6 us
    pallas_call x1, Pallas kernels, gradient_products(): pl.pallas_call(functools.partial(gradient_kernel, n_feat, n_dp), out_shap...  24.2 us
    all_to_all x4, starting transfers between devices, exchange(): lax.all_to_all(shaped, 'tensor', split_axis=0, concat_axis=0, tiled=True)  23.1 us
    pallas_call x2, Pallas kernels, adam_step(): pl.pallas_call(kernel, out_shape=jax.ShapeDtypeStruct(moments[0].shape, F...  22.5 us
    pallas_call x1, Pallas kernels, forward_products(): pl.pallas_call(functools.partial(forward_kernel, n_feat, n_dp, row_blocks...  19.1 us
    pallas_call x2, Pallas kernels, output_products(): pl.pallas_call(functools.partial(output_kernel, pieces, turned), out_shap...  16.7 us
  transfers between devices with their start and end apart: 26, of which 12 were waited for; matrix products, arithmetic and copies ran while one was open for 4% of the time, Pallas kernels for 19%

profile of v3, /device:TPU:0, one launch (start us, length us, event | category | flops | bytes accessed | tf_op | source)
XLA Modules:
  0.0 455.6 jit_solution(1672052768763909687)
XLA Ops:
  0.6 0.7 broadcast_divide_fusion
  1.3 0.7 sign_compare_fusion
  4.0 0.6 reshape.141.send_ref
  4.7 3.8 pack_weight.3
  8.5 7.3 %all-to-all-start.1 = ((bf16[8,28,32,128]{3,2,1,0:T(8,128)(2,1)}), bf16[8,28,32,128]{3,2,1,0:T(8,128)(2,1)S(1)}, u32[]{:S(2)}, u32[]{:S(2)}) async-start(bf16[8,28,32,128]{3,2,1,0:T(8,128)(2,1)} %bitcast.30), calls=%async_computation.1 | async-start | bytes 3670016 | tf_op jit(solution)/shard_map/all_to_all | solution.py:581
  15.8 3.8 pack_weight.2
  19.6 38.8 %all-to-all-done.1 = bf16[8,28,32,128]{3,2,1,0:T(8,128)(2,1)S(1)} async-done(((bf16[8,28,32,128]{3,2,1,0:T(8,128)(2,1)}), bf16[8,28,32,128]{3,2,1,0:T(8,128)(2,1)S(1)}, u32[]{:S(2)}, u32[]{:S(2)}) %all-to-all-start.1) | async-done | bytes 1835040 | tf_op jit(solution)/shard_map/all_to_all | solution.py:581
  58.4 4.3 all-to-all-start
  62.8 6.4 %pack_moments.3 = bf16[224,2,32,128]{3,2,1,0:T(8,128)(2,1)} custom-call(s32[224]{0:T(256)} %reshape.141.send_ref, f32[224,32,128]{2,1,0:T(8,128)} %refs_3_.3, f32[224,32,128]{2,1,0:T(8,128)} %refs_4_.3), custom_call_target="tpu_custom_call" | custom-call | bytes 11010048 | tf_op jit(solution)/shard_map/pack_moments/pallas_call | solution.py:85
  69.2 35.8 %all-to-all-done = bf16[8,28,32,128]{3,2,1,0:T(8,128)(2,1)} async-done(((bf16[8,28,32,128]{3,2,1,0:T(8,128)(2,1)}), bf16[8,28,32,128]{3,2,1,0:T(8,128)(2,1)}, u32[]{:S(2)}, u32[]{:S(2)}) %all-to-all-start) | async-done | bytes 1835040 | tf_op jit(solution)/shard_map/all_to_all | solution.py:581
  105.0 4.6 %all-to-all-start.3 = ((bf16[8,28,2,32,128]{4,3,2,1,0:T(8,128)(2,1)}), bf16[8,28,2,32,128]{4,3,2,1,0:T(8,128)(2,1)}, u32[]{:S(2)}, u32[]{:S(2)}) async-start(bf16[8,28,2,32,128]{4,3,2,1,0:T(8,128)(2,1)} %bitcast.24), calls=%async_computation.3 | async-start | bytes 7340032 | tf_op jit(solution)/shard_map/all_to_all | solution.py:581
  109.6 1.6 collective-permute-start.11
  111.8 2.8 collective-permute-start.3
  114.6 1.5 collective-permute-start.1
  116.1 1.5 collective-permute-start
  117.6 93.0 %collective-permute-done.3.refs_10_ = bf16[2,128,896]{2,1,0:T(8,128)(2,1)S(1)} collective-permute-done((bf16[2,128,896]{2,1,0:T(8,128)(2,1)S(1)}, bf16[2,128,896]{2,1,0:T(8,128)(2,1)S(1)}, u32[]{:S(2)}, u32[]{:S(2)}) %collective-permute-start.3) | collective-permute-done | bytes 458784 | tf_op jit(solution)/shard_map/ppermute | solution.py:615
  211.7 9.4 %collective-permute-done.5.refs_12_ = bf16[2,128,896]{2,1,0:T(8,128)(2,1)S(1)} collective-permute-done((bf16[2,128,896]{2,1,0:T(8,128)(2,1)S(1)}, bf16[2,128,896]{2,1,0:T(8,128)(2,1)S(1)}, u32[]{:S(2)}, u32[]{:S(2)}) %collective-permute-start.5) | collective-permute-done | bytes 458784 | tf_op jit(solution)/shard_map/ppermute | solution.py:615
  221.1 0.8 copy-done.6
  221.9 2.4 collective-permute-start.4
  224.3 9.0 %collective-permute-done.4.refs_11_ = bf16[2,128,896]{2,1,0:T(8,128)(2,1)} collective-permute-done((bf16[2,128,896]{2,1,0:T(8,128)(2,1)S(1)}, bf16[2,128,896]{2,1,0:T(8,128)(2,1)}, u32[]{:S(2)}, u32[]{:S(2)}) %collective-permute-start.4) | collective-permute-done | bytes 458784 | tf_op jit(solution)/shard_map/ppermute | solution.py:615
  233.4 1.7 collective-permute-start.2
  235.5 8.3 %collective-permute-done.2.refs_9_ = bf16[2,128,896]{2,1,0:T(8,128)(2,1)} collective-permute-done((bf16[2,128,896]{2,1,0:T(8,128)(2,1)S(1)}, bf16[2,128,896]{2,1,0:T(8,128)(2,1)}, u32[]{:S(2)}, u32[]{:S(2)}) %collective-permute-start.2) | collective-permute-done | bytes 458784 | tf_op jit(solution)/shard_map/ppermute | solution.py:615
  243.8 1.7 collective-permute-start.6
  246.2 1.9 gather_fusion
  249.2 4.2 collective-permute-done.6.refs_13_
  253.4 19.1 %forward_products.1 = (bf16[16,128,128]{2,1,0:T(8,128)(2,1)}, bf16[16,128,128]{2,1,0:T(8,128)(2,1)}, f32[16,128,128]{2,1,0:T(8,128)}, bf16[56,128,128]{2,1,0:T(8,128)(2,1)}, bf16[224,128,128]{2,1,0:T(8,128)(2,1)}) custom-call(s32[224]{0:T(256)} %refs_0_.9, s32[224]{0:T(256)} %and_select_fusion.1.refs_1_, s32[224]{0:T(256)} %get-tuple-element.45.refs_2_.home_ref, ...), custom_call_target="tpu_custom_call" | custom-call | flops 939524096 | bytes 44040192 | tf_op jit(solution)/shard_map/forward_products/pallas_call | solution.py:348
  272.5 24.2 %gradient_products.1 = (bf16[16,128,128]{2,1,0:T(8,128)(2,1)}, bf16[224,128,128]{2,1,0:T(8,128)(2,1)}, bf16[2,224,32,128]{3,2,1,0:T(8,128)(2,1)}, bf16[2,224,32,...) custom-call(s32[224]{0:T(256)} %refs_0_.9, ...), custom_call_target="tpu_custom_call" | custom-call | flops 2818572288 | bytes 73400320 | tf_op jit(solution)/shard_map/gradient_products/pallas_call | solution.py:382
  296.8 6.3 %pack_moments.2 = bf16[224,2,32,128]{3,2,1,0:T(8,128)(2,1)} custom-call(s32[224]{0:T(256)} %reshape.141.send_ref, f32[224,32,128]{2,1,0:T(8,128)} %refs_3_.2, f32[224,32,128]{2,1,0:T(8,128)} %refs_4_.2), custom_call_target="tpu_custom_call" | custom-call | bytes 11010048 | tf_op jit(solution)/shard_map/pack_moments/pallas_call | solution.py:85
  303.2 6.8 %all-to-all-start.2 = ((bf16[8,28,2,32,128]{4,3,2,1,0:T(8,128)(2,1)}), bf16[8,28,2,32,128]{4,3,2,1,0:T(8,128)(2,1)}, u32[]{:S(2)}, u32[]{:S(2)}) async-start(bf16[8,28,2,32,128]{4,3,2,1,0:T(8,128)(2,1)} %bitcast.25), calls=%async_computation.2 | async-start | bytes 7340032 | tf_op jit(solution)/shard_map/all_to_all | solution.py:581
  310.2 5.9 %add_convert_fusion = bf16[2,224,32,128]{3,2,1,0:T(8,128)(2,1)} fusion(bf16[2,224,32,128]{3,2,1,0:T(8,128)(2,1)} %collective-permute-done.20, bf16[2,224,32,128]{3,2,1,0:T(8,128)(2,1)} %get-tuple-element.32), kind=kLoop, calls=%fused_computation.1 | loop fusion | flops 7340032 | bytes 11010048 | tf_op jit(solution)/shard_map/convert_element_type | solution.py:644
  316.1 1.5 collective-permute-start.21
  317.6 9.7 %output_products.3 = (bf16[4,128,896]{2,1,0:T(8,128)(2,1)}, bf16[4,128,896]{2,1,0:T(8,128)(2,1)}) custom-call(s32[224]{0:T(256)} %refs_0_.9, s32[224]{0:T(256)} %and_select_fusion.1.refs_1_, s32[3]{0:T(128)} %pad_add_fusion.refs_5_.refs_2_, bf16[224,128,128]{2,1,0:T(8,128)(2,1)} %get-tuple-element.26.refs_3_, bf16[16,128,128]{2,1,0:T(8,128)(2,1)} %get-tuple-element.27.refs_4_), custom_call_target="tpu_custom_call" | custom-call | flops 939524096 | bytes 14680064 | tf_op jit(solution)/shard_map/output_products/pallas_call | solution.py:410
  327.3 1.9 collective-permute-start.16
  329.1 7.0 %output_products.2 = (bf16[4,128,896]{2,1,0:T(8,128)(2,1)}, bf16[4,128,896]{2,1,0:T(8,128)(2,1)}) custom-call(s32[224]{0:T(256)} %refs_0_.9, s32[224]{0:T(256)} %and_select_fusion.1.refs_1_, s32[3]{0:T(128)} %pad_add_fusion.refs_5_.refs_2_, bf16[224,128,128]{2,1,0:T(8,128)(2,1)} %get-tuple-element.22.refs_3_, bf16[16,128,128]{2,1,0:T(8,128)(2,1)} %get-tuple-element.23.refs_4_), custom_call_target="tpu_custom_call" | custom-call | flops 939524096 | bytes 14680064 | tf_op jit(solution)/shard_map/output_products/pallas_call | solution.py:410
  336.5 36.6 %collective-permute-done.16 = bf16[4,128,896]{2,1,0:T(8,128)(2,1)} collective-permute-done((bf16[4,128,896]{2,1,0:T(8,128)(2,1)}, bf16[4,128,896]{2,1,0:T(8,128)(2,1)}, u32[]{:S(2)}, u32[]{:S(2)}) %collective-permute-start.16) | collective-permute-done | bytes 917536 | tf_op jit(solution)/shard_map/ppermute | solution.py:661
  373.0 1.3 add_convert_fusion.1
  374.4 18.1 %collective-permute-done.13 = bf16[4,128,896]{2,1,0:T(8,128)(2,1)S(1)} collective-permute-done((bf16[4,128,896]{2,1,0:T(8,128)(2,1)}, bf16[4,128,896]{2,1,0:T(8,128)(2,1)S(1)}, u32[]{:S(2)}, u32[]{:S(2)}) %collective-permute-start.13) | collective-permute-done | bytes 917536 | tf_op jit(solution)/shard_map/ppermute | solution.py:661
  392.5 1.1 add_convert_fusion.2
  394.3 8.9 %collective-permute-done.17 = bf16[2,128,896]{2,1,0:T(8,128)(2,1)S(1)} collective-permute-done((bf16[2,128,896]{2,1,0:T(8,128)(2,1)S(1)}, bf16[2,128,896]{2,1,0:T(8,128)(2,1)S(1)}, u32[]{:S(2)}, u32[]{:S(2)}) %collective-permute-start.17) | collective-permute-done | bytes 458784 | tf_op jit(solution)/shard_map/ppermute | solution.py:661
  403.2 1.1 add_convert_fusion.4
  404.4 0.9 collective-permute-start.18
  405.3 12.6 %collective-permute-done.14 = bf16[2,128,896]{2,1,0:T(8,128)(2,1)S(1)} collective-permute-done((bf16[2,128,896]{2,1,0:T(8,128)(2,1)S(1)}, bf16[2,128,896]{2,1,0:T(8,128)(2,1)S(1)}, u32[]{:S(2)}, u32[]{:S(2)}) %collective-permute-start.14) | collective-permute-done | bytes 458784 | tf_op jit(solution)/shard_map/ppermute | solution.py:661
  418.5 1.9 fusion.1
  420.4 10.0 %collective-permute-done.15 = bf16[1,128,896]{2,1,0:T(8,128)(2,1)S(1)} collective-permute-done((bf16[1,128,896]{2,1,0:T(8,128)(2,1)S(1)}, bf16[1,128,896]{2,1,0:T(8,128)(2,1)S(1)}, u32[]{:S(2)}, u32[]{:S(2)}) %collective-permute-start.15) | collective-permute-done | bytes 229408 | tf_op jit(solution)/shard_map/ppermute | solution.py:661
  430.4 0.8 fusion
  431.2 1.8 copy-done
  433.0 11.2 %adam_step.3 = f32[224,32,128]{2,1,0:T(8,128)} custom-call(s32[224]{0:T(256)} %get-tuple-element.45.refs_2_.home_ref, s32[224]{0:T(256)} %get-tuple-element.44.refs_3_.came_ref, s32[224]{0:T(256)} %get-tuple-element.43.refs_4_.kind_ref, bf16[2,224,32,128]{3,2,1,0:T(8,128)(2,1)} %get-tuple-element.30.refs_0_, bf16[2,224,32,128]{3,2,1,0:T(8,128)(2,1)} %copy-done, ...), custom_call_target="tpu_custom_call" | custom-call | flops 13762560 | bytes 15597568 | tf_op jit(solution)/shard_map/adam_step/pallas_call | solution.py:503
  444.2 11.2 %adam_step.2 = f32[224,32,128]{2,1,0:T(8,128)} custom-call(s32[224]{0:T(256)} %get-tuple-element.45.refs_2_.home_ref, s32[224]{0:T(256)} %get-tuple-element.44.refs_3_.came_ref, s32[224]{0:T(256)} %get-tuple-element.43.refs_4_.kind_ref, bf16[2,224,32,128]{3,2,1,0:T(8,128)(2,1)} %get-tuple-element.30.refs_0_, bf16[2,224,32,128]{3,2,1,0:T(8,128)(2,1)} %copy-done, ...), custom_call_target="tpu_custom_call" | custom-call | flops 13762560 | bytes 15597568 | tf_op jit(solution)/shard_map/adam_step/pallas_call | solution.py:503
  (74 shorter events, 7.8 us)
Async XLA Ops:
  8.5 49.9 %all-to-all-start.1 = ((bf16[8,28,32,128]{3,2,1,0:T(8,128)(2,1)}), bf16[8,28,32,128]{3,2,1,0:T(8,128)(2,1)S(1)}, u32[]{:S(2)}, u32[]{:S(2)}) async-start(bf16[8,28,32,128]{3,2,1,0:T(8,128)(2,1)} %bitcast.30), calls=%async_computation.1 | async-start | bytes 3670016 | tf_op jit(solution)/shard_map/all_to_all | solution.py:581
  58.4 152.2 %copy-start.1 = (bf16[8,28,32,128]{3,2,1,0:T(8,128)(2,1)}, bf16[8,28,32,128]{3,2,1,0:T(8,128)(2,1)S(1)}, u32[]{:S(2)}) copy-start(bf16[8,28,32,128]{3,2,1,0:T(8,128)(2,1)S(1)} %all-to-all-done.1) | copy-start | bytes 5505028
  58.4 46.6 %all-to-all-start = ((bf16[8,28,32,128]{3,2,1,0:T(8,128)(2,1)}), bf16[8,28,32,128]{3,2,1,0:T(8,128)(2,1)}, u32[]{:S(2)}, u32[]{:S(2)}) async-start(bf16[8,28,32,128]{3,2,1,0:T(8,128)(2,1)} %bitcast.29), calls=%async_computation | async-start | bytes 3670016 | tf_op jit(solution)/shard_map/all_to_all | solution.py:581
  105.0 6.8 %copy-start.8 = (bf16[128,896]{1,0:T(8,128)(2,1)S(1)}, bf16[128,896]{1,0:T(8,128)(2,1)}, u32[]{:S(2)}) copy-start(bf16[128,896]{1,0:T(8,128)(2,1)} %param.13) | copy-start | bytes 688132
  105.0 6.8 %copy-start.9 = (bf16[128,896]{1,0:T(8,128)(2,1)S(1)}, bf16[128,896]{1,0:T(8,128)(2,1)}, u32[]{:S(2)}) copy-start(bf16[128,896]{1,0:T(8,128)(2,1)} %param.12) | copy-start | bytes 688132
  105.0 119.3 %copy-start.10 = (s32[224]{0:T(256)S(1)}, s32[224]{0:T(256)}, u32[]{:S(2)}) copy-start(s32[224]{0:T(256)} %param.22) | copy-start | bytes 2692
  105.0 130.2 %copy-start.11 = (s32[128]{0:T(128)S(1)}, s32[128]{0:T(128)}, u32[]{:S(2)}) copy-start(s32[128]{0:T(128)} %param.23) | copy-start | bytes 1540
  105.0 198.2 %all-to-all-start.3 = ((bf16[8,28,2,32,128]{4,3,2,1,0:T(8,128)(2,1)}), bf16[8,28,2,32,128]{4,3,2,1,0:T(8,128)(2,1)}, u32[]{:S(2)}, u32[]{:S(2)}) async-start(bf16[8,28,2,32,128]{4,3,2,1,0:T(8,128)(2,1)} %bitcast.24), calls=%async_computation.3 | async-start | bytes 7340032 | tf_op jit(solution)/shard_map/all_to_all | solution.py:581
  109.6 101.0 %collective-permute-start.11 = (bf16[224,32,128]{2,1,0:T(8,128)(2,1)S(1)}, bf16[224,32,128]{2,1,0:T(8,128)(2,1)}, u32[]{:S(2)}, u32[]{:S(2)}) collective-permute-start(bf16[224,32,128]{2,1,0:T(8,128)(2,1)S(1)} %bitcast.26), channel_id=1, source_target_pairs={{0,16},{8,24},{16,0},{24,8},{1,17},{9,25},{17,1},{25,9},{2,18},{10... | collective-permute-start | bytes 5505032 | tf_op jit(solution)/shard_map/ppermute | solution.py:597
  111.2 100.1 %collective-permute-start.8 = (bf16[224,32,128]{2,1,0:T(8,128)(2,1)}, bf16[224,32,128]{2,1,0:T(8,128)(2,1)}, u32[]{:S(2)}, u32[]{:S(2)}) collective-permute-start(bf16[224,32,128]{2,1,0:T(8,128)(2,1)} %bitcast.11.refs_15_), channel_id=1, source_target_pairs={{0,16},{8,24},{16,0},{24,8},{1,17},{9,25},{17,1},{25,9},{2,18},{10... | collective-permute-start | bytes 5505032 | tf_op jit(solution)/shard_map/ppermute | solution.py:597
  111.8 141.6 %copy-start.2 = (bf16[2,128,896]{2,1,0:T(8,128)(2,1)}, bf16[2,128,896]{2,1,0:T(8,128)(2,1)S(1)}, u32[]{:S(2)}) copy-start(bf16[2,128,896]{2,1,0:T(8,128)(2,1)S(1)} %pad_maximum_fusion.refs_6_) | copy-start | bytes 1376260
  111.8 98.8 %collective-permute-start.3 = (bf16[2,128,896]{2,1,0:T(8,128)(2,1)S(1)}, bf16[2,128,896]{2,1,0:T(8,128)(2,1)S(1)}, u32[]{:S(2)}, u32[]{:S(2)}) collective-permute-start(bf16[2,128,896]{2,1,0:T(8,128)(2,1)S(1)} %pad_maximum_fusion.refs_6_), channel_id=1, source_target_pairs={{0,4},{1,5},{2,6},{3,7},{4,0},{5,1},{6,2},{7,3},{8,12},{9,13},{10,... | collective-permute-start | bytes 1376264 | tf_op jit(solution)/shard_map/ppermute | solution.py:615
  114.6 95.9 %collective-permute-start.1 = (bf16[2,128,896]{2,1,0:T(8,128)(2,1)S(1)}, bf16[2,128,896]{2,1,0:T(8,128)(2,1)S(1)}, u32[]{:S(2)}, u32[]{:S(2)}) collective-permute-start(bf16[2,128,896]{2,1,0:T(8,128)(2,1)S(1)} %pad_maximum_fusion.refs_6_), channel_id=1, source_target_pairs={{0,2},{1,3},{2,0},{3,1},{4,6},{5,7},{6,4},{7,5},{8,10},{9,11},{10,... | collective-permute-start | bytes 1376264 | tf_op jit(solution)/shard_map/ppermute | solution.py:615
  116.1 95.1 %collective-permute-start = (bf16[2,128,896]{2,1,0:T(8,128)(2,1)S(1)}, bf16[2,128,896]{2,1,0:T(8,128)(2,1)S(1)}, u32[]{:S(2)}, u32[]{:S(2)}) collective-permute-start(bf16[2,128,896]{2,1,0:T(8,128)(2,1)S(1)} %pad_maximum_fusion.refs_6_), channel_id=1, source_target_pairs={{0,1},{1,0},{2,3},{3,2},{4,5},{5,4},{6,7},{7,6},{8,9},{9,8},{10,11... | collective-permute-start | bytes 1376264 | tf_op jit(solution)/shard_map/ppermute | solution.py:615
  210.6 42.9 %copy-start.3 = (bf16[2,128,896]{2,1,0:T(8,128)(2,1)}, bf16[2,128,896]{2,1,0:T(8,128)(2,1)S(1)}, u32[]{:S(2)}) copy-start(bf16[2,128,896]{2,1,0:T(8,128)(2,1)S(1)} %collective-permute-done.3.refs_10_) | copy-start | bytes 1376260
  210.6 10.6 %collective-permute-start.5 = (bf16[2,128,896]{2,1,0:T(8,128)(2,1)S(1)}, bf16[2,128,896]{2,1,0:T(8,128)(2,1)S(1)}, u32[]{:S(2)}, u32[]{:S(2)}) collective-permute-start(bf16[2,128,896]{2,1,0:T(8,128)(2,1)S(1)} %collective-permute-done.3.refs_10_), channel_id=1, source_target_pairs={{0,2},{1,3},{2,0},{3,1},{4,6},{5,7},{6,4},{7,5},{8,10},{9,11},{10,... | collective-permute-start | bytes 1376264 | tf_op jit(solution)/shard_map/ppermute | solution.py:615
  210.6 42.9 %copy-start.4 = (bf16[2,128,896]{2,1,0:T(8,128)(2,1)}, bf16[2,128,896]{2,1,0:T(8,128)(2,1)S(1)}, u32[]{:S(2)}) copy-start(bf16[2,128,896]{2,1,0:T(8,128)(2,1)S(1)} %collective-permute-done.1.refs_8_) | copy-start | bytes 1376260
  210.6 42.8 %collective-permute-start.10 = (bf16[224,32,128]{2,1,0:T(8,128)(2,1)S(1)}, bf16[224,32,128]{2,1,0:T(8,128)(2,1)}, u32[]{:S(2)}, u32[]{:S(2)}) collective-permute-start(bf16[224,32,128]{2,1,0:T(8,128)(2,1)S(1)} %bitcast.27), channel_id=1, source_target_pairs={{0,8},{8,0},{16,24},{24,16},{1,9},{9,1},{17,25},{25,17},{2,10},{10... | collective-permute-start | bytes 5505032 | tf_op jit(solution)/shard_map/ppermute | solution.py:598
  210.7 42.7 %collective-permute-start.12 = (bf16[224,32,128]{2,1,0:T(8,128)(2,1)}, bf16[224,32,128]{2,1,0:T(8,128)(2,1)}, u32[]{:S(2)}, u32[]{:S(2)}) collective-permute-start(bf16[224,32,128]{2,1,0:T(8,128)(2,1)} %collective-permute-done.11.refs_17_), channel_id=1, source_target_pairs={{0,8},{8,0},{16,24},{24,16},{1,9},{9,1},{17,25},{25,17},{2,10},{10... | collective-permute-start | bytes 5505032 | tf_op jit(solution)/shard_map/ppermute | solution.py:598
  211.2 10.0 %copy-start.5 = (bf16[2,128,896]{2,1,0:T(8,128)(2,1)}, bf16[2,128,896]{2,1,0:T(8,128)(2,1)S(1)}, u32[]{:S(2)}) copy-start(bf16[2,128,896]{2,1,0:T(8,128)(2,1)S(1)} %collective-permute-done.refs_7_) | copy-start | bytes 1376260
  211.2 61.3 %collective-permute-start.7 = (bf16[224,32,128]{2,1,0:T(8,128)(2,1)}, bf16[224,32,128]{2,1,0:T(8,128)(2,1)}, u32[]{:S(2)}, u32[]{:S(2)}) collective-permute-start(bf16[224,32,128]{2,1,0:T(8,128)(2,1)} %bitcast.11.refs_15_), channel_id=1, source_target_pairs={{0,8},{8,0},{16,24},{24,16},{1,9},{9,1},{17,25},{25,17},{2,10},{10... | collective-permute-start | bytes 5505032 | tf_op jit(solution)/shard_map/ppermute | solution.py:598
  211.3 61.3 %collective-permute-start.9 = (bf16[224,32,128]{2,1,0:T(8,128)(2,1)}, bf16[224,32,128]{2,1,0:T(8,128)(2,1)}, u32[]{:S(2)}, u32[]{:S(2)}) collective-permute-start(bf16[224,32,128]{2,1,0:T(8,128)(2,1)} %collective-permute-done.8.refs_17_), channel_id=1, source_target_pairs={{0,8},{8,0},{16,24},{24,16},{1,9},{9,1},{17,25},{25,17},{2,10},{10... | collective-permute-start | bytes 5505032 | tf_op jit(solution)/shard_map/ppermute | solution.py:598
  221.1 0.8 copy-start.6
  221.9 11.5 %collective-permute-start.4 = (bf16[2,128,896]{2,1,0:T(8,128)(2,1)S(1)}, bf16[2,128,896]{2,1,0:T(8,128)(2,1)}, u32[]{:S(2)}, u32[]{:S(2)}) collective-permute-start(bf16[2,128,896]{2,1,0:T(8,128)(2,1)S(1)} %collective-permute-done.3.refs_10_), channel_id=1, source_target_pairs={{0,1},{1,0},{2,3},{3,2},{4,5},{5,4},{6,7},{7,6},{8,9},{9,8},{10,11... | collective-permute-start | bytes 1376264 | tf_op jit(solution)/shard_map/ppermute | solution.py:615
  233.4 10.5 %collective-permute-start.2 = (bf16[2,128,896]{2,1,0:T(8,128)(2,1)S(1)}, bf16[2,128,896]{2,1,0:T(8,128)(2,1)}, u32[]{:S(2)}, u32[]{:S(2)}) collective-permute-start(bf16[2,128,896]{2,1,0:T(8,128)(2,1)S(1)} %collective-permute-done.1.refs_8_), channel_id=1, source_target_pairs={{0,1},{1,0},{2,3},{3,2},{4,5},{5,4},{6,7},{7,6},{8,9},{9,8},{10,11... | collective-permute-start | bytes 1376264 | tf_op jit(solution)/shard_map/ppermute | solution.py:615
  243.8 9.6 %collective-permute-start.6 = (bf16[2,128,896]{2,1,0:T(8,128)(2,1)}, bf16[2,128,896]{2,1,0:T(8,128)(2,1)}, u32[]{:S(2)}, u32[]{:S(2)}) collective-permute-start(bf16[2,128,896]{2,1,0:T(8,128)(2,1)} %copy-done.6), channel_id=1, source_target_pairs={{0,1},{1,0},{2,3},{3,2},{4,5},{5,4},{6,7},{7,6},{8,9},{9,8},{10,11... | collective-permute-start | bytes 1376264 | tf_op jit(solution)/shard_map/ppermute | solution.py:615
  296.8 13.4 %collective-permute-start.20 = (bf16[2,224,32,128]{3,2,1,0:T(8,128)(2,1)}, bf16[2,224,32,128]{3,2,1,0:T(8,128)(2,1)}, u32[]{:S(2)}, u32[]{:S(2)}) collective-permute-start(bf16[2,224,32,128]{3,2,1,0:T(8,128)(2,1)} %get-tuple-element.33), channel_id=1, source_target_pairs={{0,8},{8,0},{16,24},{24,16},{1,9},{9,1},{17,25},{25,17},{2,10},{10... | collective-permute-start | bytes 11010056 | tf_op jit(solution)/shard_map/ppermute | solution.py:640
  303.2 141.0 %all-to-all-start.2 = ((bf16[8,28,2,32,128]{4,3,2,1,0:T(8,128)(2,1)}), bf16[8,28,2,32,128]{4,3,2,1,0:T(8,128)(2,1)}, u32[]{:S(2)}, u32[]{:S(2)}) async-start(bf16[8,28,2,32,128]{4,3,2,1,0:T(8,128)(2,1)} %bitcast.25), calls=%async_computation.2 | async-start | bytes 7340032 | tf_op jit(solution)/shard_map/all_to_all | solution.py:581
  310.0 121.2 %collective-permute-start.19 = (bf16[2,224,32,128]{3,2,1,0:T(8,128)(2,1)}, bf16[2,224,32,128]{3,2,1,0:T(8,128)(2,1)S(1)}, u32[]{:S(2)}, u32[]{:S(2)}) collective-permute-start(bf16[2,224,32,128]{3,2,1,0:T(8,128)(2,1)} %get-tuple-element.31), channel_id=1, source_target_pairs={{0,8},{8,0},{16,24},{24,16},{1,9},{9,1},{17,25},{25,17},{2,10},{10... | collective-permute-start | bytes 11010056 | tf_op jit(solution)/shard_map/ppermute | solution.py:640
  316.1 115.1 %collective-permute-start.21 = (bf16[2,224,32,128]{3,2,1,0:T(8,128)(2,1)}, bf16[2,224,32,128]{3,2,1,0:T(8,128)(2,1)}, u32[]{:S(2)}, u32[]{:S(2)}) collective-permute-start(bf16[2,224,32,128]{3,2,1,0:T(8,128)(2,1)} %add_convert_fusion), channel_id=1, source_target_pairs={{0,16},{8,24},{16,0},{24,8},{1,17},{9,25},{17,1},{25,9},{2,18},{10... | collective-permute-start | bytes 11010056 | tf_op jit(solution)/shard_map/ppermute | solution.py:645
  327.3 45.8 %collective-permute-start.16 = (bf16[4,128,896]{2,1,0:T(8,128)(2,1)}, bf16[4,128,896]{2,1,0:T(8,128)(2,1)}, u32[]{:S(2)}, u32[]{:S(2)}) collective-permute-start(bf16[4,128,896]{2,1,0:T(8,128)(2,1)} %get-tuple-element.29), channel_id=1, source_target_pairs={{0,1},{1,0},{2,3},{3,2},{4,5},{5,4},{6,7},{7,6},{8,9},{9,8},{10,11... | collective-permute-start | bytes 2752520 | tf_op jit(solution)/shard_map/ppermute | solution.py:661
  336.2 81.7 %copy-start.7 = (bf16[4,128,896]{2,1,0:T(8,128)(2,1)S(1)}, bf16[4,128,896]{2,1,0:T(8,128)(2,1)}, u32[]{:S(2)}) copy-start(bf16[4,128,896]{2,1,0:T(8,128)(2,1)} %get-tuple-element.24) | copy-start | bytes 2752516
  336.2 56.3 %collective-permute-start.13 = (bf16[4,128,896]{2,1,0:T(8,128)(2,1)}, bf16[4,128,896]{2,1,0:T(8,128)(2,1)S(1)}, u32[]{:S(2)}, u32[]{:S(2)}) collective-permute-start(bf16[4,128,896]{2,1,0:T(8,128)(2,1)} %get-tuple-element.25), channel_id=1, source_target_pairs={{0,1},{1,0},{2,3},{3,2},{4,5},{5,4},{6,7},{7,6},{8,9},{9,8},{10,11... | collective-permute-start | bytes 2752520 | tf_op jit(solution)/shard_map/ppermute | solution.py:661
  374.3 28.9 %collective-permute-start.17 = (bf16[2,128,896]{2,1,0:T(8,128)(2,1)S(1)}, bf16[2,128,896]{2,1,0:T(8,128)(2,1)S(1)}, u32[]{:S(2)}, u32[]{:S(2)}) collective-permute-start(bf16[2,128,896]{2,1,0:T(8,128)(2,1)S(1)} %add_convert_fusion.1), channel_id=1, source_target_pairs={{0,2},{1,3},{2,0},{3,1},{4,6},{5,7},{6,4},{7,5},{8,10},{9,11},{10,... | collective-permute-start | bytes 1376264 | tf_op jit(solution)/shard_map/ppermute | solution.py:661
  393.7 24.2 %collective-permute-start.14 = (bf16[2,128,896]{2,1,0:T(8,128)(2,1)S(1)}, bf16[2,128,896]{2,1,0:T(8,128)(2,1)S(1)}, u32[]{:S(2)}, u32[]{:S(2)}) collective-permute-start(bf16[2,128,896]{2,1,0:T(8,128)(2,1)S(1)} %add_convert_fusion.2), channel_id=1, source_target_pairs={{0,2},{1,3},{2,0},{3,1},{4,6},{5,7},{6,4},{7,5},{8,10},{9,11},{10,... | collective-permute-start | bytes 1376264 | tf_op jit(solution)/shard_map/ppermute | solution.py:661
  404.4 14.2 %collective-permute-start.18 = (bf16[1,128,896]{2,1,0:T(8,128)(2,1)S(1)}, bf16[1,128,896]{2,1,0:T(8,128)(2,1)S(1)}, u32[]{:S(2)}, u32[]{:S(2)}) collective-permute-start(bf16[1,128,896]{2,1,0:T(8,128)(2,1)S(1)} %add_convert_fusion.4), channel_id=1, source_target_pairs={{0,4},{1,5},{2,6},{3,7},{4,0},{5,1},{6,2},{7,3},{8,12},{9,13},{10,... | collective-permute-start | bytes 688136 | tf_op jit(solution)/shard_map/ppermute | solution.py:661
  418.0 12.4 %collective-permute-start.15 = (bf16[1,128,896]{2,1,0:T(8,128)(2,1)S(1)}, bf16[1,128,896]{2,1,0:T(8,128)(2,1)S(1)}, u32[]{:S(2)}, u32[]{:S(2)}) collective-permute-start(bf16[1,128,896]{2,1,0:T(8,128)(2,1)S(1)} %add_convert_fusion.6), channel_id=1, source_target_pairs={{0,4},{1,5},{2,6},{3,7},{4,0},{5,1},{6,2},{7,3},{8,12},{9,13},{10,... | collective-permute-start | bytes 688136 | tf_op jit(solution)/shard_map/ppermute | solution.py:661
  431.2 1.8 copy-start

commit v4 on v3

--- a/solution.py
+++ b/solution.py
@@ -115,11 +115,11 @@
     return lax.select(kind == 0, jnp.zeros_like(picked), picked)
 
 
-def feature_copies(parts, which, place_ref, buf, sem):
+def feature_copies(parts, place_ref, buf, sem):
     copies = []
     for m, part in enumerate(parts):
         at = (place_ref[2] ^ m) if len(parts) > 1 else 0
-        copies.append(pltpu.make_async_copy(part.at[which], buf.at[at], sem.at[m]))
+        copies.append(pltpu.make_async_copy(part, buf.at[at], sem.at[m]))
     return copies
 
 
@@ -142,7 +142,7 @@
     parts = refs[7 + n_feat : 7 + n_feat + n_dp]
     act, act_t, slopes, x_t, wu_hbm, x_v, up_v, up_a, wu, pre, feat_sem, in_sem, out_sem = refs[7 + n_feat + n_dp :]
     slots, block, _ = up_v.shape
-    copies = feature_copies(feats, 0, place_ref, x_v, feat_sem)
+    copies = feature_copies(feats, place_ref, x_v, feat_sem)
     copies += weight_copies(up_hbm, up_v, parts, up_a, place_ref, in_sem)
     for copy in copies:
         copy.start()
@@ -199,7 +199,7 @@
     rows = block // n_dp
     nx = n_dp // 2
     chunk = stage.shape[2]
-    copies = feature_copies(feats, 1, place_ref, back_v, feat_sem)
+    copies = feature_copies(feats, place_ref, back_v, feat_sem)
     copies += weight_copies(down_hbm, down_v, parts, down_a, place_ref, in_sem)
     for copy in copies:
         copy.start()
@@ -278,7 +278,7 @@
     keep.wait()
 
 
-def output_kernel(pieces, turned, *refs):
+def output_kernel(pieces, turned, bits, *refs):
     row_ref, col_ref, place_ref = refs[:3]
     w_hbm, left = refs[3:5]
     outs = refs[5 : 5 + len(pieces)]
@@ -312,15 +312,14 @@
 
     count = staged.shape[0]
     per = staged.shape[2] // block
-    bits = count.bit_length() - 1
     for a in range(count):
         if count == 1:
             at = 0
         else:
             far = place_ref[2] ^ a
             at = 0
-            for b in range(bits):
-                at = at + ((far >> b) & 1) * (count >> (b + 1))
+            for b, bit in enumerate(bits):
+                at = at + lax.div(far, bit) % 2 * (count >> (b + 1))
         for q in range(per):
             staged[at, :, q * block : (q + 1) * block] = acc[a * per + q].astype(BF16)
     copies = [
@@ -404,11 +403,11 @@
     )(*tables, place, *feats, down, *parts, act_t, slopes, x_t)
 
 
-def output_products(row, col, place, w, left, turned, pieces, feat_shape, row_blocks):
+def output_products(row, col, place, w, left, turned, bits, pieces, feat_shape, row_blocks):
     slots, block, _ = w.shape
     count, tokens, shard = feat_shape
     return pl.pallas_call(
-        functools.partial(output_kernel, pieces, turned),
+        functools.partial(output_kernel, pieces, turned, bits),
         out_shape=[jax.ShapeDtypeStruct((size, tokens, shard), BF16) for _, size in pieces],
         in_specs=[SMEM] * 3 + [ANY, VMEM],
         out_specs=[ANY] * len(pieces),
@@ -599,7 +598,9 @@
         return parts
 
     up_pack = pack_weight(up_weight_blocks, send_slots, dp_index, rows)
-    down_pack = pack_weight(down_weight_blocks, send_slots, dp_index, rows)
+    later_slots, tables, place = lax.optimization_barrier((send_slots, tables, place))
+    new_row, col_slot, home, came, kind = tables
+    down_pack = pack_weight(down_weight_blocks, later_slots, dp_index, rows)
     up_in = exchange(up_pack)
     down_in = exchange(down_pack)
     up_parts = spread(up_in)
@@ -609,17 +610,21 @@
     stacked = shard % block == 0 and tensor_size & (tensor_size - 1) == 0
     if stacked:
         bits = [1 << k for k in reversed(range(tensor_size.bit_length() - 1))]
-        held = {0: jnp.stack([activations, cotangent])}
-        for bit in bits:
-            for m in list(held):
-                held[m ^ bit] = lax.ppermute(held[m], "tensor", far_pairs(bit))
-        feats = [held[m] for m in range(tensor_size)]
+
+        def gather(own):
+            held = {0: own}
+            for bit in bits:
+                for m in list(held):
+                    held[m ^ bit] = lax.ppermute(held[m], "tensor", far_pairs(bit))
+            return [held[m] for m in range(tensor_size)]
+
+        feats = gather(activations)
+        backs = gather(cotangent)
         feat_shape = (tensor_size,) + activations.shape
     else:
-        x = lax.all_gather(activations, "tensor", axis=1, tiled=True)
-        back = lax.all_gather(cotangent, "tensor", axis=1, tiled=True)
-        feats = [jnp.stack([x, back])[:, None].reshape((2,) + x.shape)]
-        feat_shape = (1,) + x.shape
+        feats = [lax.all_gather(activations, "tensor", axis=1, tiled=True)]
+        backs = [lax.all_gather(cotangent, "tensor", axis=1, tiled=True)]
+        feat_shape = (1,) + feats[0].shape
     row_blocks = feat_shape[0] * feat_shape[2] // block
 
     ups = (up_first_moment, up_second_moment)
@@ -633,7 +638,7 @@
         tables, place, feats, up_weight_blocks, up_parts, col_count, row_blocks, feat_shape
     )
     bpre, wd, *grads = gradient_products(
-        tables, place, feats, down_weight_blocks, down_parts, act_t, slopes, x_t, feat_shape
+        tables, place, backs, down_weight_blocks, down_parts, act_t, slopes, x_t, feat_shape
     )
     terms = []
     for j in range(nx):
@@ -645,26 +650,25 @@
             terms.append(lax.ppermute(both, "dp", x_pairs(j)))
 
     sums = []
-    for w, left, turned in ((wd, act, False), (wu, bpre, True)):
+    near = [1 << k for k in range(tensor_size.bit_length() - 1)] if stacked else []
+    swapped = near[1::-1] + near[2:]
+    for w, left, turned, order in ((wd, act, False, near), (wu, bpre, True, swapped)):
         half = tensor_size // 2
         pieces = ((0, half), (half, half)) if stacked else ((0, 1),)
         got = output_products(
-            new_row, col_slot, place, w, left, turned, pieces, feat_shape, row_blocks
+            new_row, col_slot, place, w, left, turned, order, pieces, feat_shape, row_blocks
         )
         if not stacked:
             sums.append(lax.psum_scatter(got[0][0], "tensor", scatter_dimension=1, tiled=True))
             continue
         held, send = got
         held = [held]
-        bit = 1
-        while True:
+        for step, bit in enumerate(order):
+            if step:
+                half = held[-1].shape[0] // 2
+                send = sum(s[half : 2 * half].astype(F32) for s in held).astype(BF16)
+                held = [s[:half] for s in held]
             held.append(lax.ppermute(send, "tensor", far_pairs(bit)))
-            bit *= 2
-            if bit >= tensor_size:
-                break
-            half = held[-1].shape[0] // 2
-            send = sum(s[half : 2 * half].astype(F32) for s in held).astype(BF16)
-            held = [s[:half] for s in held]
         sums.append(sum(s[0].astype(F32) for s in held).astype(BF16))
     out_sum, in_sum = sums
 

time: 456 us -> 460 us (level)
  waiting for transfers between devices: 285 us -> 273 us
  starting transfers between devices: 44 us -> 55.8 us
    ppermute x6, waiting for transfers between devices: 86.3 us -> 76.3 us  [layer(): held.append(lax.ppermute(send, 'tensor', far_pairs(bit)))]
    ppermute x6, starting transfers between devices: 4.31 us -> 11.8 us  [layer(): held.append(lax.ppermute(send, 'tensor', far_pairs(bit)))]
    ppermute x7 -> x14, starting transfers between devices: 11.7 us -> 18.4 us  [gather(): held[m ^ bit] = lax.ppermute(held[m], 'tensor', far_pairs(bit))]
    ppermute x7 -> x14, waiting for transfers between devices: 124 us -> 126 us  [gather(): held[m ^ bit] = lax.ppermute(held[m], 'tensor', far_pairs(bit))]
  transfers between devices with their start and end apart: 26 -> 33, of which waited for: 12 -> 15; matrix products, arithmetic and copies ran while one was open for 4% -> 4% of each run, Pallas kernels for 19% -> 19%
where the time goes in v4:
time: 460 us; the launch traced here: 459 us
  waiting for transfers between devices  273 us (59%)
  Pallas kernels  103 us (22%)
  starting transfers between devices  55.8 us (12%)
  other arithmetic  17.2 us (4%)
  local copies, waits for them, and re-layouts  9.05 us (2%)
    ppermute x14, waiting for transfers between devices, gather(): held[m ^ bit] = lax.ppermute(held[m], 'tensor', far_pairs(bit))  126 us
    ppermute x6, waiting for transfers between devices, layer(): held.append(lax.ppermute(send, 'tensor', far_pairs(bit)))  76.3 us
    all_to_all x4, waiting for transfers between devices, exchange(): lax.all_to_all(shaped, 'tensor', split_axis=0, concat_axis=0, tiled=True)  71.1 us
    pallas_call x1, Pallas kernels, gradient_products(): pl.pallas_call(functools.partial(gradient_kernel, n_feat, n_dp), out_shap...  24.3 us
    pallas_call x2, Pallas kernels, adam_step(): pl.pallas_call(kernel, out_shape=jax.ShapeDtypeStruct(moments[0].shape, F...  22.5 us
    all_to_all x4, starting transfers between devices, exchange(): lax.all_to_all(shaped, 'tensor', split_axis=0, concat_axis=0, tiled=True)  20.4 us
    pallas_call x1, Pallas kernels, forward_products(): pl.pallas_call(functools.partial(forward_kernel, n_feat, n_dp, row_blocks...  19.2 us
    ppermute x14, starting transfers between devices, gather(): held[m ^ bit] = lax.ppermute(held[m], 'tensor', far_pairs(bit))  18.4 us
  transfers between devices with their start and end apart: 33, of which 15 were waited for; matrix products, arithmetic and copies ran while one was open for 4% of the time, Pallas kernels for 19%

profile of v4, /device:TPU:0, one launch (start us, length us, event | category | flops | bytes accessed | tf_op | source)
XLA Modules:
  0.0 459.5 jit_solution(17165281622137821384)
XLA Ops:
  4.7 3.8 pack_weight.3
  8.5 7.4 %all-to-all-start.1 = ((bf16[8,28,32,128]{3,2,1,0:T(8,128)(2,1)}), bf16[8,28,32,128]{3,2,1,0:T(8,128)(2,1)S(1)}, u32[]{:S(2)}, u32[]{:S(2)}) async-start(bf16[8,28,32,128]{3,2,1,0:T(8,128)(2,1)} %bitcast.27), calls=%async_computation.1 | async-start | bytes 3670016 | tf_op jit(solution)/shard_map/all_to_all | solution.py:580
  16.2 1.9 gather_fusion
  20.1 3.8 pack_weight.2
  23.9 34.7 %all-to-all-done.1 = bf16[8,28,32,128]{3,2,1,0:T(8,128)(2,1)S(1)} async-done(((bf16[8,28,32,128]{3,2,1,0:T(8,128)(2,1)}), bf16[8,28,32,128]{3,2,1,0:T(8,128)(2,1)S(1)}, u32[]{:S(2)}, u32[]{:S(2)}) %all-to-all-start.1) | async-done | bytes 1835040 | tf_op jit(solution)/shard_map/all_to_all | solution.py:580
  59.8 3.6 all-to-all-start
  63.4 6.4 %pack_moments.3 = bf16[224,2,32,128]{3,2,1,0:T(8,128)(2,1)} custom-call(s32[224]{0:T(256)} %reshape.141.send_ref, f32[224,32,128]{2,1,0:T(8,128)} %refs_3_.3, f32[224,32,128]{2,1,0:T(8,128)} %refs_4_.3), custom_call_target="tpu_custom_call" | custom-call | bytes 11010048 | tf_op jit(solution)/shard_map/pack_moments/pallas_call | solution.py:85
  69.8 36.4 %all-to-all-done = bf16[8,28,32,128]{3,2,1,0:T(8,128)(2,1)S(1)} async-done(((bf16[8,28,32,128]{3,2,1,0:T(8,128)(2,1)}), bf16[8,28,32,128]{3,2,1,0:T(8,128)(2,1)S(1)}, u32[]{:S(2)}, u32[]{:S(2)}) %all-to-all-start) | async-done | bytes 1835040 | tf_op jit(solution)/shard_map/all_to_all | solution.py:580
  106.3 4.7 %all-to-all-start.3 = ((bf16[8,28,2,32,128]{4,3,2,1,0:T(8,128)(2,1)}), bf16[8,28,2,32,128]{4,3,2,1,0:T(8,128)(2,1)}, u32[]{:S(2)}, u32[]{:S(2)}) async-start(bf16[8,28,2,32,128]{4,3,2,1,0:T(8,128)(2,1)} %bitcast.22), calls=%async_computation.3 | async-start | bytes 7340032 | tf_op jit(solution)/shard_map/all_to_all | solution.py:580
  110.9 1.6 collective-permute-start.18
  113.0 2.7 collective-permute-start.13
  115.8 1.5 collective-permute-start.11
  117.2 1.5 collective-permute-start.10
  118.7 83.3 %collective-permute-done.13.refs_10_ = bf16[128,896]{1,0:T(8,128)(2,1)S(1)} collective-permute-done((bf16[128,896]{1,0:T(8,128)(2,1)S(1)}, bf16[128,896]{1,0:T(8,128)(2,1)S(1)}, u32[]{:S(2)}, u32[]{:S(2)}) %collective-permute-start.13) | collective-permute-done | bytes 229408 | tf_op jit(solution)/shard_map/ppermute | solution.py:618
  202.6 2.7 collective-permute-start.1
  205.4 8.2 %collective-permute-done.3.refs_10_ = bf16[128,896]{1,0:T(8,128)(2,1)S(1)} collective-permute-done((bf16[128,896]{1,0:T(8,128)(2,1)S(1)}, bf16[128,896]{1,0:T(8,128)(2,1)S(1)}, u32[]{:S(2)}, u32[]{:S(2)}) %collective-permute-start.3) | collective-permute-done | bytes 229408 | tf_op jit(solution)/shard_map/ppermute | solution.py:618
  214.5 2.2 collective-permute-start
  216.7 5.4 %collective-permute-done.refs_7_ = bf16[128,896]{1,0:T(8,128)(2,1)S(1)} collective-permute-done((bf16[128,896]{1,0:T(8,128)(2,1)S(1)}, bf16[128,896]{1,0:T(8,128)(2,1)S(1)}, u32[]{:S(2)}, u32[]{:S(2)}) %collective-permute-start) | collective-permute-done | bytes 229408 | tf_op jit(solution)/shard_map/ppermute | solution.py:618
  222.1 6.6 %collective-permute-done.15.refs_12_ = bf16[128,896]{1,0:T(8,128)(2,1)S(1)} collective-permute-done((bf16[128,896]{1,0:T(8,128)(2,1)S(1)}, bf16[128,896]{1,0:T(8,128)(2,1)S(1)}, u32[]{:S(2)}, u32[]{:S(2)}) %collective-permute-start.15) | collective-permute-done | bytes 229408 | tf_op jit(solution)/shard_map/ppermute | solution.py:618
  228.7 1.5 collective-permute-start.14
  230.1 4.9 %collective-permute-done.14.refs_11_ = bf16[128,896]{1,0:T(8,128)(2,1)S(1)} collective-permute-done((bf16[128,896]{1,0:T(8,128)(2,1)S(1)}, bf16[128,896]{1,0:T(8,128)(2,1)S(1)}, u32[]{:S(2)}, u32[]{:S(2)}) %collective-permute-start.14) | collective-permute-done | bytes 229408 | tf_op jit(solution)/shard_map/ppermute | solution.py:618
  235.0 1.7 collective-permute-start.12
  236.8 4.3 collective-permute-done.12.refs_9_
  241.1 6.0 %collective-permute-done.5.refs_12_ = bf16[128,896]{1,0:T(8,128)(2,1)S(1)} collective-permute-done((bf16[128,896]{1,0:T(8,128)(2,1)S(1)}, bf16[128,896]{1,0:T(8,128)(2,1)S(1)}, u32[]{:S(2)}, u32[]{:S(2)}) %collective-permute-start.5) | collective-permute-done | bytes 229408 | tf_op jit(solution)/shard_map/ppermute | solution.py:618
  247.1 1.7 collective-permute-start.16
  248.8 6.7 %collective-permute-done.16.refs_13_ = bf16[128,896]{1,0:T(8,128)(2,1)S(1)} collective-permute-done((bf16[128,896]{1,0:T(8,128)(2,1)S(1)}, bf16[128,896]{1,0:T(8,128)(2,1)S(1)}, u32[]{:S(2)}, u32[]{:S(2)}) %collective-permute-start.16) | collective-permute-done | bytes 229408 | tf_op jit(solution)/shard_map/ppermute | solution.py:618
  255.6 1.7 collective-permute-start.4
  260.6 19.2 %forward_products.1 = (bf16[16,128,128]{2,1,0:T(8,128)(2,1)}, bf16[16,128,128]{2,1,0:T(8,128)(2,1)}, f32[16,128,128]{2,1,0:T(8,128)}, bf16[56,128,128]{2,1,0:T(8,128)(2,1)}, bf16[224,128,128]{2,1,0:T(8,128)(2,1)}) custom-call(s32[224]{0:T(256)} %refs_0_.5, s32[224]{0:T(256)} %and_select_fusion.1.refs_1_, s32[224]{0:T(256)} %get-tuple-element.29.refs_2_.home_ref, ...), custom_call_target="tpu_custom_call" | custom-call | flops 939524096 | bytes 44040192 | tf_op jit(solution)/shard_map/forward_products/pallas_call | solution.py:347
  280.5 24.3 %gradient_products.1 = (bf16[16,128,128]{2,1,0:T(8,128)(2,1)}, bf16[224,128,128]{2,1,0:T(8,128)(2,1)}, bf16[2,224,32,128]{3,2,1,0:T(8,128)(2,1)}, bf16[2,224,32,...) custom-call(s32[224]{0:T(256)} %refs_0_.5, ...), custom_call_target="tpu_custom_call" | custom-call | flops 2818572288 | bytes 73400320 | tf_op jit(solution)/shard_map/gradient_products/pallas_call | solution.py:381
  304.9 6.3 %pack_moments.2 = bf16[224,2,32,128]{3,2,1,0:T(8,128)(2,1)} custom-call(s32[224]{0:T(256)} %reshape.141.send_ref, f32[224,32,128]{2,1,0:T(8,128)} %refs_3_.2, f32[224,32,128]{2,1,0:T(8,128)} %refs_4_.2), custom_call_target="tpu_custom_call" | custom-call | bytes 11010048 | tf_op jit(solution)/shard_map/pack_moments/pallas_call | solution.py:85
  311.2 4.7 %all-to-all-start.2 = ((bf16[8,28,2,32,128]{4,3,2,1,0:T(8,128)(2,1)}), bf16[8,28,2,32,128]{4,3,2,1,0:T(8,128)(2,1)}, u32[]{:S(2)}, u32[]{:S(2)}) async-start(bf16[8,28,2,32,128]{4,3,2,1,0:T(8,128)(2,1)} %bitcast.23), calls=%async_computation.2 | async-start | bytes 7340032 | tf_op jit(solution)/shard_map/all_to_all | solution.py:580
  316.5 5.9 %add_convert_fusion = bf16[2,224,32,128]{3,2,1,0:T(8,128)(2,1)} fusion(bf16[2,224,32,128]{3,2,1,0:T(8,128)(2,1)} %collective-permute-done.27, bf16[2,224,32,128]{3,2,1,0:T(8,128)(2,1)} %get-tuple-element.46), kind=kLoop, calls=%fused_computation.1 | loop fusion | flops 7340032 | bytes 11010048 | tf_op jit(solution)/shard_map/convert_element_type | solution.py:649
  322.4 1.5 collective-permute-start.28
  323.9 9.7 %output_products.3 = (bf16[4,128,896]{2,1,0:T(8,128)(2,1)}, bf16[4,128,896]{2,1,0:T(8,128)(2,1)}) custom-call(s32[224]{0:T(256)} %refs_0_.5, s32[224]{0:T(256)} %and_select_fusion.1.refs_1_, s32[3]{0:T(128)} %pad_add_fusion.refs_5_.refs_2_, bf16[224,128,128]{2,1,0:T(8,128)(2,1)} %get-tuple-element.40.refs_3_, bf16[16,128,128]{2,1,0:T(8,128)(2,1)} %get-tuple-element.41.refs_4_), custom_call_target="tpu_custom_call" | custom-call | flops 939524096 | bytes 14680064 | tf_op jit(solution)/shard_map/output_products/pallas_call | solution.py:409
  333.6 1.4 collective-permute-start.23
  335.0 7.0 %output_products.2 = (bf16[4,128,896]{2,1,0:T(8,128)(2,1)}, bf16[4,128,896]{2,1,0:T(8,128)(2,1)}) custom-call(s32[224]{0:T(256)} %refs_0_.5, s32[224]{0:T(256)} %and_select_fusion.1.refs_1_, s32[3]{0:T(128)} %pad_add_fusion.refs_5_.refs_2_, bf16[224,128,128]{2,1,0:T(8,128)(2,1)} %get-tuple-element.36.refs_3_, bf16[16,128,128]{2,1,0:T(8,128)(2,1)} %get-tuple-element.37.refs_4_), custom_call_target="tpu_custom_call" | custom-call | flops 939524096 | bytes 14680064 | tf_op jit(solution)/shard_map/output_products/pallas_call | solution.py:409
  342.1 1.5 collective-permute-start.20
  343.6 53.2 %collective-permute-done.23 = bf16[4,128,896]{2,1,0:T(8,128)(2,1)} collective-permute-done((bf16[4,128,896]{2,1,0:T(8,128)(2,1)}, bf16[4,128,896]{2,1,0:T(8,128)(2,1)}, u32[]{:S(2)}, u32[]{:S(2)}) %collective-permute-start.23) | collective-permute-done | bytes 917536 | tf_op jit(solution)/shard_map/ppermute | solution.py:671
  398.1 1.8 collective-permute-start.24
  401.0 2.5 collective-permute-start.21
  403.5 7.0 %collective-permute-done.24 = bf16[2,128,896]{2,1,0:T(8,128)(2,1)S(1)} collective-permute-done((bf16[2,128,896]{2,1,0:T(8,128)(2,1)S(1)}, bf16[2,128,896]{2,1,0:T(8,128)(2,1)S(1)}, u32[]{:S(2)}, u32[]{:S(2)}) %collective-permute-start.24) | collective-permute-done | bytes 458784 | tf_op jit(solution)/shard_map/ppermute | solution.py:671
  411.6 3.3 collective-permute-start.25
  416.2 14.8 %collective-permute-done.25 = bf16[1,128,896]{2,1,0:T(8,128)(2,1)S(1)} collective-permute-done((bf16[1,128,896]{2,1,0:T(8,128)(2,1)S(1)}, bf16[1,128,896]{2,1,0:T(8,128)(2,1)S(1)}, u32[]{:S(2)}, u32[]{:S(2)}) %collective-permute-start.25) | collective-permute-done | bytes 229408 | tf_op jit(solution)/shard_map/ppermute | solution.py:671
  431.0 1.9 fusion.1
  432.8 1.3 collective-permute-done.22
  435.0 1.8 copy-done
  436.8 11.2 %adam_step.3 = f32[224,32,128]{2,1,0:T(8,128)} custom-call(s32[224]{0:T(256)} %get-tuple-element.29.refs_2_.home_ref, s32[224]{0:T(256)} %get-tuple-element.30.refs_3_.came_ref, s32[224]{0:T(256)} %get-tuple-element.31.refs_4_.kind_ref, bf16[2,224,32,128]{3,2,1,0:T(8,128)(2,1)} %get-tuple-element.44.refs_0_, bf16[2,224,32,128]{3,2,1,0:T(8,128)(2,1)} %copy-done, ...), custom_call_target="tpu_custom_call" | custom-call | flops 13762560 | bytes 15597568 | tf_op jit(solution)/shard_map/adam_step/pallas_call | solution.py:502
  448.1 11.2 %adam_step.2 = f32[224,32,128]{2,1,0:T(8,128)} custom-call(s32[224]{0:T(256)} %get-tuple-element.29.refs_2_.home_ref, s32[224]{0:T(256)} %get-tuple-element.30.refs_3_.came_ref, s32[224]{0:T(256)} %get-tuple-element.31.refs_4_.kind_ref, bf16[2,224,32,128]{3,2,1,0:T(8,128)(2,1)} %get-tuple-element.44.refs_0_, bf16[2,224,32,128]{3,2,1,0:T(8,128)(2,1)} %copy-done, ...), custom_call_target="tpu_custom_call" | custom-call | flops 13762560 | bytes 15597568 | tf_op jit(solution)/shard_map/adam_step/pallas_call | solution.py:502
  (109 shorter events, 19.8 us)
Async XLA Ops:
  8.5 7.4 %copy-start.21 = (s32[224]{0:T(256)S(1)}, s32[224]{0:T(256)}, u32[]{:S(2)}) copy-start(s32[224]{0:T(256)} %param.22) | copy-start | bytes 2692
  8.5 7.5 %copy-start.22 = (s32[128]{0:T(128)S(1)}, s32[128]{0:T(128)}, u32[]{:S(2)}) copy-start(s32[128]{0:T(128)} %param.23) | copy-start | bytes 1540
  8.5 50.1 %all-to-all-start.1 = ((bf16[8,28,32,128]{3,2,1,0:T(8,128)(2,1)}), bf16[8,28,32,128]{3,2,1,0:T(8,128)(2,1)S(1)}, u32[]{:S(2)}, u32[]{:S(2)}) async-start(bf16[8,28,32,128]{3,2,1,0:T(8,128)(2,1)} %bitcast.27), calls=%async_computation.1 | async-start | bytes 3670016 | tf_op jit(solution)/shard_map/all_to_all | solution.py:580
  59.8 46.4 %all-to-all-start = ((bf16[8,28,32,128]{3,2,1,0:T(8,128)(2,1)}), bf16[8,28,32,128]{3,2,1,0:T(8,128)(2,1)S(1)}, u32[]{:S(2)}, u32[]{:S(2)}) async-start(bf16[8,28,32,128]{3,2,1,0:T(8,128)(2,1)} %bitcast.28), calls=%async_computation | async-start | bytes 3670016 | tf_op jit(solution)/shard_map/all_to_all | solution.py:580
  106.2 107.3 %copy-start.1 = (bf16[8,28,32,128]{3,2,1,0:T(8,128)(2,1)}, bf16[8,28,32,128]{3,2,1,0:T(8,128)(2,1)S(1)}, u32[]{:S(2)}) copy-start(bf16[8,28,32,128]{3,2,1,0:T(8,128)(2,1)S(1)} %all-to-all-done) | copy-start | bytes 5505028
  106.2 95.7 %copy-start.8 = (bf16[128,896]{1,0:T(8,128)(2,1)S(1)}, bf16[128,896]{1,0:T(8,128)(2,1)}, u32[]{:S(2)}) copy-start(bf16[128,896]{1,0:T(8,128)(2,1)} %refs_6_.3) | copy-start | bytes 688132
  106.3 205.0 %all-to-all-start.3 = ((bf16[8,28,2,32,128]{4,3,2,1,0:T(8,128)(2,1)}), bf16[8,28,2,32,128]{4,3,2,1,0:T(8,128)(2,1)}, u32[]{:S(2)}, u32[]{:S(2)}) async-start(bf16[8,28,2,32,128]{4,3,2,1,0:T(8,128)(2,1)} %bitcast.22), calls=%async_computation.3 | async-start | bytes 7340032 | tf_op jit(solution)/shard_map/all_to_all | solution.py:580
  110.9 91.2 %collective-permute-start.18 = (bf16[224,32,128]{2,1,0:T(8,128)(2,1)}, bf16[224,32,128]{2,1,0:T(8,128)(2,1)S(1)}, u32[]{:S(2)}, u32[]{:S(2)}) collective-permute-start(bf16[224,32,128]{2,1,0:T(8,128)(2,1)} %bitcast.29), channel_id=1, source_target_pairs={{0,16},{8,24},{16,0},{24,8},{1,17},{9,25},{17,1},{25,9},{2,18},{10... | collective-permute-start | bytes 5505032 | tf_op jit(solution)/shard_map/ppermute | solution.py:596
  112.5 101.1 %collective-permute-start.8 = (bf16[224,32,128]{2,1,0:T(8,128)(2,1)S(1)}, bf16[224,32,128]{2,1,0:T(8,128)(2,1)}, u32[]{:S(2)}, u32[]{:S(2)}) collective-permute-start(bf16[224,32,128]{2,1,0:T(8,128)(2,1)S(1)} %bitcast.24), channel_id=1, source_target_pairs={{0,16},{8,24},{16,0},{24,8},{1,17},{9,25},{17,1},{25,9},{2,18},{10... | collective-permute-start | bytes 5505032 | tf_op jit(solution)/shard_map/ppermute | solution.py:596
  113.0 89.0 %collective-permute-start.13 = (bf16[128,896]{1,0:T(8,128)(2,1)S(1)}, bf16[128,896]{1,0:T(8,128)(2,1)S(1)}, u32[]{:S(2)}, u32[]{:S(2)}) collective-permute-start(bf16[128,896]{1,0:T(8,128)(2,1)S(1)} %copy-done.7), channel_id=1, source_target_pairs={{0,4},{1,5},{2,6},{3,7},{4,0},{5,1},{6,2},{7,3},{8,12},{9,13},{10,... | collective-permute-start | bytes 688136 | tf_op jit(solution)/shard_map/ppermute | solution.py:618
  115.8 86.2 %collective-permute-start.11 = (bf16[128,896]{1,0:T(8,128)(2,1)S(1)}, bf16[128,896]{1,0:T(8,128)(2,1)S(1)}, u32[]{:S(2)}, u32[]{:S(2)}) collective-permute-start(bf16[128,896]{1,0:T(8,128)(2,1)S(1)} %copy-done.7), channel_id=1, source_target_pairs={{0,2},{1,3},{2,0},{3,1},{4,6},{5,7},{6,4},{7,5},{8,10},{9,11},{10,... | collective-permute-start | bytes 688136 | tf_op jit(solution)/shard_map/ppermute | solution.py:618
  117.2 85.4 %collective-permute-start.10 = (bf16[128,896]{1,0:T(8,128)(2,1)S(1)}, bf16[128,896]{1,0:T(8,128)(2,1)S(1)}, u32[]{:S(2)}, u32[]{:S(2)}) collective-permute-start(bf16[128,896]{1,0:T(8,128)(2,1)S(1)} %copy-done.7), channel_id=1, source_target_pairs={{0,1},{1,0},{2,3},{3,2},{4,5},{5,4},{6,7},{7,6},{8,9},{9,8},{10,11... | collective-permute-start | bytes 688136 | tf_op jit(solution)/shard_map/ppermute | solution.py:618
  202.0 58.6 %copy-start.10 = (bf16[128,896]{1,0:T(8,128)(2,1)}, bf16[128,896]{1,0:T(8,128)(2,1)S(1)}, u32[]{:S(2)}) copy-start(bf16[128,896]{1,0:T(8,128)(2,1)S(1)} %collective-permute-done.13.refs_10_) | copy-start | bytes 688132
  202.0 11.6 %collective-permute-start.3 = (bf16[128,896]{1,0:T(8,128)(2,1)S(1)}, bf16[128,896]{1,0:T(8,128)(2,1)S(1)}, u32[]{:S(2)}, u32[]{:S(2)}) collective-permute-start(bf16[128,896]{1,0:T(8,128)(2,1)S(1)} %copy-done.8), channel_id=1, source_target_pairs={{0,4},{1,5},{2,6},{3,7},{4,0},{5,1},{6,2},{7,3},{8,12},{9,13},{10,... | collective-permute-start | bytes 688136 | tf_op jit(solution)/shard_map/ppermute | solution.py:618
  202.0 58.6 %copy-start.12 = (bf16[128,896]{1,0:T(8,128)(2,1)}, bf16[128,896]{1,0:T(8,128)(2,1)S(1)}, u32[]{:S(2)}) copy-start(bf16[128,896]{1,0:T(8,128)(2,1)S(1)} %collective-permute-done.11.refs_8_) | copy-start | bytes 688132
  202.0 55.3 %collective-permute-start.17 = (bf16[224,32,128]{2,1,0:T(8,128)(2,1)}, bf16[224,32,128]{2,1,0:T(8,128)(2,1)S(1)}, u32[]{:S(2)}, u32[]{:S(2)}) collective-permute-start(bf16[224,32,128]{2,1,0:T(8,128)(2,1)} %bitcast.30), channel_id=1, source_target_pairs={{0,8},{8,0},{16,24},{24,16},{1,9},{9,1},{17,25},{25,17},{2,10},{10... | collective-permute-start | bytes 5505032 | tf_op jit(solution)/shard_map/ppermute | solution.py:597
  202.1 11.5 %copy-start.3 = (bf16[224,32,128]{2,1,0:T(8,128)(2,1)}, bf16[224,32,128]{2,1,0:T(8,128)(2,1)S(1)}, u32[]{:S(2)}) copy-start(bf16[224,32,128]{2,1,0:T(8,128)(2,1)S(1)} %collective-permute-done.18.refs_17_) | copy-start | bytes 5505028
  202.1 55.5 %collective-permute-start.19 = (bf16[224,32,128]{2,1,0:T(8,128)(2,1)S(1)}, bf16[224,32,128]{2,1,0:T(8,128)(2,1)S(1)}, u32[]{:S(2)}, u32[]{:S(2)}) collective-permute-start(bf16[224,32,128]{2,1,0:T(8,128)(2,1)S(1)} %collective-permute-done.18.refs_17_), channel_id=1, source_target_pairs={{0,8},{8,0},{16,24},{24,16},{1,9},{9,1},{17,25},{25,17},{2,10},{10... | collective-permute-start | bytes 5505032 | tf_op jit(solution)/shard_map/ppermute | solution.py:597
  202.6 58.0 %copy-start.13 = (bf16[128,896]{1,0:T(8,128)(2,1)}, bf16[128,896]{1,0:T(8,128)(2,1)S(1)}, u32[]{:S(2)}) copy-start(bf16[128,896]{1,0:T(8,128)(2,1)S(1)} %collective-permute-done.10.refs_7_) | copy-start | bytes 688132
  202.6 11.9 %collective-permute-start.1 = (bf16[128,896]{1,0:T(8,128)(2,1)S(1)}, bf16[128,896]{1,0:T(8,128)(2,1)S(1)}, u32[]{:S(2)}, u32[]{:S(2)}) collective-permute-start(bf16[128,896]{1,0:T(8,128)(2,1)S(1)} %copy-done.8), channel_id=1, source_target_pairs={{0,2},{1,3},{2,0},{3,1},{4,6},{5,7},{6,4},{7,5},{8,10},{9,11},{10,... | collective-permute-start | bytes 688136 | tf_op jit(solution)/shard_map/ppermute | solution.py:618
  213.6 66.3 %copy-start.9 = (bf16[128,896]{1,0:T(8,128)(2,1)}, bf16[128,896]{1,0:T(8,128)(2,1)S(1)}, u32[]{:S(2)}) copy-start(bf16[128,896]{1,0:T(8,128)(2,1)S(1)} %collective-permute-done.3.refs_10_) | copy-start | bytes 688132
  213.6 66.3 %collective-permute-start.7 = (bf16[224,32,128]{2,1,0:T(8,128)(2,1)S(1)}, bf16[224,32,128]{2,1,0:T(8,128)(2,1)}, u32[]{:S(2)}, u32[]{:S(2)}) collective-permute-start(bf16[224,32,128]{2,1,0:T(8,128)(2,1)S(1)} %bitcast.25), channel_id=1, source_target_pairs={{0,8},{8,0},{16,24},{24,16},{1,9},{9,1},{17,25},{25,17},{2,10},{10... | collective-permute-start | bytes 5505032 | tf_op jit(solution)/shard_map/ppermute | solution.py:597
  213.6 66.3 %collective-permute-start.9 = (bf16[224,32,128]{2,1,0:T(8,128)(2,1)}, bf16[224,32,128]{2,1,0:T(8,128)(2,1)}, u32[]{:S(2)}, u32[]{:S(2)}) collective-permute-start(bf16[224,32,128]{2,1,0:T(8,128)(2,1)} %collective-permute-done.8.refs_17_), channel_id=1, source_target_pairs={{0,8},{8,0},{16,24},{24,16},{1,9},{9,1},{17,25},{25,17},{2,10},{10... | collective-permute-start | bytes 5505032 | tf_op jit(solution)/shard_map/ppermute | solution.py:597
  214.5 65.3 %copy-start.11 = (bf16[128,896]{1,0:T(8,128)(2,1)}, bf16[128,896]{1,0:T(8,128)(2,1)S(1)}, u32[]{:S(2)}) copy-start(bf16[128,896]{1,0:T(8,128)(2,1)S(1)} %collective-permute-done.1.refs_8_) | copy-start | bytes 688132
  214.5 7.6 %collective-permute-start = (bf16[128,896]{1,0:T(8,128)(2,1)S(1)}, bf16[128,896]{1,0:T(8,128)(2,1)S(1)}, u32[]{:S(2)}, u32[]{:S(2)}) collective-permute-start(bf16[128,896]{1,0:T(8,128)(2,1)S(1)} %copy-done.8), channel_id=1, source_target_pairs={{0,1},{1,0},{2,3},{3,2},{4,5},{5,4},{6,7},{7,6},{8,9},{9,8},{10,11... | collective-permute-start | bytes 688136 | tf_op jit(solution)/shard_map/ppermute | solution.py:618
  222.1 57.8 %copy-start.14 = (bf16[128,896]{1,0:T(8,128)(2,1)}, bf16[128,896]{1,0:T(8,128)(2,1)S(1)}, u32[]{:S(2)}) copy-start(bf16[128,896]{1,0:T(8,128)(2,1)S(1)} %collective-permute-done.refs_7_) | copy-start | bytes 688132
  222.1 6.6 %collective-permute-start.15 = (bf16[128,896]{1,0:T(8,128)(2,1)S(1)}, bf16[128,896]{1,0:T(8,128)(2,1)S(1)}, u32[]{:S(2)}, u32[]{:S(2)}) collective-permute-start(bf16[128,896]{1,0:T(8,128)(2,1)S(1)} %collective-permute-done.13.refs_10_), channel_id=1, source_target_pairs={{0,2},{1,3},{2,0},{3,1},{4,6},{5,7},{6,4},{7,5},{8,10},{9,11},{10,... | collective-permute-start | bytes 688136 | tf_op jit(solution)/shard_map/ppermute | solution.py:618
  228.7 31.9 %copy-start.16 = (bf16[128,896]{1,0:T(8,128)(2,1)}, bf16[128,896]{1,0:T(8,128)(2,1)S(1)}, u32[]{:S(2)}) copy-start(bf16[128,896]{1,0:T(8,128)(2,1)S(1)} %collective-permute-done.15.refs_12_) | copy-start | bytes 688132
  228.7 6.4 %collective-permute-start.14 = (bf16[128,896]{1,0:T(8,128)(2,1)S(1)}, bf16[128,896]{1,0:T(8,128)(2,1)S(1)}, u32[]{:S(2)}, u32[]{:S(2)}) collective-permute-start(bf16[128,896]{1,0:T(8,128)(2,1)S(1)} %collective-permute-done.13.refs_10_), channel_id=1, source_target_pairs={{0,1},{1,0},{2,3},{3,2},{4,5},{5,4},{6,7},{7,6},{8,9},{9,8},{10,11... | collective-permute-start | bytes 688136 | tf_op jit(solution)/shard_map/ppermute | solution.py:618
  235.0 6.0 %collective-permute-start.12 = (bf16[128,896]{1,0:T(8,128)(2,1)S(1)}, bf16[128,896]{1,0:T(8,128)(2,1)S(1)}, u32[]{:S(2)}, u32[]{:S(2)}) collective-permute-start(bf16[128,896]{1,0:T(8,128)(2,1)S(1)} %collective-permute-done.11.refs_8_), channel_id=1, source_target_pairs={{0,1},{1,0},{2,3},{3,2},{4,5},{5,4},{6,7},{7,6},{8,9},{9,8},{10,11... | collective-permute-start | bytes 688136 | tf_op jit(solution)/shard_map/ppermute | solution.py:618
  241.1 16.5 %copy-start.19 = (bf16[128,896]{1,0:T(8,128)(2,1)}, bf16[128,896]{1,0:T(8,128)(2,1)S(1)}, u32[]{:S(2)}) copy-start(bf16[128,896]{1,0:T(8,128)(2,1)S(1)} %collective-permute-done.12.refs_9_) | copy-start | bytes 688132
  241.1 6.0 %collective-permute-start.5 = (bf16[128,896]{1,0:T(8,128)(2,1)S(1)}, bf16[128,896]{1,0:T(8,128)(2,1)S(1)}, u32[]{:S(2)}, u32[]{:S(2)}) collective-permute-start(bf16[128,896]{1,0:T(8,128)(2,1)S(1)} %collective-permute-done.3.refs_10_), channel_id=1, source_target_pairs={{0,2},{1,3},{2,0},{3,1},{4,6},{5,7},{6,4},{7,5},{8,10},{9,11},{10,... | collective-permute-start | bytes 688136 | tf_op jit(solution)/shard_map/ppermute | solution.py:618
  247.1 32.8 %copy-start.15 = (bf16[128,896]{1,0:T(8,128)(2,1)}, bf16[128,896]{1,0:T(8,128)(2,1)S(1)}, u32[]{:S(2)}) copy-start(bf16[128,896]{1,0:T(8,128)(2,1)S(1)} %collective-permute-done.5.refs_12_) | copy-start | bytes 688132
  247.1 8.5 %collective-permute-start.16 = (bf16[128,896]{1,0:T(8,128)(2,1)S(1)}, bf16[128,896]{1,0:T(8,128)(2,1)S(1)}, u32[]{:S(2)}, u32[]{:S(2)}) collective-permute-start(bf16[128,896]{1,0:T(8,128)(2,1)S(1)} %collective-permute-done.15.refs_12_), channel_id=1, source_target_pairs={{0,1},{1,0},{2,3},{3,2},{4,5},{5,4},{6,7},{7,6},{8,9},{9,8},{10,11... | collective-permute-start | bytes 688136 | tf_op jit(solution)/shard_map/ppermute | solution.py:618
  255.6 24.2 %collective-permute-start.4 = (bf16[128,896]{1,0:T(8,128)(2,1)S(1)}, bf16[128,896]{1,0:T(8,128)(2,1)S(1)}, u32[]{:S(2)}, u32[]{:S(2)}) collective-permute-start(bf16[128,896]{1,0:T(8,128)(2,1)S(1)} %collective-permute-done.3.refs_10_), channel_id=1, source_target_pairs={{0,1},{1,0},{2,3},{3,2},{4,5},{5,4},{6,7},{7,6},{8,9},{9,8},{10,11... | collective-permute-start | bytes 688136 | tf_op jit(solution)/shard_map/ppermute | solution.py:618
  257.3 22.5 %collective-permute-start.2 = (bf16[128,896]{1,0:T(8,128)(2,1)S(1)}, bf16[128,896]{1,0:T(8,128)(2,1)}, u32[]{:S(2)}, u32[]{:S(2)}) collective-permute-start(bf16[128,896]{1,0:T(8,128)(2,1)S(1)} %collective-permute-done.1.refs_8_), channel_id=1, source_target_pairs={{0,1},{1,0},{2,3},{3,2},{4,5},{5,4},{6,7},{7,6},{8,9},{9,8},{10,11... | collective-permute-start | bytes 688136 | tf_op jit(solution)/shard_map/ppermute | solution.py:618
  259.8 20.0 %collective-permute-start.6 = (bf16[128,896]{1,0:T(8,128)(2,1)S(1)}, bf16[128,896]{1,0:T(8,128)(2,1)}, u32[]{:S(2)}, u32[]{:S(2)}) collective-permute-start(bf16[128,896]{1,0:T(8,128)(2,1)S(1)} %collective-permute-done.5.refs_12_), channel_id=1, source_target_pairs={{0,1},{1,0},{2,3},{3,2},{4,5},{5,4},{6,7},{7,6},{8,9},{9,8},{10,11... | collective-permute-start | bytes 688136 | tf_op jit(solution)/shard_map/ppermute | solution.py:618
  304.8 11.7 %collective-permute-start.27 = (bf16[2,224,32,128]{3,2,1,0:T(8,128)(2,1)}, bf16[2,224,32,128]{3,2,1,0:T(8,128)(2,1)}, u32[]{:S(2)}, u32[]{:S(2)}) collective-permute-start(bf16[2,224,32,128]{3,2,1,0:T(8,128)(2,1)} %get-tuple-element.47), channel_id=1, source_target_pairs={{0,8},{8,0},{16,24},{24,16},{1,9},{9,1},{17,25},{25,17},{2,10},{10... | collective-permute-start | bytes 11010056 | tf_op jit(solution)/shard_map/ppermute | solution.py:645
  311.2 136.8 %all-to-all-start.2 = ((bf16[8,28,2,32,128]{4,3,2,1,0:T(8,128)(2,1)}), bf16[8,28,2,32,128]{4,3,2,1,0:T(8,128)(2,1)}, u32[]{:S(2)}, u32[]{:S(2)}) async-start(bf16[8,28,2,32,128]{4,3,2,1,0:T(8,128)(2,1)} %bitcast.23), calls=%async_computation.2 | async-start | bytes 7340032 | tf_op jit(solution)/shard_map/all_to_all | solution.py:580
  315.9 119.1 %collective-permute-start.26 = (bf16[2,224,32,128]{3,2,1,0:T(8,128)(2,1)}, bf16[2,224,32,128]{3,2,1,0:T(8,128)(2,1)S(1)}, u32[]{:S(2)}, u32[]{:S(2)}) collective-permute-start(bf16[2,224,32,128]{3,2,1,0:T(8,128)(2,1)} %get-tuple-element.45), channel_id=1, source_target_pairs={{0,8},{8,0},{16,24},{24,16},{1,9},{9,1},{17,25},{25,17},{2,10},{10... | collective-permute-start | bytes 11010056 | tf_op jit(solution)/shard_map/ppermute | solution.py:645
  322.4 112.6 %collective-permute-start.28 = (bf16[2,224,32,128]{3,2,1,0:T(8,128)(2,1)}, bf16[2,224,32,128]{3,2,1,0:T(8,128)(2,1)}, u32[]{:S(2)}, u32[]{:S(2)}) collective-permute-start(bf16[2,224,32,128]{3,2,1,0:T(8,128)(2,1)} %add_convert_fusion), channel_id=1, source_target_pairs={{0,16},{8,24},{16,0},{24,8},{1,17},{9,25},{17,1},{25,9},{2,18},{10... | collective-permute-start | bytes 11010056 | tf_op jit(solution)/shard_map/ppermute | solution.py:650
  333.6 63.2 %collective-permute-start.23 = (bf16[4,128,896]{2,1,0:T(8,128)(2,1)}, bf16[4,128,896]{2,1,0:T(8,128)(2,1)}, u32[]{:S(2)}, u32[]{:S(2)}) collective-permute-start(bf16[4,128,896]{2,1,0:T(8,128)(2,1)} %get-tuple-element.43), channel_id=1, source_target_pairs={{0,2},{1,3},{2,0},{3,1},{4,6},{5,7},{6,4},{7,5},{8,10},{9,11},{10,... | collective-permute-start | bytes 2752520 | tf_op jit(solution)/shard_map/ppermute | solution.py:671
  342.1 72.8 %copy-start.6 = (bf16[4,128,896]{2,1,0:T(8,128)(2,1)S(1)}, bf16[4,128,896]{2,1,0:T(8,128)(2,1)}, u32[]{:S(2)}) copy-start(bf16[4,128,896]{2,1,0:T(8,128)(2,1)} %get-tuple-element.38) | copy-start | bytes 2752516
  342.1 57.8 %collective-permute-start.20 = (bf16[4,128,896]{2,1,0:T(8,128)(2,1)}, bf16[4,128,896]{2,1,0:T(8,128)(2,1)S(1)}, u32[]{:S(2)}, u32[]{:S(2)}) collective-permute-start(bf16[4,128,896]{2,1,0:T(8,128)(2,1)} %get-tuple-element.39), channel_id=1, source_target_pairs={{0,1},{1,0},{2,3},{3,2},{4,5},{5,4},{6,7},{7,6},{8,9},{9,8},{10,11... | collective-permute-start | bytes 2752520 | tf_op jit(solution)/shard_map/ppermute | solution.py:671
  398.1 12.4 %collective-permute-start.24 = (bf16[2,128,896]{2,1,0:T(8,128)(2,1)S(1)}, bf16[2,128,896]{2,1,0:T(8,128)(2,1)S(1)}, u32[]{:S(2)}, u32[]{:S(2)}) collective-permute-start(bf16[2,128,896]{2,1,0:T(8,128)(2,1)S(1)} %add_convert_fusion.1), channel_id=1, source_target_pairs={{0,1},{1,0},{2,3},{3,2},{4,5},{5,4},{6,7},{7,6},{8,9},{9,8},{10,11... | collective-permute-start | bytes 1376264 | tf_op jit(solution)/shard_map/ppermute | solution.py:671
  401.0 13.9 %collective-permute-start.21 = (bf16[2,128,896]{2,1,0:T(8,128)(2,1)S(1)}, bf16[2,128,896]{2,1,0:T(8,128)(2,1)S(1)}, u32[]{:S(2)}, u32[]{:S(2)}) collective-permute-start(bf16[2,128,896]{2,1,0:T(8,128)(2,1)S(1)} %add_convert_fusion.2), channel_id=1, source_target_pairs={{0,2},{1,3},{2,0},{3,1},{4,6},{5,7},{6,4},{7,5},{8,10},{9,11},{10,... | collective-permute-start | bytes 1376264 | tf_op jit(solution)/shard_map/ppermute | solution.py:671
  411.6 19.4 %collective-permute-start.25 = (bf16[1,128,896]{2,1,0:T(8,128)(2,1)S(1)}, bf16[1,128,896]{2,1,0:T(8,128)(2,1)S(1)}, u32[]{:S(2)}, u32[]{:S(2)}) collective-permute-start(bf16[1,128,896]{2,1,0:T(8,128)(2,1)S(1)} %add_convert_fusion.4), channel_id=1, source_target_pairs={{0,4},{1,5},{2,6},{3,7},{4,0},{5,1},{6,2},{7,3},{8,12},{9,13},{10,... | collective-permute-start | bytes 688136 | tf_op jit(solution)/shard_map/ppermute | solution.py:671
  415.0 19.2 %collective-permute-start.22 = (bf16[1,128,896]{2,1,0:T(8,128)(2,1)S(1)}, bf16[1,128,896]{2,1,0:T(8,128)(2,1)S(1)}, u32[]{:S(2)}, u32[]{:S(2)}) collective-permute-start(bf16[1,128,896]{2,1,0:T(8,128)(2,1)S(1)} %add_convert_fusion.6), channel_id=1, source_target_pairs={{0,4},{1,5},{2,6},{3,7},{4,0},{5,1},{6,2},{7,3},{8,12},{9,13},{10,... | collective-permute-start | bytes 688136 | tf_op jit(solution)/shard_map/ppermute | solution.py:671
  (8 other events, 16.7 us)

commit v5 on v4

--- a/solution.py
+++ b/solution.py
@@ -185,20 +185,13 @@
     keep.wait()
 
 
-def gradient_kernel(n_feat, n_dp, *refs):
+def back_kernel(n_feat, n_dp, *refs):
     row_ref, col_ref, home_ref, came_ref, kind_ref, place_ref = refs[:6]
     feats = refs[6 : 6 + n_feat]
     down_hbm = refs[6 + n_feat]
     parts = refs[7 + n_feat : 7 + n_feat + n_dp]
-    act_t, slopes, x_t = refs[7 + n_feat + n_dp : 10 + n_feat + n_dp]
-    outs = refs[10 + n_feat + n_dp :]
-    bpre, wd_hbm = outs[:2]
-    grad_refs = outs[2 : 2 + n_dp]
-    back_v, down_v, down_a, wd, back, stage, feat_sem, in_sem, keep_sem, out_sem = outs[2 + n_dp :]
+    slopes, bpre, wd_hbm, back_v, down_v, down_a, wd, back, feat_sem, in_sem, keep_sem = refs[7 + n_feat + n_dp :]
     slots, block, _ = down_v.shape
-    rows = block // n_dp
-    nx = n_dp // 2
-    chunk = stage.shape[2]
     copies = feature_copies(feats, place_ref, back_v, feat_sem)
     copies += weight_copies(down_hbm, down_v, parts, down_a, place_ref, in_sem)
     for copy in copies:
@@ -233,24 +226,45 @@
         return carry
 
     lax.fori_loop(0, slopes.shape[0], bend, 0)
+    keep.wait()
+
+
+def gradient_kernel(n_feat, n_dp, *refs):
+    row_ref, col_ref, place_ref = refs[:3]
+    feats = refs[3 : 3 + n_feat]
+    left = refs[3 + n_feat]
+    right = None if n_feat else refs[4]
+    start = 4 + n_feat if n_feat else 5
+    grad_refs = refs[start : start + n_dp]
+    stage, out_sem = refs[start + n_dp : start + n_dp + 2]
+    slots = row_ref.shape[0]
+    chunk, block = stage.shape[1:3]
+    rows = block // n_dp
+    nx = n_dp // 2
+    if n_feat:
+        back_v, feat_sem = refs[start + n_dp + 2 :]
+        copies = feature_copies(feats, place_ref, back_v, feat_sem)
+        for copy in copies:
+            copy.start()
+        for copy in copies:
+            copy.wait()
 
     def ship(i, slot):
         out = []
         for j in range(nx):
             for other in range(2):
                 owner = lax.rem(place_ref[0] + j, nx) * 2 + (place_ref[1] + other) % 2
-                start = pl.multiple_of(owner * rows, rows)
-                for p in range(2):
-                    out.append(
-                        pltpu.make_async_copy(
-                            stage.at[slot, p, :, pl.ds(start, rows), :],
-                            grad_refs[2 * j + other].at[p, pl.ds(i * chunk, chunk)],
-                            out_sem.at[slot, 2 * (2 * j + other) + p],
-                        )
+                at = pl.multiple_of(owner * rows, rows)
+                out.append(
+                    pltpu.make_async_copy(
+                        stage.at[slot, :, pl.ds(at, rows), :],
+                        grad_refs[2 * j + other].at[pl.ds(i * chunk, chunk)],
+                        out_sem.at[slot, 2 * j + other],
                     )
+                )
         return out
 
-    def last(i, carry):
+    def step(i, carry):
         slot = lax.rem(i, 2)
 
         @pl.when(i >= 2)
@@ -262,20 +276,20 @@
             g = i * chunk + u
             r = row_ref[g]
             c = col_ref[g]
-            stage[slot, 0, u] = jnp.dot(x_t[r], bpre[c], preferred_element_type=F32).astype(BF16)
-            stage[slot, 1, u] = jnp.dot(
-                act_t[c], columns(back_v, r, block), preferred_element_type=F32
-            ).astype(BF16)
+            if n_feat:
+                product = jnp.dot(left[c], columns(back_v, r, block), preferred_element_type=F32)
+            else:
+                product = jnp.dot(left[r], right[c], preferred_element_type=F32)
+            stage[slot, u] = product.astype(BF16)
         for copy in ship(i, slot):
             copy.start()
         return carry
 
     chunks = slots // chunk
-    lax.fori_loop(0, chunks, last, 0)
+    lax.fori_loop(0, chunks, step, 0)
     for i in range(max(chunks - 2, 0), chunks):
         for copy in ship(i, i % 2):
             copy.wait()
-    keep.wait()
 
 
 def output_kernel(pieces, turned, bits, *refs):
@@ -371,36 +385,51 @@
     )(*tables, place, *feats, up, *parts)
 
 
-def gradient_products(tables, place, feats, down, parts, act_t, slopes, x_t, feat_shape):
+def back_products(tables, place, feats, down, parts, slopes, feat_shape):
     slots, block, _ = down.shape
     n_dp, n_feat = len(parts), len(feats)
-    rows = block // n_dp
-    chunk = math.gcd(slots, CHUNK)
     tokens = slopes.shape[1]
-    grad = jax.ShapeDtypeStruct((2, slots, rows, block), BF16)
     return pl.pallas_call(
-        functools.partial(gradient_kernel, n_feat, n_dp),
-        out_shape=[jax.ShapeDtypeStruct(slopes.shape, BF16)]
-        + [jax.ShapeDtypeStruct(down.shape, BF16)]
-        + [grad] * n_dp,
-        in_specs=[SMEM] * 6 + [ANY] * (n_feat + 1 + n_dp) + [VMEM] * 3,
-        out_specs=[VMEM] + [ANY] * (1 + n_dp),
+        functools.partial(back_kernel, n_feat, n_dp),
+        out_shape=[jax.ShapeDtypeStruct(slopes.shape, BF16), jax.ShapeDtypeStruct(down.shape, BF16)],
+        in_specs=[SMEM] * 6 + [ANY] * (n_feat + 1 + n_dp) + [VMEM],
+        out_specs=[VMEM, ANY],
         scratch_shapes=[
             pltpu.VMEM(feat_shape, BF16),
             pltpu.VMEM(down.shape, BF16),
             pltpu.VMEM((n_dp,) + parts[0].shape, BF16),
             pltpu.VMEM(down.shape, BF16),
             pltpu.VMEM(slopes.shape, F32),
-            pltpu.VMEM((2, 2, chunk, block, block), BF16),
             pltpu.SemaphoreType.DMA((n_feat,)),
             pltpu.SemaphoreType.DMA((1 + n_dp,)),
             pltpu.SemaphoreType.DMA,
-            pltpu.SemaphoreType.DMA((2, 2 * n_dp)),
         ],
         compiler_params=pltpu.CompilerParams(vmem_limit_bytes=VMEM_LIMIT),
-        cost_estimate=cost(6 * slots * tokens * block * block, 20 * slots * block * block),
+        cost_estimate=cost(2 * slots * tokens * block * block, 12 * slots * block * block),
+        name="back_products",
+    )(*tables, place, *feats, down, *parts, slopes)
+
+
+def gradient_products(row, col, place, feats, blocks, n_dp, block, feat_shape):
+    slots = row.shape[0]
+    n_feat = len(feats)
+    chunk = math.gcd(slots, CHUNK)
+    tokens = feat_shape[1]
+    extra = [pltpu.VMEM(feat_shape, BF16), pltpu.SemaphoreType.DMA((n_feat,))] if n_feat else []
+    return pl.pallas_call(
+        functools.partial(gradient_kernel, n_feat, n_dp),
+        out_shape=[jax.ShapeDtypeStruct((slots, block // n_dp, block), BF16)] * n_dp,
+        in_specs=[SMEM] * 3 + [ANY] * n_feat + [VMEM] * len(blocks),
+        out_specs=[ANY] * n_dp,
+        scratch_shapes=[
+            pltpu.VMEM((2, chunk, block, block), BF16),
+            pltpu.SemaphoreType.DMA((2, n_dp)),
+        ]
+        + extra,
+        compiler_params=pltpu.CompilerParams(vmem_limit_bytes=VMEM_LIMIT),
+        cost_estimate=cost(2 * slots * tokens * block * block, 3 * slots * block * block),
         name="gradient_products",
-    )(*tables, place, *feats, down, *parts, act_t, slopes, x_t)
+    )(row, col, place, *feats, *blocks)
 
 
 def output_products(row, col, place, w, left, turned, bits, pieces, feat_shape, row_blocks):
@@ -424,7 +453,7 @@
     )(row, col, place, w, left)
 
 
-def adam_step(tables, grads, which, moments, arrived):
+def adam_step(tables, grads, moments, arrived):
     slots, rows, block = moments[0].shape
     n_grads = len(grads)
     n_from = len(arrived)
@@ -448,7 +477,7 @@
         later = [
             [
                 pltpu.make_async_copy(
-                    grad_refs[k].at[which, pl.ds(q * some, some)],
+                    grad_refs[k].at[pl.ds(q * some, some)],
                     grad_v.at[k, pl.ds(q * some, some)],
                     grad_sem.at[q, k],
                 )
@@ -637,22 +666,29 @@
     act, act_t, slopes, x_t, wu = forward_products(
         tables, place, feats, up_weight_blocks, up_parts, col_count, row_blocks, feat_shape
     )
-    bpre, wd, *grads = gradient_products(
-        tables, place, backs, down_weight_blocks, down_parts, act_t, slopes, x_t, feat_shape
+
+    def share(grads):
+        terms = []
+        for j in range(nx):
+            there = lax.ppermute(grads[2 * j + 1], "dp", core_pairs)
+            if j == 0:
+                terms += [grads[0], there]
+            else:
+                both = (grads[2 * j].astype(F32) + there.astype(F32)).astype(BF16)
+                terms.append(lax.ppermute(both, "dp", x_pairs(j)))
+        return terms
+
+    down_grads = gradient_products(new_row, col_slot, place, backs, (act_t,), n_dp, block, feat_shape)
+    down_terms = share(down_grads)
+    bpre, wd = back_products(
+        tables, place, backs, down_weight_blocks, down_parts, slopes, feat_shape
     )
-    terms = []
-    for j in range(nx):
-        there = lax.ppermute(grads[2 * j + 1], "dp", core_pairs)
-        if j == 0:
-            terms += [grads[0], there]
-        else:
-            both = (grads[2 * j].astype(F32) + there.astype(F32)).astype(BF16)
-            terms.append(lax.ppermute(both, "dp", x_pairs(j)))
-
+    up_grads = gradient_products(new_row, col_slot, place, (), (x_t, bpre), n_dp, block, feat_shape)
+    up_terms = share(up_grads)
     sums = []
     near = [1 << k for k in range(tensor_size.bit_length() - 1)] if stacked else []
-    swapped = near[1::-1] + near[2:]
-    for w, left, turned, order in ((wd, act, False, near), (wu, bpre, True, swapped)):
+    order = near
+    for w, left, turned in ((wd, act, False), (wu, bpre, True)):
         half = tensor_size // 2
         pieces = ((0, half), (half, half)) if stacked else ((0, 1),)
         got = output_products(
@@ -672,8 +708,8 @@
         sums.append(sum(s[0].astype(F32) for s in held).astype(BF16))
     out_sum, in_sum = sums
 
-    up_step = adam_step((home, came, kind), terms, 0, ups, ups_in)
-    down_step = adam_step((home, came, kind), terms, 1, downs, downs_in)
+    up_step = adam_step((home, came, kind), up_terms, ups, ups_in)
+    down_step = adam_step((home, came, kind), down_terms, downs, downs_in)
     return (out_sum, in_sum, up_step, down_step)
 
 

time: 460 us -> 519 us (1.13)
  waiting for transfers between devices: 273 us -> 327 us
  Pallas kernels: 103 us -> 112 us
    ppermute x2, waiting for transfers between devices: 0.01 us -> 37.9 us  [spread(): mine = lax.ppermute(own, 'dp', x_pairs(j))]
    all_to_all x4, waiting for transfers between devices: 71.1 us -> 88.5 us  [exchange(): lax.all_to_all(shaped, 'tensor', split_axis=0, concat_axis=0, tiled=True)]
    pallas_call x0 -> x1, Pallas kernels: none -> 16.6 us  [back_products(): pl.pallas_call(functools.partial(back_kernel, n_feat, n_dp), out_shape=[j...]
    ppermute x6, waiting for transfers between devices: 76.3 us -> 65.2 us  [layer(): held.append(lax.ppermute(send, 'tensor', far_pairs(bit)))]
    ppermute x14, waiting for transfers between devices: 126 us -> 135 us  [gather(): held[m ^ bit] = lax.ppermute(held[m], 'tensor', far_pairs(bit))]
    pallas_call x1 -> x2, Pallas kernels: 24.3 us -> 16.3 us  [gradient_products(): pl.pallas_call(functools.partial(gradient_kernel, n_feat, n_dp), out_shap...]
    ppermute x6, starting transfers between devices: 11.8 us -> 4.97 us  [layer(): held.append(lax.ppermute(send, 'tensor', far_pairs(bit)))]
    ppermute x14, starting transfers between devices: 18.4 us -> 24.2 us  [gather(): held[m ^ bit] = lax.ppermute(held[m], 'tensor', far_pairs(bit))]
  transfers between devices with their start and end apart: 33 -> 36, of which waited for: 15 -> 18; matrix products, arithmetic and copies ran while one was open for 4% -> 2% of each run, Pallas kernels for 19% -> 19%
where the time goes in v5:
time: 519 us; the launch traced here: 518 us
  waiting for transfers between devices  327 us (63%)
  Pallas kernels  112 us (22%)
  starting transfers between devices  57 us (11%)
  other arithmetic  15.1 us (3%)
  local copies, waits for them, and re-layouts  6.47 us (1%)
    ppermute x14, waiting for transfers between devices, gather(): held[m ^ bit] = lax.ppermute(held[m], 'tensor', far_pairs(bit))  135 us
    all_to_all x4, waiting for transfers between devices, exchange(): lax.all_to_all(shaped, 'tensor', split_axis=0, concat_axis=0, tiled=True)  88.5 us
    ppermute x6, waiting for transfers between devices, layer(): held.append(lax.ppermute(send, 'tensor', far_pairs(bit)))  65.2 us
    ppermute x2, waiting for transfers between devices, spread(): mine = lax.ppermute(own, 'dp', x_pairs(j))  37.9 us
    ppermute x14, starting transfers between devices, gather(): held[m ^ bit] = lax.ppermute(held[m], 'tensor', far_pairs(bit))  24.2 us
    pallas_call x2, Pallas kernels, adam_step(): pl.pallas_call(kernel, out_shape=jax.ShapeDtypeStruct(moments[0].shape, F...  22.5 us
    all_to_all x4, starting transfers between devices, exchange(): lax.all_to_all(shaped, 'tensor', split_axis=0, concat_axis=0, tiled=True)  20.9 us
    pallas_call x1, Pallas kernels, forward_products(): pl.pallas_call(functools.partial(forward_kernel, n_feat, n_dp, row_blocks...  19.1 us
  transfers between devices with their start and end apart: 36, of which 18 were waited for; matrix products, arithmetic and copies ran while one was open for 2% of the time, Pallas kernels for 19%

profile of v5, /device:TPU:0, one launch (start us, length us, event | category | flops | bytes accessed | tf_op | source)
XLA Modules:
  0.0 517.9 jit_solution(13488905794079502670)
XLA Ops:
  3.7 1.9 gather_fusion
  10.9 3.8 pack_weight.2
  14.7 7.3 %all-to-all-start = ((bf16[8,28,32,128]{3,2,1,0:T(8,128)(2,1)}), bf16[8,28,32,128]{3,2,1,0:T(8,128)(2,1)S(1)}, u32[]{:S(2)}, u32[]{:S(2)}) async-start(bf16[8,28,32,128]{3,2,1,0:T(8,128)(2,1)} %bitcast.28), calls=%async_computation | async-start | bytes 3670016 | tf_op jit(solution)/shard_map/all_to_all | solution.py:609
  22.0 3.8 pack_weight.3
  25.8 38.8 %all-to-all-done = bf16[8,28,32,128]{3,2,1,0:T(8,128)(2,1)S(1)} async-done(((bf16[8,28,32,128]{3,2,1,0:T(8,128)(2,1)}), bf16[8,28,32,128]{3,2,1,0:T(8,128)(2,1)S(1)}, u32[]{:S(2)}, u32[]{:S(2)}) %all-to-all-start) | async-done | bytes 1835040 | tf_op jit(solution)/shard_map/all_to_all | solution.py:609
  64.6 4.3 all-to-all-start.1
  69.0 6.4 %pack_moments.3 = bf16[224,2,32,128]{3,2,1,0:T(8,128)(2,1)} custom-call(s32[224]{0:T(256)} %reshape.141.send_ref, f32[224,32,128]{2,1,0:T(8,128)} %refs_3_.5, f32[224,32,128]{2,1,0:T(8,128)} %refs_4_.3), custom_call_target="tpu_custom_call" | custom-call | bytes 11010048 | tf_op jit(solution)/shard_map/pack_moments/pallas_call | solution.py:85
  75.3 35.8 %all-to-all-done.1 = bf16[8,28,32,128]{3,2,1,0:T(8,128)(2,1)} async-done(((bf16[8,28,32,128]{3,2,1,0:T(8,128)(2,1)}), bf16[8,28,32,128]{3,2,1,0:T(8,128)(2,1)}, u32[]{:S(2)}, u32[]{:S(2)}) %all-to-all-start.1) | async-done | bytes 1835040 | tf_op jit(solution)/shard_map/all_to_all | solution.py:609
  111.2 4.6 all-to-all-start.3
  115.8 1.6 collective-permute-start.18
  117.9 1.8 collective-permute-start.11
  121.2 37.9 %collective-permute-done.18.refs_17_ = bf16[224,32,128]{2,1,0:T(8,128)(2,1)} collective-permute-done((bf16[224,32,128]{2,1,0:T(8,128)(2,1)}, bf16[224,32,128]{2,1,0:T(8,128)(2,1)}, u32[]{:S(2)}, u32[]{:S(2)}) %collective-permute-start.18) | collective-permute-done | bytes 1835040 | tf_op jit(solution)/shard_map/ppermute | solution.py:625
  159.1 20.9 %collective-permute-done.11.refs_8_ = bf16[128,896]{1,0:T(8,128)(2,1)S(1)} collective-permute-done((bf16[128,896]{1,0:T(8,128)(2,1)S(1)}, bf16[128,896]{1,0:T(8,128)(2,1)S(1)}, u32[]{:S(2)}, u32[]{:S(2)}) %collective-permute-start.11) | collective-permute-done | bytes 229408 | tf_op jit(solution)/shard_map/ppermute | solution.py:647
  180.0 3.9 collective-permute-start.13
  183.9 6.4 %pack_moments.2 = bf16[224,2,32,128]{3,2,1,0:T(8,128)(2,1)} custom-call(s32[224]{0:T(256)} %reshape.141.send_ref, f32[224,32,128]{2,1,0:T(8,128)} %refs_3_.3, f32[224,32,128]{2,1,0:T(8,128)} %refs_4_.2), custom_call_target="tpu_custom_call" | custom-call | bytes 11010048 | tf_op jit(solution)/shard_map/pack_moments/pallas_call | solution.py:85
  190.3 13.8 %all-to-all-done.3 = bf16[8,28,2,32,128]{4,3,2,1,0:T(8,128)(2,1)} async-done(((bf16[8,28,2,32,128]{4,3,2,1,0:T(8,128)(2,1)}), bf16[8,28,2,32,128]{4,3,2,1,0:T(8,128)(2,1)}, u32[]{:S(2)}, u32[]{:S(2)}) %all-to-all-start.3) | async-done | bytes 3670048 | tf_op jit(solution)/shard_map/all_to_all | solution.py:609
  204.1 4.7 all-to-all-start.2
  208.8 2.9 collective-permute-start.3
  213.1 84.7 %collective-permute-done.3.refs_10_.refs_7_ = bf16[128,896]{1,0:T(8,128)(2,1)S(1)} collective-permute-done((bf16[128,896]{1,0:T(8,128)(2,1)S(1)}, bf16[128,896]{1,0:T(8,128)(2,1)S(1)}, u32[]{:S(2)}, u32[]{:S(2)}) %collective-permute-start.3) | collective-permute-done | bytes 229408 | tf_op jit(solution)/shard_map/ppermute | solution.py:647
  299.9 4.3 collective-permute-done.refs_7_.refs_4_
  304.2 1.7 collective-permute-start.12
  305.9 4.3 collective-permute-done.12.refs_9_
  311.3 4.9 collective-permute-done.15.refs_12_
  316.2 1.7 collective-permute-start.14
  318.0 4.4 collective-permute-done.14.refs_11_
  323.5 4.9 collective-permute-done.5.refs_12_.refs_9_
  328.4 1.7 collective-permute-start.16
  330.1 6.7 %collective-permute-done.16.refs_13_ = bf16[128,896]{1,0:T(8,128)(2,1)S(1)} collective-permute-done((bf16[128,896]{1,0:T(8,128)(2,1)S(1)}, bf16[128,896]{1,0:T(8,128)(2,1)S(1)}, u32[]{:S(2)}, u32[]{:S(2)}) %collective-permute-start.16) | collective-permute-done | bytes 229408 | tf_op jit(solution)/shard_map/ppermute | solution.py:647
  336.9 1.7 collective-permute-start.4
  338.9 1.7 collective-permute-start.6
  340.6 19.1 %forward_products.1 = (bf16[16,128,128]{2,1,0:T(8,128)(2,1)}, bf16[16,128,128]{2,1,0:T(8,128)(2,1)}, f32[16,128,128]{2,1,0:T(8,128)}, bf16[56,128,128]{2,1,0:T(8,128)(2,1)}, bf16[224,128,128]{2,1,0:T(8,128)(2,1)}) custom-call(s32[224]{0:T(256)} %refs_0_.8, s32[224]{0:T(256)} %and_select_fusion.1.refs_1_, s32[224]{0:T(256)} %get-tuple-element.33.refs_2_.home_ref, ...), custom_call_target="tpu_custom_call" | custom-call | flops 939524096 | bytes 44040192 | tf_op jit(solution)/shard_map/forward_products/pallas_call | solution.py:361
  360.6 8.8 %gradient_products.3 = (bf16[224,32,128]{2,1,0:T(8,128)(2,1)}, bf16[224,32,128]{2,1,0:T(8,128)(2,1)}, bf16[224,32,128]{2,1,0:T(8,128)(2,1)}, bf16[224,32,128]{2,1,0:T(8,128)(2,1)}) custom-call(s32[224]{0:T(256)} %refs_0_.8, s32[224]{0:T(256)} %and_select_fusion.1.refs_1_, s32[3]{0:T(128)} %pad_add_fusion.refs_5_.refs_2_, bf16[128,896]{1,0:T(8,128)(2,1)} %refs_3_.4, ...), custom_call_target="tpu_custom_call" | custom-call | flops 939524096 | bytes 11010048 | tf_op jit(solution)/shard_map/gradient_products/pallas_call | solution.py:419
  369.5 16.6 %back_products.1 = (bf16[16,128,128]{2,1,0:T(8,128)(2,1)}, bf16[224,128,128]{2,1,0:T(8,128)(2,1)}) custom-call(s32[224]{0:T(256)} %refs_0_.8, s32[224]{0:T(256)} %and_select_fusion.1.refs_1_, s32[224]{0:T(256)} %get-tuple-element.33.refs_2_.home_ref, s32[224]{0:T(256)} %get-tuple-element.34.refs_3_.came_ref, s32[224]{0:T(256)} %get-tuple-element.35.refs_4_.kind_ref, ...), custom_call_target="tpu_custom_call" | custom-call | flops 939524096 | bytes 44040192 | tf_op jit(solution)/shard_map/back_products/pallas_call | solution.py:392
  386.1 7.5 %gradient_products.2 = (bf16[224,32,128]{2,1,0:T(8,128)(2,1)}, bf16[224,32,128]{2,1,0:T(8,128)(2,1)}, bf16[224,32,128]{2,1,0:T(8,128)(2,1)}, bf16[224,32,128]{2,1,0:T(8,128)(2,1)}) custom-call(s32[224]{0:T(256)} %refs_0_.8, s32[224]{0:T(256)} %and_select_fusion.1.refs_1_, s32[3]{0:T(128)} %pad_add_fusion.refs_5_.refs_2_, ...), custom_call_target="tpu_custom_call" | custom-call | flops 939524096 | bytes 11010048 | tf_op jit(solution)/shard_map/gradient_products/pallas_call | solution.py:419
  394.1 9.7 %output_products.3 = (bf16[4,128,896]{2,1,0:T(8,128)(2,1)}, bf16[4,128,896]{2,1,0:T(8,128)(2,1)}) custom-call(s32[224]{0:T(256)} %refs_0_.8, s32[224]{0:T(256)} %and_select_fusion.1.refs_1_, s32[3]{0:T(128)} %pad_add_fusion.refs_5_.refs_2_, bf16[224,128,128]{2,1,0:T(8,128)(2,1)} %get-tuple-element.42.refs_3_, bf16[16,128,128]{2,1,0:T(8,128)(2,1)} %get-tuple-element.43.refs_4_), custom_call_target="tpu_custom_call" | custom-call | flops 939524096 | bytes 14680064 | tf_op jit(solution)/shard_map/output_products/pallas_call | solution.py:438
  404.2 7.0 %output_products.2 = (bf16[4,128,896]{2,1,0:T(8,128)(2,1)}, bf16[4,128,896]{2,1,0:T(8,128)(2,1)}) custom-call(s32[224]{0:T(256)} %refs_0_.8, s32[224]{0:T(256)} %and_select_fusion.1.refs_1_, s32[3]{0:T(128)} %pad_add_fusion.refs_5_.refs_2_, bf16[224,128,128]{2,1,0:T(8,128)(2,1)} %get-tuple-element.38.refs_3_, bf16[16,128,128]{2,1,0:T(8,128)(2,1)} %get-tuple-element.39.refs_4_), custom_call_target="tpu_custom_call" | custom-call | flops 939524096 | bytes 14680064 | tf_op jit(solution)/shard_map/output_products/pallas_call | solution.py:438
  411.2 1.8 collective-permute-start.20
  413.5 2.7 add_convert_fusion
  417.7 3.3 add_convert_fusion.1
  421.1 6.2 %collective-permute-done.23 = bf16[4,128,896]{2,1,0:T(8,128)(2,1)S(1)} collective-permute-done((bf16[4,128,896]{2,1,0:T(8,128)(2,1)}, bf16[4,128,896]{2,1,0:T(8,128)(2,1)S(1)}, u32[]{:S(2)}, u32[]{:S(2)}) %collective-permute-start.23) | collective-permute-done | bytes 917536 | tf_op jit(solution)/shard_map/ppermute | solution.py:707
  428.9 17.1 %collective-permute-done.20 = bf16[4,128,896]{2,1,0:T(8,128)(2,1)S(1)} collective-permute-done((bf16[4,128,896]{2,1,0:T(8,128)(2,1)}, bf16[4,128,896]{2,1,0:T(8,128)(2,1)S(1)}, u32[]{:S(2)}, u32[]{:S(2)}) %collective-permute-start.20) | collective-permute-done | bytes 917536 | tf_op jit(solution)/shard_map/ppermute | solution.py:707
  446.4 11.3 %collective-permute-done.24 = bf16[2,128,896]{2,1,0:T(8,128)(2,1)S(1)} collective-permute-done((bf16[2,128,896]{2,1,0:T(8,128)(2,1)S(1)}, bf16[2,128,896]{2,1,0:T(8,128)(2,1)S(1)}, u32[]{:S(2)}, u32[]{:S(2)}) %collective-permute-start.24) | collective-permute-done | bytes 458784 | tf_op jit(solution)/shard_map/ppermute | solution.py:707
  458.0 10.4 %collective-permute-done.21 = bf16[2,128,896]{2,1,0:T(8,128)(2,1)S(1)} collective-permute-done((bf16[2,128,896]{2,1,0:T(8,128)(2,1)S(1)}, bf16[2,128,896]{2,1,0:T(8,128)(2,1)S(1)}, u32[]{:S(2)}, u32[]{:S(2)}) %collective-permute-start.21) | collective-permute-done | bytes 458784 | tf_op jit(solution)/shard_map/ppermute | solution.py:707
  468.4 2.3 collective-permute-start.25
  470.8 8.5 %collective-permute-done.25 = bf16[1,128,896]{2,1,0:T(8,128)(2,1)S(1)} collective-permute-done((bf16[1,128,896]{2,1,0:T(8,128)(2,1)S(1)}, bf16[1,128,896]{2,1,0:T(8,128)(2,1)S(1)}, u32[]{:S(2)}, u32[]{:S(2)}) %collective-permute-start.25) | collective-permute-done | bytes 229408 | tf_op jit(solution)/shard_map/ppermute | solution.py:707
  480.1 11.7 %collective-permute-done.22 = bf16[1,128,896]{2,1,0:T(8,128)(2,1)S(1)} collective-permute-done((bf16[1,128,896]{2,1,0:T(8,128)(2,1)S(1)}, bf16[1,128,896]{2,1,0:T(8,128)(2,1)S(1)}, u32[]{:S(2)}, u32[]{:S(2)}) %collective-permute-start.22) | collective-permute-done | bytes 229408 | tf_op jit(solution)/shard_map/ppermute | solution.py:707
  494.0 11.2 %adam_step.3 = f32[224,32,128]{2,1,0:T(8,128)} custom-call(s32[224]{0:T(256)} %get-tuple-element.33.refs_2_.home_ref, s32[224]{0:T(256)} %get-tuple-element.34.refs_3_.came_ref, s32[224]{0:T(256)} %get-tuple-element.35.refs_4_.kind_ref, bf16[224,32,128]{2,1,0:T(8,128)(2,1)} %get-tuple-element.52.refs_0_, ...), custom_call_target="tpu_custom_call" | custom-call | flops 13762560 | bytes 15597568 | tf_op jit(solution)/shard_map/adam_step/pallas_call | solution.py:531
  506.5 11.2 %adam_step.2 = f32[224,32,128]{2,1,0:T(8,128)} custom-call(s32[224]{0:T(256)} %get-tuple-element.33.refs_2_.home_ref, s32[224]{0:T(256)} %get-tuple-element.34.refs_3_.came_ref, s32[224]{0:T(256)} %get-tuple-element.35.refs_4_.kind_ref, bf16[224,32,128]{2,1,0:T(8,128)(2,1)} %get-tuple-element.47.refs_0_, bf16[224,32,128]{2,1,0:T(8,128)(2,1)} %copy-done.1, ...), custom_call_target="tpu_custom_call" | custom-call | flops 13762560 | bytes 15597568 | tf_op jit(solution)/shard_map/adam_step/pallas_call | solution.py:531
  (112 shorter events, 26.8 us)
Async XLA Ops:
  14.7 49.9 %all-to-all-start = ((bf16[8,28,32,128]{3,2,1,0:T(8,128)(2,1)}), bf16[8,28,32,128]{3,2,1,0:T(8,128)(2,1)S(1)}, u32[]{:S(2)}, u32[]{:S(2)}) async-start(bf16[8,28,32,128]{3,2,1,0:T(8,128)(2,1)} %bitcast.28), calls=%async_computation | async-start | bytes 3670016 | tf_op jit(solution)/shard_map/all_to_all | solution.py:609
  64.6 234.7 %copy-start = (bf16[8,28,32,128]{3,2,1,0:T(8,128)(2,1)}, bf16[8,28,32,128]{3,2,1,0:T(8,128)(2,1)S(1)}, u32[]{:S(2)}) copy-start(bf16[8,28,32,128]{3,2,1,0:T(8,128)(2,1)S(1)} %all-to-all-done) | copy-start | bytes 5505028
  64.6 46.6 %all-to-all-start.1 = ((bf16[8,28,32,128]{3,2,1,0:T(8,128)(2,1)}), bf16[8,28,32,128]{3,2,1,0:T(8,128)(2,1)}, u32[]{:S(2)}, u32[]{:S(2)}) async-start(bf16[8,28,32,128]{3,2,1,0:T(8,128)(2,1)} %bitcast.27), calls=%async_computation.1 | async-start | bytes 3670016 | tf_op jit(solution)/shard_map/all_to_all | solution.py:609
  111.2 92.9 %all-to-all-start.3 = ((bf16[8,28,2,32,128]{4,3,2,1,0:T(8,128)(2,1)}), bf16[8,28,2,32,128]{4,3,2,1,0:T(8,128)(2,1)}, u32[]{:S(2)}, u32[]{:S(2)}) async-start(bf16[8,28,2,32,128]{4,3,2,1,0:T(8,128)(2,1)} %bitcast.23), calls=%async_computation.3 | async-start | bytes 7340032 | tf_op jit(solution)/shard_map/all_to_all | solution.py:609
  115.8 43.3 %collective-permute-start.18 = (bf16[224,32,128]{2,1,0:T(8,128)(2,1)}, bf16[224,32,128]{2,1,0:T(8,128)(2,1)}, u32[]{:S(2)}, u32[]{:S(2)}) collective-permute-start(bf16[224,32,128]{2,1,0:T(8,128)(2,1)} %bitcast.11.refs_15_), channel_id=1, source_target_pairs={{0,16},{8,24},{16,0},{24,8},{1,17},{9,25},{17,1},{25,9},{2,18},{10... | collective-permute-start | bytes 5505032 | tf_op jit(solution)/shard_map/ppermute | solution.py:625
  117.4 182.0 %collective-permute-start.8 = (bf16[224,32,128]{2,1,0:T(8,128)(2,1)S(1)}, bf16[224,32,128]{2,1,0:T(8,128)(2,1)}, u32[]{:S(2)}, u32[]{:S(2)}) collective-permute-start(bf16[224,32,128]{2,1,0:T(8,128)(2,1)S(1)} %bitcast.24), channel_id=1, source_target_pairs={{0,16},{8,24},{16,0},{24,8},{1,17},{9,25},{17,1},{25,9},{2,18},{10... | collective-permute-start | bytes 5505032 | tf_op jit(solution)/shard_map/ppermute | solution.py:625
  117.9 62.1 %collective-permute-start.11 = (bf16[128,896]{1,0:T(8,128)(2,1)S(1)}, bf16[128,896]{1,0:T(8,128)(2,1)S(1)}, u32[]{:S(2)}, u32[]{:S(2)}) collective-permute-start(bf16[128,896]{1,0:T(8,128)(2,1)S(1)} %copy-done.6), channel_id=1, source_target_pairs={{0,2},{1,3},{2,0},{3,1},{4,6},{5,7},{6,4},{7,5},{8,10},{9,11},{10,... | collective-permute-start | bytes 688136 | tf_op jit(solution)/shard_map/ppermute | solution.py:647
  119.8 89.0 %collective-permute-start.10 = (bf16[128,896]{1,0:T(8,128)(2,1)S(1)}, bf16[128,896]{1,0:T(8,128)(2,1)S(1)}, u32[]{:S(2)}, u32[]{:S(2)}) collective-permute-start(bf16[128,896]{1,0:T(8,128)(2,1)S(1)} %copy-done.6), channel_id=1, source_target_pairs={{0,1},{1,0},{2,3},{3,2},{4,5},{5,4},{6,7},{7,6},{8,9},{9,8},{10,11... | collective-permute-start | bytes 688136 | tf_op jit(solution)/shard_map/ppermute | solution.py:647
  121.2 217.3 %collective-permute-start.17 = (bf16[224,32,128]{2,1,0:T(8,128)(2,1)}, bf16[224,32,128]{2,1,0:T(8,128)(2,1)}, u32[]{:S(2)}, u32[]{:S(2)}) collective-permute-start(bf16[224,32,128]{2,1,0:T(8,128)(2,1)} %bitcast.11.refs_15_), channel_id=1, source_target_pairs={{0,8},{8,0},{16,24},{24,16},{1,9},{9,1},{17,25},{25,17},{2,10},{10... | collective-permute-start | bytes 5505032 | tf_op jit(solution)/shard_map/ppermute | solution.py:626
  159.1 179.8 %collective-permute-start.19 = (bf16[224,32,128]{2,1,0:T(8,128)(2,1)}, bf16[224,32,128]{2,1,0:T(8,128)(2,1)}, u32[]{:S(2)}, u32[]{:S(2)}) collective-permute-start(bf16[224,32,128]{2,1,0:T(8,128)(2,1)} %collective-permute-done.18.refs_17_), channel_id=1, source_target_pairs={{0,8},{8,0},{16,24},{24,16},{1,9},{9,1},{17,25},{25,17},{2,10},{10... | collective-permute-start | bytes 5505032 | tf_op jit(solution)/shard_map/ppermute | solution.py:626
  180.0 124.2 %copy-start.8 = (bf16[128,896]{1,0:T(8,128)(2,1)}, bf16[128,896]{1,0:T(8,128)(2,1)S(1)}, u32[]{:S(2)}) copy-start(bf16[128,896]{1,0:T(8,128)(2,1)S(1)} %collective-permute-done.11.refs_8_) | copy-start | bytes 688132
  180.0 31.6 %collective-permute-start.13 = (bf16[128,896]{1,0:T(8,128)(2,1)S(1)}, bf16[128,896]{1,0:T(8,128)(2,1)S(1)}, u32[]{:S(2)}, u32[]{:S(2)}) collective-permute-start(bf16[128,896]{1,0:T(8,128)(2,1)S(1)} %copy-done.6), channel_id=1, source_target_pairs={{0,4},{1,5},{2,6},{3,7},{4,0},{5,1},{6,2},{7,3},{8,12},{9,13},{10,... | collective-permute-start | bytes 688136 | tf_op jit(solution)/shard_map/ppermute | solution.py:647
  204.1 301.2 %all-to-all-start.2 = ((bf16[8,28,2,32,128]{4,3,2,1,0:T(8,128)(2,1)}), bf16[8,28,2,32,128]{4,3,2,1,0:T(8,128)(2,1)}, u32[]{:S(2)}, u32[]{:S(2)}) async-start(bf16[8,28,2,32,128]{4,3,2,1,0:T(8,128)(2,1)} %bitcast.22), calls=%async_computation.2 | async-start | bytes 7340032 | tf_op jit(solution)/shard_map/all_to_all | solution.py:609
  208.8 131.9 %copy-start.10 = (bf16[128,896]{1,0:T(8,128)(2,1)}, bf16[128,896]{1,0:T(8,128)(2,1)S(1)}, u32[]{:S(2)}) copy-start(bf16[128,896]{1,0:T(8,128)(2,1)S(1)} %collective-permute-done.10.refs_7_) | copy-start | bytes 688132
  208.8 89.1 %collective-permute-start.3 = (bf16[128,896]{1,0:T(8,128)(2,1)S(1)}, bf16[128,896]{1,0:T(8,128)(2,1)S(1)}, u32[]{:S(2)}, u32[]{:S(2)}) collective-permute-start(bf16[128,896]{1,0:T(8,128)(2,1)S(1)} %copy-done.7), channel_id=1, source_target_pairs={{0,4},{1,5},{2,6},{3,7},{4,0},{5,1},{6,2},{7,3},{8,12},{9,13},{10,... | collective-permute-start | bytes 688136 | tf_op jit(solution)/shard_map/ppermute | solution.py:647
  211.6 129.0 %copy-start.13 = (bf16[128,896]{1,0:T(8,128)(2,1)}, bf16[128,896]{1,0:T(8,128)(2,1)S(1)}, u32[]{:S(2)}) copy-start(bf16[128,896]{1,0:T(8,128)(2,1)S(1)} %collective-permute-done.13.refs_10_) | copy-start | bytes 688132
  211.6 87.6 %collective-permute-start.1 = (bf16[128,896]{1,0:T(8,128)(2,1)S(1)}, bf16[128,896]{1,0:T(8,128)(2,1)S(1)}, u32[]{:S(2)}, u32[]{:S(2)}) collective-permute-start(bf16[128,896]{1,0:T(8,128)(2,1)S(1)} %copy-done.7), channel_id=1, source_target_pairs={{0,2},{1,3},{2,0},{3,1},{4,6},{5,7},{6,4},{7,5},{8,10},{9,11},{10,... | collective-permute-start | bytes 688136 | tf_op jit(solution)/shard_map/ppermute | solution.py:647
  297.8 61.9 %copy-start.9 = (bf16[128,896]{1,0:T(8,128)(2,1)}, bf16[128,896]{1,0:T(8,128)(2,1)S(1)}, u32[]{:S(2)}) copy-start(bf16[128,896]{1,0:T(8,128)(2,1)S(1)} %collective-permute-done.3.refs_10_.refs_7_) | copy-start | bytes 688132
  297.8 6.3 %collective-permute-start = (bf16[128,896]{1,0:T(8,128)(2,1)S(1)}, bf16[128,896]{1,0:T(8,128)(2,1)S(1)}, u32[]{:S(2)}, u32[]{:S(2)}) collective-permute-start(bf16[128,896]{1,0:T(8,128)(2,1)S(1)} %copy-done.7), channel_id=1, source_target_pairs={{0,1},{1,0},{2,3},{3,2},{4,5},{5,4},{6,7},{7,6},{8,9},{9,8},{10,11... | collective-permute-start | bytes 688136 | tf_op jit(solution)/shard_map/ppermute | solution.py:647
  299.3 60.5 %copy-start.11 = (bf16[128,896]{1,0:T(8,128)(2,1)}, bf16[128,896]{1,0:T(8,128)(2,1)S(1)}, u32[]{:S(2)}) copy-start(bf16[128,896]{1,0:T(8,128)(2,1)S(1)} %collective-permute-done.1.refs_8_.refs_5_) | copy-start | bytes 688132
  299.3 70.1 %collective-permute-start.7 = (bf16[224,32,128]{2,1,0:T(8,128)(2,1)S(1)}, bf16[224,32,128]{2,1,0:T(8,128)(2,1)}, u32[]{:S(2)}, u32[]{:S(2)}) collective-permute-start(bf16[224,32,128]{2,1,0:T(8,128)(2,1)S(1)} %bitcast.25), channel_id=1, source_target_pairs={{0,8},{8,0},{16,24},{24,16},{1,9},{9,1},{17,25},{25,17},{2,10},{10... | collective-permute-start | bytes 5505032 | tf_op jit(solution)/shard_map/ppermute | solution.py:626
  299.4 70.1 %collective-permute-start.9 = (bf16[224,32,128]{2,1,0:T(8,128)(2,1)}, bf16[224,32,128]{2,1,0:T(8,128)(2,1)}, u32[]{:S(2)}, u32[]{:S(2)}) collective-permute-start(bf16[224,32,128]{2,1,0:T(8,128)(2,1)} %collective-permute-done.8.refs_17_), channel_id=1, source_target_pairs={{0,8},{8,0},{16,24},{24,16},{1,9},{9,1},{17,25},{25,17},{2,10},{10... | collective-permute-start | bytes 5505032 | tf_op jit(solution)/shard_map/ppermute | solution.py:626
  304.2 55.6 %copy-start.12 = (bf16[128,896]{1,0:T(8,128)(2,1)}, bf16[128,896]{1,0:T(8,128)(2,1)S(1)}, u32[]{:S(2)}) copy-start(bf16[128,896]{1,0:T(8,128)(2,1)S(1)} %collective-permute-done.refs_7_.refs_4_) | copy-start | bytes 688132
  304.2 6.0 %collective-permute-start.12 = (bf16[128,896]{1,0:T(8,128)(2,1)S(1)}, bf16[128,896]{1,0:T(8,128)(2,1)S(1)}, u32[]{:S(2)}, u32[]{:S(2)}) collective-permute-start(bf16[128,896]{1,0:T(8,128)(2,1)S(1)} %collective-permute-done.11.refs_8_), channel_id=1, source_target_pairs={{0,1},{1,0},{2,3},{3,2},{4,5},{5,4},{6,7},{7,6},{8,9},{9,8},{10,11... | collective-permute-start | bytes 688136 | tf_op jit(solution)/shard_map/ppermute | solution.py:647
  310.2 30.4 %copy-start.16 = (bf16[128,896]{1,0:T(8,128)(2,1)}, bf16[128,896]{1,0:T(8,128)(2,1)S(1)}, u32[]{:S(2)}) copy-start(bf16[128,896]{1,0:T(8,128)(2,1)S(1)} %collective-permute-done.12.refs_9_) | copy-start | bytes 688132
  310.2 6.0 %collective-permute-start.15 = (bf16[128,896]{1,0:T(8,128)(2,1)S(1)}, bf16[128,896]{1,0:T(8,128)(2,1)S(1)}, u32[]{:S(2)}, u32[]{:S(2)}) collective-permute-start(bf16[128,896]{1,0:T(8,128)(2,1)S(1)} %collective-permute-done.13.refs_10_), channel_id=1, source_target_pairs={{0,2},{1,3},{2,0},{3,1},{4,6},{5,7},{6,4},{7,5},{8,10},{9,11},{10,... | collective-permute-start | bytes 688136 | tf_op jit(solution)/shard_map/ppermute | solution.py:647
  316.2 13.9 %copy-start.18 = (bf16[128,896]{1,0:T(8,128)(2,1)}, bf16[128,896]{1,0:T(8,128)(2,1)S(1)}, u32[]{:S(2)}) copy-start(bf16[128,896]{1,0:T(8,128)(2,1)S(1)} %collective-permute-done.15.refs_12_) | copy-start | bytes 688132
  316.2 6.1 %collective-permute-start.14 = (bf16[128,896]{1,0:T(8,128)(2,1)S(1)}, bf16[128,896]{1,0:T(8,128)(2,1)}, u32[]{:S(2)}, u32[]{:S(2)}) collective-permute-start(bf16[128,896]{1,0:T(8,128)(2,1)S(1)} %collective-permute-done.13.refs_10_), channel_id=1, source_target_pairs={{0,1},{1,0},{2,3},{3,2},{4,5},{5,4},{6,7},{7,6},{8,9},{9,8},{10,11... | collective-permute-start | bytes 688136 | tf_op jit(solution)/shard_map/ppermute | solution.py:647
  322.4 6.0 %collective-permute-start.5 = (bf16[128,896]{1,0:T(8,128)(2,1)S(1)}, bf16[128,896]{1,0:T(8,128)(2,1)S(1)}, u32[]{:S(2)}, u32[]{:S(2)}) collective-permute-start(bf16[128,896]{1,0:T(8,128)(2,1)S(1)} %collective-permute-done.3.refs_10_.refs_7_), channel_id=1, source_target_pairs={{0,2},{1,3},{2,0},{3,1},{4,6},{5,7},{6,4},{7,5},{8,10},{9,11},{10,... | collective-permute-start | bytes 688136 | tf_op jit(solution)/shard_map/ppermute | solution.py:647
  328.4 31.4 %copy-start.14 = (bf16[128,896]{1,0:T(8,128)(2,1)}, bf16[128,896]{1,0:T(8,128)(2,1)S(1)}, u32[]{:S(2)}) copy-start(bf16[128,896]{1,0:T(8,128)(2,1)S(1)} %collective-permute-done.5.refs_12_.refs_9_) | copy-start | bytes 688132
  328.4 8.5 %collective-permute-start.16 = (bf16[128,896]{1,0:T(8,128)(2,1)S(1)}, bf16[128,896]{1,0:T(8,128)(2,1)S(1)}, u32[]{:S(2)}, u32[]{:S(2)}) collective-permute-start(bf16[128,896]{1,0:T(8,128)(2,1)S(1)} %collective-permute-done.15.refs_12_), channel_id=1, source_target_pairs={{0,1},{1,0},{2,3},{3,2},{4,5},{5,4},{6,7},{7,6},{8,9},{9,8},{10,11... | collective-permute-start | bytes 688136 | tf_op jit(solution)/shard_map/ppermute | solution.py:647
  336.9 23.0 %collective-permute-start.4 = (bf16[128,896]{1,0:T(8,128)(2,1)S(1)}, bf16[128,896]{1,0:T(8,128)(2,1)S(1)}, u32[]{:S(2)}, u32[]{:S(2)}) collective-permute-start(bf16[128,896]{1,0:T(8,128)(2,1)S(1)} %collective-permute-done.3.refs_10_.refs_7_), channel_id=1, source_target_pairs={{0,1},{1,0},{2,3},{3,2},{4,5},{5,4},{6,7},{7,6},{8,9},{9,8},{10,11... | collective-permute-start | bytes 688136 | tf_op jit(solution)/shard_map/ppermute | solution.py:647
  338.6 21.2 %collective-permute-start.2 = (bf16[128,896]{1,0:T(8,128)(2,1)S(1)}, bf16[128,896]{1,0:T(8,128)(2,1)S(1)}, u32[]{:S(2)}, u32[]{:S(2)}) collective-permute-start(bf16[128,896]{1,0:T(8,128)(2,1)S(1)} %collective-permute-done.1.refs_8_.refs_5_), channel_id=1, source_target_pairs={{0,1},{1,0},{2,3},{3,2},{4,5},{5,4},{6,7},{7,6},{8,9},{9,8},{10,11... | collective-permute-start | bytes 688136 | tf_op jit(solution)/shard_map/ppermute | solution.py:647
  338.9 21.0 %collective-permute-start.6 = (bf16[128,896]{1,0:T(8,128)(2,1)S(1)}, bf16[128,896]{1,0:T(8,128)(2,1)}, u32[]{:S(2)}, u32[]{:S(2)}) collective-permute-start(bf16[128,896]{1,0:T(8,128)(2,1)S(1)} %collective-permute-done.5.refs_12_.refs_9_), channel_id=1, source_target_pairs={{0,1},{1,0},{2,3},{3,2},{4,5},{5,4},{6,7},{7,6},{8,9},{9,8},{10,11... | collective-permute-start | bytes 688136 | tf_op jit(solution)/shard_map/ppermute | solution.py:647
  369.4 43.6 %collective-permute-start.30 = (bf16[224,32,128]{2,1,0:T(8,128)(2,1)}, bf16[224,32,128]{2,1,0:T(8,128)(2,1)}, u32[]{:S(2)}, u32[]{:S(2)}) collective-permute-start(bf16[224,32,128]{2,1,0:T(8,128)(2,1)} %get-tuple-element.55), channel_id=1, source_target_pairs={{0,8},{8,0},{16,24},{24,16},{1,9},{9,1},{17,25},{25,17},{2,10},{10... | collective-permute-start | bytes 5505032 | tf_op jit(solution)/shard_map/ppermute | solution.py:673
  393.6 22.6 %collective-permute-start.27 = (bf16[224,32,128]{2,1,0:T(8,128)(2,1)}, bf16[224,32,128]{2,1,0:T(8,128)(2,1)}, u32[]{:S(2)}, u32[]{:S(2)}) collective-permute-start(bf16[224,32,128]{2,1,0:T(8,128)(2,1)} %get-tuple-element.50), channel_id=1, source_target_pairs={{0,8},{8,0},{16,24},{24,16},{1,9},{9,1},{17,25},{25,17},{2,10},{10... | collective-permute-start | bytes 5505032 | tf_op jit(solution)/shard_map/ppermute | solution.py:673
  403.8 23.5 %collective-permute-start.23 = (bf16[4,128,896]{2,1,0:T(8,128)(2,1)}, bf16[4,128,896]{2,1,0:T(8,128)(2,1)S(1)}, u32[]{:S(2)}, u32[]{:S(2)}) collective-permute-start(bf16[4,128,896]{2,1,0:T(8,128)(2,1)} %get-tuple-element.45), channel_id=1, source_target_pairs={{0,1},{1,0},{2,3},{3,2},{4,5},{5,4},{6,7},{7,6},{8,9},{9,8},{10,11... | collective-permute-start | bytes 2752520 | tf_op jit(solution)/shard_map/ppermute | solution.py:707
  411.2 34.9 %collective-permute-start.20 = (bf16[4,128,896]{2,1,0:T(8,128)(2,1)}, bf16[4,128,896]{2,1,0:T(8,128)(2,1)S(1)}, u32[]{:S(2)}, u32[]{:S(2)}) collective-permute-start(bf16[4,128,896]{2,1,0:T(8,128)(2,1)} %get-tuple-element.41), channel_id=1, source_target_pairs={{0,1},{1,0},{2,3},{3,2},{4,5},{5,4},{6,7},{7,6},{8,9},{9,8},{10,11... | collective-permute-start | bytes 2752520 | tf_op jit(solution)/shard_map/ppermute | solution.py:707
  413.0 79.7 %collective-permute-start.29 = (bf16[224,32,128]{2,1,0:T(8,128)(2,1)}, bf16[224,32,128]{2,1,0:T(8,128)(2,1)}, u32[]{:S(2)}, u32[]{:S(2)}) collective-permute-start(bf16[224,32,128]{2,1,0:T(8,128)(2,1)} %get-tuple-element.53), channel_id=1, source_target_pairs={{0,8},{8,0},{16,24},{24,16},{1,9},{9,1},{17,25},{25,17},{2,10},{10... | collective-permute-start | bytes 5505032 | tf_op jit(solution)/shard_map/ppermute | solution.py:673
  413.0 92.3 %collective-permute-start.26 = (bf16[224,32,128]{2,1,0:T(8,128)(2,1)}, bf16[224,32,128]{2,1,0:T(8,128)(2,1)S(1)}, u32[]{:S(2)}, u32[]{:S(2)}) collective-permute-start(bf16[224,32,128]{2,1,0:T(8,128)(2,1)} %get-tuple-element.48), channel_id=1, source_target_pairs={{0,8},{8,0},{16,24},{24,16},{1,9},{9,1},{17,25},{25,17},{2,10},{10... | collective-permute-start | bytes 5505032 | tf_op jit(solution)/shard_map/ppermute | solution.py:673
  416.2 76.5 %collective-permute-start.31 = (bf16[224,32,128]{2,1,0:T(8,128)(2,1)S(1)}, bf16[224,32,128]{2,1,0:T(8,128)(2,1)S(1)}, u32[]{:S(2)}, u32[]{:S(2)}) collective-permute-start(bf16[224,32,128]{2,1,0:T(8,128)(2,1)S(1)} %add_convert_fusion), channel_id=1, source_target_pairs={{0,16},{8,24},{16,0},{24,8},{1,17},{9,25},{17,1},{25,9},{2,18},{10... | collective-permute-start | bytes 5505032 | tf_op jit(solution)/shard_map/ppermute | solution.py:678
  417.7 11.1 %copy-start.4 = (bf16[4,128,896]{2,1,0:T(8,128)(2,1)S(1)}, bf16[4,128,896]{2,1,0:T(8,128)(2,1)}, u32[]{:S(2)}) copy-start(bf16[4,128,896]{2,1,0:T(8,128)(2,1)} %get-tuple-element.44) | copy-start | bytes 2752516
  417.7 28.6 %copy-start.5 = (bf16[4,128,896]{2,1,0:T(8,128)(2,1)S(1)}, bf16[4,128,896]{2,1,0:T(8,128)(2,1)}, u32[]{:S(2)}) copy-start(bf16[4,128,896]{2,1,0:T(8,128)(2,1)} %get-tuple-element.40) | copy-start | bytes 2752516
  427.3 78.0 %collective-permute-start.28 = (bf16[224,32,128]{2,1,0:T(8,128)(2,1)}, bf16[224,32,128]{2,1,0:T(8,128)(2,1)}, u32[]{:S(2)}, u32[]{:S(2)}) collective-permute-start(bf16[224,32,128]{2,1,0:T(8,128)(2,1)} %add_convert_fusion.1), channel_id=1, source_target_pairs={{0,16},{8,24},{16,0},{24,8},{1,17},{9,25},{17,1},{25,9},{2,18},{10... | collective-permute-start | bytes 5505032 | tf_op jit(solution)/shard_map/ppermute | solution.py:678
  446.1 11.6 %collective-permute-start.24 = (bf16[2,128,896]{2,1,0:T(8,128)(2,1)S(1)}, bf16[2,128,896]{2,1,0:T(8,128)(2,1)S(1)}, u32[]{:S(2)}, u32[]{:S(2)}) collective-permute-start(bf16[2,128,896]{2,1,0:T(8,128)(2,1)S(1)} %add_convert_fusion.2), channel_id=1, source_target_pairs={{0,2},{1,3},{2,0},{3,1},{4,6},{5,7},{6,4},{7,5},{8,10},{9,11},{10,... | collective-permute-start | bytes 1376264 | tf_op jit(solution)/shard_map/ppermute | solution.py:707
  457.7 10.8 %collective-permute-start.21 = (bf16[2,128,896]{2,1,0:T(8,128)(2,1)S(1)}, bf16[2,128,896]{2,1,0:T(8,128)(2,1)S(1)}, u32[]{:S(2)}, u32[]{:S(2)}) collective-permute-start(bf16[2,128,896]{2,1,0:T(8,128)(2,1)S(1)} %add_convert_fusion.3), channel_id=1, source_target_pairs={{0,2},{1,3},{2,0},{3,1},{4,6},{5,7},{6,4},{7,5},{8,10},{9,11},{10,... | collective-permute-start | bytes 1376264 | tf_op jit(solution)/shard_map/ppermute | solution.py:707
  468.4 10.9 %collective-permute-start.25 = (bf16[1,128,896]{2,1,0:T(8,128)(2,1)S(1)}, bf16[1,128,896]{2,1,0:T(8,128)(2,1)S(1)}, u32[]{:S(2)}, u32[]{:S(2)}) collective-permute-start(bf16[1,128,896]{2,1,0:T(8,128)(2,1)S(1)} %add_convert_fusion.5), channel_id=1, source_target_pairs={{0,4},{1,5},{2,6},{3,7},{4,0},{5,1},{6,2},{7,3},{8,12},{9,13},{10,... | collective-permute-start | bytes 688136 | tf_op jit(solution)/shard_map/ppermute | solution.py:707
  479.3 12.5 %collective-permute-start.22 = (bf16[1,128,896]{2,1,0:T(8,128)(2,1)S(1)}, bf16[1,128,896]{2,1,0:T(8,128)(2,1)S(1)}, u32[]{:S(2)}, u32[]{:S(2)}) collective-permute-start(bf16[1,128,896]{2,1,0:T(8,128)(2,1)S(1)} %add_convert_fusion.7), channel_id=1, source_target_pairs={{0,4},{1,5},{2,6},{3,7},{4,0},{5,1},{6,2},{7,3},{8,12},{9,13},{10,... | collective-permute-start | bytes 688136 | tf_op jit(solution)/shard_map/ppermute | solution.py:707
  (8 other events, 21.7 us)

commit v6 on v5

--- a/solution.py
+++ b/solution.py
@@ -16,6 +16,7 @@
 CHUNK = 28
 ADAM_UNROLL = 8
 ADAM_PARTS = 4
+FINISH_PARTS = 2
 
 F32 = jnp.float32
 BF16 = jnp.bfloat16
@@ -549,6 +550,107 @@
     )(*tables, *grads, *moments, *arrived)
 
 
+def adam_ahead(tables, grads, moments):
+    slots, rows, block = moments[0].shape
+    n_grads = len(grads)
+
+    def kernel(home_ref, kind_ref, *refs):
+        grad_refs = refs[:n_grads]
+        moment_refs = refs[n_grads : n_grads + 2]
+        outs = refs[n_grads + 2 :]
+        unroll = math.gcd(slots, ADAM_UNROLL)
+
+        def trip(i, carry):
+            for u in range(unroll):
+                g = i * unroll + u
+                own = home_ref[g]
+                stays = kind_ref[g] == 1
+                total = grad_refs[0][g].astype(F32)
+                for ref in grad_refs[1:]:
+                    total = total + ref[g].astype(F32)
+                for k, (keep, term) in enumerate(((0.9, 0.1 * total), (0.95, 0.05 * total * total))):
+                    mine = moment_refs[k][own]
+                    outs[k][g] = keep * lax.select(stays, mine, jnp.zeros_like(mine)) + term
+            return carry
+
+        lax.fori_loop(0, slots // unroll, trip, 0)
+
+    vmem = pl.BlockSpec(memory_space=pltpu.VMEM)
+    return pl.pallas_call(
+        kernel,
+        out_shape=[jax.ShapeDtypeStruct(moments[0].shape, F32)] * 2,
+        in_specs=[SMEM] * 2 + [vmem] * (n_grads + 2),
+        out_specs=[vmem] * 2,
+        compiler_params=pltpu.CompilerParams(vmem_limit_bytes=VMEM_LIMIT),
+        cost_estimate=cost(10 * slots * rows * block, 22 * slots * rows * block),
+        name="ahead",
+    )(*tables, *grads, *moments)
+
+
+def adam_finish(tables, ahead, arrived):
+    slots, rows, block = ahead[0].shape
+    parts = math.gcd(slots, FINISH_PARTS)
+    some = slots // parts
+
+    def kernel(came_ref, kind_ref, first_hbm, second_hbm, arrived_hbm, out_hbm, ahead_v, arrived_v, out_v, sem, more, out_sem):
+        copy = pltpu.make_async_copy(arrived_hbm, arrived_v, more)
+        copy.start()
+        loads = []
+        outs = []
+        for q in range(parts):
+            at = pl.ds(q * some, some)
+            loads.append(
+                [
+                    pltpu.make_async_copy(hbm.at[at], ahead_v.at[k, at], sem.at[q, k])
+                    for k, hbm in enumerate((first_hbm, second_hbm))
+                ]
+            )
+            outs.append(pltpu.make_async_copy(out_v.at[at], out_hbm.at[at], out_sem.at[q]))
+        for pair in loads:
+            for load in pair:
+                load.start()
+        copy.wait()
+        unroll = math.gcd(some, 2 * ADAM_UNROLL)
+        for q in range(parts):
+            for load in loads[q]:
+                load.wait()
+
+            def trip(i, carry, q=q):
+                for u in range(unroll):
+                    g = q * some + i * unroll + u
+                    at = came_ref[g]
+                    comes = kind_ref[g] == 2
+                    sums = []
+                    for k, keep in enumerate((0.9, 0.95)):
+                        theirs = arrived_v[at, k].astype(F32)
+                        sums.append(ahead_v[k, g] + keep * lax.select(comes, theirs, jnp.zeros_like(theirs)))
+                    out_v[g] = sums[0] / (jnp.sqrt(sums[1]) + 1.0)
+                return carry
+
+            lax.fori_loop(0, some // unroll, trip, 0)
+            outs[q].start()
+        for out in outs:
+            out.wait()
+
+    return pl.pallas_call(
+        kernel,
+        out_shape=jax.ShapeDtypeStruct(ahead[0].shape, F32),
+        in_specs=[SMEM] * 2 + [ANY] * 3,
+        out_specs=ANY,
+        scratch_shapes=[
+            pltpu.VMEM((2, slots, rows, block), F32),
+            pltpu.VMEM(arrived.shape, BF16),
+            pltpu.VMEM((slots, rows, block), F32),
+            pltpu.SemaphoreType.DMA((parts, 2)),
+            pltpu.SemaphoreType.DMA,
+            pltpu.SemaphoreType.DMA((parts,)),
+        ],
+        compiler_params=pltpu.CompilerParams(vmem_limit_bytes=VMEM_LIMIT),
+        cost_estimate=cost(10 * slots * rows * block, 18 * slots * rows * block),
+        name="finish",
+    )(*tables, *ahead, arrived)
+
+
 def layer(
     activations,
     cotangent,
@@ -709,7 +811,8 @@
     out_sum, in_sum = sums
 
     up_step = adam_step((home, came, kind), up_terms, ups, ups_in)
-    down_step = adam_step((home, came, kind), down_terms, downs, downs_in)
+    ahead = adam_ahead((home, kind), down_terms, downs)
+    down_step = adam_finish((came, kind), ahead, downs_in[0])
     return (out_sum, in_sum, up_step, down_step)
 
 

time: 519 us -> 525 us (1.012)
  Pallas kernels: 112 us -> 118 us
    pallas_call x0 -> x2, Pallas kernels: none -> 17.3 us  [the longest x1 9.21 us: adam_ahead(): pl.pallas_call(kernel, out_shape=[jax.ShapeDtypeStruct(moments[0].shape,...]
    pallas_call x2 -> x1, Pallas kernels: 22.5 us -> 11.2 us  [adam_step(): pl.pallas_call(kernel, out_shape=jax.ShapeDtypeStruct(moments[0].shape, F...]
  transfers between devices with their start and end apart: 36 -> 36, of which waited for: 18 -> 18; matrix products, arithmetic and copies ran while one was open for 2% -> 2% of each run, Pallas kernels for 19% -> 20%
where the time goes in v6:
time: 525 us; the launch traced here: 524 us
  waiting for transfers between devices  327 us (62%)
  Pallas kernels  118 us (22%)
  starting transfers between devices  57 us (11%)
  other arithmetic  15 us (3%)
  local copies, waits for them, and re-layouts  6.48 us (1%)
    ppermute x14, waiting for transfers between devices, gather(): held[m ^ bit] = lax.ppermute(held[m], 'tensor', far_pairs(bit))  135 us
    all_to_all x4, waiting for transfers between devices, exchange(): lax.all_to_all(shaped, 'tensor', split_axis=0, concat_axis=0, tiled=True)  88.5 us
    ppermute x6, waiting for transfers between devices, layer(): held.append(lax.ppermute(send, 'tensor', far_pairs(bit)))  65.1 us
    ppermute x2, waiting for transfers between devices, spread(): mine = lax.ppermute(own, 'dp', x_pairs(j))  37.9 us
    ppermute x14, starting transfers between devices, gather(): held[m ^ bit] = lax.ppermute(held[m], 'tensor', far_pairs(bit))  24.2 us
    all_to_all x4, starting transfers between devices, exchange(): lax.all_to_all(shaped, 'tensor', split_axis=0, concat_axis=0, tiled=True)  21 us
    pallas_call x1, Pallas kernels, forward_products(): pl.pallas_call(functools.partial(forward_kernel, n_feat, n_dp, row_blocks...  19.1 us
    pallas_call x2, Pallas kernels, output_products(): pl.pallas_call(functools.partial(output_kernel, pieces, turned, bits), ou...  16.7 us
  transfers between devices with their start and end apart: 36, of which 18 were waited for; matrix products, arithmetic and copies ran while one was open for 2% of the time, Pallas kernels for 20%

profile of v6, /device:TPU:0, one launch (start us, length us, event | category | flops | bytes accessed | tf_op | source)
XLA Modules:
  0.0 523.9 jit_solution(9721994724217300515)
XLA Ops:
  3.7 1.9 gather_fusion
  10.8 3.8 pack_weight.2
  14.6 7.3 %all-to-all-start = ((bf16[8,28,32,128]{3,2,1,0:T(8,128)(2,1)}), bf16[8,28,32,128]{3,2,1,0:T(8,128)(2,1)S(1)}, u32[]{:S(2)}, u32[]{:S(2)}) async-start(bf16[8,28,32,128]{3,2,1,0:T(8,128)(2,1)} %bitcast.28), calls=%async_computation | async-start | bytes 3670016 | tf_op jit(solution)/shard_map/all_to_all | solution.py:711
  21.9 3.8 pack_weight.3
  25.8 38.8 %all-to-all-done = bf16[8,28,32,128]{3,2,1,0:T(8,128)(2,1)S(1)} async-done(((bf16[8,28,32,128]{3,2,1,0:T(8,128)(2,1)}), bf16[8,28,32,128]{3,2,1,0:T(8,128)(2,1)S(1)}, u32[]{:S(2)}, u32[]{:S(2)}) %all-to-all-start) | async-done | bytes 1835040 | tf_op jit(solution)/shard_map/all_to_all | solution.py:711
  64.6 4.3 all-to-all-start.1
  68.9 6.4 %pack_moments.3 = bf16[224,2,32,128]{3,2,1,0:T(8,128)(2,1)} custom-call(s32[224]{0:T(256)} %reshape.141.send_ref, f32[224,32,128]{2,1,0:T(8,128)} %refs_0_.9, f32[224,32,128]{2,1,0:T(8,128)} %refs_1_.3), custom_call_target="tpu_custom_call" | custom-call | bytes 11010048 | tf_op jit(solution)/shard_map/pack_moments/pallas_call | solution.py:86
  75.3 35.8 %all-to-all-done.1 = bf16[8,28,32,128]{3,2,1,0:T(8,128)(2,1)} async-done(((bf16[8,28,32,128]{3,2,1,0:T(8,128)(2,1)}), bf16[8,28,32,128]{3,2,1,0:T(8,128)(2,1)}, u32[]{:S(2)}, u32[]{:S(2)}) %all-to-all-start.1) | async-done | bytes 1835040 | tf_op jit(solution)/shard_map/all_to_all | solution.py:711
  111.1 4.7 all-to-all-start.3
  117.9 1.8 collective-permute-start.11
  121.2 37.9 %collective-permute-done.18.refs_17_ = bf16[224,32,128]{2,1,0:T(8,128)(2,1)} collective-permute-done((bf16[224,32,128]{2,1,0:T(8,128)(2,1)}, bf16[224,32,128]{2,1,0:T(8,128)(2,1)}, u32[]{:S(2)}, u32[]{:S(2)}) %collective-permute-start.18) | collective-permute-done | bytes 1835040 | tf_op jit(solution)/shard_map/ppermute | solution.py:727
  159.1 20.9 %collective-permute-done.11.refs_8_ = bf16[128,896]{1,0:T(8,128)(2,1)S(1)} collective-permute-done((bf16[128,896]{1,0:T(8,128)(2,1)S(1)}, bf16[128,896]{1,0:T(8,128)(2,1)S(1)}, u32[]{:S(2)}, u32[]{:S(2)}) %collective-permute-start.11) | collective-permute-done | bytes 229408 | tf_op jit(solution)/shard_map/ppermute | solution.py:749
  179.9 3.9 collective-permute-start.13
  183.8 6.4 %pack_moments.2 = bf16[224,2,32,128]{3,2,1,0:T(8,128)(2,1)} custom-call(s32[224]{0:T(256)} %reshape.141.send_ref, f32[224,32,128]{2,1,0:T(8,128)} %refs_3_.3, f32[224,32,128]{2,1,0:T(8,128)} %refs_4_.2), custom_call_target="tpu_custom_call" | custom-call | bytes 11010048 | tf_op jit(solution)/shard_map/pack_moments/pallas_call | solution.py:86
  190.2 13.8 %all-to-all-done.3 = bf16[8,28,2,32,128]{4,3,2,1,0:T(8,128)(2,1)} async-done(((bf16[8,28,2,32,128]{4,3,2,1,0:T(8,128)(2,1)}), bf16[8,28,2,32,128]{4,3,2,1,0:T(8,128)(2,1)}, u32[]{:S(2)}, u32[]{:S(2)}) %all-to-all-start.3) | async-done | bytes 3670048 | tf_op jit(solution)/shard_map/all_to_all | solution.py:711
  204.0 4.7 all-to-all-start.2
  208.7 2.9 collective-permute-start.3
  213.1 84.7 %collective-permute-done.3.refs_10_.refs_7_ = bf16[128,896]{1,0:T(8,128)(2,1)S(1)} collective-permute-done((bf16[128,896]{1,0:T(8,128)(2,1)S(1)}, bf16[128,896]{1,0:T(8,128)(2,1)S(1)}, u32[]{:S(2)}, u32[]{:S(2)}) %collective-permute-start.3) | collective-permute-done | bytes 229408 | tf_op jit(solution)/shard_map/ppermute | solution.py:749
  299.8 4.3 collective-permute-done.refs_7_.refs_4_
  304.1 1.7 collective-permute-start.12
  305.9 4.3 collective-permute-done.12.refs_9_
  311.2 4.9 collective-permute-done.15.refs_12_
  316.2 1.7 collective-permute-start.14
  317.9 4.4 collective-permute-done.14.refs_11_
  323.4 4.9 collective-permute-done.5.refs_12_.refs_9_
  328.3 1.7 collective-permute-start.16
  330.1 6.7 %collective-permute-done.16.refs_13_ = bf16[128,896]{1,0:T(8,128)(2,1)S(1)} collective-permute-done((bf16[128,896]{1,0:T(8,128)(2,1)S(1)}, bf16[128,896]{1,0:T(8,128)(2,1)S(1)}, u32[]{:S(2)}, u32[]{:S(2)}) %collective-permute-start.16) | collective-permute-done | bytes 229408 | tf_op jit(solution)/shard_map/ppermute | solution.py:749
  336.8 1.7 collective-permute-start.4
  338.8 1.7 collective-permute-start.6
  340.6 19.1 %forward_products.1 = (bf16[16,128,128]{2,1,0:T(8,128)(2,1)}, bf16[16,128,128]{2,1,0:T(8,128)(2,1)}, f32[16,128,128]{2,1,0:T(8,128)}, bf16[56,128,128]{2,1,0:T(8,128)(2,1)}, bf16[224,128,128]{2,1,0:T(8,128)(2,1)}) custom-call(s32[224]{0:T(256)} %refs_0_.8, s32[224]{0:T(256)} %and_select_fusion.1.refs_1_, s32[224]{0:T(256)} %get-tuple-element.35.refs_2_.home_ref, ...), custom_call_target="tpu_custom_call" | custom-call | flops 939524096 | bytes 44040192 | tf_op jit(solution)/shard_map/forward_products/pallas_call | solution.py:362
  360.5 8.8 %gradient_products.3 = (bf16[224,32,128]{2,1,0:T(8,128)(2,1)}, bf16[224,32,128]{2,1,0:T(8,128)(2,1)}, bf16[224,32,128]{2,1,0:T(8,128)(2,1)}, bf16[224,32,128]{2,1,0:T(8,128)(2,1)}) custom-call(s32[224]{0:T(256)} %refs_0_.8, s32[224]{0:T(256)} %and_select_fusion.1.refs_1_, s32[3]{0:T(128)} %pad_add_fusion.refs_5_.refs_2_, bf16[128,896]{1,0:T(8,128)(2,1)} %refs_3_.4, ...), custom_call_target="tpu_custom_call" | custom-call | flops 939524096 | bytes 11010048 | tf_op jit(solution)/shard_map/gradient_products/pallas_call | solution.py:420
  369.4 16.7 %back_products.1 = (bf16[16,128,128]{2,1,0:T(8,128)(2,1)}, bf16[224,128,128]{2,1,0:T(8,128)(2,1)}) custom-call(s32[224]{0:T(256)} %refs_0_.8, s32[224]{0:T(256)} %and_select_fusion.1.refs_1_, s32[224]{0:T(256)} %get-tuple-element.35.refs_2_.home_ref, s32[224]{0:T(256)} %get-tuple-element.36.refs_3_.came_ref, s32[224]{0:T(256)} %get-tuple-element.37.refs_4_.kind_ref, ...), custom_call_target="tpu_custom_call" | custom-call | flops 939524096 | bytes 44040192 | tf_op jit(solution)/shard_map/back_products/pallas_call | solution.py:393
  386.1 7.5 %gradient_products.2 = (bf16[224,32,128]{2,1,0:T(8,128)(2,1)}, bf16[224,32,128]{2,1,0:T(8,128)(2,1)}, bf16[224,32,128]{2,1,0:T(8,128)(2,1)}, bf16[224,32,128]{2,1,0:T(8,128)(2,1)}) custom-call(s32[224]{0:T(256)} %refs_0_.8, s32[224]{0:T(256)} %and_select_fusion.1.refs_1_, s32[3]{0:T(128)} %pad_add_fusion.refs_5_.refs_2_, ...), custom_call_target="tpu_custom_call" | custom-call | flops 939524096 | bytes 11010048 | tf_op jit(solution)/shard_map/gradient_products/pallas_call | solution.py:420
  394.1 9.7 %output_products.3 = (bf16[4,128,896]{2,1,0:T(8,128)(2,1)}, bf16[4,128,896]{2,1,0:T(8,128)(2,1)}) custom-call(s32[224]{0:T(256)} %refs_0_.8, s32[224]{0:T(256)} %and_select_fusion.1.refs_1_, s32[3]{0:T(128)} %pad_add_fusion.refs_5_.refs_2_, bf16[224,128,128]{2,1,0:T(8,128)(2,1)} %get-tuple-element.44.refs_3_, bf16[16,128,128]{2,1,0:T(8,128)(2,1)} %get-tuple-element.45.refs_4_), custom_call_target="tpu_custom_call" | custom-call | flops 939524096 | bytes 14680064 | tf_op jit(solution)/shard_map/output_products/pallas_call | solution.py:439
  404.2 7.0 %output_products.2 = (bf16[4,128,896]{2,1,0:T(8,128)(2,1)}, bf16[4,128,896]{2,1,0:T(8,128)(2,1)}) custom-call(s32[224]{0:T(256)} %refs_0_.8, s32[224]{0:T(256)} %and_select_fusion.1.refs_1_, s32[3]{0:T(128)} %pad_add_fusion.refs_5_.refs_2_, bf16[224,128,128]{2,1,0:T(8,128)(2,1)} %get-tuple-element.40.refs_3_, bf16[16,128,128]{2,1,0:T(8,128)(2,1)} %get-tuple-element.41.refs_4_), custom_call_target="tpu_custom_call" | custom-call | flops 939524096 | bytes 14680064 | tf_op jit(solution)/shard_map/output_products/pallas_call | solution.py:439
  411.2 1.8 collective-permute-start.20
  413.6 2.7 add_convert_fusion
  417.8 3.3 add_convert_fusion.1
  421.2 6.2 %collective-permute-done.23 = bf16[4,128,896]{2,1,0:T(8,128)(2,1)S(1)} collective-permute-done((bf16[4,128,896]{2,1,0:T(8,128)(2,1)}, bf16[4,128,896]{2,1,0:T(8,128)(2,1)S(1)}, u32[]{:S(2)}, u32[]{:S(2)}) %collective-permute-start.23) | collective-permute-done | bytes 917536 | tf_op jit(solution)/shard_map/ppermute | solution.py:809
  429.0 17.1 %collective-permute-done.20 = bf16[4,128,896]{2,1,0:T(8,128)(2,1)S(1)} collective-permute-done((bf16[4,128,896]{2,1,0:T(8,128)(2,1)}, bf16[4,128,896]{2,1,0:T(8,128)(2,1)S(1)}, u32[]{:S(2)}, u32[]{:S(2)}) %collective-permute-start.20) | collective-permute-done | bytes 917536 | tf_op jit(solution)/shard_map/ppermute | solution.py:809
  446.4 11.2 %collective-permute-done.24 = bf16[2,128,896]{2,1,0:T(8,128)(2,1)S(1)} collective-permute-done((bf16[2,128,896]{2,1,0:T(8,128)(2,1)S(1)}, bf16[2,128,896]{2,1,0:T(8,128)(2,1)S(1)}, u32[]{:S(2)}, u32[]{:S(2)}) %collective-permute-start.24) | collective-permute-done | bytes 458784 | tf_op jit(solution)/shard_map/ppermute | solution.py:809
  458.0 10.4 %collective-permute-done.21 = bf16[2,128,896]{2,1,0:T(8,128)(2,1)S(1)} collective-permute-done((bf16[2,128,896]{2,1,0:T(8,128)(2,1)S(1)}, bf16[2,128,896]{2,1,0:T(8,128)(2,1)S(1)}, u32[]{:S(2)}, u32[]{:S(2)}) %collective-permute-start.21) | collective-permute-done | bytes 458784 | tf_op jit(solution)/shard_map/ppermute | solution.py:809
  468.4 2.3 collective-permute-start.25
  470.8 8.5 %collective-permute-done.25 = bf16[1,128,896]{2,1,0:T(8,128)(2,1)S(1)} collective-permute-done((bf16[1,128,896]{2,1,0:T(8,128)(2,1)S(1)}, bf16[1,128,896]{2,1,0:T(8,128)(2,1)S(1)}, u32[]{:S(2)}, u32[]{:S(2)}) %collective-permute-start.25) | collective-permute-done | bytes 229408 | tf_op jit(solution)/shard_map/ppermute | solution.py:809
  480.1 11.7 %collective-permute-done.22 = bf16[1,128,896]{2,1,0:T(8,128)(2,1)S(1)} collective-permute-done((bf16[1,128,896]{2,1,0:T(8,128)(2,1)S(1)}, bf16[1,128,896]{2,1,0:T(8,128)(2,1)S(1)}, u32[]{:S(2)}, u32[]{:S(2)}) %collective-permute-start.22) | collective-permute-done | bytes 229408 | tf_op jit(solution)/shard_map/ppermute | solution.py:809
  493.8 9.2 %ahead.1 = (f32[224,32,128]{2,1,0:T(8,128)}, f32[224,32,128]{2,1,0:T(8,128)}) custom-call(s32[224]{0:T(256)} %get-tuple-element.35.refs_2_.home_ref, s32[224]{0:T(256)} %get-tuple-element.37.refs_4_.kind_ref, bf16[224,32,128]{2,1,0:T(8,128)(2,1)} %get-tuple-element.54.refs_0_, bf16[224,32,128]{2,1,0:T(8,128)(2,1)} %collective-permute-done.29.refs_1_, ...), custom_call_target="tpu_custom_call" | custom-call | flops 9175040 | bytes 20185088 | tf_op jit(solution)/shard_map/ahead/pallas_call | solution.py:579
  503.0 8.1 %finish.1 = f32[224,32,128]{2,1,0:T(8,128)} custom-call(s32[224]{0:T(256)} %get-tuple-element.36.refs_3_.came_ref, s32[224]{0:T(256)} %get-tuple-element.37.refs_4_.kind_ref, f32[224,32,128]{2,1,0:T(8,128)} %get-tuple-element.58.first_hbm, f32[224,32,128]{2,1,0:T(8,128)} %get-tuple-element.59.second_hbm, bf16[224,2,32,128]{3,2,1,0:T(8,128)(2,1)} %bitcast.17.arrived_hbm), custom_call_target="tpu_custom_call" | custom-call | flops 9175040 | bytes 16515072 | tf_op jit(solution)/shard_map/finish/pallas_call | solution.py:635
  512.5 11.2 %adam_step.1 = f32[224,32,128]{2,1,0:T(8,128)} custom-call(s32[224]{0:T(256)} %get-tuple-element.35.refs_2_.home_ref, s32[224]{0:T(256)} %get-tuple-element.36.refs_3_.came_ref, s32[224]{0:T(256)} %get-tuple-element.37.refs_4_.kind_ref, bf16[224,32,128]{2,1,0:T(8,128)(2,1)} %get-tuple-element.49.refs_0_, bf16[224,32,128]{2,1,0:T(8,128)(2,1)} %copy-done.1, ...), custom_call_target="tpu_custom_call" | custom-call | flops 13762560 | bytes 15597568 | tf_op jit(solution)/shard_map/adam_step/pallas_call | solution.py:532
  (113 shorter events, 28.3 us)
Async XLA Ops:
  14.6 49.9 %all-to-all-start = ((bf16[8,28,32,128]{3,2,1,0:T(8,128)(2,1)}), bf16[8,28,32,128]{3,2,1,0:T(8,128)(2,1)S(1)}, u32[]{:S(2)}, u32[]{:S(2)}) async-start(bf16[8,28,32,128]{3,2,1,0:T(8,128)(2,1)} %bitcast.28), calls=%async_computation | async-start | bytes 3670016 | tf_op jit(solution)/shard_map/all_to_all | solution.py:711
  64.6 234.7 %copy-start = (bf16[8,28,32,128]{3,2,1,0:T(8,128)(2,1)}, bf16[8,28,32,128]{3,2,1,0:T(8,128)(2,1)S(1)}, u32[]{:S(2)}) copy-start(bf16[8,28,32,128]{3,2,1,0:T(8,128)(2,1)S(1)} %all-to-all-done) | copy-start | bytes 5505028
  64.6 46.6 %all-to-all-start.1 = ((bf16[8,28,32,128]{3,2,1,0:T(8,128)(2,1)}), bf16[8,28,32,128]{3,2,1,0:T(8,128)(2,1)}, u32[]{:S(2)}, u32[]{:S(2)}) async-start(bf16[8,28,32,128]{3,2,1,0:T(8,128)(2,1)} %bitcast.27), calls=%async_computation.1 | async-start | bytes 3670016 | tf_op jit(solution)/shard_map/all_to_all | solution.py:711
  111.1 92.9 %all-to-all-start.3 = ((bf16[8,28,2,32,128]{4,3,2,1,0:T(8,128)(2,1)}), bf16[8,28,2,32,128]{4,3,2,1,0:T(8,128)(2,1)}, u32[]{:S(2)}, u32[]{:S(2)}) async-start(bf16[8,28,2,32,128]{4,3,2,1,0:T(8,128)(2,1)} %bitcast.23), calls=%async_computation.3 | async-start | bytes 7340032 | tf_op jit(solution)/shard_map/all_to_all | solution.py:711
  115.8 43.3 %collective-permute-start.18 = (bf16[224,32,128]{2,1,0:T(8,128)(2,1)}, bf16[224,32,128]{2,1,0:T(8,128)(2,1)}, u32[]{:S(2)}, u32[]{:S(2)}) collective-permute-start(bf16[224,32,128]{2,1,0:T(8,128)(2,1)} %bitcast.11.refs_15_), channel_id=1, source_target_pairs={{0,16},{8,24},{16,0},{24,8},{1,17},{9,25},{17,1},{25,9},{2,18},{10... | collective-permute-start | bytes 5505032 | tf_op jit(solution)/shard_map/ppermute | solution.py:727
  117.4 182.0 %collective-permute-start.8 = (bf16[224,32,128]{2,1,0:T(8,128)(2,1)S(1)}, bf16[224,32,128]{2,1,0:T(8,128)(2,1)}, u32[]{:S(2)}, u32[]{:S(2)}) collective-permute-start(bf16[224,32,128]{2,1,0:T(8,128)(2,1)S(1)} %bitcast.24), channel_id=1, source_target_pairs={{0,16},{8,24},{16,0},{24,8},{1,17},{9,25},{17,1},{25,9},{2,18},{10... | collective-permute-start | bytes 5505032 | tf_op jit(solution)/shard_map/ppermute | solution.py:727
  117.9 62.0 %collective-permute-start.11 = (bf16[128,896]{1,0:T(8,128)(2,1)S(1)}, bf16[128,896]{1,0:T(8,128)(2,1)S(1)}, u32[]{:S(2)}, u32[]{:S(2)}) collective-permute-start(bf16[128,896]{1,0:T(8,128)(2,1)S(1)} %copy-done.6), channel_id=1, source_target_pairs={{0,2},{1,3},{2,0},{3,1},{4,6},{5,7},{6,4},{7,5},{8,10},{9,11},{10,... | collective-permute-start | bytes 688136 | tf_op jit(solution)/shard_map/ppermute | solution.py:749
  119.7 89.0 %collective-permute-start.10 = (bf16[128,896]{1,0:T(8,128)(2,1)S(1)}, bf16[128,896]{1,0:T(8,128)(2,1)S(1)}, u32[]{:S(2)}, u32[]{:S(2)}) collective-permute-start(bf16[128,896]{1,0:T(8,128)(2,1)S(1)} %copy-done.6), channel_id=1, source_target_pairs={{0,1},{1,0},{2,3},{3,2},{4,5},{5,4},{6,7},{7,6},{8,9},{9,8},{10,11... | collective-permute-start | bytes 688136 | tf_op jit(solution)/shard_map/ppermute | solution.py:749
  121.2 217.3 %collective-permute-start.17 = (bf16[224,32,128]{2,1,0:T(8,128)(2,1)}, bf16[224,32,128]{2,1,0:T(8,128)(2,1)}, u32[]{:S(2)}, u32[]{:S(2)}) collective-permute-start(bf16[224,32,128]{2,1,0:T(8,128)(2,1)} %bitcast.11.refs_15_), channel_id=1, source_target_pairs={{0,8},{8,0},{16,24},{24,16},{1,9},{9,1},{17,25},{25,17},{2,10},{10... | collective-permute-start | bytes 5505032 | tf_op jit(solution)/shard_map/ppermute | solution.py:728
  159.1 179.8 %collective-permute-start.19 = (bf16[224,32,128]{2,1,0:T(8,128)(2,1)}, bf16[224,32,128]{2,1,0:T(8,128)(2,1)}, u32[]{:S(2)}, u32[]{:S(2)}) collective-permute-start(bf16[224,32,128]{2,1,0:T(8,128)(2,1)} %collective-permute-done.18.refs_17_), channel_id=1, source_target_pairs={{0,8},{8,0},{16,24},{24,16},{1,9},{9,1},{17,25},{25,17},{2,10},{10... | collective-permute-start | bytes 5505032 | tf_op jit(solution)/shard_map/ppermute | solution.py:728
  179.9 124.2 %copy-start.8 = (bf16[128,896]{1,0:T(8,128)(2,1)}, bf16[128,896]{1,0:T(8,128)(2,1)S(1)}, u32[]{:S(2)}) copy-start(bf16[128,896]{1,0:T(8,128)(2,1)S(1)} %collective-permute-done.11.refs_8_) | copy-start | bytes 688132
  179.9 31.7 %collective-permute-start.13 = (bf16[128,896]{1,0:T(8,128)(2,1)S(1)}, bf16[128,896]{1,0:T(8,128)(2,1)S(1)}, u32[]{:S(2)}, u32[]{:S(2)}) collective-permute-start(bf16[128,896]{1,0:T(8,128)(2,1)S(1)} %copy-done.6), channel_id=1, source_target_pairs={{0,4},{1,5},{2,6},{3,7},{4,0},{5,1},{6,2},{7,3},{8,12},{9,13},{10,... | collective-permute-start | bytes 688136 | tf_op jit(solution)/shard_map/ppermute | solution.py:749
  204.0 307.1 %all-to-all-start.2 = ((bf16[8,28,2,32,128]{4,3,2,1,0:T(8,128)(2,1)}), bf16[8,28,2,32,128]{4,3,2,1,0:T(8,128)(2,1)}, u32[]{:S(2)}, u32[]{:S(2)}) async-start(bf16[8,28,2,32,128]{4,3,2,1,0:T(8,128)(2,1)} %bitcast.22), calls=%async_computation.2 | async-start | bytes 7340032 | tf_op jit(solution)/shard_map/all_to_all | solution.py:711
  208.7 131.9 %copy-start.10 = (bf16[128,896]{1,0:T(8,128)(2,1)}, bf16[128,896]{1,0:T(8,128)(2,1)S(1)}, u32[]{:S(2)}) copy-start(bf16[128,896]{1,0:T(8,128)(2,1)S(1)} %collective-permute-done.10.refs_7_) | copy-start | bytes 688132
  208.7 89.0 %collective-permute-start.3 = (bf16[128,896]{1,0:T(8,128)(2,1)S(1)}, bf16[128,896]{1,0:T(8,128)(2,1)S(1)}, u32[]{:S(2)}, u32[]{:S(2)}) collective-permute-start(bf16[128,896]{1,0:T(8,128)(2,1)S(1)} %copy-done.7), channel_id=1, source_target_pairs={{0,4},{1,5},{2,6},{3,7},{4,0},{5,1},{6,2},{7,3},{8,12},{9,13},{10,... | collective-permute-start | bytes 688136 | tf_op jit(solution)/shard_map/ppermute | solution.py:749
  211.6 129.0 %copy-start.13 = (bf16[128,896]{1,0:T(8,128)(2,1)}, bf16[128,896]{1,0:T(8,128)(2,1)S(1)}, u32[]{:S(2)}) copy-start(bf16[128,896]{1,0:T(8,128)(2,1)S(1)} %collective-permute-done.13.refs_10_) | copy-start | bytes 688132
  211.6 87.6 %collective-permute-start.1 = (bf16[128,896]{1,0:T(8,128)(2,1)S(1)}, bf16[128,896]{1,0:T(8,128)(2,1)S(1)}, u32[]{:S(2)}, u32[]{:S(2)}) collective-permute-start(bf16[128,896]{1,0:T(8,128)(2,1)S(1)} %copy-done.7), channel_id=1, source_target_pairs={{0,2},{1,3},{2,0},{3,1},{4,6},{5,7},{6,4},{7,5},{8,10},{9,11},{10,... | collective-permute-start | bytes 688136 | tf_op jit(solution)/shard_map/ppermute | solution.py:749
  297.8 61.9 %copy-start.9 = (bf16[128,896]{1,0:T(8,128)(2,1)}, bf16[128,896]{1,0:T(8,128)(2,1)S(1)}, u32[]{:S(2)}) copy-start(bf16[128,896]{1,0:T(8,128)(2,1)S(1)} %collective-permute-done.3.refs_10_.refs_7_) | copy-start | bytes 688132
  297.8 6.3 %collective-permute-start = (bf16[128,896]{1,0:T(8,128)(2,1)S(1)}, bf16[128,896]{1,0:T(8,128)(2,1)S(1)}, u32[]{:S(2)}, u32[]{:S(2)}) collective-permute-start(bf16[128,896]{1,0:T(8,128)(2,1)S(1)} %copy-done.7), channel_id=1, source_target_pairs={{0,1},{1,0},{2,3},{3,2},{4,5},{5,4},{6,7},{7,6},{8,9},{9,8},{10,11... | collective-permute-start | bytes 688136 | tf_op jit(solution)/shard_map/ppermute | solution.py:749
  299.2 60.5 %copy-start.11 = (bf16[128,896]{1,0:T(8,128)(2,1)}, bf16[128,896]{1,0:T(8,128)(2,1)S(1)}, u32[]{:S(2)}) copy-start(bf16[128,896]{1,0:T(8,128)(2,1)S(1)} %collective-permute-done.1.refs_8_.refs_5_) | copy-start | bytes 688132
  299.2 70.1 %collective-permute-start.7 = (bf16[224,32,128]{2,1,0:T(8,128)(2,1)S(1)}, bf16[224,32,128]{2,1,0:T(8,128)(2,1)}, u32[]{:S(2)}, u32[]{:S(2)}) collective-permute-start(bf16[224,32,128]{2,1,0:T(8,128)(2,1)S(1)} %bitcast.25), channel_id=1, source_target_pairs={{0,8},{8,0},{16,24},{24,16},{1,9},{9,1},{17,25},{25,17},{2,10},{10... | collective-permute-start | bytes 5505032 | tf_op jit(solution)/shard_map/ppermute | solution.py:728
  299.3 70.1 %collective-permute-start.9 = (bf16[224,32,128]{2,1,0:T(8,128)(2,1)}, bf16[224,32,128]{2,1,0:T(8,128)(2,1)}, u32[]{:S(2)}, u32[]{:S(2)}) collective-permute-start(bf16[224,32,128]{2,1,0:T(8,128)(2,1)} %collective-permute-done.8.refs_17_), channel_id=1, source_target_pairs={{0,8},{8,0},{16,24},{24,16},{1,9},{9,1},{17,25},{25,17},{2,10},{10... | collective-permute-start | bytes 5505032 | tf_op jit(solution)/shard_map/ppermute | solution.py:728
  304.1 55.6 %copy-start.12 = (bf16[128,896]{1,0:T(8,128)(2,1)}, bf16[128,896]{1,0:T(8,128)(2,1)S(1)}, u32[]{:S(2)}) copy-start(bf16[128,896]{1,0:T(8,128)(2,1)S(1)} %collective-permute-done.refs_7_.refs_4_) | copy-start | bytes 688132
  304.1 6.0 %collective-permute-start.12 = (bf16[128,896]{1,0:T(8,128)(2,1)S(1)}, bf16[128,896]{1,0:T(8,128)(2,1)S(1)}, u32[]{:S(2)}, u32[]{:S(2)}) collective-permute-start(bf16[128,896]{1,0:T(8,128)(2,1)S(1)} %collective-permute-done.11.refs_8_), channel_id=1, source_target_pairs={{0,1},{1,0},{2,3},{3,2},{4,5},{5,4},{6,7},{7,6},{8,9},{9,8},{10,11... | collective-permute-start | bytes 688136 | tf_op jit(solution)/shard_map/ppermute | solution.py:749
  310.1 30.4 %copy-start.16 = (bf16[128,896]{1,0:T(8,128)(2,1)}, bf16[128,896]{1,0:T(8,128)(2,1)S(1)}, u32[]{:S(2)}) copy-start(bf16[128,896]{1,0:T(8,128)(2,1)S(1)} %collective-permute-done.12.refs_9_) | copy-start | bytes 688132
  310.1 6.0 %collective-permute-start.15 = (bf16[128,896]{1,0:T(8,128)(2,1)S(1)}, bf16[128,896]{1,0:T(8,128)(2,1)S(1)}, u32[]{:S(2)}, u32[]{:S(2)}) collective-permute-start(bf16[128,896]{1,0:T(8,128)(2,1)S(1)} %collective-permute-done.13.refs_10_), channel_id=1, source_target_pairs={{0,2},{1,3},{2,0},{3,1},{4,6},{5,7},{6,4},{7,5},{8,10},{9,11},{10,... | collective-permute-start | bytes 688136 | tf_op jit(solution)/shard_map/ppermute | solution.py:749
  316.2 13.9 %copy-start.18 = (bf16[128,896]{1,0:T(8,128)(2,1)}, bf16[128,896]{1,0:T(8,128)(2,1)S(1)}, u32[]{:S(2)}) copy-start(bf16[128,896]{1,0:T(8,128)(2,1)S(1)} %collective-permute-done.15.refs_12_) | copy-start | bytes 688132
  316.2 6.1 %collective-permute-start.14 = (bf16[128,896]{1,0:T(8,128)(2,1)S(1)}, bf16[128,896]{1,0:T(8,128)(2,1)}, u32[]{:S(2)}, u32[]{:S(2)}) collective-permute-start(bf16[128,896]{1,0:T(8,128)(2,1)S(1)} %collective-permute-done.13.refs_10_), channel_id=1, source_target_pairs={{0,1},{1,0},{2,3},{3,2},{4,5},{5,4},{6,7},{7,6},{8,9},{9,8},{10,11... | collective-permute-start | bytes 688136 | tf_op jit(solution)/shard_map/ppermute | solution.py:749
  322.3 6.0 %collective-permute-start.5 = (bf16[128,896]{1,0:T(8,128)(2,1)S(1)}, bf16[128,896]{1,0:T(8,128)(2,1)S(1)}, u32[]{:S(2)}, u32[]{:S(2)}) collective-permute-start(bf16[128,896]{1,0:T(8,128)(2,1)S(1)} %collective-permute-done.3.refs_10_.refs_7_), channel_id=1, source_target_pairs={{0,2},{1,3},{2,0},{3,1},{4,6},{5,7},{6,4},{7,5},{8,10},{9,11},{10,... | collective-permute-start | bytes 688136 | tf_op jit(solution)/shard_map/ppermute | solution.py:749
  328.3 31.4 %copy-start.14 = (bf16[128,896]{1,0:T(8,128)(2,1)}, bf16[128,896]{1,0:T(8,128)(2,1)S(1)}, u32[]{:S(2)}) copy-start(bf16[128,896]{1,0:T(8,128)(2,1)S(1)} %collective-permute-done.5.refs_12_.refs_9_) | copy-start | bytes 688132
  328.3 8.5 %collective-permute-start.16 = (bf16[128,896]{1,0:T(8,128)(2,1)S(1)}, bf16[128,896]{1,0:T(8,128)(2,1)S(1)}, u32[]{:S(2)}, u32[]{:S(2)}) collective-permute-start(bf16[128,896]{1,0:T(8,128)(2,1)S(1)} %collective-permute-done.15.refs_12_), channel_id=1, source_target_pairs={{0,1},{1,0},{2,3},{3,2},{4,5},{5,4},{6,7},{7,6},{8,9},{9,8},{10,11... | collective-permute-start | bytes 688136 | tf_op jit(solution)/shard_map/ppermute | solution.py:749
  336.8 22.9 %collective-permute-start.4 = (bf16[128,896]{1,0:T(8,128)(2,1)S(1)}, bf16[128,896]{1,0:T(8,128)(2,1)S(1)}, u32[]{:S(2)}, u32[]{:S(2)}) collective-permute-start(bf16[128,896]{1,0:T(8,128)(2,1)S(1)} %collective-permute-done.3.refs_10_.refs_7_), channel_id=1, source_target_pairs={{0,1},{1,0},{2,3},{3,2},{4,5},{5,4},{6,7},{7,6},{8,9},{9,8},{10,11... | collective-permute-start | bytes 688136 | tf_op jit(solution)/shard_map/ppermute | solution.py:749
  338.5 21.2 %collective-permute-start.2 = (bf16[128,896]{1,0:T(8,128)(2,1)S(1)}, bf16[128,896]{1,0:T(8,128)(2,1)S(1)}, u32[]{:S(2)}, u32[]{:S(2)}) collective-permute-start(bf16[128,896]{1,0:T(8,128)(2,1)S(1)} %collective-permute-done.1.refs_8_.refs_5_), channel_id=1, source_target_pairs={{0,1},{1,0},{2,3},{3,2},{4,5},{5,4},{6,7},{7,6},{8,9},{9,8},{10,11... | collective-permute-start | bytes 688136 | tf_op jit(solution)/shard_map/ppermute | solution.py:749
  338.8 20.9 %collective-permute-start.6 = (bf16[128,896]{1,0:T(8,128)(2,1)S(1)}, bf16[128,896]{1,0:T(8,128)(2,1)}, u32[]{:S(2)}, u32[]{:S(2)}) collective-permute-start(bf16[128,896]{1,0:T(8,128)(2,1)S(1)} %collective-permute-done.5.refs_12_.refs_9_), channel_id=1, source_target_pairs={{0,1},{1,0},{2,3},{3,2},{4,5},{5,4},{6,7},{7,6},{8,9},{9,8},{10,11... | collective-permute-start | bytes 688136 | tf_op jit(solution)/shard_map/ppermute | solution.py:749
  369.3 43.8 %collective-permute-start.30 = (bf16[224,32,128]{2,1,0:T(8,128)(2,1)}, bf16[224,32,128]{2,1,0:T(8,128)(2,1)}, u32[]{:S(2)}, u32[]{:S(2)}) collective-permute-start(bf16[224,32,128]{2,1,0:T(8,128)(2,1)} %get-tuple-element.57), channel_id=1, source_target_pairs={{0,8},{8,0},{16,24},{24,16},{1,9},{9,1},{17,25},{25,17},{2,10},{10... | collective-permute-start | bytes 5505032 | tf_op jit(solution)/shard_map/ppermute | solution.py:775
  393.6 22.6 %collective-permute-start.27 = (bf16[224,32,128]{2,1,0:T(8,128)(2,1)}, bf16[224,32,128]{2,1,0:T(8,128)(2,1)}, u32[]{:S(2)}, u32[]{:S(2)}) collective-permute-start(bf16[224,32,128]{2,1,0:T(8,128)(2,1)} %get-tuple-element.52), channel_id=1, source_target_pairs={{0,8},{8,0},{16,24},{24,16},{1,9},{9,1},{17,25},{25,17},{2,10},{10... | collective-permute-start | bytes 5505032 | tf_op jit(solution)/shard_map/ppermute | solution.py:775
  403.8 23.5 %collective-permute-start.23 = (bf16[4,128,896]{2,1,0:T(8,128)(2,1)}, bf16[4,128,896]{2,1,0:T(8,128)(2,1)S(1)}, u32[]{:S(2)}, u32[]{:S(2)}) collective-permute-start(bf16[4,128,896]{2,1,0:T(8,128)(2,1)} %get-tuple-element.47), channel_id=1, source_target_pairs={{0,1},{1,0},{2,3},{3,2},{4,5},{5,4},{6,7},{7,6},{8,9},{9,8},{10,11... | collective-permute-start | bytes 2752520 | tf_op jit(solution)/shard_map/ppermute | solution.py:809
  411.2 34.8 %collective-permute-start.20 = (bf16[4,128,896]{2,1,0:T(8,128)(2,1)}, bf16[4,128,896]{2,1,0:T(8,128)(2,1)S(1)}, u32[]{:S(2)}, u32[]{:S(2)}) collective-permute-start(bf16[4,128,896]{2,1,0:T(8,128)(2,1)} %get-tuple-element.43), channel_id=1, source_target_pairs={{0,1},{1,0},{2,3},{3,2},{4,5},{5,4},{6,7},{7,6},{8,9},{9,8},{10,11... | collective-permute-start | bytes 2752520 | tf_op jit(solution)/shard_map/ppermute | solution.py:809
  413.1 79.5 %collective-permute-start.29 = (bf16[224,32,128]{2,1,0:T(8,128)(2,1)}, bf16[224,32,128]{2,1,0:T(8,128)(2,1)}, u32[]{:S(2)}, u32[]{:S(2)}) collective-permute-start(bf16[224,32,128]{2,1,0:T(8,128)(2,1)} %get-tuple-element.55), channel_id=1, source_target_pairs={{0,8},{8,0},{16,24},{24,16},{1,9},{9,1},{17,25},{25,17},{2,10},{10... | collective-permute-start | bytes 5505032 | tf_op jit(solution)/shard_map/ppermute | solution.py:775
  413.1 98.1 %collective-permute-start.26 = (bf16[224,32,128]{2,1,0:T(8,128)(2,1)}, bf16[224,32,128]{2,1,0:T(8,128)(2,1)S(1)}, u32[]{:S(2)}, u32[]{:S(2)}) collective-permute-start(bf16[224,32,128]{2,1,0:T(8,128)(2,1)} %get-tuple-element.50), channel_id=1, source_target_pairs={{0,8},{8,0},{16,24},{24,16},{1,9},{9,1},{17,25},{25,17},{2,10},{10... | collective-permute-start | bytes 5505032 | tf_op jit(solution)/shard_map/ppermute | solution.py:775
  416.2 76.4 %collective-permute-start.31 = (bf16[224,32,128]{2,1,0:T(8,128)(2,1)S(1)}, bf16[224,32,128]{2,1,0:T(8,128)(2,1)S(1)}, u32[]{:S(2)}, u32[]{:S(2)}) collective-permute-start(bf16[224,32,128]{2,1,0:T(8,128)(2,1)S(1)} %add_convert_fusion), channel_id=1, source_target_pairs={{0,16},{8,24},{16,0},{24,8},{1,17},{9,25},{17,1},{25,9},{2,18},{10... | collective-permute-start | bytes 5505032 | tf_op jit(solution)/shard_map/ppermute | solution.py:780
  417.8 11.0 %copy-start.4 = (bf16[4,128,896]{2,1,0:T(8,128)(2,1)S(1)}, bf16[4,128,896]{2,1,0:T(8,128)(2,1)}, u32[]{:S(2)}) copy-start(bf16[4,128,896]{2,1,0:T(8,128)(2,1)} %get-tuple-element.46) | copy-start | bytes 2752516
  417.8 28.5 %copy-start.5 = (bf16[4,128,896]{2,1,0:T(8,128)(2,1)S(1)}, bf16[4,128,896]{2,1,0:T(8,128)(2,1)}, u32[]{:S(2)}) copy-start(bf16[4,128,896]{2,1,0:T(8,128)(2,1)} %get-tuple-element.42) | copy-start | bytes 2752516
  427.3 83.8 %collective-permute-start.28 = (bf16[224,32,128]{2,1,0:T(8,128)(2,1)}, bf16[224,32,128]{2,1,0:T(8,128)(2,1)}, u32[]{:S(2)}, u32[]{:S(2)}) collective-permute-start(bf16[224,32,128]{2,1,0:T(8,128)(2,1)} %add_convert_fusion.1), channel_id=1, source_target_pairs={{0,16},{8,24},{16,0},{24,8},{1,17},{9,25},{17,1},{25,9},{2,18},{10... | collective-permute-start | bytes 5505032 | tf_op jit(solution)/shard_map/ppermute | solution.py:780
  446.1 11.6 %collective-permute-start.24 = (bf16[2,128,896]{2,1,0:T(8,128)(2,1)S(1)}, bf16[2,128,896]{2,1,0:T(8,128)(2,1)S(1)}, u32[]{:S(2)}, u32[]{:S(2)}) collective-permute-start(bf16[2,128,896]{2,1,0:T(8,128)(2,1)S(1)} %add_convert_fusion.2), channel_id=1, source_target_pairs={{0,2},{1,3},{2,0},{3,1},{4,6},{5,7},{6,4},{7,5},{8,10},{9,11},{10,... | collective-permute-start | bytes 1376264 | tf_op jit(solution)/shard_map/ppermute | solution.py:809
  457.7 10.7 %collective-permute-start.21 = (bf16[2,128,896]{2,1,0:T(8,128)(2,1)S(1)}, bf16[2,128,896]{2,1,0:T(8,128)(2,1)S(1)}, u32[]{:S(2)}, u32[]{:S(2)}) collective-permute-start(bf16[2,128,896]{2,1,0:T(8,128)(2,1)S(1)} %add_convert_fusion.3), channel_id=1, source_target_pairs={{0,2},{1,3},{2,0},{3,1},{4,6},{5,7},{6,4},{7,5},{8,10},{9,11},{10,... | collective-permute-start | bytes 1376264 | tf_op jit(solution)/shard_map/ppermute | solution.py:809
  468.4 10.9 %collective-permute-start.25 = (bf16[1,128,896]{2,1,0:T(8,128)(2,1)S(1)}, bf16[1,128,896]{2,1,0:T(8,128)(2,1)S(1)}, u32[]{:S(2)}, u32[]{:S(2)}) collective-permute-start(bf16[1,128,896]{2,1,0:T(8,128)(2,1)S(1)} %add_convert_fusion.5), channel_id=1, source_target_pairs={{0,4},{1,5},{2,6},{3,7},{4,0},{5,1},{6,2},{7,3},{8,12},{9,13},{10,... | collective-permute-start | bytes 688136 | tf_op jit(solution)/shard_map/ppermute | solution.py:809
  479.3 12.5 %collective-permute-start.22 = (bf16[1,128,896]{2,1,0:T(8,128)(2,1)S(1)}, bf16[1,128,896]{2,1,0:T(8,128)(2,1)S(1)}, u32[]{:S(2)}, u32[]{:S(2)}) collective-permute-start(bf16[1,128,896]{2,1,0:T(8,128)(2,1)S(1)} %add_convert_fusion.7), channel_id=1, source_target_pairs={{0,4},{1,5},{2,6},{3,7},{4,0},{5,1},{6,2},{7,3},{8,12},{9,13},{10,... | collective-permute-start | bytes 688136 | tf_op jit(solution)/shard_map/ppermute | solution.py:809
  (8 other events, 21.7 us)

commit v7 on v6

--- a/solution.py
+++ b/solution.py
@@ -191,10 +191,13 @@
     feats = refs[6 : 6 + n_feat]
     down_hbm = refs[6 + n_feat]
     parts = refs[7 + n_feat : 7 + n_feat + n_dp]
-    slopes, bpre, wd_hbm, back_v, down_v, down_a, wd, back, feat_sem, in_sem, keep_sem = refs[7 + n_feat + n_dp :]
+    slopes_hbm, bpre, wd_hbm, back_v, down_v, down_a, wd, back, slopes, feat_sem, in_sem, slope_sem, keep_sem = refs[
+        7 + n_feat + n_dp :
+    ]
     slots, block, _ = down_v.shape
     copies = feature_copies(feats, place_ref, back_v, feat_sem)
     copies += weight_copies(down_hbm, down_v, parts, down_a, place_ref, in_sem)
+    copies.append(pltpu.make_async_copy(slopes_hbm, slopes, slope_sem))
     for copy in copies:
         copy.start()
     back[...] = jnp.zeros(back.shape, F32)
@@ -393,7 +396,7 @@
     return pl.pallas_call(
         functools.partial(back_kernel, n_feat, n_dp),
         out_shape=[jax.ShapeDtypeStruct(slopes.shape, BF16), jax.ShapeDtypeStruct(down.shape, BF16)],
-        in_specs=[SMEM] * 6 + [ANY] * (n_feat + 1 + n_dp) + [VMEM],
+        in_specs=[SMEM] * 6 + [ANY] * (n_feat + 2 + n_dp),
         out_specs=[VMEM, ANY],
         scratch_shapes=[
             pltpu.VMEM(feat_shape, BF16),
@@ -401,8 +404,10 @@
             pltpu.VMEM((n_dp,) + parts[0].shape, BF16),
             pltpu.VMEM(down.shape, BF16),
             pltpu.VMEM(slopes.shape, F32),
+            pltpu.VMEM(slopes.shape, F32),
             pltpu.SemaphoreType.DMA((n_feat,)),
             pltpu.SemaphoreType.DMA((1 + n_dp,)),
+            pltpu.SemaphoreType.DMA,
             pltpu.SemaphoreType.DMA,
         ],
         compiler_params=pltpu.CompilerParams(vmem_limit_bytes=VMEM_LIMIT),

time: 525 us -> 525 us (level)
  no operation moved by 1% of the time
where the time goes in v7:
time: 525 us; the launch traced here: 524 us
  waiting for transfers between devices  327 us (62%)
  Pallas kernels  117 us (22%)
  starting transfers between devices  57 us (11%)
  other arithmetic  15 us (3%)
  local copies, waits for them, and re-layouts  6.48 us (1%)
    ppermute x14, waiting for transfers between devices, gather(): held[m ^ bit] = lax.ppermute(held[m], 'tensor', far_pairs(bit))  135 us
    all_to_all x4, waiting for transfers between devices, exchange(): lax.all_to_all(shaped, 'tensor', split_axis=0, concat_axis=0, tiled=True)  88.5 us
    ppermute x6, waiting for transfers between devices, layer(): held.append(lax.ppermute(send, 'tensor', far_pairs(bit)))  65.1 us
    ppermute x2, waiting for transfers between devices, spread(): mine = lax.ppermute(own, 'dp', x_pairs(j))  37.9 us
    ppermute x14, starting transfers between devices, gather(): held[m ^ bit] = lax.ppermute(held[m], 'tensor', far_pairs(bit))  24.2 us
    all_to_all x4, starting transfers between devices, exchange(): lax.all_to_all(shaped, 'tensor', split_axis=0, concat_axis=0, tiled=True)  21 us
    pallas_call x1, Pallas kernels, forward_products(): pl.pallas_call(functools.partial(forward_kernel, n_feat, n_dp, row_blocks...  19.1 us
    pallas_call x2, Pallas kernels, output_products(): pl.pallas_call(functools.partial(output_kernel, pieces, turned, bits), ou...  16.7 us
  transfers between devices with their start and end apart: 36, of which 18 were waited for; matrix products, arithmetic and copies ran while one was open for 2% of the time, Pallas kernels for 20%

profile of v7, /device:TPU:0, one launch (start us, length us, event | category | flops | bytes accessed | tf_op | source)
XLA Modules:
  0.0 523.7 jit_solution(9244534134429042586)
XLA Ops:
  3.7 1.9 gather_fusion
  10.8 3.8 pack_weight.2
  14.6 7.3 %all-to-all-start = ((bf16[8,28,32,128]{3,2,1,0:T(8,128)(2,1)}), bf16[8,28,32,128]{3,2,1,0:T(8,128)(2,1)S(1)}, u32[]{:S(2)}, u32[]{:S(2)}) async-start(bf16[8,28,32,128]{3,2,1,0:T(8,128)(2,1)} %bitcast.28), calls=%async_computation | async-start | bytes 3670016 | tf_op jit(solution)/shard_map/all_to_all | solution.py:716
  21.9 3.8 pack_weight.3
  25.8 38.8 %all-to-all-done = bf16[8,28,32,128]{3,2,1,0:T(8,128)(2,1)S(1)} async-done(((bf16[8,28,32,128]{3,2,1,0:T(8,128)(2,1)}), bf16[8,28,32,128]{3,2,1,0:T(8,128)(2,1)S(1)}, u32[]{:S(2)}, u32[]{:S(2)}) %all-to-all-start) | async-done | bytes 1835040 | tf_op jit(solution)/shard_map/all_to_all | solution.py:716
  64.6 4.3 all-to-all-start.1
  68.9 6.4 %pack_moments.3 = bf16[224,2,32,128]{3,2,1,0:T(8,128)(2,1)} custom-call(s32[224]{0:T(256)} %reshape.141.send_ref, f32[224,32,128]{2,1,0:T(8,128)} %refs_0_.9, f32[224,32,128]{2,1,0:T(8,128)} %refs_1_.3), custom_call_target="tpu_custom_call" | custom-call | bytes 11010048 | tf_op jit(solution)/shard_map/pack_moments/pallas_call | solution.py:86
  75.3 35.8 %all-to-all-done.1 = bf16[8,28,32,128]{3,2,1,0:T(8,128)(2,1)} async-done(((bf16[8,28,32,128]{3,2,1,0:T(8,128)(2,1)}), bf16[8,28,32,128]{3,2,1,0:T(8,128)(2,1)}, u32[]{:S(2)}, u32[]{:S(2)}) %all-to-all-start.1) | async-done | bytes 1835040 | tf_op jit(solution)/shard_map/all_to_all | solution.py:716
  111.1 4.7 all-to-all-start.3
  117.9 1.8 collective-permute-start.11
  121.2 37.9 %collective-permute-done.18.refs_17_ = bf16[224,32,128]{2,1,0:T(8,128)(2,1)} collective-permute-done((bf16[224,32,128]{2,1,0:T(8,128)(2,1)}, bf16[224,32,128]{2,1,0:T(8,128)(2,1)}, u32[]{:S(2)}, u32[]{:S(2)}) %collective-permute-start.18) | collective-permute-done | bytes 1835040 | tf_op jit(solution)/shard_map/ppermute | solution.py:732
  159.1 20.9 %collective-permute-done.11.refs_8_ = bf16[128,896]{1,0:T(8,128)(2,1)S(1)} collective-permute-done((bf16[128,896]{1,0:T(8,128)(2,1)S(1)}, bf16[128,896]{1,0:T(8,128)(2,1)S(1)}, u32[]{:S(2)}, u32[]{:S(2)}) %collective-permute-start.11) | collective-permute-done | bytes 229408 | tf_op jit(solution)/shard_map/ppermute | solution.py:754
  179.9 3.9 collective-permute-start.13
  183.8 6.4 %pack_moments.2 = bf16[224,2,32,128]{3,2,1,0:T(8,128)(2,1)} custom-call(s32[224]{0:T(256)} %reshape.141.send_ref, f32[224,32,128]{2,1,0:T(8,128)} %refs_3_.3, f32[224,32,128]{2,1,0:T(8,128)} %refs_4_.2), custom_call_target="tpu_custom_call" | custom-call | bytes 11010048 | tf_op jit(solution)/shard_map/pack_moments/pallas_call | solution.py:86
  190.2 13.8 %all-to-all-done.3 = bf16[8,28,2,32,128]{4,3,2,1,0:T(8,128)(2,1)} async-done(((bf16[8,28,2,32,128]{4,3,2,1,0:T(8,128)(2,1)}), bf16[8,28,2,32,128]{4,3,2,1,0:T(8,128)(2,1)}, u32[]{:S(2)}, u32[]{:S(2)}) %all-to-all-start.3) | async-done | bytes 3670048 | tf_op jit(solution)/shard_map/all_to_all | solution.py:716
  204.0 4.7 all-to-all-start.2
  208.7 2.9 collective-permute-start.3
  213.1 84.7 %collective-permute-done.3.refs_10_.refs_7_ = bf16[128,896]{1,0:T(8,128)(2,1)S(1)} collective-permute-done((bf16[128,896]{1,0:T(8,128)(2,1)S(1)}, bf16[128,896]{1,0:T(8,128)(2,1)S(1)}, u32[]{:S(2)}, u32[]{:S(2)}) %collective-permute-start.3) | collective-permute-done | bytes 229408 | tf_op jit(solution)/shard_map/ppermute | solution.py:754
  299.8 4.3 collective-permute-done.refs_7_.refs_4_
  304.1 1.7 collective-permute-start.12
  305.9 4.3 collective-permute-done.12.refs_9_
  311.2 4.9 collective-permute-done.15.refs_12_
  316.2 1.7 collective-permute-start.14
  317.9 4.4 collective-permute-done.14.refs_11_
  323.4 4.9 collective-permute-done.5.refs_12_.refs_9_
  328.3 1.7 collective-permute-start.16
  330.1 6.7 %collective-permute-done.16.refs_13_ = bf16[128,896]{1,0:T(8,128)(2,1)S(1)} collective-permute-done((bf16[128,896]{1,0:T(8,128)(2,1)S(1)}, bf16[128,896]{1,0:T(8,128)(2,1)S(1)}, u32[]{:S(2)}, u32[]{:S(2)}) %collective-permute-start.16) | collective-permute-done | bytes 229408 | tf_op jit(solution)/shard_map/ppermute | solution.py:754
  336.8 1.7 collective-permute-start.4
  338.8 1.7 collective-permute-start.6
  340.6 19.1 %forward_products.1 = (bf16[16,128,128]{2,1,0:T(8,128)(2,1)}, bf16[16,128,128]{2,1,0:T(8,128)(2,1)}, f32[16,128,128]{2,1,0:T(8,128)}, bf16[56,128,128]{2,1,0:T(8,128)(2,1)}, bf16[224,128,128]{2,1,0:T(8,128)(2,1)}) custom-call(s32[224]{0:T(256)} %refs_0_.8, s32[224]{0:T(256)} %and_select_fusion.1.refs_1_, s32[224]{0:T(256)} %get-tuple-element.35.refs_2_.home_ref, ...), custom_call_target="tpu_custom_call" | custom-call | flops 939524096 | bytes 44040192 | tf_op jit(solution)/shard_map/forward_products/pallas_call | solution.py:365
  360.5 8.8 %gradient_products.3 = (bf16[224,32,128]{2,1,0:T(8,128)(2,1)}, bf16[224,32,128]{2,1,0:T(8,128)(2,1)}, bf16[224,32,128]{2,1,0:T(8,128)(2,1)}, bf16[224,32,128]{2,1,0:T(8,128)(2,1)}) custom-call(s32[224]{0:T(256)} %refs_0_.8, s32[224]{0:T(256)} %and_select_fusion.1.refs_1_, s32[3]{0:T(128)} %pad_add_fusion.refs_5_.refs_2_, bf16[128,896]{1,0:T(8,128)(2,1)} %refs_3_.4, ...), custom_call_target="tpu_custom_call" | custom-call | flops 939524096 | bytes 11010048 | tf_op jit(solution)/shard_map/gradient_products/pallas_call | solution.py:425
  369.4 16.5 %back_products.1 = (bf16[16,128,128]{2,1,0:T(8,128)(2,1)}, bf16[224,128,128]{2,1,0:T(8,128)(2,1)}) custom-call(s32[224]{0:T(256)} %refs_0_.8, s32[224]{0:T(256)} %and_select_fusion.1.refs_1_, s32[224]{0:T(256)} %get-tuple-element.35.refs_2_.home_ref, s32[224]{0:T(256)} %get-tuple-element.36.refs_3_.came_ref, s32[224]{0:T(256)} %get-tuple-element.37.refs_4_.kind_ref, ...), custom_call_target="tpu_custom_call" | custom-call | flops 939524096 | bytes 44040192 | tf_op jit(solution)/shard_map/back_products/pallas_call | solution.py:396
  385.9 7.5 %gradient_products.2 = (bf16[224,32,128]{2,1,0:T(8,128)(2,1)}, bf16[224,32,128]{2,1,0:T(8,128)(2,1)}, bf16[224,32,128]{2,1,0:T(8,128)(2,1)}, bf16[224,32,128]{2,1,0:T(8,128)(2,1)}) custom-call(s32[224]{0:T(256)} %refs_0_.8, s32[224]{0:T(256)} %and_select_fusion.1.refs_1_, s32[3]{0:T(128)} %pad_add_fusion.refs_5_.refs_2_, ...), custom_call_target="tpu_custom_call" | custom-call | flops 939524096 | bytes 11010048 | tf_op jit(solution)/shard_map/gradient_products/pallas_call | solution.py:425
  393.9 9.7 %output_products.3 = (bf16[4,128,896]{2,1,0:T(8,128)(2,1)}, bf16[4,128,896]{2,1,0:T(8,128)(2,1)}) custom-call(s32[224]{0:T(256)} %refs_0_.8, s32[224]{0:T(256)} %and_select_fusion.1.refs_1_, s32[3]{0:T(128)} %pad_add_fusion.refs_5_.refs_2_, bf16[224,128,128]{2,1,0:T(8,128)(2,1)} %get-tuple-element.44.refs_3_, bf16[16,128,128]{2,1,0:T(8,128)(2,1)} %get-tuple-element.45.refs_4_), custom_call_target="tpu_custom_call" | custom-call | flops 939524096 | bytes 14680064 | tf_op jit(solution)/shard_map/output_products/pallas_call | solution.py:444
  404.0 7.0 %output_products.2 = (bf16[4,128,896]{2,1,0:T(8,128)(2,1)}, bf16[4,128,896]{2,1,0:T(8,128)(2,1)}) custom-call(s32[224]{0:T(256)} %refs_0_.8, s32[224]{0:T(256)} %and_select_fusion.1.refs_1_, s32[3]{0:T(128)} %pad_add_fusion.refs_5_.refs_2_, bf16[224,128,128]{2,1,0:T(8,128)(2,1)} %get-tuple-element.40.refs_3_, bf16[16,128,128]{2,1,0:T(8,128)(2,1)} %get-tuple-element.41.refs_4_), custom_call_target="tpu_custom_call" | custom-call | flops 939524096 | bytes 14680064 | tf_op jit(solution)/shard_map/output_products/pallas_call | solution.py:444
  411.0 1.8 collective-permute-start.20
  413.4 2.7 add_convert_fusion
  417.6 3.3 add_convert_fusion.1
  420.9 6.2 %collective-permute-done.23 = bf16[4,128,896]{2,1,0:T(8,128)(2,1)S(1)} collective-permute-done((bf16[4,128,896]{2,1,0:T(8,128)(2,1)}, bf16[4,128,896]{2,1,0:T(8,128)(2,1)S(1)}, u32[]{:S(2)}, u32[]{:S(2)}) %collective-permute-start.23) | collective-permute-done | bytes 917536 | tf_op jit(solution)/shard_map/ppermute | solution.py:814
  428.8 17.1 %collective-permute-done.20 = bf16[4,128,896]{2,1,0:T(8,128)(2,1)S(1)} collective-permute-done((bf16[4,128,896]{2,1,0:T(8,128)(2,1)}, bf16[4,128,896]{2,1,0:T(8,128)(2,1)S(1)}, u32[]{:S(2)}, u32[]{:S(2)}) %collective-permute-start.20) | collective-permute-done | bytes 917536 | tf_op jit(solution)/shard_map/ppermute | solution.py:814
  446.2 11.2 %collective-permute-done.24 = bf16[2,128,896]{2,1,0:T(8,128)(2,1)S(1)} collective-permute-done((bf16[2,128,896]{2,1,0:T(8,128)(2,1)S(1)}, bf16[2,128,896]{2,1,0:T(8,128)(2,1)S(1)}, u32[]{:S(2)}, u32[]{:S(2)}) %collective-permute-start.24) | collective-permute-done | bytes 458784 | tf_op jit(solution)/shard_map/ppermute | solution.py:814
  457.9 10.4 %collective-permute-done.21 = bf16[2,128,896]{2,1,0:T(8,128)(2,1)S(1)} collective-permute-done((bf16[2,128,896]{2,1,0:T(8,128)(2,1)S(1)}, bf16[2,128,896]{2,1,0:T(8,128)(2,1)S(1)}, u32[]{:S(2)}, u32[]{:S(2)}) %collective-permute-start.21) | collective-permute-done | bytes 458784 | tf_op jit(solution)/shard_map/ppermute | solution.py:814
  468.2 2.3 collective-permute-start.25
  470.6 8.5 %collective-permute-done.25 = bf16[1,128,896]{2,1,0:T(8,128)(2,1)S(1)} collective-permute-done((bf16[1,128,896]{2,1,0:T(8,128)(2,1)S(1)}, bf16[1,128,896]{2,1,0:T(8,128)(2,1)S(1)}, u32[]{:S(2)}, u32[]{:S(2)}) %collective-permute-start.25) | collective-permute-done | bytes 229408 | tf_op jit(solution)/shard_map/ppermute | solution.py:814
  479.9 11.7 %collective-permute-done.22 = bf16[1,128,896]{2,1,0:T(8,128)(2,1)S(1)} collective-permute-done((bf16[1,128,896]{2,1,0:T(8,128)(2,1)S(1)}, bf16[1,128,896]{2,1,0:T(8,128)(2,1)S(1)}, u32[]{:S(2)}, u32[]{:S(2)}) %collective-permute-start.22) | collective-permute-done | bytes 229408 | tf_op jit(solution)/shard_map/ppermute | solution.py:814
  493.6 9.2 %ahead.1 = (f32[224,32,128]{2,1,0:T(8,128)}, f32[224,32,128]{2,1,0:T(8,128)}) custom-call(s32[224]{0:T(256)} %get-tuple-element.35.refs_2_.home_ref, s32[224]{0:T(256)} %get-tuple-element.37.refs_4_.kind_ref, bf16[224,32,128]{2,1,0:T(8,128)(2,1)} %get-tuple-element.54.refs_0_, bf16[224,32,128]{2,1,0:T(8,128)(2,1)} %collective-permute-done.29.refs_1_, ...), custom_call_target="tpu_custom_call" | custom-call | flops 9175040 | bytes 20185088 | tf_op jit(solution)/shard_map/ahead/pallas_call | solution.py:584
  502.8 8.1 %finish.1 = f32[224,32,128]{2,1,0:T(8,128)} custom-call(s32[224]{0:T(256)} %get-tuple-element.36.refs_3_.came_ref, s32[224]{0:T(256)} %get-tuple-element.37.refs_4_.kind_ref, f32[224,32,128]{2,1,0:T(8,128)} %get-tuple-element.58.first_hbm, f32[224,32,128]{2,1,0:T(8,128)} %get-tuple-element.59.second_hbm, bf16[224,2,32,128]{3,2,1,0:T(8,128)(2,1)} %bitcast.17.arrived_hbm), custom_call_target="tpu_custom_call" | custom-call | flops 9175040 | bytes 16515072 | tf_op jit(solution)/shard_map/finish/pallas_call | solution.py:640
  512.3 11.2 %adam_step.1 = f32[224,32,128]{2,1,0:T(8,128)} custom-call(s32[224]{0:T(256)} %get-tuple-element.35.refs_2_.home_ref, s32[224]{0:T(256)} %get-tuple-element.36.refs_3_.came_ref, s32[224]{0:T(256)} %get-tuple-element.37.refs_4_.kind_ref, bf16[224,32,128]{2,1,0:T(8,128)(2,1)} %get-tuple-element.49.refs_0_, bf16[224,32,128]{2,1,0:T(8,128)(2,1)} %copy-done.1, ...), custom_call_target="tpu_custom_call" | custom-call | flops 13762560 | bytes 15597568 | tf_op jit(solution)/shard_map/adam_step/pallas_call | solution.py:537
  (113 shorter events, 28.3 us)
Async XLA Ops:
  14.6 49.9 %all-to-all-start = ((bf16[8,28,32,128]{3,2,1,0:T(8,128)(2,1)}), bf16[8,28,32,128]{3,2,1,0:T(8,128)(2,1)S(1)}, u32[]{:S(2)}, u32[]{:S(2)}) async-start(bf16[8,28,32,128]{3,2,1,0:T(8,128)(2,1)} %bitcast.28), calls=%async_computation | async-start | bytes 3670016 | tf_op jit(solution)/shard_map/all_to_all | solution.py:716
  64.6 234.7 %copy-start = (bf16[8,28,32,128]{3,2,1,0:T(8,128)(2,1)}, bf16[8,28,32,128]{3,2,1,0:T(8,128)(2,1)S(1)}, u32[]{:S(2)}) copy-start(bf16[8,28,32,128]{3,2,1,0:T(8,128)(2,1)S(1)} %all-to-all-done) | copy-start | bytes 5505028
  64.6 46.6 %all-to-all-start.1 = ((bf16[8,28,32,128]{3,2,1,0:T(8,128)(2,1)}), bf16[8,28,32,128]{3,2,1,0:T(8,128)(2,1)}, u32[]{:S(2)}, u32[]{:S(2)}) async-start(bf16[8,28,32,128]{3,2,1,0:T(8,128)(2,1)} %bitcast.27), calls=%async_computation.1 | async-start | bytes 3670016 | tf_op jit(solution)/shard_map/all_to_all | solution.py:716
  111.1 92.9 %all-to-all-start.3 = ((bf16[8,28,2,32,128]{4,3,2,1,0:T(8,128)(2,1)}), bf16[8,28,2,32,128]{4,3,2,1,0:T(8,128)(2,1)}, u32[]{:S(2)}, u32[]{:S(2)}) async-start(bf16[8,28,2,32,128]{4,3,2,1,0:T(8,128)(2,1)} %bitcast.23), calls=%async_computation.3 | async-start | bytes 7340032 | tf_op jit(solution)/shard_map/all_to_all | solution.py:716
  115.8 43.3 %collective-permute-start.18 = (bf16[224,32,128]{2,1,0:T(8,128)(2,1)}, bf16[224,32,128]{2,1,0:T(8,128)(2,1)}, u32[]{:S(2)}, u32[]{:S(2)}) collective-permute-start(bf16[224,32,128]{2,1,0:T(8,128)(2,1)} %bitcast.11.refs_15_), channel_id=1, source_target_pairs={{0,16},{8,24},{16,0},{24,8},{1,17},{9,25},{17,1},{25,9},{2,18},{10... | collective-permute-start | bytes 5505032 | tf_op jit(solution)/shard_map/ppermute | solution.py:732
  117.4 182.0 %collective-permute-start.8 = (bf16[224,32,128]{2,1,0:T(8,128)(2,1)S(1)}, bf16[224,32,128]{2,1,0:T(8,128)(2,1)}, u32[]{:S(2)}, u32[]{:S(2)}) collective-permute-start(bf16[224,32,128]{2,1,0:T(8,128)(2,1)S(1)} %bitcast.24), channel_id=1, source_target_pairs={{0,16},{8,24},{16,0},{24,8},{1,17},{9,25},{17,1},{25,9},{2,18},{10... | collective-permute-start | bytes 5505032 | tf_op jit(solution)/shard_map/ppermute | solution.py:732
  117.9 62.0 %collective-permute-start.11 = (bf16[128,896]{1,0:T(8,128)(2,1)S(1)}, bf16[128,896]{1,0:T(8,128)(2,1)S(1)}, u32[]{:S(2)}, u32[]{:S(2)}) collective-permute-start(bf16[128,896]{1,0:T(8,128)(2,1)S(1)} %copy-done.6), channel_id=1, source_target_pairs={{0,2},{1,3},{2,0},{3,1},{4,6},{5,7},{6,4},{7,5},{8,10},{9,11},{10,... | collective-permute-start | bytes 688136 | tf_op jit(solution)/shard_map/ppermute | solution.py:754
  119.7 89.0 %collective-permute-start.10 = (bf16[128,896]{1,0:T(8,128)(2,1)S(1)}, bf16[128,896]{1,0:T(8,128)(2,1)S(1)}, u32[]{:S(2)}, u32[]{:S(2)}) collective-permute-start(bf16[128,896]{1,0:T(8,128)(2,1)S(1)} %copy-done.6), channel_id=1, source_target_pairs={{0,1},{1,0},{2,3},{3,2},{4,5},{5,4},{6,7},{7,6},{8,9},{9,8},{10,11... | collective-permute-start | bytes 688136 | tf_op jit(solution)/shard_map/ppermute | solution.py:754
  121.2 217.3 %collective-permute-start.17 = (bf16[224,32,128]{2,1,0:T(8,128)(2,1)}, bf16[224,32,128]{2,1,0:T(8,128)(2,1)}, u32[]{:S(2)}, u32[]{:S(2)}) collective-permute-start(bf16[224,32,128]{2,1,0:T(8,128)(2,1)} %bitcast.11.refs_15_), channel_id=1, source_target_pairs={{0,8},{8,0},{16,24},{24,16},{1,9},{9,1},{17,25},{25,17},{2,10},{10... | collective-permute-start | bytes 5505032 | tf_op jit(solution)/shard_map/ppermute | solution.py:733
  159.1 179.8 %collective-permute-start.19 = (bf16[224,32,128]{2,1,0:T(8,128)(2,1)}, bf16[224,32,128]{2,1,0:T(8,128)(2,1)}, u32[]{:S(2)}, u32[]{:S(2)}) collective-permute-start(bf16[224,32,128]{2,1,0:T(8,128)(2,1)} %collective-permute-done.18.refs_17_), channel_id=1, source_target_pairs={{0,8},{8,0},{16,24},{24,16},{1,9},{9,1},{17,25},{25,17},{2,10},{10... | collective-permute-start | bytes 5505032 | tf_op jit(solution)/shard_map/ppermute | solution.py:733
  179.9 124.2 %copy-start.8 = (bf16[128,896]{1,0:T(8,128)(2,1)}, bf16[128,896]{1,0:T(8,128)(2,1)S(1)}, u32[]{:S(2)}) copy-start(bf16[128,896]{1,0:T(8,128)(2,1)S(1)} %collective-permute-done.11.refs_8_) | copy-start | bytes 688132
  179.9 31.7 %collective-permute-start.13 = (bf16[128,896]{1,0:T(8,128)(2,1)S(1)}, bf16[128,896]{1,0:T(8,128)(2,1)S(1)}, u32[]{:S(2)}, u32[]{:S(2)}) collective-permute-start(bf16[128,896]{1,0:T(8,128)(2,1)S(1)} %copy-done.6), channel_id=1, source_target_pairs={{0,4},{1,5},{2,6},{3,7},{4,0},{5,1},{6,2},{7,3},{8,12},{9,13},{10,... | collective-permute-start | bytes 688136 | tf_op jit(solution)/shard_map/ppermute | solution.py:754
  204.0 306.9 %all-to-all-start.2 = ((bf16[8,28,2,32,128]{4,3,2,1,0:T(8,128)(2,1)}), bf16[8,28,2,32,128]{4,3,2,1,0:T(8,128)(2,1)}, u32[]{:S(2)}, u32[]{:S(2)}) async-start(bf16[8,28,2,32,128]{4,3,2,1,0:T(8,128)(2,1)} %bitcast.22), calls=%async_computation.2 | async-start | bytes 7340032 | tf_op jit(solution)/shard_map/all_to_all | solution.py:716
  208.7 131.9 %copy-start.10 = (bf16[128,896]{1,0:T(8,128)(2,1)}, bf16[128,896]{1,0:T(8,128)(2,1)S(1)}, u32[]{:S(2)}) copy-start(bf16[128,896]{1,0:T(8,128)(2,1)S(1)} %collective-permute-done.10.refs_7_) | copy-start | bytes 688132
  208.7 89.0 %collective-permute-start.3 = (bf16[128,896]{1,0:T(8,128)(2,1)S(1)}, bf16[128,896]{1,0:T(8,128)(2,1)S(1)}, u32[]{:S(2)}, u32[]{:S(2)}) collective-permute-start(bf16[128,896]{1,0:T(8,128)(2,1)S(1)} %copy-done.7), channel_id=1, source_target_pairs={{0,4},{1,5},{2,6},{3,7},{4,0},{5,1},{6,2},{7,3},{8,12},{9,13},{10,... | collective-permute-start | bytes 688136 | tf_op jit(solution)/shard_map/ppermute | solution.py:754
  211.6 129.0 %copy-start.13 = (bf16[128,896]{1,0:T(8,128)(2,1)}, bf16[128,896]{1,0:T(8,128)(2,1)S(1)}, u32[]{:S(2)}) copy-start(bf16[128,896]{1,0:T(8,128)(2,1)S(1)} %collective-permute-done.13.refs_10_) | copy-start | bytes 688132
  211.6 87.6 %collective-permute-start.1 = (bf16[128,896]{1,0:T(8,128)(2,1)S(1)}, bf16[128,896]{1,0:T(8,128)(2,1)S(1)}, u32[]{:S(2)}, u32[]{:S(2)}) collective-permute-start(bf16[128,896]{1,0:T(8,128)(2,1)S(1)} %copy-done.7), channel_id=1, source_target_pairs={{0,2},{1,3},{2,0},{3,1},{4,6},{5,7},{6,4},{7,5},{8,10},{9,11},{10,... | collective-permute-start | bytes 688136 | tf_op jit(solution)/shard_map/ppermute | solution.py:754
  297.8 61.9 %copy-start.9 = (bf16[128,896]{1,0:T(8,128)(2,1)}, bf16[128,896]{1,0:T(8,128)(2,1)S(1)}, u32[]{:S(2)}) copy-start(bf16[128,896]{1,0:T(8,128)(2,1)S(1)} %collective-permute-done.3.refs_10_.refs_7_) | copy-start | bytes 688132
  297.8 6.3 %collective-permute-start = (bf16[128,896]{1,0:T(8,128)(2,1)S(1)}, bf16[128,896]{1,0:T(8,128)(2,1)S(1)}, u32[]{:S(2)}, u32[]{:S(2)}) collective-permute-start(bf16[128,896]{1,0:T(8,128)(2,1)S(1)} %copy-done.7), channel_id=1, source_target_pairs={{0,1},{1,0},{2,3},{3,2},{4,5},{5,4},{6,7},{7,6},{8,9},{9,8},{10,11... | collective-permute-start | bytes 688136 | tf_op jit(solution)/shard_map/ppermute | solution.py:754
  299.2 60.5 %copy-start.11 = (bf16[128,896]{1,0:T(8,128)(2,1)}, bf16[128,896]{1,0:T(8,128)(2,1)S(1)}, u32[]{:S(2)}) copy-start(bf16[128,896]{1,0:T(8,128)(2,1)S(1)} %collective-permute-done.1.refs_8_.refs_5_) | copy-start | bytes 688132
  299.2 70.1 %collective-permute-start.7 = (bf16[224,32,128]{2,1,0:T(8,128)(2,1)S(1)}, bf16[224,32,128]{2,1,0:T(8,128)(2,1)}, u32[]{:S(2)}, u32[]{:S(2)}) collective-permute-start(bf16[224,32,128]{2,1,0:T(8,128)(2,1)S(1)} %bitcast.25), channel_id=1, source_target_pairs={{0,8},{8,0},{16,24},{24,16},{1,9},{9,1},{17,25},{25,17},{2,10},{10... | collective-permute-start | bytes 5505032 | tf_op jit(solution)/shard_map/ppermute | solution.py:733
  299.3 70.1 %collective-permute-start.9 = (bf16[224,32,128]{2,1,0:T(8,128)(2,1)}, bf16[224,32,128]{2,1,0:T(8,128)(2,1)}, u32[]{:S(2)}, u32[]{:S(2)}) collective-permute-start(bf16[224,32,128]{2,1,0:T(8,128)(2,1)} %collective-permute-done.8.refs_17_), channel_id=1, source_target_pairs={{0,8},{8,0},{16,24},{24,16},{1,9},{9,1},{17,25},{25,17},{2,10},{10... | collective-permute-start | bytes 5505032 | tf_op jit(solution)/shard_map/ppermute | solution.py:733
  304.1 55.6 %copy-start.12 = (bf16[128,896]{1,0:T(8,128)(2,1)}, bf16[128,896]{1,0:T(8,128)(2,1)S(1)}, u32[]{:S(2)}) copy-start(bf16[128,896]{1,0:T(8,128)(2,1)S(1)} %collective-permute-done.refs_7_.refs_4_) | copy-start | bytes 688132
  304.1 6.0 %collective-permute-start.12 = (bf16[128,896]{1,0:T(8,128)(2,1)S(1)}, bf16[128,896]{1,0:T(8,128)(2,1)S(1)}, u32[]{:S(2)}, u32[]{:S(2)}) collective-permute-start(bf16[128,896]{1,0:T(8,128)(2,1)S(1)} %collective-permute-done.11.refs_8_), channel_id=1, source_target_pairs={{0,1},{1,0},{2,3},{3,2},{4,5},{5,4},{6,7},{7,6},{8,9},{9,8},{10,11... | collective-permute-start | bytes 688136 | tf_op jit(solution)/shard_map/ppermute | solution.py:754
  310.1 30.4 %copy-start.16 = (bf16[128,896]{1,0:T(8,128)(2,1)}, bf16[128,896]{1,0:T(8,128)(2,1)S(1)}, u32[]{:S(2)}) copy-start(bf16[128,896]{1,0:T(8,128)(2,1)S(1)} %collective-permute-done.12.refs_9_) | copy-start | bytes 688132
  310.1 6.0 %collective-permute-start.15 = (bf16[128,896]{1,0:T(8,128)(2,1)S(1)}, bf16[128,896]{1,0:T(8,128)(2,1)S(1)}, u32[]{:S(2)}, u32[]{:S(2)}) collective-permute-start(bf16[128,896]{1,0:T(8,128)(2,1)S(1)} %collective-permute-done.13.refs_10_), channel_id=1, source_target_pairs={{0,2},{1,3},{2,0},{3,1},{4,6},{5,7},{6,4},{7,5},{8,10},{9,11},{10,... | collective-permute-start | bytes 688136 | tf_op jit(solution)/shard_map/ppermute | solution.py:754
  316.2 13.9 %copy-start.18 = (bf16[128,896]{1,0:T(8,128)(2,1)}, bf16[128,896]{1,0:T(8,128)(2,1)S(1)}, u32[]{:S(2)}) copy-start(bf16[128,896]{1,0:T(8,128)(2,1)S(1)} %collective-permute-done.15.refs_12_) | copy-start | bytes 688132
  316.2 6.1 %collective-permute-start.14 = (bf16[128,896]{1,0:T(8,128)(2,1)S(1)}, bf16[128,896]{1,0:T(8,128)(2,1)}, u32[]{:S(2)}, u32[]{:S(2)}) collective-permute-start(bf16[128,896]{1,0:T(8,128)(2,1)S(1)} %collective-permute-done.13.refs_10_), channel_id=1, source_target_pairs={{0,1},{1,0},{2,3},{3,2},{4,5},{5,4},{6,7},{7,6},{8,9},{9,8},{10,11... | collective-permute-start | bytes 688136 | tf_op jit(solution)/shard_map/ppermute | solution.py:754
  322.3 6.0 %collective-permute-start.5 = (bf16[128,896]{1,0:T(8,128)(2,1)S(1)}, bf16[128,896]{1,0:T(8,128)(2,1)S(1)}, u32[]{:S(2)}, u32[]{:S(2)}) collective-permute-start(bf16[128,896]{1,0:T(8,128)(2,1)S(1)} %collective-permute-done.3.refs_10_.refs_7_), channel_id=1, source_target_pairs={{0,2},{1,3},{2,0},{3,1},{4,6},{5,7},{6,4},{7,5},{8,10},{9,11},{10,... | collective-permute-start | bytes 688136 | tf_op jit(solution)/shard_map/ppermute | solution.py:754
  328.3 31.4 %copy-start.14 = (bf16[128,896]{1,0:T(8,128)(2,1)}, bf16[128,896]{1,0:T(8,128)(2,1)S(1)}, u32[]{:S(2)}) copy-start(bf16[128,896]{1,0:T(8,128)(2,1)S(1)} %collective-permute-done.5.refs_12_.refs_9_) | copy-start | bytes 688132
  328.3 8.5 %collective-permute-start.16 = (bf16[128,896]{1,0:T(8,128)(2,1)S(1)}, bf16[128,896]{1,0:T(8,128)(2,1)S(1)}, u32[]{:S(2)}, u32[]{:S(2)}) collective-permute-start(bf16[128,896]{1,0:T(8,128)(2,1)S(1)} %collective-permute-done.15.refs_12_), channel_id=1, source_target_pairs={{0,1},{1,0},{2,3},{3,2},{4,5},{5,4},{6,7},{7,6},{8,9},{9,8},{10,11... | collective-permute-start | bytes 688136 | tf_op jit(solution)/shard_map/ppermute | solution.py:754
  336.8 22.9 %collective-permute-start.4 = (bf16[128,896]{1,0:T(8,128)(2,1)S(1)}, bf16[128,896]{1,0:T(8,128)(2,1)S(1)}, u32[]{:S(2)}, u32[]{:S(2)}) collective-permute-start(bf16[128,896]{1,0:T(8,128)(2,1)S(1)} %collective-permute-done.3.refs_10_.refs_7_), channel_id=1, source_target_pairs={{0,1},{1,0},{2,3},{3,2},{4,5},{5,4},{6,7},{7,6},{8,9},{9,8},{10,11... | collective-permute-start | bytes 688136 | tf_op jit(solution)/shard_map/ppermute | solution.py:754
  338.5 21.2 %collective-permute-start.2 = (bf16[128,896]{1,0:T(8,128)(2,1)S(1)}, bf16[128,896]{1,0:T(8,128)(2,1)S(1)}, u32[]{:S(2)}, u32[]{:S(2)}) collective-permute-start(bf16[128,896]{1,0:T(8,128)(2,1)S(1)} %collective-permute-done.1.refs_8_.refs_5_), channel_id=1, source_target_pairs={{0,1},{1,0},{2,3},{3,2},{4,5},{5,4},{6,7},{7,6},{8,9},{9,8},{10,11... | collective-permute-start | bytes 688136 | tf_op jit(solution)/shard_map/ppermute | solution.py:754
  338.8 20.9 %collective-permute-start.6 = (bf16[128,896]{1,0:T(8,128)(2,1)S(1)}, bf16[128,896]{1,0:T(8,128)(2,1)}, u32[]{:S(2)}, u32[]{:S(2)}) collective-permute-start(bf16[128,896]{1,0:T(8,128)(2,1)S(1)} %collective-permute-done.5.refs_12_.refs_9_), channel_id=1, source_target_pairs={{0,1},{1,0},{2,3},{3,2},{4,5},{5,4},{6,7},{7,6},{8,9},{9,8},{10,11... | collective-permute-start | bytes 688136 | tf_op jit(solution)/shard_map/ppermute | solution.py:754
  369.3 43.6 %collective-permute-start.30 = (bf16[224,32,128]{2,1,0:T(8,128)(2,1)}, bf16[224,32,128]{2,1,0:T(8,128)(2,1)}, u32[]{:S(2)}, u32[]{:S(2)}) collective-permute-start(bf16[224,32,128]{2,1,0:T(8,128)(2,1)} %get-tuple-element.57), channel_id=1, source_target_pairs={{0,8},{8,0},{16,24},{24,16},{1,9},{9,1},{17,25},{25,17},{2,10},{10... | collective-permute-start | bytes 5505032 | tf_op jit(solution)/shard_map/ppermute | solution.py:780
  393.4 22.6 %collective-permute-start.27 = (bf16[224,32,128]{2,1,0:T(8,128)(2,1)}, bf16[224,32,128]{2,1,0:T(8,128)(2,1)}, u32[]{:S(2)}, u32[]{:S(2)}) collective-permute-start(bf16[224,32,128]{2,1,0:T(8,128)(2,1)} %get-tuple-element.52), channel_id=1, source_target_pairs={{0,8},{8,0},{16,24},{24,16},{1,9},{9,1},{17,25},{25,17},{2,10},{10... | collective-permute-start | bytes 5505032 | tf_op jit(solution)/shard_map/ppermute | solution.py:780
  403.7 23.5 %collective-permute-start.23 = (bf16[4,128,896]{2,1,0:T(8,128)(2,1)}, bf16[4,128,896]{2,1,0:T(8,128)(2,1)S(1)}, u32[]{:S(2)}, u32[]{:S(2)}) collective-permute-start(bf16[4,128,896]{2,1,0:T(8,128)(2,1)} %get-tuple-element.47), channel_id=1, source_target_pairs={{0,1},{1,0},{2,3},{3,2},{4,5},{5,4},{6,7},{7,6},{8,9},{9,8},{10,11... | collective-permute-start | bytes 2752520 | tf_op jit(solution)/shard_map/ppermute | solution.py:814
  411.0 34.8 %collective-permute-start.20 = (bf16[4,128,896]{2,1,0:T(8,128)(2,1)}, bf16[4,128,896]{2,1,0:T(8,128)(2,1)S(1)}, u32[]{:S(2)}, u32[]{:S(2)}) collective-permute-start(bf16[4,128,896]{2,1,0:T(8,128)(2,1)} %get-tuple-element.43), channel_id=1, source_target_pairs={{0,1},{1,0},{2,3},{3,2},{4,5},{5,4},{6,7},{7,6},{8,9},{9,8},{10,11... | collective-permute-start | bytes 2752520 | tf_op jit(solution)/shard_map/ppermute | solution.py:814
  412.9 79.5 %collective-permute-start.29 = (bf16[224,32,128]{2,1,0:T(8,128)(2,1)}, bf16[224,32,128]{2,1,0:T(8,128)(2,1)}, u32[]{:S(2)}, u32[]{:S(2)}) collective-permute-start(bf16[224,32,128]{2,1,0:T(8,128)(2,1)} %get-tuple-element.55), channel_id=1, source_target_pairs={{0,8},{8,0},{16,24},{24,16},{1,9},{9,1},{17,25},{25,17},{2,10},{10... | collective-permute-start | bytes 5505032 | tf_op jit(solution)/shard_map/ppermute | solution.py:780
  412.9 98.1 %collective-permute-start.26 = (bf16[224,32,128]{2,1,0:T(8,128)(2,1)}, bf16[224,32,128]{2,1,0:T(8,128)(2,1)S(1)}, u32[]{:S(2)}, u32[]{:S(2)}) collective-permute-start(bf16[224,32,128]{2,1,0:T(8,128)(2,1)} %get-tuple-element.50), channel_id=1, source_target_pairs={{0,8},{8,0},{16,24},{24,16},{1,9},{9,1},{17,25},{25,17},{2,10},{10... | collective-permute-start | bytes 5505032 | tf_op jit(solution)/shard_map/ppermute | solution.py:780
  416.1 76.4 %collective-permute-start.31 = (bf16[224,32,128]{2,1,0:T(8,128)(2,1)S(1)}, bf16[224,32,128]{2,1,0:T(8,128)(2,1)S(1)}, u32[]{:S(2)}, u32[]{:S(2)}) collective-permute-start(bf16[224,32,128]{2,1,0:T(8,128)(2,1)S(1)} %add_convert_fusion), channel_id=1, source_target_pairs={{0,16},{8,24},{16,0},{24,8},{1,17},{9,25},{17,1},{25,9},{2,18},{10... | collective-permute-start | bytes 5505032 | tf_op jit(solution)/shard_map/ppermute | solution.py:785
  417.6 11.0 %copy-start.4 = (bf16[4,128,896]{2,1,0:T(8,128)(2,1)S(1)}, bf16[4,128,896]{2,1,0:T(8,128)(2,1)}, u32[]{:S(2)}) copy-start(bf16[4,128,896]{2,1,0:T(8,128)(2,1)} %get-tuple-element.46) | copy-start | bytes 2752516
  417.6 28.5 %copy-start.5 = (bf16[4,128,896]{2,1,0:T(8,128)(2,1)S(1)}, bf16[4,128,896]{2,1,0:T(8,128)(2,1)}, u32[]{:S(2)}) copy-start(bf16[4,128,896]{2,1,0:T(8,128)(2,1)} %get-tuple-element.42) | copy-start | bytes 2752516
  427.2 83.8 %collective-permute-start.28 = (bf16[224,32,128]{2,1,0:T(8,128)(2,1)}, bf16[224,32,128]{2,1,0:T(8,128)(2,1)}, u32[]{:S(2)}, u32[]{:S(2)}) collective-permute-start(bf16[224,32,128]{2,1,0:T(8,128)(2,1)} %add_convert_fusion.1), channel_id=1, source_target_pairs={{0,16},{8,24},{16,0},{24,8},{1,17},{9,25},{17,1},{25,9},{2,18},{10... | collective-permute-start | bytes 5505032 | tf_op jit(solution)/shard_map/ppermute | solution.py:785
  445.9 11.6 %collective-permute-start.24 = (bf16[2,128,896]{2,1,0:T(8,128)(2,1)S(1)}, bf16[2,128,896]{2,1,0:T(8,128)(2,1)S(1)}, u32[]{:S(2)}, u32[]{:S(2)}) collective-permute-start(bf16[2,128,896]{2,1,0:T(8,128)(2,1)S(1)} %add_convert_fusion.2), channel_id=1, source_target_pairs={{0,2},{1,3},{2,0},{3,1},{4,6},{5,7},{6,4},{7,5},{8,10},{9,11},{10,... | collective-permute-start | bytes 1376264 | tf_op jit(solution)/shard_map/ppermute | solution.py:814
  457.5 10.7 %collective-permute-start.21 = (bf16[2,128,896]{2,1,0:T(8,128)(2,1)S(1)}, bf16[2,128,896]{2,1,0:T(8,128)(2,1)S(1)}, u32[]{:S(2)}, u32[]{:S(2)}) collective-permute-start(bf16[2,128,896]{2,1,0:T(8,128)(2,1)S(1)} %add_convert_fusion.3), channel_id=1, source_target_pairs={{0,2},{1,3},{2,0},{3,1},{4,6},{5,7},{6,4},{7,5},{8,10},{9,11},{10,... | collective-permute-start | bytes 1376264 | tf_op jit(solution)/shard_map/ppermute | solution.py:814
  468.2 10.9 %collective-permute-start.25 = (bf16[1,128,896]{2,1,0:T(8,128)(2,1)S(1)}, bf16[1,128,896]{2,1,0:T(8,128)(2,1)S(1)}, u32[]{:S(2)}, u32[]{:S(2)}) collective-permute-start(bf16[1,128,896]{2,1,0:T(8,128)(2,1)S(1)} %add_convert_fusion.5), channel_id=1, source_target_pairs={{0,4},{1,5},{2,6},{3,7},{4,0},{5,1},{6,2},{7,3},{8,12},{9,13},{10,... | collective-permute-start | bytes 688136 | tf_op jit(solution)/shard_map/ppermute | solution.py:814
  479.1 12.5 %collective-permute-start.22 = (bf16[1,128,896]{2,1,0:T(8,128)(2,1)S(1)}, bf16[1,128,896]{2,1,0:T(8,128)(2,1)S(1)}, u32[]{:S(2)}, u32[]{:S(2)}) collective-permute-start(bf16[1,128,896]{2,1,0:T(8,128)(2,1)S(1)} %add_convert_fusion.7), channel_id=1, source_target_pairs={{0,4},{1,5},{2,6},{3,7},{4,0},{5,1},{6,2},{7,3},{8,12},{9,13},{10,... | collective-permute-start | bytes 688136 | tf_op jit(solution)/shard_map/ppermute | solution.py:814
  (8 other events, 21.7 us)
